TPU v7x, 32 devices: a whole 2x2x4 slice. The times are simulated.
32 devices in a mesh: gx: 4 (over x, core), gy: 8 (over z, y).
Axes of the slice: x: 2, y: 2, z: 4, core: 2. Of those that a mesh axis runs over, the one named last changes fastest.
Arguments:
- volume: bfloat16 [16, 64, 16, 128], P('gx', 'gy'), may hold values from -6 to 6
- basin_mask: int32 [16, 64, 32], P('gx', 'gy'), may hold values 0 or 1
- w_first: bfloat16 [27, 64, 128], replicated, may hold values from -0.15625 to 0.15625
- b_first: float32 [128], replicated, may hold values from -3 to 3
- w_second: bfloat16 [27, 128, 128], replicated, may hold values from -0.109375 to 0.109375
- b_second: float32 [128], replicated, may hold values from -3 to 3
- upstream: bfloat16 [16, 64, 32, 128], P('gx', 'gy'), may hold values from -6 to 6
Outputs:
- features: bfloat16 [16, 64, 32, 128], P('gx', 'gy')
- step_first: float32 [27, 64, 128], replicated
- step_second: float32 [27, 128, 128], replicated
Inputs may be any that keep to these rules, and one draw needn't show every extreme that they name: basin_mask holds only 0 and 1.
All inputs are finite; a program needn't handle non-finite values. No bound on the sum of `basin_mask` on one device may be relied on, other than what follows from the above.
Results may differ from a plain program's by a relative error of at most 0.0054.
Values may be sent and summed in bfloat16 or wider, within the bound.
No kernel may reach another device: no remote copies, remote signals or barrier semaphores. Data moves between devices by JAX's collectives and lax.ppermute only.
A program may use at most 64 MiB of HBM per device.

v0:
```python
import jax
import jax.numpy as jnp
from jax import lax
from jax.sharding import PartitionSpec as P


def extended_2(block, sides, width):
    for axis, dim in sides:
        count = lax.axis_size(axis)
        forward = [(i, i + 1) for i in range(count - 1)]
        backward = [(target, source) for source, target in forward]
        low = lax.ppermute(
            lax.slice_in_dim(block, block.shape[dim] - width, None, axis=dim), axis, forward
        )
        high = lax.ppermute(lax.slice_in_dim(block, 0, width, axis=dim), axis, backward)
        block = jnp.concatenate([low, block, high], axis=dim)
    return block


def pad_depth(extended):
    return jnp.pad(extended, ((0, 0), (0, 0), (1, 1), (0, 0)))


def group_window(padded, tap_x, tap_y, cells_x, cells_y, cells_z):
    parts = [
        padded[tap_x : tap_x + cells_x, tap_y : tap_y + cells_y, tap_z : tap_z + cells_z]
        for tap_z in range(3)
    ]
    joined = jnp.concatenate(parts, axis=-1)
    return joined.reshape(cells_x * cells_y * cells_z, joined.shape[3])


def convolve(padded, weights, cells_x, cells_y, cells_z):
    chan_in = weights.shape[1]
    total = jnp.zeros((cells_x * cells_y * cells_z, weights.shape[2]), jnp.float32)
    for tap_x in range(3):
        for tap_y in range(3):
            window = group_window(padded, tap_x, tap_y, cells_x, cells_y, cells_z)
            first = 9 * tap_x + 3 * tap_y
            kernel = weights[first : first + 3].reshape(3 * chan_in, weights.shape[2])
            total = total + jnp.dot(window, kernel, preferred_element_type=jnp.float32)
    return total


def weight_grad(padded, grad, cells_x, cells_y, cells_z):
    pieces = []
    for tap_x in range(3):
        for tap_y in range(3):
            window = group_window(padded, tap_x, tap_y, cells_x, cells_y, cells_z)
            product = lax.dot_general(
                window, grad, (((0,), (0,)), ((), ())), preferred_element_type=jnp.float32
            )
            pieces.append(product.reshape(3, padded.shape[3], grad.shape[1]))
    return jnp.concatenate(pieces, axis=0)


def normalized_with(grad, total, count):
    return grad * lax.rsqrt(total / count + 1e-06)


def on_device(volume, basin_mask, w_first, b_first, w_second, b_second, upstream):
    cells_x, cells_y, half_z, doubled = volume.shape
    chan_in = doubled // 2
    cells_z = 2 * half_z
    chan_out = w_first.shape[2]
    field = volume.reshape(cells_x, cells_y, cells_z, chan_in)
    active = basin_mask.astype(jnp.float32).reshape(-1, 1)
    padded_in = pad_depth(extended_2(field, (("gx", 0), ("gy", 1)), 1))
    pre_first = convolve(padded_in, w_first, cells_x, cells_y, cells_z) + b_first
    sig_first = jax.nn.sigmoid(pre_first)
    hidden = (
        (pre_first * sig_first * active)
        .astype(jnp.bfloat16)
        .reshape(cells_x, cells_y, cells_z, chan_out)
    )
    padded_hidden = pad_depth(extended_2(hidden, (("gx", 0), ("gy", 1)), 1))
    pre_second = convolve(padded_hidden, w_second, cells_x, cells_y, cells_z) + b_second
    sig_second = jax.nn.sigmoid(pre_second)
    features = (
        (pre_second * sig_second * active)
        .astype(jnp.bfloat16)
        .reshape(cells_x, cells_y, cells_z, chan_out)
    )
    grad_second = (
        upstream.reshape(-1, chan_out).astype(jnp.float32)
        * active
        * sig_second
        * (1.0 + pre_second * (1.0 - sig_second))
    ).astype(jnp.bfloat16)
    dw_second = weight_grad(padded_hidden, grad_second, cells_x, cells_y, cells_z)
    flipped = jnp.transpose(w_second[::-1], (0, 2, 1))
    grad_field = grad_second.reshape(cells_x, cells_y, cells_z, chan_out)
    padded_grad = pad_depth(extended_2(grad_field, (("gx", 0), ("gy", 1)), 1))
    back_hidden = convolve(padded_grad, flipped, cells_x, cells_y, cells_z)
    grad_first = (back_hidden * active * sig_first * (1.0 + pre_first * (1.0 - sig_first))).astype(
        jnp.bfloat16
    )
    dw_first = weight_grad(padded_in, grad_first, cells_x, cells_y, cells_z)
    count_first = float(dw_first.size)
    count_second = float(dw_second.size)
    sum_first, sum_second = lax.psum((dw_first, dw_second), ("gx", "gy"))
    step_first = normalized_with(sum_first, jnp.sum(sum_first * sum_first), count_first)
    step_second = normalized_with(sum_second, jnp.sum(sum_second * sum_second), count_second)
    return (features, step_first, step_second)


def solution(mesh):
    in_specs = (
        P("gx", "gy", None, None),
        P("gx", "gy", None),
        P(),
        P(),
        P(),
        P(),
        P("gx", "gy", None, None),
    )
    out_specs = (P("gx", "gy", None, None), P(), P())
    return jax.shard_map(
        on_device, mesh=mesh, in_specs=in_specs, out_specs=out_specs, check_vma=False
    )
```

profile of v0, /device:TPU:0, one launch (start us, length us, event | category | flops | bytes accessed | tf_op | source)
XLA Modules:
  0.0 280.9 jit_solution(11516559743100319684)
XLA Ops:
  8.2 2.4 collective-permute-start
  10.7 1.4 collective-permute-start.1
  12.1 2.2 fusion.62
  15.1 1.3 copy.31
  16.6 4.2 %collective-permute-start.2 = (bf16[6,1,32,64]{3,2,1,0:T(8,128)(2,1)S(1)}, bf16[6,1,32,64]{3,2,1,0:T(8,128)(2,1)S(1)}, u32[]{:S(2)}, u32[]{:S(2)}) collective-permute-start(bf16[6,1,32,64]{3,2,1,0:T(8,128)(2,1)S(1)} %get-tuple-element.116), channel_id=1, source_target_pairs={{0,1},{1,2},{2,3},{3,4},{4,5},{5,6},{6,7},{8,9},{9,10},{10,11},{11... | collective-permute-start | bytes 73736 | tf_op jit(solution)/shard_map/ppermute | solution.py:12
  20.8 1.3 collective-permute-start.3
  24.0 2.9 %collective-permute-done.3 = bf16[6,1,32,64]{3,2,1,0:T(8,128)(2,1)S(1)} collective-permute-done((bf16[6,1,32,64]{3,2,1,0:T(8,128)(2,1)S(1)}, bf16[6,1,32,64]{3,2,1,0:T(8,128)(2,1)S(1)}, u32[]{:S(2)}, u32[]{:S(2)}) %collective-permute-start.3) | collective-permute-done | bytes 24608 | tf_op jit(solution)/shard_map/ppermute | solution.py:15
  32.9 1.1 multiply_convert_fusion.1
  34.0 3.0 %collective-permute-start.4 = (bf16[1,8,32,128]{3,2,1,0:T(8,128)(2,1)S(1)}, bf16[1,8,32,128]{3,2,1,0:T(8,128)(2,1)S(1)}, u32[]{:S(2)}, u32[]{:S(2)}) collective-permute-start(bf16[1,8,32,128]{3,2,1,0:T(8,128)(2,1)S(1)} %bitcast.334), channel_id=1, source_target_pairs={{0,8},{8,16},{16,24},{1,9},{9,17},{17,25},{2,10},{10,18},{18,26},{... | collective-permute-start | bytes 196616 | tf_op jit(solution)/shard_map/ppermute | solution.py:12
  37.0 1.3 collective-permute-start.5
  39.3 3.5 %collective-permute-done.5 = bf16[1,8,32,128]{3,2,1,0:T(8,128)(2,1)S(1)} collective-permute-done((bf16[1,8,32,128]{3,2,1,0:T(8,128)(2,1)S(1)}, bf16[1,8,32,128]{3,2,1,0:T(8,128)(2,1)S(1)}, u32[]{:S(2)}, u32[]{:S(2)}) %collective-permute-start.5) | collective-permute-done | bytes 65568 | tf_op jit(solution)/shard_map/ppermute | solution.py:15
  43.5 5.0 %collective-permute-start.6 = (bf16[6,1,32,128]{3,2,1,0:T(8,128)(2,1)}, bf16[6,1,32,128]{3,2,1,0:T(8,128)(2,1)}, u32[]{:S(2)}, u32[]{:S(2)}) collective-permute-start(bf16[6,1,32,128]{3,2,1,0:T(8,128)(2,1)} %get-tuple-element.110), channel_id=1, source_target_pairs={{0,1},{1,2},{2,3},{3,4},{4,5},{5,6},{6,7},{8,9},{9,10},{10,11},{11... | collective-permute-start | bytes 147464 | tf_op jit(solution)/shard_map/ppermute | solution.py:12
  48.4 1.5 collective-permute-start.7
  49.9 1.0 fusion.57
  51.0 2.0 copy.30
  62.5 1.1 select_maximum_fusion.4
  63.6 1.7 fusion.64
  66.4 1.2 copy.40
  67.6 2.1 fusion.76
  69.6 1.1 fusion.14
  70.7 1.2 copy.41
  72.0 1.2 copy.42
  73.2 1.1 pad_maximum_fusion.6
  74.4 1.2 copy.43
  75.7 1.2 copy.45
  76.8 1.2 pad_maximum_fusion.9
  78.1 1.2 copy.46
  79.3 2.3 copy.47
  81.6 1.7 convolution_add_fusion.15
  87.6 1.3 fusion.42
  89.5 1.0 convolution_dynamic-update-slice_fusion.8
  90.6 1.2 copy.44
  91.7 4.7 %collective-permute-start.8 = (bf16[1,8,32,128]{3,2,1,0:T(8,128)(2,1)}, bf16[1,8,32,128]{3,2,1,0:T(8,128)(2,1)S(1)}, u32[]{:S(2)}, u32[]{:S(2)}) collective-permute-start(bf16[1,8,32,128]{3,2,1,0:T(8,128)(2,1)} %bitcast.45), channel_id=1, source_target_pairs={{0,8},{8,16},{16,24},{1,9},{9,17},{17,25},{2,10},{10,18},{18,26},{... | collective-permute-start | bytes 196616 | tf_op jit(solution)/shard_map/ppermute | solution.py:12
  96.4 1.5 collective-permute-start.9
  98.0 1.1 convolution_dynamic-update-slice_fusion.7
  99.0 1.0 convolution_dynamic-update-slice_fusion.6
  100.1 1.0 convolution_dynamic-update-slice_fusion.5
  101.1 1.1 convolution_dynamic-update-slice_fusion.4
  102.2 1.0 convolution_dynamic-update-slice_fusion.3
  103.2 1.1 convolution_dynamic-update-slice_fusion.2
  104.3 1.0 convolution_dynamic-update-slice_fusion.1
  105.7 4.3 %collective-permute-start.10 = (bf16[6,1,32,128]{3,2,1,0:T(8,128)(2,1)S(1)}, bf16[6,1,32,128]{3,2,1,0:T(8,128)(2,1)S(1)}, u32[]{:S(2)}, u32[]{:S(2)}) collective-permute-start(bf16[6,1,32,128]{3,2,1,0:T(8,128)(2,1)S(1)} %get-tuple-element.106), channel_id=1, source_target_pairs={{0,1},{1,2},{2,3},{3,4},{4,5},{5,6},{6,7},{8,9},{9,10},{10,11},{11... | collective-permute-start | bytes 147464 | tf_op jit(solution)/shard_map/ppermute | solution.py:12
  110.0 1.3 collective-permute-start.11
  111.3 1.1 convolution_dynamic-update-slice_fusion
  112.3 4.1 %collective-permute-done.11 = bf16[6,1,32,128]{3,2,1,0:T(8,128)(2,1)S(1)} collective-permute-done((bf16[6,1,32,128]{3,2,1,0:T(8,128)(2,1)S(1)}, bf16[6,1,32,128]{3,2,1,0:T(8,128)(2,1)S(1)}, u32[]{:S(2)}, u32[]{:S(2)}) %collective-permute-start.11) | collective-permute-done | bytes 49184 | tf_op jit(solution)/shard_map/ppermute | solution.py:15
  128.5 138.2 %all-reduce.6.cloned.1.call-done = (f32[27,64,128]{2,1,0:T(8,128)}, f32[27,128,128]{2,1,0:T(8,128)}) async-done(((f32[27,64,128]{2,1,0:T(8,128)}, f32[27,128,128]{2,1,0:T(8,128)}), (f32[27,64,128]{2,1,0:T(8,128)}, f32[27,128,128]{2,1,0:T(8,128)})) %all-reduce.6.cloned.1.call-update) | async-done | bytes 2654224 | tf_op jit(solution)/shard_map/psum | solution.py:101
  266.7 2.7 multiply_reduce_fusion
  270.1 1.3 broadcast_multiply_fusion
  (226 shorter events, 40.8 us)
Async XLA Ops:
  7.2 7.8 %copy-start.37 = (bf16[4,8,16,128]{3,2,1,0:T(8,128)(2,1)S(1)}, bf16[4,8,16,128]{3,2,1,0:T(8,128)(2,1)}, u32[]{:S(2)}) copy-start(bf16[4,8,16,128]{3,2,1,0:T(8,128)(2,1)} %param.7) | copy-start | bytes 393220
  7.2 7.1 %copy-start.38 = (bf16[27,64,128]{2,1,0:T(8,128)(2,1)S(1)}, bf16[27,64,128]{2,1,0:T(8,128)(2,1)}, u32[]{:S(2)}) copy-start(bf16[27,64,128]{2,1,0:T(8,128)(2,1)} %param.9) | copy-start | bytes 1327108
  7.2 259.5 %all-reduce.6.cloned.1.call-start = ((), (), s32[]{:S(2)}) async-start(), calls=%async_computation | async-start | bytes 5308416 | tf_op jit(solution)/shard_map/psum | solution.py:101
  8.2 8.3 %collective-permute-start = (bf16[1,8,32,64]{3,2,1,0:T(8,128)(2,1)S(1)}, bf16[1,8,32,64]{3,2,1,0:T(8,128)(2,1)S(1)}, u32[]{:S(2)}, u32[]{:S(2)}) collective-permute-start(bf16[1,8,32,64]{3,2,1,0:T(8,128)(2,1)S(1)} %slice.487), channel_id=1, source_target_pairs={{0,8},{8,16},{16,24},{1,9},{9,17},{17,25},{2,10},{10,18},{18,26},{... | collective-permute-start | bytes 98312 | tf_op jit(solution)/shard_map/ppermute | solution.py:12
  10.6 4.6 %copy-start.4 = (bf16[27,128,128]{2,1,0:T(8,128)(2,1)S(1)}, bf16[27,128,128]{2,1,0:T(8,128)(2,1)}, u32[]{:S(2)}) copy-start(bf16[27,128,128]{2,1,0:T(8,128)(2,1)} %param.11) | copy-start | bytes 2654212
  10.7 5.9 %collective-permute-start.1 = (bf16[1,8,32,64]{3,2,1,0:T(8,128)(2,1)S(1)}, bf16[1,8,32,64]{3,2,1,0:T(8,128)(2,1)S(1)}, u32[]{:S(2)}, u32[]{:S(2)}) collective-permute-start(bf16[1,8,32,64]{3,2,1,0:T(8,128)(2,1)S(1)} %slice.489), channel_id=1, source_target_pairs={{8,0},{16,8},{24,16},{9,1},{17,9},{25,17},{10,2},{18,10},{26,18},{... | collective-permute-start | bytes 98312 | tf_op jit(solution)/shard_map/ppermute | solution.py:15
  16.5 6.8 %copy-start.58 = (s32[4,8,32]{2,1,0:T(8,128)S(1)}, s32[4,8,32]{2,1,0:T(8,128)}, u32[]{:S(2)}) copy-start(s32[4,8,32]{2,1,0:T(8,128)} %param.8) | copy-start | bytes 12292
  16.6 7.4 %collective-permute-start.2 = (bf16[6,1,32,64]{3,2,1,0:T(8,128)(2,1)S(1)}, bf16[6,1,32,64]{3,2,1,0:T(8,128)(2,1)S(1)}, u32[]{:S(2)}, u32[]{:S(2)}) collective-permute-start(bf16[6,1,32,64]{3,2,1,0:T(8,128)(2,1)S(1)} %get-tuple-element.116), channel_id=1, source_target_pairs={{0,1},{1,2},{2,3},{3,4},{4,5},{5,6},{6,7},{8,9},{9,10},{10,11},{11... | collective-permute-start | bytes 73736 | tf_op jit(solution)/shard_map/ppermute | solution.py:12
  20.8 6.0 %collective-permute-start.3 = (bf16[6,1,32,64]{3,2,1,0:T(8,128)(2,1)S(1)}, bf16[6,1,32,64]{3,2,1,0:T(8,128)(2,1)S(1)}, u32[]{:S(2)}, u32[]{:S(2)}) collective-permute-start(bf16[6,1,32,64]{3,2,1,0:T(8,128)(2,1)S(1)} %get-tuple-element.117), channel_id=1, source_target_pairs={{1,0},{2,1},{3,2},{4,3},{5,4},{6,5},{7,6},{9,8},{10,9},{11,10},{12... | collective-permute-start | bytes 73736 | tf_op jit(solution)/shard_map/ppermute | solution.py:15
  23.3 8.1 %copy-start.15 = (bf16[1024,64]{1,0:T(8,128)(2,1)}, bf16[1024,64]{1,0:T(8,128)(2,1)S(1)}, u32[]{:S(2)}) copy-start(bf16[1024,64]{1,0:T(8,128)(2,1)S(1)} %concatenate.198) | copy-start | bytes 393220
  28.4 1.3 copy-start.3
  29.7 3.0 %copy-start.17 = (bf16[4,8,32,192]{3,2,1,0:T(8,128)(2,1)}, bf16[4,8,32,192]{3,2,1,0:T(8,128)(2,1)S(1)}, u32[]{:S(2)}) copy-start(bf16[4,8,32,192]{3,2,1,0:T(8,128)(2,1)S(1)} %get-tuple-element.112) | copy-start | bytes 1179652
  32.9 5.5 %copy-start.5 = (bf16[27,128,128]{2,1,0:T(8,128)(2,1)S(1)}, bf16[27,128,128]{2,1,0:T(8,128)(2,1)}, u32[]{:S(2)}) copy-start(bf16[27,128,128]{2,1,0:T(8,128)(2,1)} %reverse_bitcast_fusion) | copy-start | bytes 2654212
  34.0 15.9 %copy-start.16 = (bf16[1024,64]{1,0:T(8,128)(2,1)S(1)}, bf16[1024,64]{1,0:T(8,128)(2,1)}, u32[]{:S(2)}) copy-start(bf16[1024,64]{1,0:T(8,128)(2,1)} %copy-done.15) | copy-start | bytes 393220
  34.0 5.3 %collective-permute-start.4 = (bf16[1,8,32,128]{3,2,1,0:T(8,128)(2,1)S(1)}, bf16[1,8,32,128]{3,2,1,0:T(8,128)(2,1)S(1)}, u32[]{:S(2)}, u32[]{:S(2)}) collective-permute-start(bf16[1,8,32,128]{3,2,1,0:T(8,128)(2,1)S(1)} %bitcast.334), channel_id=1, source_target_pairs={{0,8},{8,16},{16,24},{1,9},{9,17},{17,25},{2,10},{10,18},{18,26},{... | collective-permute-start | bytes 196616 | tf_op jit(solution)/shard_map/ppermute | solution.py:12
  37.0 5.8 %collective-permute-start.5 = (bf16[1,8,32,128]{3,2,1,0:T(8,128)(2,1)S(1)}, bf16[1,8,32,128]{3,2,1,0:T(8,128)(2,1)S(1)}, u32[]{:S(2)}, u32[]{:S(2)}) collective-permute-start(bf16[1,8,32,128]{3,2,1,0:T(8,128)(2,1)S(1)} %bitcast.333), channel_id=1, source_target_pairs={{8,0},{16,8},{24,16},{9,1},{17,9},{25,17},{10,2},{18,10},{26,18},{... | collective-permute-start | bytes 196616 | tf_op jit(solution)/shard_map/ppermute | solution.py:15
  43.5 17.2 %collective-permute-start.6 = (bf16[6,1,32,128]{3,2,1,0:T(8,128)(2,1)}, bf16[6,1,32,128]{3,2,1,0:T(8,128)(2,1)}, u32[]{:S(2)}, u32[]{:S(2)}) collective-permute-start(bf16[6,1,32,128]{3,2,1,0:T(8,128)(2,1)} %get-tuple-element.110), channel_id=1, source_target_pairs={{0,1},{1,2},{2,3},{3,4},{4,5},{5,6},{6,7},{8,9},{9,10},{10,11},{11... | collective-permute-start | bytes 147464 | tf_op jit(solution)/shard_map/ppermute | solution.py:12
  48.4 12.2 %collective-permute-start.7 = (bf16[6,1,32,128]{3,2,1,0:T(8,128)(2,1)}, bf16[6,1,32,128]{3,2,1,0:T(8,128)(2,1)}, u32[]{:S(2)}, u32[]{:S(2)}) collective-permute-start(bf16[6,1,32,128]{3,2,1,0:T(8,128)(2,1)} %get-tuple-element.111), channel_id=1, source_target_pairs={{1,0},{2,1},{3,2},{4,3},{5,4},{6,5},{7,6},{9,8},{10,9},{11,10},{12... | collective-permute-start | bytes 147464 | tf_op jit(solution)/shard_map/ppermute | solution.py:15
  54.0 1.9 copy-start.19
  56.9 2.8 %copy-start.18 = (bf16[4,8,32,192]{3,2,1,0:T(8,128)(2,1)S(1)}, bf16[4,8,32,192]{3,2,1,0:T(8,128)(2,1)}, u32[]{:S(2)}) copy-start(bf16[4,8,32,192]{3,2,1,0:T(8,128)(2,1)} %copy-done.17) | copy-start | bytes 1179652
  70.7 1.3 copy-start.2
  71.9 1.3 copy-start.34
  74.4 1.2 copy-start.36
  79.3 4.1 %copy-start.49 = (bf16[3,128,128]{2,1,0:T(8,128)(2,1)S(1)}, bf16[3,128,128]{2,1,0:T(8,128)(2,1)}, u32[]{:S(2)}) copy-start(bf16[3,128,128]{2,1,0:T(8,128)(2,1)} %get-tuple-element.20) | copy-start | bytes 294916
  81.6 2.1 copy-start.48
  85.4 1.1 copy-start.1
  85.4 1.1 copy-start.43
  86.0 1.2 copy-start.35
  87.6 1.9 copy-start.7
  88.8 9.1 %copy-start.8 = (bf16[1024,384]{0,1:T(8,128)(2,1)S(1)}, bf16[1024,384]{0,1:T(8,128)(2,1)}, u32[]{:S(2)}) copy-start(bf16[1024,384]{0,1:T(8,128)(2,1)} %copy.41) | copy-start | bytes 2359300
  90.6 8.5 %copy-start.9 = (bf16[1024,384]{0,1:T(8,128)(2,1)S(1)}, bf16[1024,384]{0,1:T(8,128)(2,1)}, u32[]{:S(2)}) copy-start(bf16[1024,384]{0,1:T(8,128)(2,1)} %copy.42) | copy-start | bytes 2359300
  91.7 8.3 %copy-start.11 = (bf16[1024,384]{0,1:T(8,128)(2,1)S(1)}, bf16[1024,384]{0,1:T(8,128)(2,1)}, u32[]{:S(2)}) copy-start(bf16[1024,384]{0,1:T(8,128)(2,1)} %copy.43) | copy-start | bytes 2359300
  91.7 13.9 %collective-permute-start.8 = (bf16[1,8,32,128]{3,2,1,0:T(8,128)(2,1)}, bf16[1,8,32,128]{3,2,1,0:T(8,128)(2,1)S(1)}, u32[]{:S(2)}, u32[]{:S(2)}) collective-permute-start(bf16[1,8,32,128]{3,2,1,0:T(8,128)(2,1)} %bitcast.45), channel_id=1, source_target_pairs={{0,8},{8,16},{16,24},{1,9},{9,17},{17,25},{2,10},{10,18},{18,26},{... | collective-permute-start | bytes 196616 | tf_op jit(solution)/shard_map/ppermute | solution.py:12
  96.4 9.2 %collective-permute-start.9 = (bf16[1,8,32,128]{3,2,1,0:T(8,128)(2,1)}, bf16[1,8,32,128]{3,2,1,0:T(8,128)(2,1)S(1)}, u32[]{:S(2)}, u32[]{:S(2)}) collective-permute-start(bf16[1,8,32,128]{3,2,1,0:T(8,128)(2,1)} %bitcast.332), channel_id=1, source_target_pairs={{8,0},{16,8},{24,16},{9,1},{17,9},{25,17},{10,2},{18,10},{26,18},{... | collective-permute-start | bytes 196616 | tf_op jit(solution)/shard_map/ppermute | solution.py:15
  98.0 3.2 %copy-start.14 = (bf16[384,1024]{1,0:T(8,128)(2,1)S(1)}, bf16[384,1024]{1,0:T(8,128)(2,1)}, u32[]{:S(2)}) copy-start(bf16[384,1024]{1,0:T(8,128)(2,1)} %copy.44) | copy-start | bytes 2359300
  99.0 3.2 %copy-start.10 = (bf16[1024,384]{0,1:T(8,128)(2,1)S(1)}, bf16[1024,384]{0,1:T(8,128)(2,1)}, u32[]{:S(2)}) copy-start(bf16[1024,384]{0,1:T(8,128)(2,1)} %copy.45) | copy-start | bytes 2359300
  100.1 3.2 %copy-start.13 = (bf16[1024,384]{0,1:T(8,128)(2,1)S(1)}, bf16[1024,384]{0,1:T(8,128)(2,1)}, u32[]{:S(2)}) copy-start(bf16[1024,384]{0,1:T(8,128)(2,1)} %copy.46) | copy-start | bytes 2359300
  101.1 3.2 %copy-start.12 = (bf16[1024,384]{0,1:T(8,128)(2,1)S(1)}, bf16[1024,384]{0,1:T(8,128)(2,1)}, u32[]{:S(2)}) copy-start(bf16[1024,384]{0,1:T(8,128)(2,1)} %copy.47) | copy-start | bytes 2359300
  105.7 6.6 %collective-permute-start.10 = (bf16[6,1,32,128]{3,2,1,0:T(8,128)(2,1)S(1)}, bf16[6,1,32,128]{3,2,1,0:T(8,128)(2,1)S(1)}, u32[]{:S(2)}, u32[]{:S(2)}) collective-permute-start(bf16[6,1,32,128]{3,2,1,0:T(8,128)(2,1)S(1)} %get-tuple-element.106), channel_id=1, source_target_pairs={{0,1},{1,2},{2,3},{3,4},{4,5},{5,6},{6,7},{8,9},{9,10},{10,11},{11... | collective-permute-start | bytes 147464 | tf_op jit(solution)/shard_map/ppermute | solution.py:12
  110.0 6.4 %collective-permute-start.11 = (bf16[6,1,32,128]{3,2,1,0:T(8,128)(2,1)S(1)}, bf16[6,1,32,128]{3,2,1,0:T(8,128)(2,1)S(1)}, u32[]{:S(2)}, u32[]{:S(2)}) collective-permute-start(bf16[6,1,32,128]{3,2,1,0:T(8,128)(2,1)S(1)} %get-tuple-element.107), channel_id=1, source_target_pairs={{1,0},{2,1},{3,2},{4,3},{5,4},{6,5},{7,6},{9,8},{10,9},{11,10},{12... | collective-permute-start | bytes 147464 | tf_op jit(solution)/shard_map/ppermute | solution.py:15
  124.1 1.3 copy-start.28
  124.6 1.4 copy-start.25
  124.6 1.6 copy-start.24
  125.4 1.1 copy-start.23
  125.7 1.1 copy-start.22
  125.9 1.1 copy-start.21
  266.7 3.4 %copy-start = (f32[27,128,128]{2,1,0:T(8,128)S(1)}, f32[27,128,128]{2,1,0:T(8,128)}, u32[]{:S(2)}) copy-start(f32[27,128,128]{2,1,0:T(8,128)} %get-tuple-element.4) | copy-start | bytes 5308420
  270.1 1.5 copy-start.6
  (29 other events, 27.6 us)
Sparse Core Ops, SparseCore 0:
  128.7 138.0 all-reduce.5
where the time goes:
time: 282 us; the launch traced here: 281 us
  waiting for transfers between devices  149 us (53%)
  local copies, waits for them, and re-layouts  40.8 us (14%)
  starting transfers between devices  31.9 us (11%)
  matrix products  25.8 us (9%)
  other arithmetic  17.3 us (6%)
  between operations  16.5 us (6%)
    psum x1, waiting for transfers between devices, on_device(): sum_first, sum_second = lax.psum((dw_first, dw_second), ('gx', 'gy'))  138 us
    ppermute x6, starting transfers between devices, extended_2(): lax.ppermute(lax.slice_in_dim(block, block.shape[dim] - width, None, axis...  23.6 us
    dot_general x27, matrix products, convolve(): total = total + jnp.dot(window, kernel, preferred_element_type=jnp.float32)  14.1 us
    dot_general x18, matrix products, weight_grad(): lax.dot_general(window, grad, (((0,), (0,)), ((), ())), preferred_element...  11.8 us
    dot_general x10, local copies, waits for them, and re-layouts, weight_grad(): lax.dot_general(window, grad, (((0,), (0,)), ((), ())), preferred_element...  10.8 us
    ppermute x6, waiting for transfers between devices, extended_2(): lax.ppermute(lax.slice_in_dim(block, 0, width, axis=dim), axis, backward)  10.4 us
    reshape x8, local copies, waits for them, and re-layouts, group_window(): return joined.reshape(cells_x * cells_y * cells_z, joined.shape[3])  9.72 us
    ppermute x6, starting transfers between devices, extended_2(): lax.ppermute(lax.slice_in_dim(block, 0, width, axis=dim), axis, backward)  8.27 us
  transfers between devices with their start and end apart: 13, of which 4 were waited for; matrix products, arithmetic and copies ran while one was open for 9% of the time, Pallas kernels for 0%

commit v1 on v0

--- a/solution.py
+++ b/solution.py
@@ -54,6 +54,54 @@
     return jnp.concatenate(pieces, axis=0)
 
 
+def bit_levels(axes):
+    levels = []
+    for axis in axes:
+        size = lax.axis_size(axis)
+        bit = 1
+        while bit < size:
+            levels.append((axis, bit))
+            bit *= 2
+    return levels
+
+
+def swap_with(part, axis, bit):
+    return lax.ppermute(part, axis, [(i, i ^ bit) for i in range(lax.axis_size(axis))])
+
+
+def side_of(axis, bit):
+    return lax.rem(lax.axis_index(axis) // bit, 2)
+
+
+def halves_summed(part, levels):
+    for axis, bit in levels:
+        half = part.shape[0] // 2
+        side = side_of(axis, bit)
+        sent = lax.dynamic_slice_in_dim(part, (1 - side) * half, half, 0).astype(jnp.bfloat16)
+        kept = lax.dynamic_slice_in_dim(part, side * half, half, 0)
+        part = kept + swap_with(sent, axis, bit).astype(jnp.float32)
+    return part
+
+
+def halves_joined(part, levels):
+    for axis, bit in reversed(levels):
+        other = swap_with(part, axis, bit)
+        part = jnp.where(
+            side_of(axis, bit) == 0,
+            jnp.concatenate([part, other], axis=0),
+            jnp.concatenate([other, part], axis=0),
+        )
+    return part
+
+
+def summed_everywhere(rows, axes):
+    levels = bit_levels(axes)
+    pieces = 2 ** len(levels)
+    padded = jnp.pad(rows, ((0, -rows.shape[0] % pieces), (0, 0)))
+    summed = halves_summed(padded, levels).astype(jnp.bfloat16)
+    return halves_joined(summed, levels)[: rows.shape[0]].astype(jnp.float32)
+
+
 def normalized_with(grad, total, count):
     return grad * lax.rsqrt(total / count + 1e-06)
 
@@ -98,7 +146,11 @@
     dw_first = weight_grad(padded_in, grad_first, cells_x, cells_y, cells_z)
     count_first = float(dw_first.size)
     count_second = float(dw_second.size)
-    sum_first, sum_second = lax.psum((dw_first, dw_second), ("gx", "gy"))
+    rows_first = dw_first.shape[0] * dw_first.shape[1]
+    rows = jnp.concatenate([dw_first.reshape(-1, chan_out), dw_second.reshape(-1, chan_out)], axis=0)
+    sums = summed_everywhere(rows, ("gx", "gy"))
+    sum_first = sums[:rows_first].reshape(dw_first.shape)
+    sum_second = sums[rows_first:].reshape(dw_second.shape)
     step_first = normalized_with(sum_first, jnp.sum(sum_first * sum_first), count_first)
     step_second = normalized_with(sum_second, jnp.sum(sum_second * sum_second), count_second)
     return (features, step_first, step_second)

time: 282 us -> 185 us (0.66)
  waiting for transfers between devices: 149 us -> 36.5 us
  starting transfers between devices: 31.9 us -> 56.3 us
  between operations: 16.5 us -> 3.32 us
  other arithmetic: 17.3 us -> 22.1 us
  matrix products: 25.8 us -> 21.2 us
  local copies, waits for them, and re-layouts: 40.8 us -> 43.9 us
    psum x1 -> x0, waiting for transfers between devices: 138 us -> none  [on_device(): sum_first, sum_second = lax.psum((dw_first, dw_second), ('gx', 'gy'))]
    ppermute x0 -> x10, waiting for transfers between devices: none -> 36.3 us  [swap_with(): lax.ppermute(part, axis, [(i, i ^ bit) for i in range(lax.axis_size(axis))])]
    ppermute x0 -> x10, starting transfers between devices: none -> 20.1 us  [swap_with(): lax.ppermute(part, axis, [(i, i ^ bit) for i in range(lax.axis_size(axis))])]
    ppermute x6, waiting for transfers between devices: 10.4 us -> 0.02 us  [extended_2(): lax.ppermute(lax.slice_in_dim(block, 0, width, axis=dim), axis, backward)]
    ppermute x6, starting transfers between devices: 23.6 us -> 28.2 us  [extended_2(): lax.ppermute(lax.slice_in_dim(block, block.shape[dim] - width, None, axis...]
    dot_general x18, matrix products: 11.8 us -> 7.95 us  [weight_grad(): lax.dot_general(window, grad, (((0,), (0,)), ((), ())), preferred_element...]
    unnamed x131 -> x137, local copies, waits for them, and re-layouts: 7.53 us -> 8.56 us
  transfers between devices with their start and end apart: 13 -> 22, of which waited for: 4 -> 11; matrix products, arithmetic and copies ran while one was open for 9% -> 14% of each run, Pallas kernels for 0% -> 0%
where the time goes in v1:
time: 185 us; the launch traced here: 183 us
  starting transfers between devices  56.3 us (30%)
  local copies, waits for them, and re-layouts  43.9 us (24%)
  waiting for transfers between devices  36.5 us (20%)
  other arithmetic  22.1 us (12%)
  matrix products  21.2 us (11%)
  between operations  3.32 us (2%)
    ppermute x10, waiting for transfers between devices, swap_with(): lax.ppermute(part, axis, [(i, i ^ bit) for i in range(lax.axis_size(axis))])  36.3 us
    ppermute x6, starting transfers between devices, extended_2(): lax.ppermute(lax.slice_in_dim(block, block.shape[dim] - width, None, axis...  28.2 us
    ppermute x10, starting transfers between devices, swap_with(): lax.ppermute(part, axis, [(i, i ^ bit) for i in range(lax.axis_size(axis))])  20.1 us
    dot_general x27, matrix products, convolve(): total = total + jnp.dot(window, kernel, preferred_element_type=jnp.float32)  13.3 us
    dot_general x10, local copies, waits for them, and re-layouts, weight_grad(): lax.dot_general(window, grad, (((0,), (0,)), ((), ())), preferred_element...  11.9 us
    reshape x8, local copies, waits for them, and re-layouts, group_window(): return joined.reshape(cells_x * cells_y * cells_z, joined.shape[3])  10.6 us
    unnamed x137, local copies, waits for them, and re-layouts  8.56 us
    ppermute x6, starting transfers between devices, extended_2(): lax.ppermute(lax.slice_in_dim(block, 0, width, axis=dim), axis, backward)  7.98 us
  transfers between devices with their start and end apart: 22, of which 11 were waited for; matrix products, arithmetic and copies ran while one was open for 14% of the time, Pallas kernels for 0%

profile of v1, /device:TPU:0, one launch (start us, length us, event | category | flops | bytes accessed | tf_op | source)
XLA Modules:
  0.0 183.3 jit_solution(7137353281088814810)
XLA Ops:
  1.6 2.4 %collective-permute-start = (bf16[1,8,32,64]{3,2,1,0:T(8,128)(2,1)S(1)}, bf16[1,8,32,64]{3,2,1,0:T(8,128)(2,1)S(1)}, u32[]{:S(2)}, u32[]{:S(2)}) collective-permute-start(bf16[1,8,32,64]{3,2,1,0:T(8,128)(2,1)S(1)} %slice.493), channel_id=1, source_target_pairs={{0,8},{8,16},{16,24},{1,9},{9,17},{17,25},{2,10},{10,18},{18,26},{... | collective-permute-start | bytes 98312 | tf_op jit(solution)/shard_map/ppermute | solution.py:12
  4.1 1.4 collective-permute-start.1
  5.5 2.2 %fusion.67 = (bf16[3,128,128]{2,1,0:T(8,128)(2,1)}, bf16[3,128,128]{2,1,0:T(8,128)(2,1)}, bf16[3,128,128]{2,1,0:T(8,128)(2,1)}, bf16[3,128,128]{2,1,0:T(8,128)(2...) fusion(bf16[27,128,128]{2,1,0:T(8,128)(2,1)} %param.11), kind=kLoop, calls=%fused_computation.193 | loop fusion | bytes 1769472 | tf_op jit(solution)/shard_map/slice | solution.py:40
  8.6 1.3 copy.31
  10.0 1.3 collective-permute-start.3
  11.3 4.9 %collective-permute-start.2 = (bf16[6,1,32,64]{3,2,1,0:T(8,128)(2,1)S(1)}, bf16[6,1,32,64]{3,2,1,0:T(8,128)(2,1)S(1)}, u32[]{:S(2)}, u32[]{:S(2)}) collective-permute-start(bf16[6,1,32,64]{3,2,1,0:T(8,128)(2,1)S(1)} %get-tuple-element.114), channel_id=1, source_target_pairs={{0,1},{1,2},{2,3},{3,4},{4,5},{5,6},{6,7},{8,9},{9,10},{10,11},{11... | collective-permute-start | bytes 73736 | tf_op jit(solution)/shard_map/ppermute | solution.py:12
  26.4 1.3 collective-permute-start.5
  27.7 4.9 %collective-permute-start.4 = (bf16[1,8,32,128]{3,2,1,0:T(8,128)(2,1)}, bf16[1,8,32,128]{3,2,1,0:T(8,128)(2,1)S(1)}, u32[]{:S(2)}, u32[]{:S(2)}) collective-permute-start(bf16[1,8,32,128]{3,2,1,0:T(8,128)(2,1)} %bitcast.19), channel_id=1, source_target_pairs={{0,8},{8,16},{16,24},{1,9},{9,17},{17,25},{2,10},{10,18},{18,26},{... | collective-permute-start | bytes 196616 | tf_op jit(solution)/shard_map/ppermute | solution.py:12
  34.3 1.3 collective-permute-start.7
  35.6 5.6 %collective-permute-start.6 = (bf16[6,1,32,128]{3,2,1,0:T(8,128)(2,1)}, bf16[6,1,32,128]{3,2,1,0:T(8,128)(2,1)}, u32[]{:S(2)}, u32[]{:S(2)}) collective-permute-start(bf16[6,1,32,128]{3,2,1,0:T(8,128)(2,1)} %get-tuple-element.108), channel_id=1, source_target_pairs={{0,1},{1,2},{2,3},{3,4},{4,5},{5,6},{6,7},{8,9},{9,10},{10,11},{11... | collective-permute-start | bytes 147464 | tf_op jit(solution)/shard_map/ppermute | solution.py:12
  41.2 2.1 %fusion.62 = bf16[192,1024]{0,1:T(8,128)(2,1)} fusion(bf16[1024,64]{1,0:T(8,128)(2,1)} %bitcast.293, bf16[1024,64]{1,0:T(8,128)(2,1)} %copy-done.17, bf16[1024,64]{1,0:T(8,128)(2,1)} %bitcast.295), kind=kLoop, calls=%fused_computation.179 | loop fusion | flops 1179648 | bytes 786432 | tf_op jit(solution)/shard_map/dot_general | solution.py:50
  43.3 2.0 %copy.30 = bf16[192,1024]{1,0:T(8,128)(2,1)} copy(bf16[192,1024]{0,1:T(8,128)(2,1)} %bitcast.271) | data formatting | bytes 786432 | tf_op jit(solution)/shard_map/dot_general | solution.py:50
  54.0 1.9 %fusion.69 = (bf16[4,8,32,128]{3,2,1,0:T(8,128)(2,1)}, bf16[4,8,32,128]{3,2,1,0:T(8,128)(2,1)S(1)}, bf16[4,8,32,128]{3,2,1,0:T(8,128)(2,1)S(1)}, bf16[4,8,32,128...) fusion(bf16[6,10,34,128]{3,2,1,0:T(8,128)(2,1)S(1)} %select_max, ...), kind=kLoop, calls=%fused_computation.195 | loop fusion | bytes 9437184 | tf_op jit(solution)/shard_map/slice | solution.py:26
  62.2 1.2 copy.41
  63.5 1.2 copy.42
  64.7 1.2 pad_maximum_fusion.6
  67.2 1.2 copy.45
  68.4 1.2 pad_maximum_fusion.9
  70.8 2.3 %copy.47 = bf16[1024,384]{0,1:T(8,128)(2,1)} copy(bf16[1024,384]{1,0:T(8,128)(2,1)} %bitcast.254) | data formatting | bytes 1572864 | tf_op jit(solution)/shard_map/reshape | solution.py:30
  73.1 1.7 convolution_add_fusion.15
  80.0 1.2 fusion.47
  81.6 2.3 %copy.44 = bf16[384,1024]{1,0:T(8,128)(2,1)} copy(bf16[384,1024]{0,1:T(8,128)(2,1)} %fusion.48) | data formatting | bytes 1572864 | tf_op jit(solution)/shard_map/dot_general | solution.py:50
  83.9 1.4 collective-permute-start.9
  85.3 5.1 %collective-permute-start.8 = (bf16[1,8,32,128]{3,2,1,0:T(8,128)(2,1)S(1)}, bf16[1,8,32,128]{3,2,1,0:T(8,128)(2,1)S(1)}, u32[]{:S(2)}, u32[]{:S(2)}) collective-permute-start(bf16[1,8,32,128]{3,2,1,0:T(8,128)(2,1)S(1)} %bitcast.342), channel_id=1, source_target_pairs={{0,8},{8,16},{16,24},{1,9},{9,17},{17,25},{2,10},{10,18},{18,26},{... | collective-permute-start | bytes 196616 | tf_op jit(solution)/shard_map/ppermute | solution.py:12
  90.8 1.6 convolution_dynamic-update-slice_fusion.6
  95.7 1.3 collective-permute-start.11
  97.0 5.5 %collective-permute-start.10 = (bf16[6,1,32,128]{3,2,1,0:T(8,128)(2,1)S(1)}, bf16[6,1,32,128]{3,2,1,0:T(8,128)(2,1)S(1)}, u32[]{:S(2)}, u32[]{:S(2)}) collective-permute-start(bf16[6,1,32,128]{3,2,1,0:T(8,128)(2,1)S(1)} %get-tuple-element.104), channel_id=1, source_target_pairs={{0,1},{1,2},{2,3},{3,4},{4,5},{5,6},{6,7},{8,9},{9,10},{10,11},{11... | collective-permute-start | bytes 147464 | tf_op jit(solution)/shard_map/ppermute | solution.py:12
  102.4 1.5 convolution_dynamic-update-slice_fusion
  117.3 2.2 %collective-permute-start.12 = (bf16[2592,128]{1,0:T(8,128)(2,1)S(1)}, bf16[2592,128]{1,0:T(8,128)(2,1)}, u32[]{:S(2)}, u32[]{:S(2)}) collective-permute-start(bf16[2592,128]{1,0:T(8,128)(2,1)S(1)} %fusion.1), channel_id=1, source_target_pairs={{0,8},{8,0},{16,24},{24,16},{1,9},{9,1},{17,25},{25,17},{2,10},{10... | collective-permute-start | bytes 1990664 | tf_op jit(solution)/shard_map/ppermute | solution.py:69
  119.5 1.9 %collective-permute-done.12 = bf16[2592,128]{1,0:T(8,128)(2,1)} collective-permute-done((bf16[2592,128]{1,0:T(8,128)(2,1)S(1)}, bf16[2592,128]{1,0:T(8,128)(2,1)}, u32[]{:S(2)}, u32[]{:S(2)}) %collective-permute-start.12) | collective-permute-done | bytes 663584 | tf_op jit(solution)/shard_map/ppermute | solution.py:69
  121.4 1.7 fusion.3
  124.3 8.8 %collective-permute-done.13 = bf16[1296,128]{1,0:T(8,128)(2,1)S(1)} collective-permute-done((bf16[1296,128]{1,0:T(8,128)(2,1)S(1)}, bf16[1296,128]{1,0:T(8,128)(2,1)S(1)}, u32[]{:S(2)}, u32[]{:S(2)}) %collective-permute-start.13) | collective-permute-done | bytes 331808 | tf_op jit(solution)/shard_map/ppermute | solution.py:69
  133.2 2.7 %collective-permute-start.14 = (bf16[648,128]{1,0:T(8,128)(2,1)S(1)}, bf16[648,128]{1,0:T(8,128)(2,1)S(1)}, u32[]{:S(2)}, u32[]{:S(2)}) collective-permute-start(bf16[648,128]{1,0:T(8,128)(2,1)S(1)} %dynamic-slice_convert_fusion.1), channel_id=1, source_target_pairs={{0,1},{1,0},{2,3},{3,2},{4,5},{5,4},{6,7},{7,6},{8,9},{9,8},{10,11... | collective-permute-start | bytes 497672 | tf_op jit(solution)/shard_map/ppermute | solution.py:69
  135.9 3.7 %collective-permute-done.14 = bf16[648,128]{1,0:T(8,128)(2,1)S(1)} collective-permute-done((bf16[648,128]{1,0:T(8,128)(2,1)S(1)}, bf16[648,128]{1,0:T(8,128)(2,1)S(1)}, u32[]{:S(2)}, u32[]{:S(2)}) %collective-permute-start.14) | collective-permute-done | bytes 165920 | tf_op jit(solution)/shard_map/ppermute | solution.py:69
  139.6 2.9 %collective-permute-start.15 = (bf16[324,128]{1,0:T(8,128)(2,1)S(1)}, bf16[324,128]{1,0:T(8,128)(2,1)S(1)}, u32[]{:S(2)}, u32[]{:S(2)}) collective-permute-start(bf16[324,128]{1,0:T(8,128)(2,1)S(1)} %dynamic-slice_convert_fusion.2), channel_id=1, source_target_pairs={{0,2},{1,3},{2,0},{3,1},{4,6},{5,7},{6,4},{7,5},{8,10},{9,11},{10,... | collective-permute-start | bytes 248840 | tf_op jit(solution)/shard_map/ppermute | solution.py:69
  142.5 2.4 %collective-permute-done.15 = bf16[324,128]{1,0:T(8,128)(2,1)S(1)} collective-permute-done((bf16[324,128]{1,0:T(8,128)(2,1)S(1)}, bf16[324,128]{1,0:T(8,128)(2,1)S(1)}, u32[]{:S(2)}, u32[]{:S(2)}) %collective-permute-start.15) | collective-permute-done | bytes 82976 | tf_op jit(solution)/shard_map/ppermute | solution.py:69
  145.0 3.2 %collective-permute-start.16 = (bf16[162,128]{1,0:T(8,128)(2,1)S(1)}, bf16[162,128]{1,0:T(8,128)(2,1)S(1)}, u32[]{:S(2)}, u32[]{:S(2)}) collective-permute-start(bf16[162,128]{1,0:T(8,128)(2,1)S(1)} %dynamic-slice_convert_fusion.3), channel_id=1, source_target_pairs={{0,4},{1,5},{2,6},{3,7},{4,0},{5,1},{6,2},{7,3},{8,12},{9,13},{10,... | collective-permute-start | bytes 124424 | tf_op jit(solution)/shard_map/ppermute | solution.py:69
  148.2 2.1 %collective-permute-done.16 = bf16[162,128]{1,0:T(8,128)(2,1)S(1)} collective-permute-done((bf16[162,128]{1,0:T(8,128)(2,1)S(1)}, bf16[162,128]{1,0:T(8,128)(2,1)S(1)}, u32[]{:S(2)}, u32[]{:S(2)}) %collective-permute-start.16) | collective-permute-done | bytes 41504 | tf_op jit(solution)/shard_map/ppermute | solution.py:69
  150.3 3.3 %collective-permute-start.17 = (bf16[162,128]{1,0:T(8,128)(2,1)S(1)}, bf16[162,128]{1,0:T(8,128)(2,1)S(1)}, u32[]{:S(2)}, u32[]{:S(2)}) collective-permute-start(bf16[162,128]{1,0:T(8,128)(2,1)S(1)} %add_convert_fusion), channel_id=1, source_target_pairs={{0,4},{1,5},{2,6},{3,7},{4,0},{5,1},{6,2},{7,3},{8,12},{9,13},{10,... | collective-permute-start | bytes 124424 | tf_op jit(solution)/shard_map/ppermute | solution.py:69
  153.6 2.0 %collective-permute-done.17 = bf16[162,128]{1,0:T(8,128)(2,1)S(1)} collective-permute-done((bf16[162,128]{1,0:T(8,128)(2,1)S(1)}, bf16[162,128]{1,0:T(8,128)(2,1)S(1)}, u32[]{:S(2)}, u32[]{:S(2)}) %collective-permute-start.17) | collective-permute-done | bytes 41504 | tf_op jit(solution)/shard_map/ppermute | solution.py:69
  155.7 2.8 %collective-permute-start.18 = (bf16[324,128]{1,0:T(8,128)(2,1)S(1)}, bf16[324,128]{1,0:T(8,128)(2,1)S(1)}, u32[]{:S(2)}, u32[]{:S(2)}) collective-permute-start(bf16[324,128]{1,0:T(8,128)(2,1)S(1)} %maximum_select_fusion.4), channel_id=1, source_target_pairs={{0,2},{1,3},{2,0},{3,1},{4,6},{5,7},{6,4},{7,5},{8,10},{9,11},{10,... | collective-permute-start | bytes 248840 | tf_op jit(solution)/shard_map/ppermute | solution.py:69
  158.5 2.4 %collective-permute-done.18 = bf16[324,128]{1,0:T(8,128)(2,1)S(1)} collective-permute-done((bf16[324,128]{1,0:T(8,128)(2,1)S(1)}, bf16[324,128]{1,0:T(8,128)(2,1)S(1)}, u32[]{:S(2)}, u32[]{:S(2)}) %collective-permute-start.18) | collective-permute-done | bytes 82976 | tf_op jit(solution)/shard_map/ppermute | solution.py:69
  161.4 5.0 %collective-permute-done.19 = bf16[648,128]{1,0:T(8,128)(2,1)S(1)} collective-permute-done((bf16[648,128]{1,0:T(8,128)(2,1)S(1)}, bf16[648,128]{1,0:T(8,128)(2,1)S(1)}, u32[]{:S(2)}, u32[]{:S(2)}) %collective-permute-start.19) | collective-permute-done | bytes 165920 | tf_op jit(solution)/shard_map/ppermute | solution.py:69
  166.5 1.3 collective-permute-start.20
  167.7 5.9 %collective-permute-done.20 = bf16[1296,128]{1,0:T(8,128)(2,1)S(1)} collective-permute-done((bf16[1296,128]{1,0:T(8,128)(2,1)S(1)}, bf16[1296,128]{1,0:T(8,128)(2,1)S(1)}, u32[]{:S(2)}, u32[]{:S(2)}) %collective-permute-start.20) | collective-permute-done | bytes 331808 | tf_op jit(solution)/shard_map/ppermute | solution.py:69
  173.9 2.2 %collective-permute-done.21 = bf16[2592,128]{1,0:T(8,128)(2,1)} collective-permute-done((bf16[2592,128]{1,0:T(8,128)(2,1)S(1)}, bf16[2592,128]{1,0:T(8,128)(2,1)}, u32[]{:S(2)}, u32[]{:S(2)}) %collective-permute-start.21) | collective-permute-done | bytes 663584 | tf_op jit(solution)/shard_map/ppermute | solution.py:69
  176.2 1.6 fusion.4
  182.0 1.3 slice_multiply_fusion
  (264 shorter events, 58.1 us)
Async XLA Ops:
  0.6 7.8 %copy-start.39 = (bf16[4,8,16,128]{3,2,1,0:T(8,128)(2,1)S(1)}, bf16[4,8,16,128]{3,2,1,0:T(8,128)(2,1)}, u32[]{:S(2)}) copy-start(bf16[4,8,16,128]{3,2,1,0:T(8,128)(2,1)} %param.7) | copy-start | bytes 393220
  0.6 7.1 %copy-start.40 = (bf16[27,64,128]{2,1,0:T(8,128)(2,1)S(1)}, bf16[27,64,128]{2,1,0:T(8,128)(2,1)}, u32[]{:S(2)}) copy-start(bf16[27,64,128]{2,1,0:T(8,128)(2,1)} %param.9) | copy-start | bytes 1327108
  1.6 8.3 %collective-permute-start = (bf16[1,8,32,64]{3,2,1,0:T(8,128)(2,1)S(1)}, bf16[1,8,32,64]{3,2,1,0:T(8,128)(2,1)S(1)}, u32[]{:S(2)}, u32[]{:S(2)}) collective-permute-start(bf16[1,8,32,64]{3,2,1,0:T(8,128)(2,1)S(1)} %slice.493), channel_id=1, source_target_pairs={{0,8},{8,16},{16,24},{1,9},{9,17},{17,25},{2,10},{10,18},{18,26},{... | collective-permute-start | bytes 98312 | tf_op jit(solution)/shard_map/ppermute | solution.py:12
  4.0 4.6 %copy-start.4 = (bf16[27,128,128]{2,1,0:T(8,128)(2,1)S(1)}, bf16[27,128,128]{2,1,0:T(8,128)(2,1)}, u32[]{:S(2)}) copy-start(bf16[27,128,128]{2,1,0:T(8,128)(2,1)} %param.11) | copy-start | bytes 2654212
  4.1 5.9 %collective-permute-start.1 = (bf16[1,8,32,64]{3,2,1,0:T(8,128)(2,1)S(1)}, bf16[1,8,32,64]{3,2,1,0:T(8,128)(2,1)S(1)}, u32[]{:S(2)}, u32[]{:S(2)}) collective-permute-start(bf16[1,8,32,64]{3,2,1,0:T(8,128)(2,1)S(1)} %slice.495), channel_id=1, source_target_pairs={{8,0},{16,8},{24,16},{9,1},{17,9},{25,17},{10,2},{18,10},{26,18},{... | collective-permute-start | bytes 98312 | tf_op jit(solution)/shard_map/ppermute | solution.py:15
  9.9 7.4 %copy-start.61 = (s32[4,8,32]{2,1,0:T(8,128)S(1)}, s32[4,8,32]{2,1,0:T(8,128)}, u32[]{:S(2)}) copy-start(s32[4,8,32]{2,1,0:T(8,128)} %param.8) | copy-start | bytes 12292
  10.0 8.0 %collective-permute-start.3 = (bf16[6,1,32,64]{3,2,1,0:T(8,128)(2,1)S(1)}, bf16[6,1,32,64]{3,2,1,0:T(8,128)(2,1)S(1)}, u32[]{:S(2)}, u32[]{:S(2)}) collective-permute-start(bf16[6,1,32,64]{3,2,1,0:T(8,128)(2,1)S(1)} %get-tuple-element.115), channel_id=1, source_target_pairs={{1,0},{2,1},{3,2},{4,3},{5,4},{6,5},{7,6},{9,8},{10,9},{11,10},{12... | collective-permute-start | bytes 73736 | tf_op jit(solution)/shard_map/ppermute | solution.py:15
  11.3 6.7 %collective-permute-start.2 = (bf16[6,1,32,64]{3,2,1,0:T(8,128)(2,1)S(1)}, bf16[6,1,32,64]{3,2,1,0:T(8,128)(2,1)S(1)}, u32[]{:S(2)}, u32[]{:S(2)}) collective-permute-start(bf16[6,1,32,64]{3,2,1,0:T(8,128)(2,1)S(1)} %get-tuple-element.114), channel_id=1, source_target_pairs={{0,1},{1,2},{2,3},{3,4},{4,5},{5,6},{6,7},{8,9},{9,10},{10,11},{11... | collective-permute-start | bytes 73736 | tf_op jit(solution)/shard_map/ppermute | solution.py:12
  17.3 5.8 %copy-start.17 = (bf16[1024,64]{1,0:T(8,128)(2,1)}, bf16[1024,64]{1,0:T(8,128)(2,1)S(1)}, u32[]{:S(2)}) copy-start(bf16[1024,64]{1,0:T(8,128)(2,1)S(1)} %concatenate.231) | copy-start | bytes 393220
  19.0 4.1 %copy-start.15 = (bf16[4,8,32,64]{3,2,1,0:T(8,128)(2,1)}, bf16[4,8,32,64]{3,2,1,0:T(8,128)(2,1)S(1)}, u32[]{:S(2)}) copy-start(bf16[4,8,32,64]{3,2,1,0:T(8,128)(2,1)S(1)} %get-tuple-element.64) | copy-start | bytes 393220
  19.0 4.1 %copy-start.16 = (bf16[4,8,32,64]{3,2,1,0:T(8,128)(2,1)}, bf16[4,8,32,64]{3,2,1,0:T(8,128)(2,1)S(1)}, u32[]{:S(2)}) copy-start(bf16[4,8,32,64]{3,2,1,0:T(8,128)(2,1)S(1)} %get-tuple-element.65) | copy-start | bytes 393220
  21.4 3.0 %copy-start.18 = (bf16[4,8,32,192]{3,2,1,0:T(8,128)(2,1)}, bf16[4,8,32,192]{3,2,1,0:T(8,128)(2,1)S(1)}, u32[]{:S(2)}) copy-start(bf16[4,8,32,192]{3,2,1,0:T(8,128)(2,1)S(1)} %get-tuple-element.110) | copy-start | bytes 1179652
  24.6 8.0 %copy-start.5 = (bf16[27,128,128]{2,1,0:T(8,128)(2,1)S(1)}, bf16[27,128,128]{2,1,0:T(8,128)(2,1)}, u32[]{:S(2)}) copy-start(bf16[27,128,128]{2,1,0:T(8,128)(2,1)} %reverse_bitcast_fusion) | copy-start | bytes 2654212
  26.4 7.1 %collective-permute-start.5 = (bf16[1,8,32,128]{3,2,1,0:T(8,128)(2,1)}, bf16[1,8,32,128]{3,2,1,0:T(8,128)(2,1)S(1)}, u32[]{:S(2)}, u32[]{:S(2)}) collective-permute-start(bf16[1,8,32,128]{3,2,1,0:T(8,128)(2,1)} %bitcast.21), channel_id=1, source_target_pairs={{8,0},{16,8},{24,16},{9,1},{17,9},{25,17},{10,2},{18,10},{26,18},{... | collective-permute-start | bytes 196616 | tf_op jit(solution)/shard_map/ppermute | solution.py:15
  27.7 6.0 %collective-permute-start.4 = (bf16[1,8,32,128]{3,2,1,0:T(8,128)(2,1)}, bf16[1,8,32,128]{3,2,1,0:T(8,128)(2,1)S(1)}, u32[]{:S(2)}, u32[]{:S(2)}) collective-permute-start(bf16[1,8,32,128]{3,2,1,0:T(8,128)(2,1)} %bitcast.19), channel_id=1, source_target_pairs={{0,8},{8,16},{16,24},{1,9},{9,17},{17,25},{2,10},{10,18},{18,26},{... | collective-permute-start | bytes 196616 | tf_op jit(solution)/shard_map/ppermute | solution.py:12
  34.3 18.6 %collective-permute-start.7 = (bf16[6,1,32,128]{3,2,1,0:T(8,128)(2,1)}, bf16[6,1,32,128]{3,2,1,0:T(8,128)(2,1)}, u32[]{:S(2)}, u32[]{:S(2)}) collective-permute-start(bf16[6,1,32,128]{3,2,1,0:T(8,128)(2,1)} %get-tuple-element.109), channel_id=1, source_target_pairs={{1,0},{2,1},{3,2},{4,3},{5,4},{6,5},{7,6},{9,8},{10,9},{11,10},{12... | collective-permute-start | bytes 147464 | tf_op jit(solution)/shard_map/ppermute | solution.py:15
  35.6 17.3 %collective-permute-start.6 = (bf16[6,1,32,128]{3,2,1,0:T(8,128)(2,1)}, bf16[6,1,32,128]{3,2,1,0:T(8,128)(2,1)}, u32[]{:S(2)}, u32[]{:S(2)}) collective-permute-start(bf16[6,1,32,128]{3,2,1,0:T(8,128)(2,1)} %get-tuple-element.108), channel_id=1, source_target_pairs={{0,1},{1,2},{2,3},{3,4},{4,5},{5,6},{6,7},{8,9},{9,10},{10,11},{11... | collective-permute-start | bytes 147464 | tf_op jit(solution)/shard_map/ppermute | solution.py:12
  46.3 1.9 %copy-start.20 = (bf16[192,1024]{0,1:T(8,128)(2,1)S(1)}, bf16[192,1024]{0,1:T(8,128)(2,1)}, u32[]{:S(2)}) copy-start(bf16[192,1024]{0,1:T(8,128)(2,1)} %fusion.62) | copy-start | bytes 1179652
  49.2 2.8 %copy-start.19 = (bf16[4,8,32,192]{3,2,1,0:T(8,128)(2,1)S(1)}, bf16[4,8,32,192]{3,2,1,0:T(8,128)(2,1)}, u32[]{:S(2)}) copy-start(bf16[4,8,32,192]{3,2,1,0:T(8,128)(2,1)} %copy-done.18) | copy-start | bytes 1179652
  57.7 1.3 copy-start.53
  62.2 1.3 copy-start.1
  63.4 1.3 copy-start.36
  64.7 2.4 %copy-start.34 = (bf16[4,8,32,128]{3,2,1,0:T(8,128)(2,1)S(1)}, bf16[4,8,32,128]{3,2,1,0:T(8,128)(2,1)}, u32[]{:S(2)}) copy-start(bf16[4,8,32,128]{3,2,1,0:T(8,128)(2,1)} %get-tuple-element.44) | copy-start | bytes 786436
  64.7 2.4 %copy-start.35 = (bf16[4,8,32,128]{3,2,1,0:T(8,128)(2,1)S(1)}, bf16[4,8,32,128]{3,2,1,0:T(8,128)(2,1)}, u32[]{:S(2)}) copy-start(bf16[4,8,32,128]{3,2,1,0:T(8,128)(2,1)} %get-tuple-element.45) | copy-start | bytes 786436
  70.8 4.1 %copy-start.49 = (bf16[3,128,128]{2,1,0:T(8,128)(2,1)S(1)}, bf16[3,128,128]{2,1,0:T(8,128)(2,1)}, u32[]{:S(2)}) copy-start(bf16[3,128,128]{2,1,0:T(8,128)(2,1)} %get-tuple-element.18) | copy-start | bytes 294916
  73.1 2.1 %copy-start.48 = (bf16[3,128,128]{2,1,0:T(8,128)(2,1)S(1)}, bf16[3,128,128]{2,1,0:T(8,128)(2,1)}, u32[]{:S(2)}) copy-start(bf16[3,128,128]{2,1,0:T(8,128)(2,1)} %get-tuple-element.17) | copy-start | bytes 294916
  75.3 1.6 copy-start.59
  79.5 1.7 copy-start.12
  81.2 9.2 %copy-start.7 = (bf16[1024,384]{0,1:T(8,128)(2,1)S(1)}, bf16[1024,384]{0,1:T(8,128)(2,1)}, u32[]{:S(2)}) copy-start(bf16[1024,384]{0,1:T(8,128)(2,1)} %copy.41) | copy-start | bytes 2359300
  83.9 8.5 %copy-start.9 = (bf16[1024,384]{0,1:T(8,128)(2,1)S(1)}, bf16[1024,384]{0,1:T(8,128)(2,1)}, u32[]{:S(2)}) copy-start(bf16[1024,384]{0,1:T(8,128)(2,1)} %copy.43) | copy-start | bytes 2359300
  83.9 11.7 %collective-permute-start.9 = (bf16[1,8,32,128]{3,2,1,0:T(8,128)(2,1)S(1)}, bf16[1,8,32,128]{3,2,1,0:T(8,128)(2,1)S(1)}, u32[]{:S(2)}, u32[]{:S(2)}) collective-permute-start(bf16[1,8,32,128]{3,2,1,0:T(8,128)(2,1)S(1)} %bitcast.343), channel_id=1, source_target_pairs={{8,0},{16,8},{24,16},{9,1},{17,9},{25,17},{10,2},{18,10},{26,18},{... | collective-permute-start | bytes 196616 | tf_op jit(solution)/shard_map/ppermute | solution.py:15
  85.3 10.3 %collective-permute-start.8 = (bf16[1,8,32,128]{3,2,1,0:T(8,128)(2,1)S(1)}, bf16[1,8,32,128]{3,2,1,0:T(8,128)(2,1)S(1)}, u32[]{:S(2)}, u32[]{:S(2)}) collective-permute-start(bf16[1,8,32,128]{3,2,1,0:T(8,128)(2,1)S(1)} %bitcast.342), channel_id=1, source_target_pairs={{0,8},{8,16},{16,24},{1,9},{9,17},{17,25},{2,10},{10,18},{18,26},{... | collective-permute-start | bytes 196616 | tf_op jit(solution)/shard_map/ppermute | solution.py:12
  90.4 2.4 %copy-start.14 = (bf16[384,1024]{1,0:T(8,128)(2,1)S(1)}, bf16[384,1024]{1,0:T(8,128)(2,1)}, u32[]{:S(2)}) copy-start(bf16[384,1024]{1,0:T(8,128)(2,1)} %copy.44) | copy-start | bytes 2359300
  90.8 2.4 %copy-start.8 = (bf16[1024,384]{0,1:T(8,128)(2,1)S(1)}, bf16[1024,384]{0,1:T(8,128)(2,1)}, u32[]{:S(2)}) copy-start(bf16[1024,384]{0,1:T(8,128)(2,1)} %copy.45) | copy-start | bytes 2359300
  95.7 8.3 %collective-permute-start.11 = (bf16[6,1,32,128]{3,2,1,0:T(8,128)(2,1)S(1)}, bf16[6,1,32,128]{3,2,1,0:T(8,128)(2,1)S(1)}, u32[]{:S(2)}, u32[]{:S(2)}) collective-permute-start(bf16[6,1,32,128]{3,2,1,0:T(8,128)(2,1)S(1)} %get-tuple-element.105), channel_id=1, source_target_pairs={{1,0},{2,1},{3,2},{4,3},{5,4},{6,5},{7,6},{9,8},{10,9},{11,10},{12... | collective-permute-start | bytes 147464 | tf_op jit(solution)/shard_map/ppermute | solution.py:15
  97.0 7.0 %collective-permute-start.10 = (bf16[6,1,32,128]{3,2,1,0:T(8,128)(2,1)S(1)}, bf16[6,1,32,128]{3,2,1,0:T(8,128)(2,1)S(1)}, u32[]{:S(2)}, u32[]{:S(2)}) collective-permute-start(bf16[6,1,32,128]{3,2,1,0:T(8,128)(2,1)S(1)} %get-tuple-element.104), channel_id=1, source_target_pairs={{0,1},{1,2},{2,3},{3,4},{4,5},{5,6},{6,7},{8,9},{9,10},{10,11},{11... | collective-permute-start | bytes 147464 | tf_op jit(solution)/shard_map/ppermute | solution.py:12
  113.4 1.4 copy-start.26
  113.4 1.6 copy-start.25
  117.3 4.1 %collective-permute-start.12 = (bf16[2592,128]{1,0:T(8,128)(2,1)S(1)}, bf16[2592,128]{1,0:T(8,128)(2,1)}, u32[]{:S(2)}, u32[]{:S(2)}) collective-permute-start(bf16[2592,128]{1,0:T(8,128)(2,1)S(1)} %fusion.1), channel_id=1, source_target_pairs={{0,8},{8,0},{16,24},{24,16},{1,9},{9,1},{17,25},{25,17},{2,10},{10... | collective-permute-start | bytes 1990664 | tf_op jit(solution)/shard_map/ppermute | solution.py:69
  123.2 9.9 %collective-permute-start.13 = (bf16[1296,128]{1,0:T(8,128)(2,1)S(1)}, bf16[1296,128]{1,0:T(8,128)(2,1)S(1)}, u32[]{:S(2)}, u32[]{:S(2)}) collective-permute-start(bf16[1296,128]{1,0:T(8,128)(2,1)S(1)} %dynamic-slice_convert_fusion), channel_id=1, source_target_pairs={{0,16},{8,24},{16,0},{24,8},{1,17},{9,25},{17,1},{25,9},{2,18},{10... | collective-permute-start | bytes 995336 | tf_op jit(solution)/shard_map/ppermute | solution.py:69
  133.2 6.4 %collective-permute-start.14 = (bf16[648,128]{1,0:T(8,128)(2,1)S(1)}, bf16[648,128]{1,0:T(8,128)(2,1)S(1)}, u32[]{:S(2)}, u32[]{:S(2)}) collective-permute-start(bf16[648,128]{1,0:T(8,128)(2,1)S(1)} %dynamic-slice_convert_fusion.1), channel_id=1, source_target_pairs={{0,1},{1,0},{2,3},{3,2},{4,5},{5,4},{6,7},{7,6},{8,9},{9,8},{10,11... | collective-permute-start | bytes 497672 | tf_op jit(solution)/shard_map/ppermute | solution.py:69
  139.6 5.4 %collective-permute-start.15 = (bf16[324,128]{1,0:T(8,128)(2,1)S(1)}, bf16[324,128]{1,0:T(8,128)(2,1)S(1)}, u32[]{:S(2)}, u32[]{:S(2)}) collective-permute-start(bf16[324,128]{1,0:T(8,128)(2,1)S(1)} %dynamic-slice_convert_fusion.2), channel_id=1, source_target_pairs={{0,2},{1,3},{2,0},{3,1},{4,6},{5,7},{6,4},{7,5},{8,10},{9,11},{10,... | collective-permute-start | bytes 248840 | tf_op jit(solution)/shard_map/ppermute | solution.py:69
  145.0 5.2 %collective-permute-start.16 = (bf16[162,128]{1,0:T(8,128)(2,1)S(1)}, bf16[162,128]{1,0:T(8,128)(2,1)S(1)}, u32[]{:S(2)}, u32[]{:S(2)}) collective-permute-start(bf16[162,128]{1,0:T(8,128)(2,1)S(1)} %dynamic-slice_convert_fusion.3), channel_id=1, source_target_pairs={{0,4},{1,5},{2,6},{3,7},{4,0},{5,1},{6,2},{7,3},{8,12},{9,13},{10,... | collective-permute-start | bytes 124424 | tf_op jit(solution)/shard_map/ppermute | solution.py:69
  150.3 5.4 %collective-permute-start.17 = (bf16[162,128]{1,0:T(8,128)(2,1)S(1)}, bf16[162,128]{1,0:T(8,128)(2,1)S(1)}, u32[]{:S(2)}, u32[]{:S(2)}) collective-permute-start(bf16[162,128]{1,0:T(8,128)(2,1)S(1)} %add_convert_fusion), channel_id=1, source_target_pairs={{0,4},{1,5},{2,6},{3,7},{4,0},{5,1},{6,2},{7,3},{8,12},{9,13},{10,... | collective-permute-start | bytes 124424 | tf_op jit(solution)/shard_map/ppermute | solution.py:69
  155.7 5.2 %collective-permute-start.18 = (bf16[324,128]{1,0:T(8,128)(2,1)S(1)}, bf16[324,128]{1,0:T(8,128)(2,1)S(1)}, u32[]{:S(2)}, u32[]{:S(2)}) collective-permute-start(bf16[324,128]{1,0:T(8,128)(2,1)S(1)} %maximum_select_fusion.4), channel_id=1, source_target_pairs={{0,2},{1,3},{2,0},{3,1},{4,6},{5,7},{6,4},{7,5},{8,10},{9,11},{10,... | collective-permute-start | bytes 248840 | tf_op jit(solution)/shard_map/ppermute | solution.py:69
  161.0 5.4 %collective-permute-start.19 = (bf16[648,128]{1,0:T(8,128)(2,1)S(1)}, bf16[648,128]{1,0:T(8,128)(2,1)S(1)}, u32[]{:S(2)}, u32[]{:S(2)}) collective-permute-start(bf16[648,128]{1,0:T(8,128)(2,1)S(1)} %maximum_select_fusion.3), channel_id=1, source_target_pairs={{0,1},{1,0},{2,3},{3,2},{4,5},{5,4},{6,7},{7,6},{8,9},{9,8},{10,11... | collective-permute-start | bytes 497672 | tf_op jit(solution)/shard_map/ppermute | solution.py:69
  166.5 7.2 %collective-permute-start.20 = (bf16[1296,128]{1,0:T(8,128)(2,1)S(1)}, bf16[1296,128]{1,0:T(8,128)(2,1)S(1)}, u32[]{:S(2)}, u32[]{:S(2)}) collective-permute-start(bf16[1296,128]{1,0:T(8,128)(2,1)S(1)} %maximum_select_fusion.2), channel_id=1, source_target_pairs={{0,16},{8,24},{16,0},{24,8},{1,17},{9,25},{17,1},{25,9},{2,18},{10... | collective-permute-start | bytes 995336 | tf_op jit(solution)/shard_map/ppermute | solution.py:69
  173.9 2.3 %collective-permute-start.21 = (bf16[2592,128]{1,0:T(8,128)(2,1)S(1)}, bf16[2592,128]{1,0:T(8,128)(2,1)}, u32[]{:S(2)}, u32[]{:S(2)}) collective-permute-start(bf16[2592,128]{1,0:T(8,128)(2,1)S(1)} %maximum_select_fusion.1), channel_id=1, source_target_pairs={{0,8},{8,0},{16,24},{24,16},{1,9},{9,1},{17,25},{25,17},{2,10},{10... | collective-permute-start | bytes 1990664 | tf_op jit(solution)/shard_map/ppermute | solution.py:69
  (41 other events, 41.5 us)

commit v2 on v1

v2 whole, which is shorter than its diff:
```python
import functools

import jax
import jax.numpy as jnp
from jax import lax
from jax.experimental import pallas as pl
from jax.experimental.pallas import tpu as pltpu
from jax.sharding import PartitionSpec as P

BF = jnp.bfloat16
F32 = jnp.float32
LANES = 128
FIELD_HALO = 3
MASK_HALO = 2


def bit_levels(axes):
    levels = []
    for axis in axes:
        bit = 1
        while bit < lax.axis_size(axis):
            levels.append((axis, bit))
            bit *= 2
    return levels


def swap_with(part, axis, bit):
    return lax.ppermute(part, axis, [(i, i ^ bit) for i in range(lax.axis_size(axis))])


def side_of(axis, bit):
    return lax.rem(lax.axis_index(axis) // bit, 2)


def halves_summed(part, levels):
    for axis, bit in levels:
        half = part.shape[0] // 2
        side = side_of(axis, bit)
        sent = lax.dynamic_slice_in_dim(part, (1 - side) * half, half, 0).astype(BF)
        kept = lax.dynamic_slice_in_dim(part, side * half, half, 0)
        part = kept + swap_with(sent, axis, bit).astype(F32)
    return part


def halves_joined(part, levels):
    for axis, bit in reversed(levels):
        other = swap_with(part, axis, bit)
        part = jnp.where(
            side_of(axis, bit) == 0,
            jnp.concatenate([part, other], axis=0),
            jnp.concatenate([other, part], axis=0),
        )
    return part


def summed_everywhere(rows, axes):
    levels = bit_levels(axes)
    pieces = 2 ** len(levels)
    padded = jnp.pad(rows, ((0, -rows.shape[0] % pieces), (0, 0)))
    summed = halves_summed(padded, levels).astype(BF)
    return halves_joined(summed, levels)[: rows.shape[0]].astype(F32)


def normalized_with(grad, total, count):
    return grad * lax.rsqrt(total / count + 1e-06)


def exchange(forward, backward, axis):
    count = lax.axis_size(axis)
    ups = [(i, i + 1) for i in range(count - 1)]
    downs = [(target, source) for source, target in ups]
    return lax.ppermute(forward, axis, ups), lax.ppermute(backward, axis, downs)


def pack_x_body(cx, field, up, tile, last, first):
    for ref, at_field, at_up in ((last, cx - FIELD_HALO, cx - 1), (first, 0, 0)):
        rows = field[at_field : at_field + FIELD_HALO].reshape(-1, LANES)
        ups = up[at_up : at_up + 1].reshape(-1, LANES)
        ref[0 : rows.shape[0]] = rows
        ref[rows.shape[0] : rows.shape[0] + ups.shape[0]] = ups
        ref[rows.shape[0] + ups.shape[0] :] = tile[...]


def pack_y_body(cx, cy, kz, field, up, tile, low, high, last, first):
    nf = FIELD_HALO * cy * kz
    nu = cy * 2 * kz
    for ref, at_field, at_up in ((last, cy - FIELD_HALO, cy - 1), (first, 0, 0)):
        row = 0
        ends = [m[0:nf].reshape(FIELD_HALO, cy, kz, LANES) for m in (low, high)]
        for part in (ends[0], field, ends[1]):
            rows = part[:, at_field : at_field + FIELD_HALO].reshape(-1, LANES)
            ref[row : row + rows.shape[0]] = rows
            row += rows.shape[0]
        ends = [m[nf : nf + nu].reshape(1, cy, 2 * kz, LANES) for m in (low, high)]
        for part in (ends[0], up, ends[1]):
            rows = part[:, at_up : at_up + 1].reshape(-1, LANES)
            ref[row : row + rows.shape[0]] = rows
            row += rows.shape[0]
        for part in (low[nf + nu :], tile[...], high[nf + nu :]):
            ref[row : row + kz] = part
            row += kz


def side_pair(pair, kz, width):
    rows = pair.shape[0]
    depth = lax.rem(lax.broadcasted_iota(jnp.int32, (rows, width), 0), kz)
    above = pltpu.roll(pair[:, :width], rows - 1, 0)
    below = pltpu.roll(pair[:, width:], 1, 0)
    above = jnp.where(depth == kz - 1, 0.0, above)
    below = jnp.where(depth == 0, 0.0, below)
    return above, below


def taps_of(pair, side, at, rows, cols):
    parts = []
    for a in range(3):
        for b in range(3):
            for ref in (pair, side):
                part = ref[pl.ds(at + a, rows), b : b + cols]
                parts.append(part.reshape(-1, part.shape[-1]))
    return jnp.concatenate(parts, axis=1)


def forward_body(
    cx, cy, kz,
    field, up, tile, low, high, left, right, w1, b1, w2, b2,
    features, d2, g2p, g2s, gate, xp, xs,
    hp, hs, act, upf, outf,
):
    fh, mh = FIELD_HALO, MASK_HALO
    nf, nu = fh * cy * kz, cy * 2 * kz
    ex = cx + 2 * fh
    xp[fh : fh + cx, fh : fh + cy] = field[...]
    xp[0:fh, fh : fh + cy] = low[0:nf].reshape(fh, cy, kz, LANES)
    xp[fh + cx :, fh : fh + cy] = high[0:nf].reshape(fh, cy, kz, LANES)
    ne = ex * fh * kz
    xp[:, 0:fh] = left[0:ne].reshape(ex, fh, kz, LANES)
    xp[:, fh + cy :] = right[0:ne].reshape(ex, fh, kz, LANES)
    ey = cy + 2 * fh

    def fill_side(i, carry):
        rows = xp[i].reshape(ey * kz, LANES).astype(F32)
        depth = lax.rem(lax.broadcasted_iota(jnp.int32, rows.shape, 0), kz)
        lane = lax.broadcasted_iota(jnp.int32, rows.shape, 1)
        above = jnp.where(depth == kz - 1, 0.0, pltpu.roll(rows, ey * kz - 1, 0))
        below = jnp.where(depth == 0, 0.0, pltpu.roll(rows, 1, 0))
        both = jnp.where(lane < LANES // 2, above, below).astype(BF)
        xs[i] = both.reshape(ey, kz, LANES)
        return carry

    lax.fori_loop(0, ex, fill_side, 0)
    uy = cy + 2
    span = uy * 2 * kz

    def put_up(x, y, cols, value):
        base = x * span + y * 2 * kz
        upf[base : base + cols * 2 * kz] = value.reshape(-1, LANES).astype(F32)

    for x in range(cx):
        put_up(x + 1, 1, cy, up[x])
    put_up(0, 1, cy, low[nf : nf + nu])
    put_up(cx + 1, 1, cy, high[nf : nf + nu])
    for x in range(cx + 2):
        at = ne + x * 2 * kz
        put_up(x, 0, 1, left[at : at + 2 * kz])
        put_up(x, cy + 1, 1, right[at : at + 2 * kz])
    nm = ne + (cx + 2) * 2 * kz

    def put_mask(source, sx, sy, x, y):
        lane = 2 * (sx * cy + sy)
        for parity in range(2):
            value = jnp.broadcast_to(source[:, lane + parity : lane + parity + 1], (kz, LANES))
            act[x, y, :, parity * LANES : (parity + 1) * LANES] = value.astype(BF)

    def row_tiles(ref, start):
        own = [(ref[start + i * kz : start + (i + 1) * kz].astype(F32)) for i in range(3)]
        rows = []
        for x in range(cx + 2 * mh):
            if x < mh:
                rows.append((own[0], cx - mh + x))
            elif x < mh + cx:
                rows.append((own[1], x - mh))
            else:
                rows.append((own[2], x - mh - cx))
        return rows

    mid = tile[...].astype(F32)
    lo_tile = low[nf + nu : nf + nu + kz].astype(F32)
    hi_tile = high[nf + nu : nf + nu + kz].astype(F32)
    left_rows, right_rows = row_tiles(left, nm), row_tiles(right, nm)
    for x in range(cx + 2 * mh):
        if x < mh:
            source, sx = lo_tile, cx - mh + x
        elif x < mh + cx:
            source, sx = mid, x - mh
        else:
            source, sx = hi_tile, x - mh - cx
        for y in range(cy):
            put_mask(source, sx, y, x, mh + y)
        for j in range(mh):
            put_mask(*left_rows[x], cy - mh + j, x, j)
            put_mask(*right_rows[x], j, x, mh + cy + j)

    hx, hy = cx + 4, cy + 4
    step = 2

    def first(i, carry):
        at = i * step
        window = taps_of(xp, xs, at, step, hy)
        z = jnp.dot(window, w1[...], preferred_element_type=F32) + b1[...]
        s = jax.nn.sigmoid(z)
        m = act[pl.ds(at, step)].reshape(step * hy * kz, 2 * LANES).astype(F32)
        h = z * s * m
        above, below = side_pair(h, kz, LANES)
        hp[pl.ds(at, step)] = h.astype(BF).reshape(step, hy, kz, 2 * LANES)
        both = jnp.concatenate([above, below], axis=1).astype(BF)
        hs[pl.ds(at, step)] = both.reshape(step, hy, kz, 2 * LANES)

        @pl.when(jnp.logical_and(i >= 2 // step, i < (2 + cx) // step))
        def _():
            factor = m * s * (1.0 + z * (1.0 - s))
            factor = factor.reshape(step, hy, kz, 2 * LANES)[:, 2 : 2 + cy]
            gate[pl.ds(at - 2, step)] = factor

        return carry

    lax.fori_loop(0, hx // step, first, 0)

    def second(i, carry):
        at = i * step
        window = taps_of(hp, hs, at, step, uy)
        z = jnp.dot(window, w2[...], preferred_element_type=F32) + b2[...]
        s = jax.nn.sigmoid(z)
        m = act[pl.ds(at + 1, step), 1 : 1 + uy].reshape(-1, 2 * LANES).astype(F32)
        rows = step * uy * kz
        base = pl.multiple_of(at * span, 8)
        u = jnp.concatenate(
            [upf[pl.ds(base, rows, stride=2), :], upf[pl.ds(base + 1, rows, stride=2), :]], axis=1
        )
        g = u * m * s * (1.0 + z * (1.0 - s))
        gb = g.astype(BF)
        above, below = side_pair(g, kz, LANES)
        g2p[pl.ds(at, step)] = gb.reshape(step, uy, kz, 2 * LANES)
        both = jnp.concatenate([above, below], axis=1).astype(BF)
        g2s[pl.ds(at, step)] = both.reshape(step, uy, kz, 2 * LANES)
        out = z * s * m
        outf[pl.ds(base, rows, stride=2), :] = out[:, :LANES]
        outf[pl.ds(base + 1, rows, stride=2), :] = out[:, LANES:]
        return carry

    lax.fori_loop(0, (cx + 2) // step, second, 0)
    for x in range(cx):
        base = (x + 1) * span + 2 * kz
        rows = outf[base : base + cy * 2 * kz].astype(BF)
        features[x] = rows.reshape(cy, 2 * kz, LANES)

    own = hp[2 : 2 + cx, 2 : 2 + cy].reshape(-1, 2 * LANES)
    turned = own.T
    for a in range(3):
        for b in range(3):
            parts = [
                ref[2 - a : 2 - a + cx, 2 - b : 2 - b + cy].reshape(-1, 2 * LANES)
                for ref in (g2p, g2s)
            ]
            for half, part in enumerate(parts):
                block = jnp.dot(turned, part, preferred_element_type=F32)
                q = [[block[r * LANES : (r + 1) * LANES, c * LANES : (c + 1) * LANES] for c in (0, 1)] for r in (0, 1)]
                t = 9 * a + 3 * b
                if half == 0:
                    d2[t + 1] = q[0][0] + q[1][1]
                    d2[t] = q[0][1]
                    d2[t + 2] = q[1][0]
                else:
                    d2[t] = d2[t] + q[1][0]
                    d2[t + 2] = d2[t + 2] + q[0][1]


def backward_body(cx, cy, kz, g2p, g2s, gate, xp, xs, w3, d1, g1):
    fh = FIELD_HALO
    step = 2
    rows = step * cy * kz

    def grad(i, carry):
        at = i * step
        window = taps_of(g2p, g2s, at, step, cy)
        e = jnp.dot(window, w3[...], preferred_element_type=F32)
        g = e * gate[pl.ds(at, step)].reshape(rows, 2 * LANES)
        g1[pl.ds(pl.multiple_of(i * rows, rows), rows)] = g.astype(BF)
        return carry

    lax.fori_loop(0, cx // step, grad, 0)
    right = g1[...]
    cells = cx * cy * kz
    half = LANES // 2
    for b in range(3):
        cols = slice(fh - 1 + b, fh - 1 + b + cy)
        parts = [ref[fh - 1 : fh + 1 + cx, cols].reshape(-1, LANES) for ref in (xp, xs)]
        turned = jnp.concatenate(parts, axis=1).T
        for a in range(3):
            at = a * cy * kz
            block = jnp.dot(turned[:, at : at + cells], right, preferred_element_type=F32)
            q = [
                [block[r * half : (r + 1) * half, c * LANES : (c + 1) * LANES] for c in (0, 1)]
                for r in range(4)
            ]
            t = 9 * a + 3 * b
            d1[t] = q[0][1] + q[3][0]
            d1[t + 1] = q[0][0] + q[1][1]
            d1[t + 2] = q[1][0] + q[2][1]


def pair_weights(w):
    w = w.reshape(9, 3, w.shape[1], w.shape[2])
    none = jnp.zeros_like(w[:, 0])
    even = jnp.concatenate([w[:, 1], w[:, 2], none, w[:, 0]], axis=1)
    odd = jnp.concatenate([w[:, 0], w[:, 1], w[:, 2], none], axis=1)
    both = jnp.concatenate([even, odd], axis=2)
    return both.reshape(-1, both.shape[2])


def on_device(volume, basin_mask, w_first, b_first, w_second, b_second, upstream):
    cx, cy, kz, _ = volume.shape
    chan = w_first.shape[2]
    tile = basin_mask.astype(BF).reshape(cx * cy, kz, 2).transpose(1, 0, 2)
    tile = tile.reshape(kz, 2 * cx * cy)
    tile = jnp.pad(tile, ((0, 0), (0, LANES - tile.shape[1])))
    shape = jax.ShapeDtypeStruct
    rows_x = FIELD_HALO * cy * kz + cy * 2 * kz + kz
    last, first = pl.pallas_call(
        functools.partial(pack_x_body, cx),
        out_shape=[shape((rows_x, LANES), BF)] * 2,
        name="pack_x",
    )(volume, upstream, tile)
    low, high = exchange(last, first, "gx")
    rows_y = (cx + 2 * FIELD_HALO) * FIELD_HALO * kz + (cx + 2) * 2 * kz + 3 * kz
    last, first = pl.pallas_call(
        functools.partial(pack_y_body, cx, cy, kz),
        out_shape=[shape((rows_y, LANES), BF)] * 2,
        name="pack_y",
    )(volume, upstream, tile, low, high)
    left, right = exchange(last, first, "gy")
    w1, w2 = pair_weights(w_first), pair_weights(w_second)
    w3 = pair_weights(jnp.transpose(w_second[::-1], (0, 2, 1)))
    b1 = jnp.concatenate([b_first, b_first]).reshape(1, -1)
    b2 = jnp.concatenate([b_second, b_second]).reshape(1, -1)
    ex, ey = cx + 2 * FIELD_HALO, cy + 2 * FIELD_HALO
    features, d2, g2p, g2s, gate, xp, xs = pl.pallas_call(
        functools.partial(forward_body, cx, cy, kz),
        out_shape=[
            shape((cx, cy, 2 * kz, chan), BF),
            shape(w_second.shape, F32),
            shape((cx + 2, cy + 2, kz, 2 * chan), BF),
            shape((cx + 2, cy + 2, kz, 2 * chan), BF),
            shape((cx, cy, kz, 2 * chan), F32),
            shape((ex, ey, kz, LANES), BF),
            shape((ex, ey, kz, LANES), BF),
        ],
        scratch_shapes=[
            pltpu.VMEM((cx + 4, cy + 4, kz, 2 * chan), BF),
            pltpu.VMEM((cx + 4, cy + 4, kz, 2 * chan), BF),
            pltpu.VMEM((cx + 4, cy + 4, kz, 2 * chan), BF),
            pltpu.VMEM(((cx + 2) * (cy + 2) * 2 * kz, LANES), F32),
            pltpu.VMEM(((cx + 2) * (cy + 2) * 2 * kz, LANES), F32),
        ],
        name="forward",
    )(volume, upstream, tile, low, high, left, right, w1, b1, w2, b2)
    d1 = pl.pallas_call(
        functools.partial(backward_body, cx, cy, kz),
        out_shape=shape(w_first.shape, F32),
        scratch_shapes=[pltpu.VMEM((cx * cy * kz, 2 * chan), BF)],
        name="backward",
    )(g2p, g2s, gate, xp, xs, w3)
    rows_first = d1.shape[0] * d1.shape[1]
    rows = jnp.concatenate([d1.reshape(-1, chan), d2.reshape(-1, chan)], axis=0)
    sums = summed_everywhere(rows, ("gx", "gy"))
    sum_first = sums[:rows_first].reshape(d1.shape)
    sum_second = sums[rows_first:].reshape(d2.shape)
    step_first = normalized_with(sum_first, jnp.sum(sum_first * sum_first), float(d1.size))
    step_second = normalized_with(sum_second, jnp.sum(sum_second * sum_second), float(d2.size))
    return (features, step_first, step_second)


def solution(mesh):
    in_specs = (
        P("gx", "gy", None, None),
        P("gx", "gy", None),
        P(),
        P(),
        P(),
        P(),
        P("gx", "gy", None, None),
    )
    out_specs = (P("gx", "gy", None, None), P(), P())
    return jax.shard_map(
        on_device, mesh=mesh, in_specs=in_specs, out_specs=out_specs, check_vma=False
    )
```

time: 185 us -> 117 us (0.63)
  local copies, waits for them, and re-layouts: 43.9 us -> 6.49 us
  starting transfers between devices: 56.3 us -> 29.1 us
  Pallas kernels: 0 us -> 21.5 us
  matrix products: 21.2 us -> 0 us
  other arithmetic: 22.1 us -> 14.8 us
  waiting for transfers between devices: 36.5 us -> 42.5 us
    ppermute x12 -> x4, starting transfers between devices: 36.2 us -> 9.35 us  [the longest x2 6.63 us: exchange(): lax.ppermute(forward, axis, ups)]
    pallas_call x0 -> x4, Pallas kernels: none -> 21.5 us  [the longest x1 12 us: on_device(): pl.pallas_call(functools.partial(forward_body, cx, cy, kz), out_shape=[sh...]
    dot_general x45 -> x0, matrix products: 21.2 us -> none  [the longest x27 13.3 us: convolve(): total = total + jnp.dot(window, kernel, preferred_element_type=jnp.float32)]
    dot_general x10 -> x0, local copies, waits for them, and re-layouts: 11.9 us -> none  [weight_grad(): lax.dot_general(window, grad, (((0,), (0,)), ((), ())), preferred_element...]
    slice x16 -> x1, local copies, waits for them, and re-layouts: 10.8 us -> 0.08 us  [pair_weights(): even = jnp.concatenate([w[:, 1], w[:, 2], none, w[:, 0]], axis=1)]
    reshape x9 -> x2, local copies, waits for them, and re-layouts: 10.7 us -> 0.16 us  [the longest x1 0.09 us: on_device(): tile = basin_mask.astype(BF).reshape(cx * cy, kz, 2).transpose(1, 0, 2)]
    ppermute x12 -> x4, waiting for transfers between devices: 0.16 us -> 5.98 us  [the longest x2 4.58 us: exchange(): lax.ppermute(backward, axis, downs)]
    concatenate x23 -> x4, other arithmetic: 9.75 us -> 5.03 us  [the longest x2 3.83 us: pair_weights(): both = jnp.concatenate([even, odd], axis=2)]
  transfers between devices with their start and end apart: 22 -> 14, of which waited for: 11 -> 12; matrix products, arithmetic and copies ran while one was open for 14% -> 6% of each run, Pallas kernels for 0% -> 0%
where the time goes in v2:
time: 117 us
  waiting for transfers between devices  42.5 us (36%)
  starting transfers between devices  29.1 us (25%)
  Pallas kernels  21.5 us (18%)
  other arithmetic  14.8 us (13%)
  local copies, waits for them, and re-layouts  6.49 us (6%)
  between operations  2.24 us (2%)
    ppermute x10, waiting for transfers between devices, swap_with(): lax.ppermute(part, axis, [(i, i ^ bit) for i in range(lax.axis_size(axis))])  36.6 us
    ppermute x10, starting transfers between devices, swap_with(): lax.ppermute(part, axis, [(i, i ^ bit) for i in range(lax.axis_size(axis))])  19.8 us
    pallas_call x1, Pallas kernels, on_device(): pl.pallas_call(functools.partial(forward_body, cx, cy, kz), out_shape=[sh...  12 us
    ppermute x2, starting transfers between devices, exchange(): lax.ppermute(forward, axis, ups)  6.63 us
    pallas_call x1, Pallas kernels, on_device(): pl.pallas_call(functools.partial(backward_body, cx, cy, kz), out_shape=sh...  5.88 us
    ppermute x2, waiting for transfers between devices, exchange(): lax.ppermute(backward, axis, downs)  4.58 us
    unnamed x25, local copies, waits for them, and re-layouts  3.93 us
    concatenate x2, other arithmetic, pair_weights(): both = jnp.concatenate([even, odd], axis=2)  3.83 us
  transfers between devices with their start and end apart: 14, of which 12 were waited for; matrix products, arithmetic and copies ran while one was open for 6% of the time, Pallas kernels for 0%

profile of v2, /device:TPU:0, one launch (start us, length us, event | category | flops | bytes accessed | tf_op | source)
XLA Modules:
  0.0 116.7 jit_solution(12188774826021650252)
XLA Ops:
  0.6 0.7 convert_element_type.41
  1.7 0.6 pad.4.tile
  2.3 1.7 %pack_x.1 = (bf16[656,128]{1,0:T(8,128)(2,1)}, bf16[656,128]{1,0:T(8,128)(2,1)}) custom-call(bf16[4,8,16,128]{3,2,1,0:T(8,128)(2,1)} %field.5, bf16[4,8,32,128]{3,2,1,0:T(8,128)(2,1)} %up.5, bf16[16,128]{1,0:T(8,128)(2,1)} %pad.4.tile), custom_call_target="tpu_custom_call" | custom-call | tf_op jit(solution)/shard_map/pack_x/pallas_call | solution.py:329
  4.1 2.4 %collective-permute-start = (bf16[656,128]{1,0:T(8,128)(2,1)}, bf16[656,128]{1,0:T(8,128)(2,1)S(1)}, u32[]{:S(2)}, u32[]{:S(2)}) collective-permute-start(bf16[656,128]{1,0:T(8,128)(2,1)} %get-tuple-element.14), channel_id=1, source_target_pairs={{0,8},{8,16},{16,24},{1,9},{9,17},{17,25},{2,10},{10,18},{18,26},{... | collective-permute-start | bytes 503816 | tf_op jit(solution)/shard_map/ppermute | solution.py:72
  6.5 1.4 %collective-permute-start.1 = (bf16[656,128]{1,0:T(8,128)(2,1)}, bf16[656,128]{1,0:T(8,128)(2,1)S(1)}, u32[]{:S(2)}, u32[]{:S(2)}) collective-permute-start(bf16[656,128]{1,0:T(8,128)(2,1)} %get-tuple-element.15), channel_id=1, source_target_pairs={{8,0},{16,8},{24,16},{9,1},{17,9},{25,17},{10,2},{18,10},{26,18},{... | collective-permute-start | bytes 503816 | tf_op jit(solution)/shard_map/ppermute | solution.py:72
  7.9 1.2 %rev.3 = bf16[27,128,128]{2,1,0:T(8,128)(2,1)S(1)} reverse(bf16[27,128,128]{2,1,0:T(8,128)(2,1)} %param.11), dimensions={0} | reverse | bytes 1769472 | tf_op jit(solution)/shard_map/rev | solution.py:343
  9.5 0.2 copy.39
  10.3 2.7 %fusion.3 = (bf16[9,512,256]{2,1,0:T(8,128)(2,1)}, bf16[9,512,256]{2,1,0:T(8,128)(2,1)}) fusion(bf16[9,128,128]{2,1,0:T(8,128)(2,1)S(1)} %broadcast.19, bf16[9,128,128]{2,1,0:T(8,128)(2,1)S(1)} %bitcast.56, bf16[9,128,128]{2,1,0:T(8,128)(2,1)S(1)} %bitcast.55, bf16[9,128,128]{2,1,0:T(8,128)(2,1)S(1)} %bitcast.57, ...), kind=kLoop, calls=%fused_computation.11 | loop fusion | flops 35389440 | bytes 6782976 | tf_op jit(solution)/shard_map/concatenate | solution.py:317
  12.9 0.6 pad_maximum_fusion.5
  13.5 0.6 pad_maximum_fusion.4
  14.2 0.7 copy-done.4
  14.8 0.7 copy-done.5
  15.5 1.9 %pack_y.1 = (bf16[720,128]{1,0:T(8,128)(2,1)}, bf16[720,128]{1,0:T(8,128)(2,1)}) custom-call(bf16[4,8,16,128]{3,2,1,0:T(8,128)(2,1)} %field.5, bf16[4,8,32,128]{3,2,1,0:T(8,128)(2,1)} %up.5, bf16[16,128]{1,0:T(8,128)(2,1)} %pad.4.tile, bf16[656,128]{1,0:T(8,128)(2,1)} %copy-done.4, bf16[656,128]{1,0:T(8,128)(2,1)} %copy-done.5), custom_call_target="tpu_custom_call" | custom-call | tf_op jit(solution)/shard_map/pack_y/pallas_call | solution.py:336
  17.4 4.2 %collective-permute-start.2 = (bf16[720,128]{1,0:T(8,128)(2,1)}, bf16[720,128]{1,0:T(8,128)(2,1)S(1)}, u32[]{:S(2)}, u32[]{:S(2)}) collective-permute-start(bf16[720,128]{1,0:T(8,128)(2,1)} %get-tuple-element.16), channel_id=1, source_target_pairs={{0,1},{1,2},{2,3},{3,4},{4,5},{5,6},{6,7},{8,9},{9,10},{10,11},{11... | collective-permute-start | bytes 552968 | tf_op jit(solution)/shard_map/ppermute | solution.py:72
  21.6 1.3 %collective-permute-start.3 = (bf16[720,128]{1,0:T(8,128)(2,1)}, bf16[720,128]{1,0:T(8,128)(2,1)S(1)}, u32[]{:S(2)}, u32[]{:S(2)}) collective-permute-start(bf16[720,128]{1,0:T(8,128)(2,1)} %get-tuple-element.17), channel_id=1, source_target_pairs={{1,0},{2,1},{3,2},{4,3},{5,4},{6,5},{7,6},{9,8},{10,9},{11,10},{12... | collective-permute-start | bytes 552968 | tf_op jit(solution)/shard_map/ppermute | solution.py:72
  23.0 1.2 maximum_maximum_fusion
  24.1 1.4 %collective-permute-done.2.left = bf16[720,128]{1,0:T(8,128)(2,1)S(1)} collective-permute-done((bf16[720,128]{1,0:T(8,128)(2,1)}, bf16[720,128]{1,0:T(8,128)(2,1)S(1)}, u32[]{:S(2)}, u32[]{:S(2)}) %collective-permute-start.2) | collective-permute-done | bytes 184352 | tf_op jit(solution)/shard_map/ppermute | solution.py:72
  25.5 4.6 %collective-permute-done.3.right = bf16[720,128]{1,0:T(8,128)(2,1)S(1)} collective-permute-done((bf16[720,128]{1,0:T(8,128)(2,1)}, bf16[720,128]{1,0:T(8,128)(2,1)S(1)}, u32[]{:S(2)}, u32[]{:S(2)}) %collective-permute-start.3) | collective-permute-done | bytes 184352 | tf_op jit(solution)/shard_map/ppermute | solution.py:72
  30.1 0.7 copy-done.8
  30.8 12.0 %forward.1 = (bf16[4,8,32,128]{3,2,1,0:T(8,128)(2,1)}, f32[27,128,128]{2,1,0:T(8,128)}, bf16[6,10,16,256]{3,2,1,0:T(8,128)(2,1)}, bf16[6,10,16,256]{3,2,1,0:T(8,...) custom-call(bf16[4,8,16,128]{3,2,1,0:T(8,128)(2,1)} %field.5, ...), custom_call_target="tpu_custom_call" | custom-call | tf_op jit(solution)/shard_map/forward/pallas_call | solution.py:347
  42.8 5.9 %backward.1 = f32[27,64,128]{2,1,0:T(8,128)} custom-call(bf16[6,10,16,256]{3,2,1,0:T(8,128)(2,1)} %get-tuple-element.19.g2p, bf16[6,10,16,256]{3,2,1,0:T(8,128)(2,1)} %get-tuple-element.20.g2s, f32[4,8,16,256]{3,2,1,0:T(8,128)} %get-tuple-element.21.gate, bf16[10,14,16,128]{3,2,1,0:T(8,128)(2,1)} %get-tuple-element.22.xp, ...), custom_call_target="tpu_custom_call" | custom-call | tf_op jit(solution)/shard_map/backward/pallas_call | solution.py:367
  48.7 1.2 %fusion.5 = bf16[2592,128]{1,0:T(8,128)(2,1)} fusion(s32[]{:T(128)S(6)} %select_n.97, f32[3456,128]{1,0:T(8,128)S(1)} %bitcast.49, f32[1728,128]{1,0:T(8,128)} %bitcast.47), kind=kLoop, calls=%fused_computation.15 | loop fusion | flops 1327104 | bytes 3317764 | tf_op jit(solution)/shard_map/convert_element_type | solution.py:39
  49.8 2.2 %collective-permute-start.4 = (bf16[2592,128]{1,0:T(8,128)(2,1)}, bf16[2592,128]{1,0:T(8,128)(2,1)S(1)}, u32[]{:S(2)}, u32[]{:S(2)}) collective-permute-start(bf16[2592,128]{1,0:T(8,128)(2,1)} %fusion.5), channel_id=1, source_target_pairs={{0,8},{8,0},{16,24},{24,16},{1,9},{9,1},{17,25},{25,17},{2,10},{10... | collective-permute-start | bytes 1990664 | tf_op jit(solution)/shard_map/ppermute | solution.py:28
  52.1 1.9 %collective-permute-done.4 = bf16[2592,128]{1,0:T(8,128)(2,1)S(1)} collective-permute-done((bf16[2592,128]{1,0:T(8,128)(2,1)}, bf16[2592,128]{1,0:T(8,128)(2,1)S(1)}, u32[]{:S(2)}, u32[]{:S(2)}) %collective-permute-start.4) | collective-permute-done | bytes 663584 | tf_op jit(solution)/shard_map/ppermute | solution.py:28
  54.0 0.5 fusion.7
  54.5 1.1 copy-done.2
  55.6 1.4 %collective-permute-start.5 = (bf16[1296,128]{1,0:T(8,128)(2,1)S(1)}, bf16[1296,128]{1,0:T(8,128)(2,1)S(1)}, u32[]{:S(2)}, u32[]{:S(2)}) collective-permute-start(bf16[1296,128]{1,0:T(8,128)(2,1)S(1)} %dynamic-slice_convert_fusion), channel_id=1, source_target_pairs={{0,16},{8,24},{16,0},{24,8},{1,17},{9,25},{17,1},{25,9},{2,18},{10... | collective-permute-start | bytes 995336 | tf_op jit(solution)/shard_map/ppermute | solution.py:28
  57.0 8.7 %collective-permute-done.5 = bf16[1296,128]{1,0:T(8,128)(2,1)S(1)} collective-permute-done((bf16[1296,128]{1,0:T(8,128)(2,1)S(1)}, bf16[1296,128]{1,0:T(8,128)(2,1)S(1)}, u32[]{:S(2)}, u32[]{:S(2)}) %collective-permute-start.5) | collective-permute-done | bytes 331808 | tf_op jit(solution)/shard_map/ppermute | solution.py:28
  65.8 1.2 convert_add_fusion
  67.0 2.5 %collective-permute-start.6 = (bf16[648,128]{1,0:T(8,128)(2,1)S(1)}, bf16[648,128]{1,0:T(8,128)(2,1)S(1)}, u32[]{:S(2)}, u32[]{:S(2)}) collective-permute-start(bf16[648,128]{1,0:T(8,128)(2,1)S(1)} %dynamic-slice_convert_fusion.1), channel_id=1, source_target_pairs={{0,1},{1,0},{2,3},{3,2},{4,5},{5,4},{6,7},{7,6},{8,9},{9,8},{10,11... | collective-permute-start | bytes 497672 | tf_op jit(solution)/shard_map/ppermute | solution.py:28
  69.5 3.9 %collective-permute-done.6 = bf16[648,128]{1,0:T(8,128)(2,1)S(1)} collective-permute-done((bf16[648,128]{1,0:T(8,128)(2,1)S(1)}, bf16[648,128]{1,0:T(8,128)(2,1)S(1)}, u32[]{:S(2)}, u32[]{:S(2)}) %collective-permute-start.6) | collective-permute-done | bytes 165920 | tf_op jit(solution)/shard_map/ppermute | solution.py:28
  73.5 2.6 %collective-permute-start.7 = (bf16[324,128]{1,0:T(8,128)(2,1)S(1)}, bf16[324,128]{1,0:T(8,128)(2,1)S(1)}, u32[]{:S(2)}, u32[]{:S(2)}) collective-permute-start(bf16[324,128]{1,0:T(8,128)(2,1)S(1)} %dynamic-slice_convert_fusion.2), channel_id=1, source_target_pairs={{0,2},{1,3},{2,0},{3,1},{4,6},{5,7},{6,4},{7,5},{8,10},{9,11},{10,... | collective-permute-start | bytes 248840 | tf_op jit(solution)/shard_map/ppermute | solution.py:28
  76.0 2.4 %collective-permute-done.7 = bf16[324,128]{1,0:T(8,128)(2,1)S(1)} collective-permute-done((bf16[324,128]{1,0:T(8,128)(2,1)S(1)}, bf16[324,128]{1,0:T(8,128)(2,1)S(1)}, u32[]{:S(2)}, u32[]{:S(2)}) %collective-permute-start.7) | collective-permute-done | bytes 82976 | tf_op jit(solution)/shard_map/ppermute | solution.py:28
  78.5 3.1 %collective-permute-start.8 = (bf16[162,128]{1,0:T(8,128)(2,1)S(1)}, bf16[162,128]{1,0:T(8,128)(2,1)S(1)}, u32[]{:S(2)}, u32[]{:S(2)}) collective-permute-start(bf16[162,128]{1,0:T(8,128)(2,1)S(1)} %dynamic-slice_convert_fusion.3), channel_id=1, source_target_pairs={{0,4},{1,5},{2,6},{3,7},{4,0},{5,1},{6,2},{7,3},{8,12},{9,13},{10,... | collective-permute-start | bytes 124424 | tf_op jit(solution)/shard_map/ppermute | solution.py:28
  81.6 2.0 %collective-permute-done.8 = bf16[162,128]{1,0:T(8,128)(2,1)S(1)} collective-permute-done((bf16[162,128]{1,0:T(8,128)(2,1)S(1)}, bf16[162,128]{1,0:T(8,128)(2,1)S(1)}, u32[]{:S(2)}, u32[]{:S(2)}) %collective-permute-start.8) | collective-permute-done | bytes 41504 | tf_op jit(solution)/shard_map/ppermute | solution.py:28
  83.7 3.0 %collective-permute-start.9 = (bf16[162,128]{1,0:T(8,128)(2,1)S(1)}, bf16[162,128]{1,0:T(8,128)(2,1)S(1)}, u32[]{:S(2)}, u32[]{:S(2)}) collective-permute-start(bf16[162,128]{1,0:T(8,128)(2,1)S(1)} %add_convert_fusion), channel_id=1, source_target_pairs={{0,4},{1,5},{2,6},{3,7},{4,0},{5,1},{6,2},{7,3},{8,12},{9,13},{10,... | collective-permute-start | bytes 124424 | tf_op jit(solution)/shard_map/ppermute | solution.py:28
  86.7 2.0 %collective-permute-done.9 = bf16[162,128]{1,0:T(8,128)(2,1)S(1)} collective-permute-done((bf16[162,128]{1,0:T(8,128)(2,1)S(1)}, bf16[162,128]{1,0:T(8,128)(2,1)S(1)}, u32[]{:S(2)}, u32[]{:S(2)}) %collective-permute-start.9) | collective-permute-done | bytes 41504 | tf_op jit(solution)/shard_map/ppermute | solution.py:28
  88.8 3.1 %collective-permute-start.10 = (bf16[324,128]{1,0:T(8,128)(2,1)S(1)}, bf16[324,128]{1,0:T(8,128)(2,1)S(1)}, u32[]{:S(2)}, u32[]{:S(2)}) collective-permute-start(bf16[324,128]{1,0:T(8,128)(2,1)S(1)} %maximum_select_fusion.4), channel_id=1, source_target_pairs={{0,2},{1,3},{2,0},{3,1},{4,6},{5,7},{6,4},{7,5},{8,10},{9,11},{10,... | collective-permute-start | bytes 248840 | tf_op jit(solution)/shard_map/ppermute | solution.py:28
  91.9 2.4 %collective-permute-done.10 = bf16[324,128]{1,0:T(8,128)(2,1)S(1)} collective-permute-done((bf16[324,128]{1,0:T(8,128)(2,1)S(1)}, bf16[324,128]{1,0:T(8,128)(2,1)S(1)}, u32[]{:S(2)}, u32[]{:S(2)}) %collective-permute-start.10) | collective-permute-done | bytes 82976 | tf_op jit(solution)/shard_map/ppermute | solution.py:28
  94.5 5.3 %collective-permute-done.11 = bf16[648,128]{1,0:T(8,128)(2,1)S(1)} collective-permute-done((bf16[648,128]{1,0:T(8,128)(2,1)S(1)}, bf16[648,128]{1,0:T(8,128)(2,1)S(1)}, u32[]{:S(2)}, u32[]{:S(2)}) %collective-permute-start.11) | collective-permute-done | bytes 165920 | tf_op jit(solution)/shard_map/ppermute | solution.py:28
  99.9 1.6 %collective-permute-start.12 = (bf16[1296,128]{1,0:T(8,128)(2,1)S(1)}, bf16[1296,128]{1,0:T(8,128)(2,1)S(1)}, u32[]{:S(2)}, u32[]{:S(2)}) collective-permute-start(bf16[1296,128]{1,0:T(8,128)(2,1)S(1)} %maximum_select_fusion.2), channel_id=1, source_target_pairs={{0,16},{8,24},{16,0},{24,8},{1,17},{9,25},{17,1},{25,9},{2,18},{10... | collective-permute-start | bytes 995336 | tf_op jit(solution)/shard_map/ppermute | solution.py:28
  101.5 5.6 %collective-permute-done.12 = bf16[1296,128]{1,0:T(8,128)(2,1)S(1)} collective-permute-done((bf16[1296,128]{1,0:T(8,128)(2,1)S(1)}, bf16[1296,128]{1,0:T(8,128)(2,1)S(1)}, u32[]{:S(2)}, u32[]{:S(2)}) %collective-permute-start.12) | collective-permute-done | bytes 331808 | tf_op jit(solution)/shard_map/ppermute | solution.py:28
  107.3 2.2 %collective-permute-done.13 = bf16[2592,128]{1,0:T(8,128)(2,1)} collective-permute-done((bf16[2592,128]{1,0:T(8,128)(2,1)S(1)}, bf16[2592,128]{1,0:T(8,128)(2,1)}, u32[]{:S(2)}, u32[]{:S(2)}) %collective-permute-start.13) | collective-permute-done | bytes 663584 | tf_op jit(solution)/shard_map/ppermute | solution.py:28
  109.6 1.6 %fusion.8 = f32[5184,128]{1,0:T(8,128)S(1)} fusion(bf16[2592,128]{1,0:T(8,128)(2,1)} %collective-permute-done.13, bf16[2592,128]{1,0:T(8,128)(2,1)S(1)} %maximum_select_fusion.1, pred[]{:T(512)S(6)} %eq.15), kind=kLoop, calls=%fused_computation.19 | loop fusion | flops 6635520 | bytes 3981313 | tf_op jit(solution)/shard_map/convert_element_type | solution.py:61
  111.1 1.1 multiply_reduce_fusion
  112.2 0.8 multiply_reduce_fusion.1
  113.7 1.3 %slice_multiply_fusion = f32[3456,128]{1,0:T(8,128)} fusion(f32[5184,128]{1,0:T(8,128)S(1)} %fusion.8, f32[]{:T(128)S(6)} %rsqrt.7), kind=kLoop, calls=%fused_computation.13 | loop fusion | flops 442368 | bytes 3538948 | tf_op jit(solution)/shard_map/mul | solution.py:65
  115.7 1.0 slice_multiply_fusion.1
  (44 shorter events, 2.0 us)
Async XLA Ops:
  4.1 10.1 %collective-permute-start = (bf16[656,128]{1,0:T(8,128)(2,1)}, bf16[656,128]{1,0:T(8,128)(2,1)S(1)}, u32[]{:S(2)}, u32[]{:S(2)}) collective-permute-start(bf16[656,128]{1,0:T(8,128)(2,1)} %get-tuple-element.14), channel_id=1, source_target_pairs={{0,8},{8,16},{16,24},{1,9},{9,17},{17,25},{2,10},{10,18},{18,26},{... | collective-permute-start | bytes 503816 | tf_op jit(solution)/shard_map/ppermute | solution.py:72
  6.5 3.5 %copy-start.3 = (bf16[27,128,128]{2,1,0:T(8,128)(2,1)S(1)}, bf16[27,128,128]{2,1,0:T(8,128)(2,1)}, u32[]{:S(2)}) copy-start(bf16[27,128,128]{2,1,0:T(8,128)(2,1)} %param.11) | copy-start | bytes 2654212
  6.5 7.7 %collective-permute-start.1 = (bf16[656,128]{1,0:T(8,128)(2,1)}, bf16[656,128]{1,0:T(8,128)(2,1)S(1)}, u32[]{:S(2)}, u32[]{:S(2)}) collective-permute-start(bf16[656,128]{1,0:T(8,128)(2,1)} %get-tuple-element.15), channel_id=1, source_target_pairs={{8,0},{16,8},{24,16},{9,1},{17,9},{25,17},{10,2},{18,10},{26,18},{... | collective-permute-start | bytes 503816 | tf_op jit(solution)/shard_map/ppermute | solution.py:72
  9.2 1.0 copy-start.6
  10.3 2.7 %copy-start.9 = (f32[128]{0:T(128)S(1)}, f32[128]{0:T(128)}, u32[]{:S(2)}) copy-start(f32[128]{0:T(128)} %param.12) | copy-start | bytes 1540
  10.3 3.3 %copy-start.10 = (f32[128]{0:T(128)S(1)}, f32[128]{0:T(128)}, u32[]{:S(2)}) copy-start(f32[128]{0:T(128)} %param.10) | copy-start | bytes 1540
  14.1 0.7 copy-start.4
  14.8 0.7 copy-start.5
  17.4 8.1 %collective-permute-start.2 = (bf16[720,128]{1,0:T(8,128)(2,1)}, bf16[720,128]{1,0:T(8,128)(2,1)S(1)}, u32[]{:S(2)}, u32[]{:S(2)}) collective-permute-start(bf16[720,128]{1,0:T(8,128)(2,1)} %get-tuple-element.16), channel_id=1, source_target_pairs={{0,1},{1,2},{2,3},{3,4},{4,5},{5,6},{6,7},{8,9},{9,10},{10,11},{11... | collective-permute-start | bytes 552968 | tf_op jit(solution)/shard_map/ppermute | solution.py:72
  21.6 8.5 %collective-permute-start.3 = (bf16[720,128]{1,0:T(8,128)(2,1)}, bf16[720,128]{1,0:T(8,128)(2,1)S(1)}, u32[]{:S(2)}, u32[]{:S(2)}) collective-permute-start(bf16[720,128]{1,0:T(8,128)(2,1)} %get-tuple-element.17), channel_id=1, source_target_pairs={{1,0},{2,1},{3,2},{4,3},{5,4},{6,5},{7,6},{9,8},{10,9},{11,10},{12... | collective-permute-start | bytes 552968 | tf_op jit(solution)/shard_map/ppermute | solution.py:72
  25.5 4.6 %copy-start.7 = (bf16[720,128]{1,0:T(8,128)(2,1)}, bf16[720,128]{1,0:T(8,128)(2,1)S(1)}, u32[]{:S(2)}) copy-start(bf16[720,128]{1,0:T(8,128)(2,1)S(1)} %collective-permute-done.2.left) | copy-start | bytes 552964
  30.1 0.7 copy-start.8
  42.8 5.9 %copy-start.1 = (f32[27,128,128]{2,1,0:T(8,128)S(1)}, f32[27,128,128]{2,1,0:T(8,128)}, u32[]{:S(2)}) copy-start(f32[27,128,128]{2,1,0:T(8,128)} %get-tuple-element.24) | copy-start | bytes 5308420
  48.6 5.4 %copy-start = (f32[27,64,128]{2,1,0:T(8,128)S(1)}, f32[27,64,128]{2,1,0:T(8,128)}, u32[]{:S(2)}) copy-start(f32[27,64,128]{2,1,0:T(8,128)} %backward.1) | copy-start | bytes 2654212
  49.8 4.2 %collective-permute-start.4 = (bf16[2592,128]{1,0:T(8,128)(2,1)}, bf16[2592,128]{1,0:T(8,128)(2,1)S(1)}, u32[]{:S(2)}, u32[]{:S(2)}) collective-permute-start(bf16[2592,128]{1,0:T(8,128)(2,1)} %fusion.5), channel_id=1, source_target_pairs={{0,8},{8,0},{16,24},{24,16},{1,9},{9,1},{17,25},{25,17},{2,10},{10... | collective-permute-start | bytes 1990664 | tf_op jit(solution)/shard_map/ppermute | solution.py:28
  54.5 1.1 copy-start.2
  55.6 10.1 %collective-permute-start.5 = (bf16[1296,128]{1,0:T(8,128)(2,1)S(1)}, bf16[1296,128]{1,0:T(8,128)(2,1)S(1)}, u32[]{:S(2)}, u32[]{:S(2)}) collective-permute-start(bf16[1296,128]{1,0:T(8,128)(2,1)S(1)} %dynamic-slice_convert_fusion), channel_id=1, source_target_pairs={{0,16},{8,24},{16,0},{24,8},{1,17},{9,25},{17,1},{25,9},{2,18},{10... | collective-permute-start | bytes 995336 | tf_op jit(solution)/shard_map/ppermute | solution.py:28
  67.0 6.4 %collective-permute-start.6 = (bf16[648,128]{1,0:T(8,128)(2,1)S(1)}, bf16[648,128]{1,0:T(8,128)(2,1)S(1)}, u32[]{:S(2)}, u32[]{:S(2)}) collective-permute-start(bf16[648,128]{1,0:T(8,128)(2,1)S(1)} %dynamic-slice_convert_fusion.1), channel_id=1, source_target_pairs={{0,1},{1,0},{2,3},{3,2},{4,5},{5,4},{6,7},{7,6},{8,9},{9,8},{10,11... | collective-permute-start | bytes 497672 | tf_op jit(solution)/shard_map/ppermute | solution.py:28
  73.5 5.0 %collective-permute-start.7 = (bf16[324,128]{1,0:T(8,128)(2,1)S(1)}, bf16[324,128]{1,0:T(8,128)(2,1)S(1)}, u32[]{:S(2)}, u32[]{:S(2)}) collective-permute-start(bf16[324,128]{1,0:T(8,128)(2,1)S(1)} %dynamic-slice_convert_fusion.2), channel_id=1, source_target_pairs={{0,2},{1,3},{2,0},{3,1},{4,6},{5,7},{6,4},{7,5},{8,10},{9,11},{10,... | collective-permute-start | bytes 248840 | tf_op jit(solution)/shard_map/ppermute | solution.py:28
  78.5 5.1 %collective-permute-start.8 = (bf16[162,128]{1,0:T(8,128)(2,1)S(1)}, bf16[162,128]{1,0:T(8,128)(2,1)S(1)}, u32[]{:S(2)}, u32[]{:S(2)}) collective-permute-start(bf16[162,128]{1,0:T(8,128)(2,1)S(1)} %dynamic-slice_convert_fusion.3), channel_id=1, source_target_pairs={{0,4},{1,5},{2,6},{3,7},{4,0},{5,1},{6,2},{7,3},{8,12},{9,13},{10,... | collective-permute-start | bytes 124424 | tf_op jit(solution)/shard_map/ppermute | solution.py:28
  83.7 5.0 %collective-permute-start.9 = (bf16[162,128]{1,0:T(8,128)(2,1)S(1)}, bf16[162,128]{1,0:T(8,128)(2,1)S(1)}, u32[]{:S(2)}, u32[]{:S(2)}) collective-permute-start(bf16[162,128]{1,0:T(8,128)(2,1)S(1)} %add_convert_fusion), channel_id=1, source_target_pairs={{0,4},{1,5},{2,6},{3,7},{4,0},{5,1},{6,2},{7,3},{8,12},{9,13},{10,... | collective-permute-start | bytes 124424 | tf_op jit(solution)/shard_map/ppermute | solution.py:28
  88.8 5.6 %collective-permute-start.10 = (bf16[324,128]{1,0:T(8,128)(2,1)S(1)}, bf16[324,128]{1,0:T(8,128)(2,1)S(1)}, u32[]{:S(2)}, u32[]{:S(2)}) collective-permute-start(bf16[324,128]{1,0:T(8,128)(2,1)S(1)} %maximum_select_fusion.4), channel_id=1, source_target_pairs={{0,2},{1,3},{2,0},{3,1},{4,6},{5,7},{6,4},{7,5},{8,10},{9,11},{10,... | collective-permute-start | bytes 248840 | tf_op jit(solution)/shard_map/ppermute | solution.py:28
  94.4 5.4 %collective-permute-start.11 = (bf16[648,128]{1,0:T(8,128)(2,1)S(1)}, bf16[648,128]{1,0:T(8,128)(2,1)S(1)}, u32[]{:S(2)}, u32[]{:S(2)}) collective-permute-start(bf16[648,128]{1,0:T(8,128)(2,1)S(1)} %maximum_select_fusion.3), channel_id=1, source_target_pairs={{0,1},{1,0},{2,3},{3,2},{4,5},{5,4},{6,7},{7,6},{8,9},{9,8},{10,11... | collective-permute-start | bytes 497672 | tf_op jit(solution)/shard_map/ppermute | solution.py:28
  99.9 7.2 %collective-permute-start.12 = (bf16[1296,128]{1,0:T(8,128)(2,1)S(1)}, bf16[1296,128]{1,0:T(8,128)(2,1)S(1)}, u32[]{:S(2)}, u32[]{:S(2)}) collective-permute-start(bf16[1296,128]{1,0:T(8,128)(2,1)S(1)} %maximum_select_fusion.2), channel_id=1, source_target_pairs={{0,16},{8,24},{16,0},{24,8},{1,17},{9,25},{17,1},{25,9},{2,18},{10... | collective-permute-start | bytes 995336 | tf_op jit(solution)/shard_map/ppermute | solution.py:28
  107.3 2.3 %collective-permute-start.13 = (bf16[2592,128]{1,0:T(8,128)(2,1)S(1)}, bf16[2592,128]{1,0:T(8,128)(2,1)}, u32[]{:S(2)}, u32[]{:S(2)}) collective-permute-start(bf16[2592,128]{1,0:T(8,128)(2,1)S(1)} %maximum_select_fusion.1), channel_id=1, source_target_pairs={{0,8},{8,0},{16,24},{24,16},{1,9},{9,1},{17,25},{25,17},{2,10},{10... | collective-permute-start | bytes 1990664 | tf_op jit(solution)/shard_map/ppermute | solution.py:28

commit v3 on v2

--- a/solution.py
+++ b/solution.py
@@ -24,45 +24,51 @@
     return levels
 
 
-def swap_with(part, axis, bit):
+def swap(part, level):
+    axis, bit = level
     return lax.ppermute(part, axis, [(i, i ^ bit) for i in range(lax.axis_size(axis))])
 
 
-def side_of(axis, bit):
+def side_of(level):
+    axis, bit = level
     return lax.rem(lax.axis_index(axis) // bit, 2)
 
 
-def halves_summed(part, levels):
-    for axis, bit in levels:
-        half = part.shape[0] // 2
-        side = side_of(axis, bit)
-        sent = lax.dynamic_slice_in_dim(part, (1 - side) * half, half, 0).astype(BF)
-        kept = lax.dynamic_slice_in_dim(part, side * half, half, 0)
-        part = kept + swap_with(sent, axis, bit).astype(F32)
-    return part
-
-
-def halves_joined(part, levels):
-    for axis, bit in reversed(levels):
-        other = swap_with(part, axis, bit)
-        part = jnp.where(
-            side_of(axis, bit) == 0,
-            jnp.concatenate([part, other], axis=0),
-            jnp.concatenate([other, part], axis=0),
+def halves(part, level):
+    half = part.shape[1] // 2
+    side = side_of(level)
+    sent = lax.dynamic_slice_in_dim(part, (1 - side) * half, half, 1).astype(BF)
+    kept = lax.dynamic_slice_in_dim(part, side * half, half, 1)
+    return sent, kept
+
+
+def joined(own, other, level):
+    return jnp.where(
+        side_of(level) == 0,
+        jnp.concatenate([own, other], axis=1),
+        jnp.concatenate([other, own], axis=1),
+    )
+
+
+def summed_inner(second, first, levels):
+    middle, final = levels[:-1], levels[-1]
+    for level in middle:
+        sent2, kept2 = halves(second, level)
+        sent1, kept1 = halves(first, level)
+        cut = sent2.shape[1]
+        got = swap(jnp.concatenate([sent2, sent1], axis=1), level).astype(F32)
+        second, first = kept2 + got[:, :cut], kept1 + got[:, cut:]
+    cut = second.shape[1]
+    both = jnp.concatenate([second, first], axis=1).astype(BF)
+    both = (both.astype(F32) + swap(both, final).astype(F32)).astype(BF)
+    for level in reversed(middle):
+        got = swap(both, level)
+        both = jnp.concatenate(
+            [joined(both[:, :cut], got[:, :cut], level), joined(both[:, cut:], got[:, cut:], level)],
+            axis=1,
         )
-    return part
-
-
-def summed_everywhere(rows, axes):
-    levels = bit_levels(axes)
-    pieces = 2 ** len(levels)
-    padded = jnp.pad(rows, ((0, -rows.shape[0] % pieces), (0, 0)))
-    summed = halves_summed(padded, levels).astype(BF)
-    return halves_joined(summed, levels)[: rows.shape[0]].astype(F32)
-
-
-def normalized_with(grad, total, count):
-    return grad * lax.rsqrt(total / count + 1e-06)
+        cut *= 2
+    return both[:, :cut], both[:, cut:]
 
 
 def exchange(forward, backward, axis):
@@ -72,7 +78,14 @@
     return lax.ppermute(forward, axis, ups), lax.ppermute(backward, axis, downs)
 
 
-def pack_x_body(cx, field, up, tile, last, first):
+def pack_x_body(cx, cy, kz, field, up, mask, last, first, tile, square, deep):
+    cells = cx * cy
+    square[...] = jnp.zeros_like(square)
+    square[0:cells, 0 : 2 * kz] = mask[...].reshape(cells, 2 * kz).astype(F32)
+    deep[...] = square[...].T
+    even = deep[pl.ds(0, kz, stride=2), :]
+    odd = deep[pl.ds(1, kz, stride=2), :]
+    tile[...] = (even + pltpu.roll(odd, LANES // 2, 1)).astype(BF)
     for ref, at_field, at_up in ((last, cx - FIELD_HALO, cx - 1), (first, 0, 0)):
         rows = field[at_field : at_field + FIELD_HALO].reshape(-1, LANES)
         ups = up[at_up : at_up + 1].reshape(-1, LANES)
@@ -123,9 +136,9 @@
 
 def forward_body(
     cx, cy, kz,
-    field, up, tile, low, high, left, right, w1, b1, w2, b2,
-    features, d2, g2p, g2s, gate, xp, xs,
-    hp, hs, act, upf, outf,
+    side, field, up, tile, low, high, left, right, w1, b1, w2, b2,
+    features, sent, kept, g2p, g2s, gate, xp, xs,
+    hp, hs, act, upf, outf, d2,
 ):
     fh, mh = FIELD_HALO, MASK_HALO
     nf, nu = fh * cy * kz, cy * 2 * kz
@@ -167,9 +180,9 @@
     nm = ne + (cx + 2) * 2 * kz
 
     def put_mask(source, sx, sy, x, y):
-        lane = 2 * (sx * cy + sy)
         for parity in range(2):
-            value = jnp.broadcast_to(source[:, lane + parity : lane + parity + 1], (kz, LANES))
+            lane = sx * cy + sy + parity * (LANES // 2)
+            value = jnp.broadcast_to(source[:, lane : lane + 1], (kz, LANES))
             act[x, y, :, parity * LANES : (parity + 1) * LANES] = value.astype(BF)
 
     def row_tiles(ref, start):
@@ -273,10 +286,18 @@
                 else:
                     d2[t] = d2[t] + q[1][0]
                     d2[t + 2] = d2[t + 2] + q[0][1]
-
-
-def backward_body(cx, cy, kz, g2p, g2s, gate, xp, xs, w3, d1, g1):
-    fh = FIELD_HALO
+    split_rows(side, d2, sent, kept)
+
+
+def split_rows(side, total, sent, kept):
+    half = total.shape[1] // 2
+    mine = pl.multiple_of(side[0] * half, half)
+    other = pl.multiple_of((1 - side[0]) * half, half)
+    sent[...] = total[:, pl.ds(other, half)].astype(BF)
+    kept[...] = total[:, pl.ds(mine, half)]
+
+
+def grad_body(cx, cy, kz, g2p, g2s, gate, w3, g1):
     step = 2
     rows = step * cy * kz
 
@@ -289,6 +310,10 @@
         return carry
 
     lax.fori_loop(0, cx // step, grad, 0)
+
+
+def first_body(cx, cy, kz, side, xp, xs, g1, sent, kept, d1):
+    fh = FIELD_HALO
     right = g1[...]
     cells = cx * cy * kz
     half = LANES // 2
@@ -307,76 +332,153 @@
             d1[t] = q[0][1] + q[3][0]
             d1[t + 1] = q[0][0] + q[1][1]
             d1[t + 2] = q[1][0] + q[2][1]
-
-
-def pair_weights(w):
-    w = w.reshape(9, 3, w.shape[1], w.shape[2])
-    none = jnp.zeros_like(w[:, 0])
-    even = jnp.concatenate([w[:, 1], w[:, 2], none, w[:, 0]], axis=1)
-    odd = jnp.concatenate([w[:, 0], w[:, 1], w[:, 2], none], axis=1)
-    both = jnp.concatenate([even, odd], axis=2)
-    return both.reshape(-1, both.shape[2])
+    split_rows(side, d1, sent, kept)
+
+
+def norm_body(side, own2, other2, own1, other1, out2, out1):
+    for own, other, out in ((own2, other2, out2), (own1, other1, out1)):
+        half = own.shape[1]
+        mine, rest = own[...].astype(F32), other[...].astype(F32)
+        total = jnp.sum(mine * mine) + jnp.sum(rest * rest)
+        scale = lax.rsqrt(jnp.full((1, LANES), total) / float(out.size) + 1e-06)
+        out[:, pl.ds(pl.multiple_of(side[0] * half, half), half)] = mine * scale
+        out[:, pl.ds(pl.multiple_of((1 - side[0]) * half, half), half)] = rest * scale
+
+
+PAIR_TAPS = ((1, 0), (2, 1), (None, 2), (0, None))
+
+
+def weights_body(first, second, w1, w2, w3):
+    taps = second.shape[0]
+
+    def group(g, carry):
+        for source, out, turn in ((first, w1, False), (second, w2, False), (second, w3, True)):
+            depth, width = source.shape[1:]
+            if turn:
+                block = [source[taps - 1 - 3 * g - c].astype(F32).T.astype(BF) for c in range(3)]
+            else:
+                block = [source[3 * g + c] for c in range(3)]
+            none = jnp.zeros((depth, width), BF)
+            for r, row in enumerate(PAIR_TAPS):
+                at = pl.multiple_of(g * 4 * depth + r * depth, depth)
+                for c, tap in enumerate(row):
+                    value = none if tap is None else block[tap]
+                    out[pl.ds(at, depth), c * width : (c + 1) * width] = value
+        return carry
+
+    lax.fori_loop(0, taps // 3, group, 0)
+
+
+def local_call(body, name, out, scratch=(), scalars=0, in_hbm=(), out_hbm=()):
+    def call(*args):
+        vmem = pl.BlockSpec(memory_space=pltpu.VMEM)
+        plain = pl.BlockSpec()
+        ins = [
+            pl.BlockSpec(memory_space=pltpu.SMEM) if i < scalars else plain if i in in_hbm else vmem
+            for i in range(len(args))
+        ]
+        return pl.pallas_call(
+            body,
+            out_shape=out,
+            in_specs=ins,
+            out_specs=[plain if i in out_hbm else vmem for i in range(len(out))],
+            scratch_shapes=list(scratch),
+            name=name,
+        )(*args)
+
+    return call
 
 
 def on_device(volume, basin_mask, w_first, b_first, w_second, b_second, upstream):
     cx, cy, kz, _ = volume.shape
-    chan = w_first.shape[2]
-    tile = basin_mask.astype(BF).reshape(cx * cy, kz, 2).transpose(1, 0, 2)
-    tile = tile.reshape(kz, 2 * cx * cy)
-    tile = jnp.pad(tile, ((0, 0), (0, LANES - tile.shape[1])))
+    taps, _, chan = w_first.shape
+    part = functools.partial
     shape = jax.ShapeDtypeStruct
+    levels = bit_levels(("gx", "gy"))
+    core, one, two = levels[:3]
+    side = side_of(core).astype(jnp.int32).reshape(1)
     rows_x = FIELD_HALO * cy * kz + cy * 2 * kz + kz
-    last, first = pl.pallas_call(
-        functools.partial(pack_x_body, cx),
-        out_shape=[shape((rows_x, LANES), BF)] * 2,
-        name="pack_x",
-    )(volume, upstream, tile)
+    last, first, tile = local_call(
+        part(pack_x_body, cx, cy, kz),
+        "pack_x",
+        [shape((rows_x, LANES), BF)] * 2 + [shape((kz, LANES), BF)],
+        [pltpu.VMEM((LANES, LANES), F32)] * 2,
+    )(volume, upstream, basin_mask)
     low, high = exchange(last, first, "gx")
+    w1, w2, w3 = local_call(
+        weights_body,
+        "weights",
+        [
+            shape((4 * taps // 3 * w_first.shape[1], 2 * chan), BF),
+            shape((4 * taps // 3 * chan, 2 * chan), BF),
+            shape((4 * taps // 3 * chan, 2 * chan), BF),
+        ],
+    )(w_first, w_second)
     rows_y = (cx + 2 * FIELD_HALO) * FIELD_HALO * kz + (cx + 2) * 2 * kz + 3 * kz
-    last, first = pl.pallas_call(
-        functools.partial(pack_y_body, cx, cy, kz),
-        out_shape=[shape((rows_y, LANES), BF)] * 2,
-        name="pack_y",
+    last, first = local_call(
+        part(pack_y_body, cx, cy, kz), "pack_y", [shape((rows_y, LANES), BF)] * 2
     )(volume, upstream, tile, low, high)
     left, right = exchange(last, first, "gy")
-    w1, w2 = pair_weights(w_first), pair_weights(w_second)
-    w3 = pair_weights(jnp.transpose(w_second[::-1], (0, 2, 1)))
     b1 = jnp.concatenate([b_first, b_first]).reshape(1, -1)
     b2 = jnp.concatenate([b_second, b_second]).reshape(1, -1)
     ex, ey = cx + 2 * FIELD_HALO, cy + 2 * FIELD_HALO
-    features, d2, g2p, g2s, gate, xp, xs = pl.pallas_call(
-        functools.partial(forward_body, cx, cy, kz),
-        out_shape=[
+    features, sent2, kept2, g2p, g2s, gate, xp, xs = local_call(
+        part(forward_body, cx, cy, kz),
+        "forward",
+        [
             shape((cx, cy, 2 * kz, chan), BF),
-            shape(w_second.shape, F32),
+            shape((taps, chan // 2, chan), BF),
+            shape((taps, chan // 2, chan), F32),
             shape((cx + 2, cy + 2, kz, 2 * chan), BF),
             shape((cx + 2, cy + 2, kz, 2 * chan), BF),
             shape((cx, cy, kz, 2 * chan), F32),
             shape((ex, ey, kz, LANES), BF),
             shape((ex, ey, kz, LANES), BF),
         ],
-        scratch_shapes=[
+        [
             pltpu.VMEM((cx + 4, cy + 4, kz, 2 * chan), BF),
             pltpu.VMEM((cx + 4, cy + 4, kz, 2 * chan), BF),
             pltpu.VMEM((cx + 4, cy + 4, kz, 2 * chan), BF),
             pltpu.VMEM(((cx + 2) * (cy + 2) * 2 * kz, LANES), F32),
             pltpu.VMEM(((cx + 2) * (cy + 2) * 2 * kz, LANES), F32),
+            pltpu.VMEM(w_second.shape, F32),
         ],
-        name="forward",
-    )(volume, upstream, tile, low, high, left, right, w1, b1, w2, b2)
-    d1 = pl.pallas_call(
-        functools.partial(backward_body, cx, cy, kz),
-        out_shape=shape(w_first.shape, F32),
-        scratch_shapes=[pltpu.VMEM((cx * cy * kz, 2 * chan), BF)],
-        name="backward",
-    )(g2p, g2s, gate, xp, xs, w3)
-    rows_first = d1.shape[0] * d1.shape[1]
-    rows = jnp.concatenate([d1.reshape(-1, chan), d2.reshape(-1, chan)], axis=0)
-    sums = summed_everywhere(rows, ("gx", "gy"))
-    sum_first = sums[:rows_first].reshape(d1.shape)
-    sum_second = sums[rows_first:].reshape(d2.shape)
-    step_first = normalized_with(sum_first, jnp.sum(sum_first * sum_first), float(d1.size))
-    step_second = normalized_with(sum_second, jnp.sum(sum_second * sum_second), float(d2.size))
+        scalars=1,
+    )(side, volume, upstream, tile, low, high, left, right, w1, b1, w2, b2)
+    got2 = swap(sent2, core)
+    (g1,) = local_call(
+        part(grad_body, cx, cy, kz), "grad_first", [shape((cx * cy * kz, 2 * chan), BF)]
+    )(g2p, g2s, gate, w3)
+    sent2, kept2 = halves(kept2 + got2.astype(F32), one)
+    sent2, g1 = lax.optimization_barrier((sent2, g1))
+    got2 = swap(sent2, one)
+    half = w_first.shape[1] // 2
+    sent1, kept1 = local_call(
+        part(first_body, cx, cy, kz),
+        "first_weights",
+        [shape((taps, half, chan), BF), shape((taps, half, chan), F32)],
+        [pltpu.VMEM(w_first.shape, F32)],
+        scalars=1,
+    )(side, xp, xs, g1)
+    got1 = swap(sent1, core)
+    sent1, kept1 = halves(kept1 + got1.astype(F32), two)
+    got1 = swap(sent1, two)
+    sent2, kept2 = halves(kept2 + got2.astype(F32), two)
+    got2 = swap(sent2, two)
+    sent1, kept1 = halves(kept1 + got1.astype(F32), one)
+    got1 = swap(sent1, one)
+    own2, own1 = summed_inner(kept2 + got2.astype(F32), kept1 + got1.astype(F32), levels[3:])
+    other2, other1 = swap(own2, two), swap(own1, one)
+    own2, own1 = joined(own2, other2, two), joined(own1, other1, one)
+    other2, other1 = swap(own2, one), swap(own1, two)
+    own2, own1 = joined(own2, other2, one), joined(own1, other1, two)
+    step_second, step_first = local_call(
+        norm_body,
+        "normalize",
+        [shape(w_second.shape, F32), shape(w_first.shape, F32)],
+        scalars=1,
+        out_hbm=(0, 1),
+    )(side, own2, swap(own2, core), own1, swap(own1, core))
     return (features, step_first, step_second)
 
 

time: 117 us -> 103 us (0.88)
  other arithmetic: 14.8 us -> 3.03 us
  Pallas kernels: 21.5 us -> 31.7 us
  waiting for transfers between devices: 42.5 us -> 36 us
  local copies, waits for them, and re-layouts: 6.49 us -> 3.07 us
  between operations: 2.24 us -> 0.94 us
    pallas_call x4 -> x7, Pallas kernels: 21.5 us -> 31.7 us  [call(): pl.pallas_call(body, out_shape=out, in_specs=ins, out_specs=[plain if i i...]
    ppermute x10 -> x15, waiting for transfers between devices: 36.6 us -> 30 us  [swap(): lax.ppermute(part, axis, [(i, i ^ bit) for i in range(lax.axis_size(axis))])]
    concatenate x2, other arithmetic: 3.83 us -> 0.05 us  [the longest x1 0.03 us: summed_inner(): got = swap(jnp.concatenate([sent2, sent1], axis=1), level).astype(F32)]
    convert_element_type x4 -> x2, other arithmetic: 3.5 us -> 0.06 us  [the longest x1 0.04 us: summed_inner(): both = (both.astype(F32) + swap(both, final).astype(F32)).astype(BF)]
    mul x2 -> x0, other arithmetic: 2.29 us -> none  [normalized_with(): return grad * lax.rsqrt(total / count + 1e-06)]
    reduce_sum x2 -> x0, other arithmetic: 1.88 us -> none  [the longest x1 1.05 us: on_device(): jnp.sum(sum_second * sum_second)]
    rev x1 -> x0, local copies, waits for them, and re-layouts: 1.23 us -> none  [on_device(): w3 = pair_weights(jnp.transpose(w_second[::-1], (0, 2, 1)))]
    unnamed x25 -> x22, local copies, waits for them, and re-layouts: 3.93 us -> 2.88 us
  transfers between devices with their start and end apart: 14 -> 19, of which waited for: 12 -> 12; matrix products, arithmetic and copies ran while one was open for 6% -> 3% of each run, Pallas kernels for 0% -> 9%
where the time goes in v3:
time: 103 us
  waiting for transfers between devices  36 us (35%)
  Pallas kernels  31.7 us (31%)
  starting transfers between devices  28.3 us (27%)
  local copies, waits for them, and re-layouts  3.07 us (3%)
  other arithmetic  3.03 us (3%)
    pallas_call x7, Pallas kernels, call(): pl.pallas_call(body, out_shape=out, in_specs=ins, out_specs=[plain if i i...  31.7 us
    ppermute x15, waiting for transfers between devices, swap(): lax.ppermute(part, axis, [(i, i ^ bit) for i in range(lax.axis_size(axis))])  30 us
    ppermute x15, starting transfers between devices, swap(): lax.ppermute(part, axis, [(i, i ^ bit) for i in range(lax.axis_size(axis))])  19.1 us
    ppermute x2, starting transfers between devices, exchange(): lax.ppermute(forward, axis, ups)  6.63 us
    ppermute x2, waiting for transfers between devices, exchange(): lax.ppermute(backward, axis, downs)  4.58 us
    unnamed x22, local copies, waits for them, and re-layouts  2.88 us
    ppermute x2, starting transfers between devices, exchange(): lax.ppermute(backward, axis, downs)  2.58 us
  transfers between devices with their start and end apart: 19, of which 12 were waited for; matrix products, arithmetic and copies ran while one was open for 3% of the time, Pallas kernels for 9%

profile of v3, /device:TPU:0, one launch (start us, length us, event | category | flops | bytes accessed | tf_op | source)
XLA Modules:
  0.0 103.1 jit_solution(13806147602383303357)
XLA Ops:
  0.7 1.9 %pack_x.1 = (bf16[656,128]{1,0:T(8,128)(2,1)}, bf16[656,128]{1,0:T(8,128)(2,1)}, bf16[16,128]{1,0:T(8,128)(2,1)}) custom-call(bf16[4,8,16,128]{3,2,1,0:T(8,128)(2,1)} %field.5, bf16[4,8,32,128]{3,2,1,0:T(8,128)(2,1)} %up.5, s32[4,8,32]{2,1,0:T(8,128)} %mask.1), custom_call_target="tpu_custom_call" | custom-call | tf_op jit(solution)/shard_map/pack_x/pallas_call | solution.py:380
  2.5 2.4 %collective-permute-start = (bf16[656,128]{1,0:T(8,128)(2,1)}, bf16[656,128]{1,0:T(8,128)(2,1)S(1)}, u32[]{:S(2)}, u32[]{:S(2)}) collective-permute-start(bf16[656,128]{1,0:T(8,128)(2,1)} %get-tuple-element.26), channel_id=1, source_target_pairs={{0,8},{8,16},{16,24},{1,9},{9,17},{17,25},{2,10},{10,18},{18,26},{... | collective-permute-start | bytes 503816 | tf_op jit(solution)/shard_map/ppermute | solution.py:78
  4.9 1.3 %collective-permute-start.1 = (bf16[656,128]{1,0:T(8,128)(2,1)}, bf16[656,128]{1,0:T(8,128)(2,1)S(1)}, u32[]{:S(2)}, u32[]{:S(2)}) collective-permute-start(bf16[656,128]{1,0:T(8,128)(2,1)} %get-tuple-element.27), channel_id=1, source_target_pairs={{8,0},{16,8},{24,16},{9,1},{17,9},{25,17},{10,2},{18,10},{26,18},{... | collective-permute-start | bytes 503816 | tf_op jit(solution)/shard_map/ppermute | solution.py:78
  6.2 5.3 %weights.1 = (bf16[2304,256]{1,0:T(8,128)(2,1)}, bf16[4608,256]{1,0:T(8,128)(2,1)}, bf16[4608,256]{1,0:T(8,128)(2,1)}) custom-call(bf16[27,64,128]{2,1,0:T(8,128)(2,1)} %first.1, bf16[27,128,128]{2,1,0:T(8,128)(2,1)} %second.1), custom_call_target="tpu_custom_call" | custom-call | tf_op jit(solution)/shard_map/weights/pallas_call | solution.py:380
  11.6 0.7 copy-done.3
  12.3 0.1 copy-done.4
  12.4 1.9 %pack_y.1 = (bf16[720,128]{1,0:T(8,128)(2,1)}, bf16[720,128]{1,0:T(8,128)(2,1)}) custom-call(bf16[4,8,16,128]{3,2,1,0:T(8,128)(2,1)} %field.5, bf16[4,8,32,128]{3,2,1,0:T(8,128)(2,1)} %up.5, bf16[16,128]{1,0:T(8,128)(2,1)} %get-tuple-element.25.tile, bf16[656,128]{1,0:T(8,128)(2,1)} %copy-done.3, bf16[656,128]{1,0:T(8,128)(2,1)} %copy-done.4), custom_call_target="tpu_custom_call" | custom-call | tf_op jit(solution)/shard_map/pack_y/pallas_call | solution.py:380
  14.2 4.2 %collective-permute-start.2 = (bf16[720,128]{1,0:T(8,128)(2,1)}, bf16[720,128]{1,0:T(8,128)(2,1)S(1)}, u32[]{:S(2)}, u32[]{:S(2)}) collective-permute-start(bf16[720,128]{1,0:T(8,128)(2,1)} %get-tuple-element.28), channel_id=1, source_target_pairs={{0,1},{1,2},{2,3},{3,4},{4,5},{5,6},{6,7},{8,9},{9,10},{10,11},{11... | collective-permute-start | bytes 552968 | tf_op jit(solution)/shard_map/ppermute | solution.py:78
  18.5 1.3 %collective-permute-start.3 = (bf16[720,128]{1,0:T(8,128)(2,1)}, bf16[720,128]{1,0:T(8,128)(2,1)S(1)}, u32[]{:S(2)}, u32[]{:S(2)}) collective-permute-start(bf16[720,128]{1,0:T(8,128)(2,1)} %get-tuple-element.29), channel_id=1, source_target_pairs={{1,0},{2,1},{3,2},{4,3},{5,4},{6,5},{7,6},{9,8},{10,9},{11,10},{12... | collective-permute-start | bytes 552968 | tf_op jit(solution)/shard_map/ppermute | solution.py:78
  19.8 0.6 pad_maximum_fusion.2
  20.4 0.5 pad_maximum_fusion.3
  20.9 1.5 %collective-permute-done.2.left = bf16[720,128]{1,0:T(8,128)(2,1)S(1)} collective-permute-done((bf16[720,128]{1,0:T(8,128)(2,1)}, bf16[720,128]{1,0:T(8,128)(2,1)S(1)}, u32[]{:S(2)}, u32[]{:S(2)}) %collective-permute-start.2) | collective-permute-done | bytes 184352 | tf_op jit(solution)/shard_map/ppermute | solution.py:78
  22.4 4.6 %collective-permute-done.3.right = bf16[720,128]{1,0:T(8,128)(2,1)S(1)} collective-permute-done((bf16[720,128]{1,0:T(8,128)(2,1)}, bf16[720,128]{1,0:T(8,128)(2,1)S(1)}, u32[]{:S(2)}, u32[]{:S(2)}) %collective-permute-start.3) | collective-permute-done | bytes 184352 | tf_op jit(solution)/shard_map/ppermute | solution.py:78
  27.0 0.7 copy-done.8
  27.6 11.8 %forward.1 = (bf16[4,8,32,128]{3,2,1,0:T(8,128)(2,1)}, bf16[27,64,128]{2,1,0:T(8,128)(2,1)}, f32[27,64,128]{2,1,0:T(8,128)}, bf16[6,10,16,256]{3,2,1,0:T(8,128)(...) custom-call(s32[1]{0:T(128)} %bitcast.side, ...), custom_call_target="tpu_custom_call" | custom-call | tf_op jit(solution)/shard_map/forward/pallas_call | solution.py:380
  39.5 1.0 %collective-permute-start.4 = (bf16[27,64,128]{2,1,0:T(8,128)(2,1)}, bf16[27,64,128]{2,1,0:T(8,128)(2,1)S(1)}, u32[]{:S(2)}, u32[]{:S(2)}) collective-permute-start(bf16[27,64,128]{2,1,0:T(8,128)(2,1)} %get-tuple-element.34), channel_id=1, source_target_pairs={{0,8},{8,0},{16,24},{24,16},{1,9},{9,1},{17,25},{25,17},{2,10},{10... | collective-permute-start | bytes 1327112 | tf_op jit(solution)/shard_map/ppermute | solution.py:29
  40.5 4.4 %grad_first.1.g1 = bf16[512,256]{1,0:T(8,128)(2,1)} custom-call(bf16[6,10,16,256]{3,2,1,0:T(8,128)(2,1)} %get-tuple-element.35.g2p, bf16[6,10,16,256]{3,2,1,0:T(8,128)(2,1)} %get-tuple-element.36.g2s, f32[4,8,16,256]{3,2,1,0:T(8,128)} %get-tuple-element.37.gate, bf16[4608,256]{1,0:T(8,128)(2,1)} %get-tuple-element.38.w3), custom_call_target="tpu_custom_call" | custom-call | tf_op jit(solution)/shard_map/grad_first/pallas_call | solution.py:380
  44.9 0.1 convert_add_fusion
  45.1 3.0 %first_weights.1 = (bf16[27,32,128]{2,1,0:T(8,128)(2,1)}, f32[27,32,128]{2,1,0:T(8,128)}) custom-call(s32[1]{0:T(128)} %bitcast.side, bf16[10,14,16,128]{3,2,1,0:T(8,128)(2,1)} %get-tuple-element.40.xp, bf16[10,14,16,128]{3,2,1,0:T(8,128)(2,1)} %get-tuple-element.41.xs, bf16[512,256]{1,0:T(8,128)(2,1)} %grad_first.1.g1), custom_call_target="tpu_custom_call" | custom-call | tf_op jit(solution)/shard_map/first_weights/pallas_call | solution.py:380
  48.1 0.1 collective-permute-start.7
  48.2 2.6 %collective-permute-start.5 = (bf16[27,32,128]{2,1,0:T(8,128)(2,1)S(1)}, bf16[27,32,128]{2,1,0:T(8,128)(2,1)S(1)}, u32[]{:S(2)}, u32[]{:S(2)}) collective-permute-start(bf16[27,32,128]{2,1,0:T(8,128)(2,1)S(1)} %dynamic-slice_convert_fusion), channel_id=1, source_target_pairs={{0,16},{8,24},{16,0},{24,8},{1,17},{9,25},{17,1},{25,9},{2,18},{10... | collective-permute-start | bytes 663560 | tf_op jit(solution)/shard_map/ppermute | solution.py:29
  50.8 1.1 %convert_add_fusion.1 = f32[27,32,128]{2,1,0:T(8,128)S(1)} fusion(f32[27,32,128]{2,1,0:T(8,128)} %get-tuple-element.43, bf16[27,32,128]{2,1,0:T(8,128)(2,1)S(1)} %collective-permute-done.7), kind=kLoop, calls=%fused_computation.2 | loop fusion | flops 221184 | bytes 1105920 | tf_op jit(solution)/shard_map/add | solution.py:464
  52.0 2.5 %collective-permute-start.8 = (bf16[27,16,128]{2,1,0:T(8,128)(2,1)S(1)}, bf16[27,16,128]{2,1,0:T(8,128)(2,1)S(1)}, u32[]{:S(2)}, u32[]{:S(2)}) collective-permute-start(bf16[27,16,128]{2,1,0:T(8,128)(2,1)S(1)} %dynamic-slice_convert_fusion.1), channel_id=1, source_target_pairs={{0,1},{1,0},{2,3},{3,2},{4,5},{5,4},{6,7},{7,6},{8,9},{9,8},{10,11... | collective-permute-start | bytes 331784 | tf_op jit(solution)/shard_map/ppermute | solution.py:29
  54.4 2.1 %collective-permute-done.5 = bf16[27,32,128]{2,1,0:T(8,128)(2,1)S(1)} collective-permute-done((bf16[27,32,128]{2,1,0:T(8,128)(2,1)S(1)}, bf16[27,32,128]{2,1,0:T(8,128)(2,1)S(1)}, u32[]{:S(2)}, u32[]{:S(2)}) %collective-permute-start.5) | collective-permute-done | bytes 221216 | tf_op jit(solution)/shard_map/ppermute | solution.py:29
  56.6 2.5 %collective-permute-start.6 = (bf16[27,16,128]{2,1,0:T(8,128)(2,1)S(1)}, bf16[27,16,128]{2,1,0:T(8,128)(2,1)S(1)}, u32[]{:S(2)}, u32[]{:S(2)}) collective-permute-start(bf16[27,16,128]{2,1,0:T(8,128)(2,1)S(1)} %dynamic-slice_convert_fusion.2), channel_id=1, source_target_pairs={{0,1},{1,0},{2,3},{3,2},{4,5},{5,4},{6,7},{7,6},{8,9},{9,8},{10,11... | collective-permute-start | bytes 331784 | tf_op jit(solution)/shard_map/ppermute | solution.py:29
  59.2 1.8 %collective-permute-start.9 = (bf16[27,8,128]{2,1,0:T(8,128)(2,1)S(1)}, bf16[27,8,128]{2,1,0:T(8,128)(2,1)S(1)}, u32[]{:S(2)}, u32[]{:S(2)}) collective-permute-start(bf16[27,8,128]{2,1,0:T(8,128)(2,1)S(1)} %dynamic-slice_convert_fusion.3), channel_id=1, source_target_pairs={{0,16},{8,24},{16,0},{24,8},{1,17},{9,25},{17,1},{25,9},{2,18},{10... | collective-permute-start | bytes 165896 | tf_op jit(solution)/shard_map/ppermute | solution.py:29
  61.0 0.9 collective-permute-done.6
  61.9 1.5 %collective-permute-done.9 = bf16[27,8,128]{2,1,0:T(8,128)(2,1)S(1)} collective-permute-done((bf16[27,8,128]{2,1,0:T(8,128)(2,1)S(1)}, bf16[27,8,128]{2,1,0:T(8,128)(2,1)S(1)}, u32[]{:S(2)}, u32[]{:S(2)}) %collective-permute-start.9) | collective-permute-done | bytes 55328 | tf_op jit(solution)/shard_map/ppermute | solution.py:29
  63.5 1.6 %collective-permute-start.10 = (bf16[27,12,128]{2,1,0:T(8,128)(2,1)S(1)}, bf16[27,12,128]{2,1,0:T(8,128)(2,1)S(1)}, u32[]{:S(2)}, u32[]{:S(2)}) collective-permute-start(bf16[27,12,128]{2,1,0:T(8,128)(2,1)S(1)} %pad_maximum_fusion), channel_id=1, source_target_pairs={{0,2},{1,3},{2,0},{3,1},{4,6},{5,7},{6,4},{7,5},{8,10},{9,11},{10,... | collective-permute-start | bytes 248840 | tf_op jit(solution)/shard_map/ppermute | solution.py:29
  65.1 3.2 %collective-permute-done.10 = bf16[27,12,128]{2,1,0:T(8,128)(2,1)S(1)} collective-permute-done((bf16[27,12,128]{2,1,0:T(8,128)(2,1)S(1)}, bf16[27,12,128]{2,1,0:T(8,128)(2,1)S(1)}, u32[]{:S(2)}, u32[]{:S(2)}) %collective-permute-start.10) | collective-permute-done | bytes 82976 | tf_op jit(solution)/shard_map/ppermute | solution.py:29
  68.4 3.1 %collective-permute-start.11 = (bf16[27,12,128]{2,1,0:T(8,128)(2,1)S(1)}, bf16[27,12,128]{2,1,0:T(8,128)(2,1)S(1)}, u32[]{:S(2)}, u32[]{:S(2)}) collective-permute-start(bf16[27,12,128]{2,1,0:T(8,128)(2,1)S(1)} %pad_maximum_fusion.1), channel_id=1, source_target_pairs={{0,4},{1,5},{2,6},{3,7},{4,0},{5,1},{6,2},{7,3},{8,12},{9,13},{10,... | collective-permute-start | bytes 248840 | tf_op jit(solution)/shard_map/ppermute | solution.py:29
  71.5 3.9 %collective-permute-done.11 = bf16[27,12,128]{2,1,0:T(8,128)(2,1)S(1)} collective-permute-done((bf16[27,12,128]{2,1,0:T(8,128)(2,1)S(1)}, bf16[27,12,128]{2,1,0:T(8,128)(2,1)S(1)}, u32[]{:S(2)}, u32[]{:S(2)}) %collective-permute-start.11) | collective-permute-done | bytes 82976 | tf_op jit(solution)/shard_map/ppermute | solution.py:29
  75.4 0.5 collective-permute-start.12
  75.9 4.3 %collective-permute-done.12 = bf16[27,12,128]{2,1,0:T(8,128)(2,1)S(1)} collective-permute-done((bf16[27,12,128]{2,1,0:T(8,128)(2,1)S(1)}, bf16[27,12,128]{2,1,0:T(8,128)(2,1)S(1)}, u32[]{:S(2)}, u32[]{:S(2)}) %collective-permute-start.12) | collective-permute-done | bytes 82976 | tf_op jit(solution)/shard_map/ppermute | solution.py:29
  80.3 0.2 collective-permute-start.13
  80.5 4.6 %collective-permute-done.13 = bf16[27,16,128]{2,1,0:T(8,128)(2,1)S(1)} collective-permute-done((bf16[27,16,128]{2,1,0:T(8,128)(2,1)S(1)}, bf16[27,16,128]{2,1,0:T(8,128)(2,1)S(1)}, u32[]{:S(2)}, u32[]{:S(2)}) %collective-permute-start.13) | collective-permute-done | bytes 110624 | tf_op jit(solution)/shard_map/ppermute | solution.py:29
  85.1 0.1 maximum_select_fusion.1
  85.2 2.1 %collective-permute-start.14 = (bf16[27,32,128]{2,1,0:T(8,128)(2,1)S(1)}, bf16[27,32,128]{2,1,0:T(8,128)(2,1)S(1)}, u32[]{:S(2)}, u32[]{:S(2)}) collective-permute-start(bf16[27,32,128]{2,1,0:T(8,128)(2,1)S(1)} %maximum_select_fusion.1), channel_id=1, source_target_pairs={{0,16},{8,24},{16,0},{24,8},{1,17},{9,25},{17,1},{25,9},{2,18},{10... | collective-permute-start | bytes 663560 | tf_op jit(solution)/shard_map/ppermute | solution.py:29
  87.3 0.1 collective-permute-start.16
  87.4 4.4 %collective-permute-done.16 = bf16[27,8,128]{2,1,0:T(8,128)(2,1)S(1)} collective-permute-done((bf16[27,8,128]{2,1,0:T(8,128)(2,1)S(1)}, bf16[27,8,128]{2,1,0:T(8,128)(2,1)S(1)}, u32[]{:S(2)}, u32[]{:S(2)}) %collective-permute-start.16) | collective-permute-done | bytes 55328 | tf_op jit(solution)/shard_map/ppermute | solution.py:29
  91.8 0.8 collective-permute-start.17
  92.6 0.1 maximum_select_fusion.own2
  92.9 3.7 %collective-permute-done.17 = bf16[27,16,128]{2,1,0:T(8,128)(2,1)S(1)} collective-permute-done((bf16[27,16,128]{2,1,0:T(8,128)(2,1)S(1)}, bf16[27,16,128]{2,1,0:T(8,128)(2,1)S(1)}, u32[]{:S(2)}, u32[]{:S(2)}) %collective-permute-start.17) | collective-permute-done | bytes 110624 | tf_op jit(solution)/shard_map/ppermute | solution.py:29
  96.6 0.1 maximum_select_fusion.2.own1
  96.8 1.5 %collective-permute-done.18.other1 = bf16[27,32,128]{2,1,0:T(8,128)(2,1)S(1)} collective-permute-done((bf16[27,32,128]{2,1,0:T(8,128)(2,1)S(1)}, bf16[27,32,128]{2,1,0:T(8,128)(2,1)S(1)}, u32[]{:S(2)}, u32[]{:S(2)}) %collective-permute-start.18) | collective-permute-done | bytes 221216 | tf_op jit(solution)/shard_map/ppermute | solution.py:29
  98.3 0.7 copy-done.6
  98.9 0.8 copy-done.5
  99.7 3.4 %normalize.1 = (f32[27,128,128]{2,1,0:T(8,128)}, f32[27,64,128]{2,1,0:T(8,128)}) custom-call(s32[1]{0:T(128)} %bitcast.side, bf16[27,64,128]{2,1,0:T(8,128)(2,1)} %copy-done, bf16[27,64,128]{2,1,0:T(8,128)(2,1)} %copy-done.5, bf16[27,32,128]{2,1,0:T(8,128)(2,1)} %copy-done.2, bf16[27,32,128]{2,1,0:T(8,128)(2,1)} %copy-done.6), custom_call_target="tpu_custom_call" | custom-call | tf_op jit(solution)/shard_map/normalize/pallas_call | solution.py:380
  (49 shorter events, 0.8 us)
Async XLA Ops:
  0.6 19.2 %copy-start.9 = (f32[128]{0:T(128)S(1)}, f32[128]{0:T(128)}, u32[]{:S(2)}) copy-start(f32[128]{0:T(128)} %param.10) | copy-start | bytes 1540
  0.6 19.7 %copy-start.10 = (f32[128]{0:T(128)S(1)}, f32[128]{0:T(128)}, u32[]{:S(2)}) copy-start(f32[128]{0:T(128)} %param.12) | copy-start | bytes 1540
  2.5 9.1 %collective-permute-start = (bf16[656,128]{1,0:T(8,128)(2,1)}, bf16[656,128]{1,0:T(8,128)(2,1)S(1)}, u32[]{:S(2)}, u32[]{:S(2)}) collective-permute-start(bf16[656,128]{1,0:T(8,128)(2,1)} %get-tuple-element.26), channel_id=1, source_target_pairs={{0,8},{8,16},{16,24},{1,9},{9,17},{17,25},{2,10},{10,18},{18,26},{... | collective-permute-start | bytes 503816 | tf_op jit(solution)/shard_map/ppermute | solution.py:78
  4.9 6.7 %collective-permute-start.1 = (bf16[656,128]{1,0:T(8,128)(2,1)}, bf16[656,128]{1,0:T(8,128)(2,1)S(1)}, u32[]{:S(2)}, u32[]{:S(2)}) collective-permute-start(bf16[656,128]{1,0:T(8,128)(2,1)} %get-tuple-element.27), channel_id=1, source_target_pairs={{8,0},{16,8},{24,16},{9,1},{17,9},{25,17},{10,2},{18,10},{26,18},{... | collective-permute-start | bytes 503816 | tf_op jit(solution)/shard_map/ppermute | solution.py:78
  11.6 0.7 copy-start.3
  11.6 0.8 copy-start.4
  14.2 8.1 %collective-permute-start.2 = (bf16[720,128]{1,0:T(8,128)(2,1)}, bf16[720,128]{1,0:T(8,128)(2,1)S(1)}, u32[]{:S(2)}, u32[]{:S(2)}) collective-permute-start(bf16[720,128]{1,0:T(8,128)(2,1)} %get-tuple-element.28), channel_id=1, source_target_pairs={{0,1},{1,2},{2,3},{3,4},{4,5},{5,6},{6,7},{8,9},{9,10},{10,11},{11... | collective-permute-start | bytes 552968 | tf_op jit(solution)/shard_map/ppermute | solution.py:78
  18.5 8.5 %collective-permute-start.3 = (bf16[720,128]{1,0:T(8,128)(2,1)}, bf16[720,128]{1,0:T(8,128)(2,1)S(1)}, u32[]{:S(2)}, u32[]{:S(2)}) collective-permute-start(bf16[720,128]{1,0:T(8,128)(2,1)} %get-tuple-element.29), channel_id=1, source_target_pairs={{1,0},{2,1},{3,2},{4,3},{5,4},{6,5},{7,6},{9,8},{10,9},{11,10},{12... | collective-permute-start | bytes 552968 | tf_op jit(solution)/shard_map/ppermute | solution.py:78
  22.4 4.6 %copy-start.7 = (bf16[720,128]{1,0:T(8,128)(2,1)}, bf16[720,128]{1,0:T(8,128)(2,1)S(1)}, u32[]{:S(2)}) copy-start(bf16[720,128]{1,0:T(8,128)(2,1)S(1)} %collective-permute-done.2.left) | copy-start | bytes 552964
  27.0 0.7 copy-start.8
  39.5 5.5 %copy-start.1 = (f32[27,64,128]{2,1,0:T(8,128)S(1)}, f32[27,64,128]{2,1,0:T(8,128)}, u32[]{:S(2)}) copy-start(f32[27,64,128]{2,1,0:T(8,128)} %get-tuple-element.33) | copy-start | bytes 2654212
  39.5 5.4 %collective-permute-start.4 = (bf16[27,64,128]{2,1,0:T(8,128)(2,1)}, bf16[27,64,128]{2,1,0:T(8,128)(2,1)S(1)}, u32[]{:S(2)}, u32[]{:S(2)}) collective-permute-start(bf16[27,64,128]{2,1,0:T(8,128)(2,1)} %get-tuple-element.34), channel_id=1, source_target_pairs={{0,8},{8,0},{16,24},{24,16},{1,9},{9,1},{17,25},{25,17},{2,10},{10... | collective-permute-start | bytes 1327112 | tf_op jit(solution)/shard_map/ppermute | solution.py:29
  48.1 2.7 %collective-permute-start.7 = (bf16[27,32,128]{2,1,0:T(8,128)(2,1)}, bf16[27,32,128]{2,1,0:T(8,128)(2,1)S(1)}, u32[]{:S(2)}, u32[]{:S(2)}) collective-permute-start(bf16[27,32,128]{2,1,0:T(8,128)(2,1)} %get-tuple-element.44), channel_id=1, source_target_pairs={{0,8},{8,0},{16,24},{24,16},{1,9},{9,1},{17,25},{25,17},{2,10},{10... | collective-permute-start | bytes 663560 | tf_op jit(solution)/shard_map/ppermute | solution.py:29
  48.2 8.3 %collective-permute-start.5 = (bf16[27,32,128]{2,1,0:T(8,128)(2,1)S(1)}, bf16[27,32,128]{2,1,0:T(8,128)(2,1)S(1)}, u32[]{:S(2)}, u32[]{:S(2)}) collective-permute-start(bf16[27,32,128]{2,1,0:T(8,128)(2,1)S(1)} %dynamic-slice_convert_fusion), channel_id=1, source_target_pairs={{0,16},{8,24},{16,0},{24,8},{1,17},{9,25},{17,1},{25,9},{2,18},{10... | collective-permute-start | bytes 663560 | tf_op jit(solution)/shard_map/ppermute | solution.py:29
  52.0 7.1 %collective-permute-start.8 = (bf16[27,16,128]{2,1,0:T(8,128)(2,1)S(1)}, bf16[27,16,128]{2,1,0:T(8,128)(2,1)S(1)}, u32[]{:S(2)}, u32[]{:S(2)}) collective-permute-start(bf16[27,16,128]{2,1,0:T(8,128)(2,1)S(1)} %dynamic-slice_convert_fusion.1), channel_id=1, source_target_pairs={{0,1},{1,0},{2,3},{3,2},{4,5},{5,4},{6,7},{7,6},{8,9},{9,8},{10,11... | collective-permute-start | bytes 331784 | tf_op jit(solution)/shard_map/ppermute | solution.py:29
  56.6 5.2 %collective-permute-start.6 = (bf16[27,16,128]{2,1,0:T(8,128)(2,1)S(1)}, bf16[27,16,128]{2,1,0:T(8,128)(2,1)S(1)}, u32[]{:S(2)}, u32[]{:S(2)}) collective-permute-start(bf16[27,16,128]{2,1,0:T(8,128)(2,1)S(1)} %dynamic-slice_convert_fusion.2), channel_id=1, source_target_pairs={{0,1},{1,0},{2,3},{3,2},{4,5},{5,4},{6,7},{7,6},{8,9},{9,8},{10,11... | collective-permute-start | bytes 331784 | tf_op jit(solution)/shard_map/ppermute | solution.py:29
  59.2 4.2 %collective-permute-start.9 = (bf16[27,8,128]{2,1,0:T(8,128)(2,1)S(1)}, bf16[27,8,128]{2,1,0:T(8,128)(2,1)S(1)}, u32[]{:S(2)}, u32[]{:S(2)}) collective-permute-start(bf16[27,8,128]{2,1,0:T(8,128)(2,1)S(1)} %dynamic-slice_convert_fusion.3), channel_id=1, source_target_pairs={{0,16},{8,24},{16,0},{24,8},{1,17},{9,25},{17,1},{25,9},{2,18},{10... | collective-permute-start | bytes 165896 | tf_op jit(solution)/shard_map/ppermute | solution.py:29
  63.5 4.8 %collective-permute-start.10 = (bf16[27,12,128]{2,1,0:T(8,128)(2,1)S(1)}, bf16[27,12,128]{2,1,0:T(8,128)(2,1)S(1)}, u32[]{:S(2)}, u32[]{:S(2)}) collective-permute-start(bf16[27,12,128]{2,1,0:T(8,128)(2,1)S(1)} %pad_maximum_fusion), channel_id=1, source_target_pairs={{0,2},{1,3},{2,0},{3,1},{4,6},{5,7},{6,4},{7,5},{8,10},{9,11},{10,... | collective-permute-start | bytes 248840 | tf_op jit(solution)/shard_map/ppermute | solution.py:29
  68.4 7.0 %collective-permute-start.11 = (bf16[27,12,128]{2,1,0:T(8,128)(2,1)S(1)}, bf16[27,12,128]{2,1,0:T(8,128)(2,1)S(1)}, u32[]{:S(2)}, u32[]{:S(2)}) collective-permute-start(bf16[27,12,128]{2,1,0:T(8,128)(2,1)S(1)} %pad_maximum_fusion.1), channel_id=1, source_target_pairs={{0,4},{1,5},{2,6},{3,7},{4,0},{5,1},{6,2},{7,3},{8,12},{9,13},{10,... | collective-permute-start | bytes 248840 | tf_op jit(solution)/shard_map/ppermute | solution.py:29
  75.4 4.8 %collective-permute-start.12 = (bf16[27,12,128]{2,1,0:T(8,128)(2,1)S(1)}, bf16[27,12,128]{2,1,0:T(8,128)(2,1)S(1)}, u32[]{:S(2)}, u32[]{:S(2)}) collective-permute-start(bf16[27,12,128]{2,1,0:T(8,128)(2,1)S(1)} %add_convert_fusion), channel_id=1, source_target_pairs={{0,2},{1,3},{2,0},{3,1},{4,6},{5,7},{6,4},{7,5},{8,10},{9,11},{10,... | collective-permute-start | bytes 248840 | tf_op jit(solution)/shard_map/ppermute | solution.py:29
  80.3 4.8 %collective-permute-start.13 = (bf16[27,16,128]{2,1,0:T(8,128)(2,1)S(1)}, bf16[27,16,128]{2,1,0:T(8,128)(2,1)S(1)}, u32[]{:S(2)}, u32[]{:S(2)}) collective-permute-start(bf16[27,16,128]{2,1,0:T(8,128)(2,1)S(1)} %maximum_select_fusion.3), channel_id=1, source_target_pairs={{0,1},{1,0},{2,3},{3,2},{4,5},{5,4},{6,7},{7,6},{8,9},{9,8},{10,11... | collective-permute-start | bytes 331784 | tf_op jit(solution)/shard_map/ppermute | solution.py:29
  85.2 7.5 %collective-permute-start.14 = (bf16[27,32,128]{2,1,0:T(8,128)(2,1)S(1)}, bf16[27,32,128]{2,1,0:T(8,128)(2,1)S(1)}, u32[]{:S(2)}, u32[]{:S(2)}) collective-permute-start(bf16[27,32,128]{2,1,0:T(8,128)(2,1)S(1)} %maximum_select_fusion.1), channel_id=1, source_target_pairs={{0,16},{8,24},{16,0},{24,8},{1,17},{9,25},{17,1},{25,9},{2,18},{10... | collective-permute-start | bytes 663560 | tf_op jit(solution)/shard_map/ppermute | solution.py:29
  87.3 4.4 %collective-permute-start.16 = (bf16[27,8,128]{2,1,0:T(8,128)(2,1)S(1)}, bf16[27,8,128]{2,1,0:T(8,128)(2,1)S(1)}, u32[]{:S(2)}, u32[]{:S(2)}) collective-permute-start(bf16[27,8,128]{2,1,0:T(8,128)(2,1)S(1)} %maximum_select_fusion.5), channel_id=1, source_target_pairs={{0,16},{8,24},{16,0},{24,8},{1,17},{9,25},{17,1},{25,9},{2,18},{10... | collective-permute-start | bytes 165896 | tf_op jit(solution)/shard_map/ppermute | solution.py:29
  91.8 4.8 %collective-permute-start.17 = (bf16[27,16,128]{2,1,0:T(8,128)(2,1)S(1)}, bf16[27,16,128]{2,1,0:T(8,128)(2,1)S(1)}, u32[]{:S(2)}, u32[]{:S(2)}) collective-permute-start(bf16[27,16,128]{2,1,0:T(8,128)(2,1)S(1)} %maximum_select_fusion.4), channel_id=1, source_target_pairs={{0,1},{1,0},{2,3},{3,2},{4,5},{5,4},{6,7},{7,6},{8,9},{9,8},{10,11... | collective-permute-start | bytes 331784 | tf_op jit(solution)/shard_map/ppermute | solution.py:29
  92.8 5.5 %copy-start = (bf16[27,64,128]{2,1,0:T(8,128)(2,1)}, bf16[27,64,128]{2,1,0:T(8,128)(2,1)S(1)}, u32[]{:S(2)}) copy-start(bf16[27,64,128]{2,1,0:T(8,128)(2,1)S(1)} %maximum_select_fusion.own2) | copy-start | bytes 1327108
  92.8 5.4 %collective-permute-start.15 = (bf16[27,64,128]{2,1,0:T(8,128)(2,1)S(1)}, bf16[27,64,128]{2,1,0:T(8,128)(2,1)S(1)}, u32[]{:S(2)}, u32[]{:S(2)}) collective-permute-start(bf16[27,64,128]{2,1,0:T(8,128)(2,1)S(1)} %maximum_select_fusion.own2), channel_id=1, source_target_pairs={{0,8},{8,0},{16,24},{24,16},{1,9},{9,1},{17,25},{25,17},{2,10},{10... | collective-permute-start | bytes 1327112 | tf_op jit(solution)/shard_map/ppermute | solution.py:29
  96.7 1.6 %copy-start.2 = (bf16[27,32,128]{2,1,0:T(8,128)(2,1)}, bf16[27,32,128]{2,1,0:T(8,128)(2,1)S(1)}, u32[]{:S(2)}) copy-start(bf16[27,32,128]{2,1,0:T(8,128)(2,1)S(1)} %maximum_select_fusion.2.own1) | copy-start | bytes 663556
  96.7 1.5 %collective-permute-start.18 = (bf16[27,32,128]{2,1,0:T(8,128)(2,1)S(1)}, bf16[27,32,128]{2,1,0:T(8,128)(2,1)S(1)}, u32[]{:S(2)}, u32[]{:S(2)}) collective-permute-start(bf16[27,32,128]{2,1,0:T(8,128)(2,1)S(1)} %maximum_select_fusion.2.own1), channel_id=1, source_target_pairs={{0,8},{8,0},{16,24},{24,16},{1,9},{9,1},{17,25},{25,17},{2,10},{10... | collective-permute-start | bytes 663560 | tf_op jit(solution)/shard_map/ppermute | solution.py:29
  98.2 0.7 copy-start.6
  98.9 0.8 copy-start.5

commit v4 on v3

--- a/solution.py
+++ b/solution.py
@@ -78,40 +78,50 @@
     return lax.ppermute(forward, axis, ups), lax.ppermute(backward, axis, downs)
 
 
-def pack_x_body(cx, cy, kz, field, up, mask, last, first, tile, square, deep):
+def pack_y_body(cx, cy, kz, hfield, hup, hmask, last, first, tile, field, up, mask, square, deep, sems):
+    copies = [
+        pltpu.make_async_copy(source, target, sems.at[i])
+        for i, (source, target) in enumerate(((hmask, mask), (hfield, field), (hup, up)))
+    ]
+    for copy in copies:
+        copy.start()
     cells = cx * cy
     square[...] = jnp.zeros_like(square)
+    copies[0].wait()
     square[0:cells, 0 : 2 * kz] = mask[...].reshape(cells, 2 * kz).astype(F32)
     deep[...] = square[...].T
     even = deep[pl.ds(0, kz, stride=2), :]
     odd = deep[pl.ds(1, kz, stride=2), :]
     tile[...] = (even + pltpu.roll(odd, LANES // 2, 1)).astype(BF)
-    for ref, at_field, at_up in ((last, cx - FIELD_HALO, cx - 1), (first, 0, 0)):
-        rows = field[at_field : at_field + FIELD_HALO].reshape(-1, LANES)
-        ups = up[at_up : at_up + 1].reshape(-1, LANES)
-        ref[0 : rows.shape[0]] = rows
-        ref[rows.shape[0] : rows.shape[0] + ups.shape[0]] = ups
-        ref[rows.shape[0] + ups.shape[0] :] = tile[...]
-
-
-def pack_y_body(cx, cy, kz, field, up, tile, low, high, last, first):
-    nf = FIELD_HALO * cy * kz
-    nu = cy * 2 * kz
+    copies[1].wait()
+    copies[2].wait()
     for ref, at_field, at_up in ((last, cy - FIELD_HALO, cy - 1), (first, 0, 0)):
         row = 0
-        ends = [m[0:nf].reshape(FIELD_HALO, cy, kz, LANES) for m in (low, high)]
-        for part in (ends[0], field, ends[1]):
-            rows = part[:, at_field : at_field + FIELD_HALO].reshape(-1, LANES)
+        for rows in (
+            field[:, at_field : at_field + FIELD_HALO].reshape(-1, LANES),
+            up[:, at_up : at_up + 1].reshape(-1, LANES),
+            tile[...],
+        ):
             ref[row : row + rows.shape[0]] = rows
             row += rows.shape[0]
-        ends = [m[nf : nf + nu].reshape(1, cy, 2 * kz, LANES) for m in (low, high)]
-        for part in (ends[0], up, ends[1]):
-            rows = part[:, at_up : at_up + 1].reshape(-1, LANES)
+
+
+def pack_x_body(cx, cy, kz, field, up, tile, left, right, last, first):
+    fh = FIELD_HALO
+    nf, nu = cx * fh * kz, cx * 2 * kz
+    ends_f = [m[0:nf].reshape(cx, fh, kz, LANES) for m in (left, right)]
+    ends_u = [m[nf : nf + nu].reshape(cx, 1, 2 * kz, LANES) for m in (left, right)]
+    for ref, at_field, at_up in ((last, cx - fh, cx - 1), (first, 0, 0)):
+        row = 0
+        parts = []
+        for r in range(at_field, at_field + fh):
+            parts += [ends_f[0][r], field[r], ends_f[1][r]]
+        parts += [ends_u[0][at_up], up[at_up], ends_u[1][at_up]]
+        parts += [left[nf + nu :], tile[...], right[nf + nu :]]
+        for part in parts:
+            rows = part.reshape(-1, LANES)
             ref[row : row + rows.shape[0]] = rows
             row += rows.shape[0]
-        for part in (low[nf + nu :], tile[...], high[nf + nu :]):
-            ref[row : row + kz] = part
-            row += kz
 
 
 def side_pair(pair, kz, width):
@@ -134,22 +144,21 @@
     return jnp.concatenate(parts, axis=1)
 
 
-def forward_body(
+def compute_body(
     cx, cy, kz,
-    side, field, up, tile, low, high, left, right, w1, b1, w2, b2,
-    features, sent, kept, g2p, g2s, gate, xp, xs,
-    hp, hs, act, upf, outf, d2,
+    side, field, up, tile, left, right, low, high, w1, b1, w2, b2, w3,
+    features, sent, kept,
+    xp, xs, hp, hs, act, upf, outf, g2p, g2s, gate, g1, d2, d1,
 ):
     fh, mh = FIELD_HALO, MASK_HALO
-    nf, nu = fh * cy * kz, cy * 2 * kz
-    ex = cx + 2 * fh
+    ex, ey, uy = cx + 2 * fh, cy + 2 * fh, cy + 2
+    nf, nu = cx * fh * kz, cx * 2 * kz
+    ne, nw = fh * ey * kz, uy * 2 * kz
     xp[fh : fh + cx, fh : fh + cy] = field[...]
-    xp[0:fh, fh : fh + cy] = low[0:nf].reshape(fh, cy, kz, LANES)
-    xp[fh + cx :, fh : fh + cy] = high[0:nf].reshape(fh, cy, kz, LANES)
-    ne = ex * fh * kz
-    xp[:, 0:fh] = left[0:ne].reshape(ex, fh, kz, LANES)
-    xp[:, fh + cy :] = right[0:ne].reshape(ex, fh, kz, LANES)
-    ey = cy + 2 * fh
+    xp[fh : fh + cx, 0:fh] = left[0:nf].reshape(cx, fh, kz, LANES)
+    xp[fh : fh + cx, fh + cy :] = right[0:nf].reshape(cx, fh, kz, LANES)
+    xp[0:fh] = low[0:ne].reshape(fh, ey, kz, LANES)
+    xp[fh + cx :] = high[0:ne].reshape(fh, ey, kz, LANES)
 
     def fill_side(i, carry):
         rows = xp[i].reshape(ey * kz, LANES).astype(F32)
@@ -162,22 +171,19 @@
         return carry
 
     lax.fori_loop(0, ex, fill_side, 0)
-    uy = cy + 2
     span = uy * 2 * kz
 
     def put_up(x, y, cols, value):
         base = x * span + y * 2 * kz
         upf[base : base + cols * 2 * kz] = value.reshape(-1, LANES).astype(F32)
 
+    put_up(0, 0, uy, low[ne : ne + nw])
+    put_up(cx + 1, 0, uy, high[ne : ne + nw])
     for x in range(cx):
+        at = nf + x * 2 * kz
+        put_up(x + 1, 0, 1, left[at : at + 2 * kz])
         put_up(x + 1, 1, cy, up[x])
-    put_up(0, 1, cy, low[nf : nf + nu])
-    put_up(cx + 1, 1, cy, high[nf : nf + nu])
-    for x in range(cx + 2):
-        at = ne + x * 2 * kz
-        put_up(x, 0, 1, left[at : at + 2 * kz])
-        put_up(x, cy + 1, 1, right[at : at + 2 * kz])
-    nm = ne + (cx + 2) * 2 * kz
+        put_up(x + 1, cy + 1, 1, right[at : at + 2 * kz])
 
     def put_mask(source, sx, sy, x, y):
         for parity in range(2):
@@ -185,34 +191,23 @@
             value = jnp.broadcast_to(source[:, lane : lane + 1], (kz, LANES))
             act[x, y, :, parity * LANES : (parity + 1) * LANES] = value.astype(BF)
 
-    def row_tiles(ref, start):
-        own = [(ref[start + i * kz : start + (i + 1) * kz].astype(F32)) for i in range(3)]
-        rows = []
-        for x in range(cx + 2 * mh):
-            if x < mh:
-                rows.append((own[0], cx - mh + x))
-            elif x < mh + cx:
-                rows.append((own[1], x - mh))
-            else:
-                rows.append((own[2], x - mh - cx))
-        return rows
-
-    mid = tile[...].astype(F32)
-    lo_tile = low[nf + nu : nf + nu + kz].astype(F32)
-    hi_tile = high[nf + nu : nf + nu + kz].astype(F32)
-    left_rows, right_rows = row_tiles(left, nm), row_tiles(right, nm)
+    def three(ref, start):
+        return [ref[start + i * kz : start + (i + 1) * kz].astype(F32) for i in range(3)]
+
+    rows_mid = [left[nf + nu :].astype(F32), tile[...].astype(F32), right[nf + nu :].astype(F32)]
+    rows_low, rows_high = three(low, ne + nw), three(high, ne + nw)
     for x in range(cx + 2 * mh):
         if x < mh:
-            source, sx = lo_tile, cx - mh + x
+            sources, sx = rows_low, cx - mh + x
         elif x < mh + cx:
-            source, sx = mid, x - mh
+            sources, sx = rows_mid, x - mh
         else:
-            source, sx = hi_tile, x - mh - cx
+            sources, sx = rows_high, x - mh - cx
         for y in range(cy):
-            put_mask(source, sx, y, x, mh + y)
+            put_mask(sources[1], sx, y, x, mh + y)
         for j in range(mh):
-            put_mask(*left_rows[x], cy - mh + j, x, j)
-            put_mask(*right_rows[x], j, x, mh + cy + j)
+            put_mask(sources[0], sx, cy - mh + j, x, j)
+            put_mask(sources[2], sx, j, x, mh + cy + j)
 
     hx, hy = cx + 4, cy + 4
     step = 2
@@ -286,19 +281,7 @@
                 else:
                     d2[t] = d2[t] + q[1][0]
                     d2[t + 2] = d2[t + 2] + q[0][1]
-    split_rows(side, d2, sent, kept)
-
-
-def split_rows(side, total, sent, kept):
-    half = total.shape[1] // 2
-    mine = pl.multiple_of(side[0] * half, half)
-    other = pl.multiple_of((1 - side[0]) * half, half)
-    sent[...] = total[:, pl.ds(other, half)].astype(BF)
-    kept[...] = total[:, pl.ds(mine, half)]
-
-
-def grad_body(cx, cy, kz, g2p, g2s, gate, w3, g1):
-    step = 2
+
     rows = step * cy * kz
 
     def grad(i, carry):
@@ -310,11 +293,7 @@
         return carry
 
     lax.fori_loop(0, cx // step, grad, 0)
-
-
-def first_body(cx, cy, kz, side, xp, xs, g1, sent, kept, d1):
-    fh = FIELD_HALO
-    right = g1[...]
+    right_side = g1[...]
     cells = cx * cy * kz
     half = LANES // 2
     for b in range(3):
@@ -323,7 +302,7 @@
         turned = jnp.concatenate(parts, axis=1).T
         for a in range(3):
             at = a * cy * kz
-            block = jnp.dot(turned[:, at : at + cells], right, preferred_element_type=F32)
+            block = jnp.dot(turned[:, at : at + cells], right_side, preferred_element_type=F32)
             q = [
                 [block[r * half : (r + 1) * half, c * LANES : (c + 1) * LANES] for c in (0, 1)]
                 for r in range(4)
@@ -332,7 +311,14 @@
             d1[t] = q[0][1] + q[3][0]
             d1[t + 1] = q[0][0] + q[1][1]
             d1[t + 2] = q[1][0] + q[2][1]
-    split_rows(side, d1, sent, kept)
+    at = 0
+    for total in (d2, d1):
+        half = total.shape[1] // 2
+        mine = pl.multiple_of(side[0] * half, half)
+        other = pl.multiple_of((1 - side[0]) * half, half)
+        sent[:, at : at + half] = total[:, pl.ds(other, half)].astype(BF)
+        kept[:, at : at + half] = total[:, pl.ds(mine, half)]
+        at += half
 
 
 def norm_body(side, own2, other2, own1, other1, out2, out1):
@@ -369,22 +355,31 @@
     lax.fori_loop(0, taps // 3, group, 0)
 
 
-def local_call(body, name, out, scratch=(), scalars=0, in_hbm=(), out_hbm=()):
+def local_call(body, name, out, scratch=(), scalars=0, in_hbm=(), out_hbm=(), limit=24):
     def call(*args):
         vmem = pl.BlockSpec(memory_space=pltpu.VMEM)
         plain = pl.BlockSpec()
+        hbm = pl.BlockSpec(memory_space=pltpu.HBM)
         ins = [
-            pl.BlockSpec(memory_space=pltpu.SMEM) if i < scalars else plain if i in in_hbm else vmem
+            pl.BlockSpec(memory_space=pltpu.SMEM) if i < scalars else hbm if i in in_hbm else vmem
             for i in range(len(args))
         ]
+        held = [
+            a
+            if i < scalars
+            else pltpu.with_memory_space_constraint(a, pltpu.HBM if i in in_hbm else pltpu.VMEM)
+            for i, a in enumerate(args)
+        ]
+        outs = [o if i in out_hbm else pltpu.VMEM(o.shape, o.dtype) for i, o in enumerate(out)]
         return pl.pallas_call(
             body,
-            out_shape=out,
+            out_shape=outs,
             in_specs=ins,
             out_specs=[plain if i in out_hbm else vmem for i in range(len(out))],
             scratch_shapes=list(scratch),
+            compiler_params=pltpu.CompilerParams(vmem_limit_bytes=limit << 20),
             name=name,
-        )(*args)
+        )(*held)
 
     return call
 
@@ -397,14 +392,19 @@
     levels = bit_levels(("gx", "gy"))
     core, one, two = levels[:3]
     side = side_of(core).astype(jnp.int32).reshape(1)
-    rows_x = FIELD_HALO * cy * kz + cy * 2 * kz + kz
-    last, first, tile = local_call(
-        part(pack_x_body, cx, cy, kz),
-        "pack_x",
-        [shape((rows_x, LANES), BF)] * 2 + [shape((kz, LANES), BF)],
-        [pltpu.VMEM((LANES, LANES), F32)] * 2,
+    ex, ey, uy = cx + 2 * FIELD_HALO, cy + 2 * FIELD_HALO, cy + 2
+    rows_y = cx * FIELD_HALO * kz + cx * 2 * kz + kz
+    last, first, tile, field, up = local_call(
+        part(pack_y_body, cx, cy, kz),
+        "pack_y",
+        [shape((rows_y, LANES), BF)] * 2
+        + [shape((kz, LANES), BF), shape(volume.shape, BF), shape(upstream.shape, BF)],
+        [pltpu.VMEM(basin_mask.shape, jnp.int32)]
+        + [pltpu.VMEM((LANES, LANES), F32)] * 2
+        + [pltpu.SemaphoreType.DMA((3,))],
+        in_hbm=(0, 1, 2),
     )(volume, upstream, basin_mask)
-    low, high = exchange(last, first, "gx")
+    left, right = exchange(last, first, "gy")
     w1, w2, w3 = local_call(
         weights_body,
         "weights",
@@ -414,63 +414,53 @@
             shape((4 * taps // 3 * chan, 2 * chan), BF),
         ],
     )(w_first, w_second)
-    rows_y = (cx + 2 * FIELD_HALO) * FIELD_HALO * kz + (cx + 2) * 2 * kz + 3 * kz
+    rows_x = FIELD_HALO * ey * kz + uy * 2 * kz + 3 * kz
     last, first = local_call(
-        part(pack_y_body, cx, cy, kz), "pack_y", [shape((rows_y, LANES), BF)] * 2
-    )(volume, upstream, tile, low, high)
-    left, right = exchange(last, first, "gy")
+        part(pack_x_body, cx, cy, kz), "pack_x", [shape((rows_x, LANES), BF)] * 2
+    )(field, up, tile, left, right)
+    low, high = exchange(last, first, "gx")
     b1 = jnp.concatenate([b_first, b_first]).reshape(1, -1)
     b2 = jnp.concatenate([b_second, b_second]).reshape(1, -1)
-    ex, ey = cx + 2 * FIELD_HALO, cy + 2 * FIELD_HALO
-    features, sent2, kept2, g2p, g2s, gate, xp, xs = local_call(
-        part(forward_body, cx, cy, kz),
-        "forward",
+    cut = chan // 2
+    rows = cut + w_first.shape[1] // 2
+    pairs = (kz, 2 * chan)
+    features, sent, kept = local_call(
+        part(compute_body, cx, cy, kz),
+        "compute",
         [
             shape((cx, cy, 2 * kz, chan), BF),
-            shape((taps, chan // 2, chan), BF),
-            shape((taps, chan // 2, chan), F32),
-            shape((cx + 2, cy + 2, kz, 2 * chan), BF),
-            shape((cx + 2, cy + 2, kz, 2 * chan), BF),
-            shape((cx, cy, kz, 2 * chan), F32),
-            shape((ex, ey, kz, LANES), BF),
-            shape((ex, ey, kz, LANES), BF),
+            shape((taps, rows, chan), BF),
+            shape((taps, rows, chan), F32),
         ],
         [
-            pltpu.VMEM((cx + 4, cy + 4, kz, 2 * chan), BF),
-            pltpu.VMEM((cx + 4, cy + 4, kz, 2 * chan), BF),
-            pltpu.VMEM((cx + 4, cy + 4, kz, 2 * chan), BF),
-            pltpu.VMEM(((cx + 2) * (cy + 2) * 2 * kz, LANES), F32),
-            pltpu.VMEM(((cx + 2) * (cy + 2) * 2 * kz, LANES), F32),
+            pltpu.VMEM((ex, ey, kz, LANES), BF),
+            pltpu.VMEM((ex, ey, kz, LANES), BF),
+            pltpu.VMEM((cx + 4, cy + 4, *pairs), BF),
+            pltpu.VMEM((cx + 4, cy + 4, *pairs), BF),
+            pltpu.VMEM((cx + 4, cy + 4, *pairs), BF),
+            pltpu.VMEM(((cx + 2) * uy * 2 * kz, LANES), F32),
+            pltpu.VMEM(((cx + 2) * uy * 2 * kz, LANES), F32),
+            pltpu.VMEM((cx + 2, uy, *pairs), BF),
+            pltpu.VMEM((cx + 2, uy, *pairs), BF),
+            pltpu.VMEM((cx, cy, *pairs), F32),
+            pltpu.VMEM((cx * cy * kz, 2 * chan), BF),
             pltpu.VMEM(w_second.shape, F32),
+            pltpu.VMEM(w_first.shape, F32),
         ],
         scalars=1,
-    )(side, volume, upstream, tile, low, high, left, right, w1, b1, w2, b2)
-    got2 = swap(sent2, core)
-    (g1,) = local_call(
-        part(grad_body, cx, cy, kz), "grad_first", [shape((cx * cy * kz, 2 * chan), BF)]
-    )(g2p, g2s, gate, w3)
-    sent2, kept2 = halves(kept2 + got2.astype(F32), one)
-    sent2, g1 = lax.optimization_barrier((sent2, g1))
-    got2 = swap(sent2, one)
-    half = w_first.shape[1] // 2
-    sent1, kept1 = local_call(
-        part(first_body, cx, cy, kz),
-        "first_weights",
-        [shape((taps, half, chan), BF), shape((taps, half, chan), F32)],
-        [pltpu.VMEM(w_first.shape, F32)],
-        scalars=1,
-    )(side, xp, xs, g1)
-    got1 = swap(sent1, core)
-    sent1, kept1 = halves(kept1 + got1.astype(F32), two)
-    got1 = swap(sent1, two)
+        limit=32,
+    )(side, field, up, tile, left, right, low, high, w1, b1, w2, b2, w3)
+    total = kept + swap(sent, core).astype(F32)
+    sent2, kept2 = halves(total[:, :cut], one)
+    sent1, kept1 = halves(total[:, cut:], two)
+    got2, got1 = lax.optimization_barrier((swap(sent2, one), swap(sent1, two)))
     sent2, kept2 = halves(kept2 + got2.astype(F32), two)
-    got2 = swap(sent2, two)
     sent1, kept1 = halves(kept1 + got1.astype(F32), one)
-    got1 = swap(sent1, one)
+    got2, got1 = lax.optimization_barrier((swap(sent2, two), swap(sent1, one)))
     own2, own1 = summed_inner(kept2 + got2.astype(F32), kept1 + got1.astype(F32), levels[3:])
-    other2, other1 = swap(own2, two), swap(own1, one)
+    other2, other1 = lax.optimization_barrier((swap(own2, two), swap(own1, one)))
     own2, own1 = joined(own2, other2, two), joined(own1, other1, one)
-    other2, other1 = swap(own2, one), swap(own1, two)
+    other2, other1 = lax.optimization_barrier((swap(own2, one), swap(own1, two)))
     own2, own1 = joined(own2, other2, one), joined(own1, other1, two)
     step_second, step_first = local_call(
         norm_body,

time: 103 us -> 84.6 us (0.82)
  Pallas kernels: 31.7 us -> 15.6 us
  other arithmetic: 3.03 us -> 0.87 us
  local copies, waits for them, and re-layouts: 3.07 us -> 1.99 us
    pallas_call x7 -> x5, Pallas kernels: 31.7 us -> 15.6 us  [call(): pl.pallas_call(body, out_shape=outs, in_specs=ins, out_specs=[plain if i...]
    unnamed x22 -> x9, local copies, waits for them, and re-layouts: 2.88 us -> 1.72 us
    add x2 -> x1, other arithmetic: 1.21 us -> 0.14 us  [on_device(): total = kept + swap(sent, core).astype(F32)]
    ppermute x15 -> x14, waiting for transfers between devices: 30 us -> 30.5 us  [swap(): lax.ppermute(part, axis, [(i, i ^ bit) for i in range(lax.axis_size(axis))])]
    ppermute x15 -> x14, starting transfers between devices: 19.1 us -> 19.4 us  [swap(): lax.ppermute(part, axis, [(i, i ^ bit) for i in range(lax.axis_size(axis))])]
  transfers between devices with their start and end apart: 19 -> 18, of which waited for: 12 -> 13; matrix products, arithmetic and copies ran while one was open for 3% -> 1% of each run, Pallas kernels for 9% -> 2%
where the time goes in v4:
time: 84.6 us; the launch traced here: 84.3 us
  waiting for transfers between devices  36.7 us (43%)
  starting transfers between devices  28.1 us (33%)
  Pallas kernels  15.6 us (18%)
  local copies, waits for them, and re-layouts  1.99 us (2%)
  between operations  0.97 us (1%)
  other arithmetic  0.87 us (1%)
    ppermute x14, waiting for transfers between devices, swap(): lax.ppermute(part, axis, [(i, i ^ bit) for i in range(lax.axis_size(axis))])  30.5 us
    ppermute x14, starting transfers between devices, swap(): lax.ppermute(part, axis, [(i, i ^ bit) for i in range(lax.axis_size(axis))])  19.4 us
    pallas_call x5, Pallas kernels, call(): pl.pallas_call(body, out_shape=outs, in_specs=ins, out_specs=[plain if i...  15.6 us
    ppermute x2, starting transfers between devices, exchange(): lax.ppermute(forward, axis, ups)  6.21 us
    ppermute x2, waiting for transfers between devices, exchange(): lax.ppermute(backward, axis, downs)  5.51 us
    ppermute x2, starting transfers between devices, exchange(): lax.ppermute(backward, axis, downs)  2.58 us
    unnamed x9, local copies, waits for them, and re-layouts  1.72 us
  transfers between devices with their start and end apart: 18, of which 13 were waited for; matrix products, arithmetic and copies ran while one was open for 1% of the time, Pallas kernels for 2%

profile of v4, /device:TPU:0, one launch (start us, length us, event | category | flops | bytes accessed | tf_op | source)
XLA Modules:
  0.0 84.3 jit_solution(8273378027325385979)
XLA Ops:
  0.7 1.1 %pack_y.1 = (bf16[336,128]{1,0:T(8,128)(2,1)S(1)}, bf16[336,128]{1,0:T(8,128)(2,1)S(1)}, bf16[16,128]{1,0:T(8,128)(2,1)S(1)}, bf16[4,8,16,128]{3,2,1,0:T(8,128)(2,1)S(1)}, bf16[4,8,32,128]{3,2,1,0:T(8,128)(2,1)S(1)}) custom-call(bf16[4,8,16,128]{3,2,1,0:T(8,128)(2,1)} %hfield.1, bf16[4,8,32,128]{3,2,1,0:T(8,128)(2,1)} %hup.1, s32[4,8,32]{2,1,0:T(8,128)} %hmask.1), custom_call_target="tpu_custom_call" | custom-call | tf_op jit(solution)/shard_map/pack_y/pallas_call | solution.py:374
  1.8 4.9 %collective-permute-start = (bf16[336,128]{1,0:T(8,128)(2,1)S(1)}, bf16[336,128]{1,0:T(8,128)(2,1)S(1)}, u32[]{:S(2)}, u32[]{:S(2)}) collective-permute-start(bf16[336,128]{1,0:T(8,128)(2,1)S(1)} %get-tuple-element.29), channel_id=1, source_target_pairs={{0,1},{1,2},{2,3},{3,4},{4,5},{5,6},{6,7},{8,9},{9,10},{10,11},{11... | collective-permute-start | bytes 258056 | tf_op jit(solution)/shard_map/ppermute | solution.py:78
  6.7 1.3 %collective-permute-start.1 = (bf16[336,128]{1,0:T(8,128)(2,1)S(1)}, bf16[336,128]{1,0:T(8,128)(2,1)S(1)}, u32[]{:S(2)}, u32[]{:S(2)}) collective-permute-start(bf16[336,128]{1,0:T(8,128)(2,1)S(1)} %get-tuple-element.30), channel_id=1, source_target_pairs={{1,0},{2,1},{3,2},{4,3},{5,4},{6,5},{7,6},{9,8},{10,9},{11,10},{12... | collective-permute-start | bytes 258056 | tf_op jit(solution)/shard_map/ppermute | solution.py:78
  8.0 0.8 collective-permute-done.left
  8.8 4.3 %collective-permute-done.1.right = bf16[336,128]{1,0:T(8,128)(2,1)S(1)} collective-permute-done((bf16[336,128]{1,0:T(8,128)(2,1)S(1)}, bf16[336,128]{1,0:T(8,128)(2,1)S(1)}, u32[]{:S(2)}, u32[]{:S(2)}) %collective-permute-start.1) | collective-permute-done | bytes 86048 | tf_op jit(solution)/shard_map/ppermute | solution.py:78
  13.1 0.1 pack_x.1
  13.2 1.3 %collective-permute-start.2 = (bf16[1040,128]{1,0:T(8,128)(2,1)S(1)}, bf16[1040,128]{1,0:T(8,128)(2,1)S(1)}, u32[]{:S(2)}, u32[]{:S(2)}) collective-permute-start(bf16[1040,128]{1,0:T(8,128)(2,1)S(1)} %get-tuple-element.31), channel_id=1, source_target_pairs={{0,8},{8,16},{16,24},{1,9},{9,17},{17,25},{2,10},{10,18},{18,26},{... | collective-permute-start | bytes 798728 | tf_op jit(solution)/shard_map/ppermute | solution.py:78
  14.5 1.3 %collective-permute-start.3 = (bf16[1040,128]{1,0:T(8,128)(2,1)S(1)}, bf16[1040,128]{1,0:T(8,128)(2,1)S(1)}, u32[]{:S(2)}, u32[]{:S(2)}) collective-permute-start(bf16[1040,128]{1,0:T(8,128)(2,1)S(1)} %get-tuple-element.32), channel_id=1, source_target_pairs={{8,0},{16,8},{24,16},{9,1},{17,9},{25,17},{10,2},{18,10},{26,18},{... | collective-permute-start | bytes 798728 | tf_op jit(solution)/shard_map/ppermute | solution.py:78
  15.8 0.0 copy-start.1
  15.8 1.0 %copy-done.1 = bf16[27,64,128]{2,1,0:T(8,128)(2,1)S(1)} copy-done((bf16[27,64,128]{2,1,0:T(8,128)(2,1)S(1)}, bf16[27,64,128]{2,1,0:T(8,128)(2,1)}, u32[]{:S(2)}) %copy-start.1) | copy-done | bytes 442392
  16.8 1.5 %weights.1 = (bf16[2304,256]{1,0:T(8,128)(2,1)S(1)}, bf16[4608,256]{1,0:T(8,128)(2,1)S(1)}, bf16[4608,256]{1,0:T(8,128)(2,1)S(1)}) custom-call(bf16[27,64,128]{2,1,0:T(8,128)(2,1)S(1)} %copy-done.1, bf16[27,128,128]{2,1,0:T(8,128)(2,1)S(1)} %copy-done), custom_call_target="tpu_custom_call" | custom-call | tf_op jit(solution)/shard_map/weights/pallas_call | solution.py:374
  18.4 1.2 %collective-permute-done.3.high = bf16[1040,128]{1,0:T(8,128)(2,1)S(1)} collective-permute-done((bf16[1040,128]{1,0:T(8,128)(2,1)S(1)}, bf16[1040,128]{1,0:T(8,128)(2,1)S(1)}, u32[]{:S(2)}, u32[]{:S(2)}) %collective-permute-start.3) | collective-permute-done | bytes 266272 | tf_op jit(solution)/shard_map/ppermute | solution.py:78
  19.6 10.7 %compute.1 = (bf16[4,8,32,128]{3,2,1,0:T(8,128)(2,1)S(1)}, bf16[27,96,128]{2,1,0:T(8,128)(2,1)S(1)}, f32[27,96,128]{2,1,0:T(8,128)S(1)}) custom-call(s32[1]{0:T(128)} %bitcast.side, bf16[4,8,16,128]{3,2,1,0:T(8,128)(2,1)S(1)} %get-tuple-element.26.field, bf16[4,8,32,128]{3,2,1,0:T(8,128)(2,1)S(1)} %get-tuple-element.27.up, ...), custom_call_target="tpu_custom_call" | custom-call | tf_op jit(solution)/shard_map/compute/pallas_call | solution.py:374
  30.4 4.9 %collective-permute-start.4 = (bf16[27,96,128]{2,1,0:T(8,128)(2,1)S(1)}, bf16[27,96,128]{2,1,0:T(8,128)(2,1)S(1)}, u32[]{:S(2)}, u32[]{:S(2)}) collective-permute-start(bf16[27,96,128]{2,1,0:T(8,128)(2,1)S(1)} %get-tuple-element.38), channel_id=1, source_target_pairs={{0,8},{8,0},{16,24},{24,16},{1,9},{9,1},{17,25},{25,17},{2,10},{10... | collective-permute-start | bytes 1990664 | tf_op jit(solution)/shard_map/ppermute | solution.py:29
  35.2 1.7 %collective-permute-done.4 = bf16[27,96,128]{2,1,0:T(8,128)(2,1)S(1)} collective-permute-done((bf16[27,96,128]{2,1,0:T(8,128)(2,1)S(1)}, bf16[27,96,128]{2,1,0:T(8,128)(2,1)S(1)}, u32[]{:S(2)}, u32[]{:S(2)}) %collective-permute-start.4) | collective-permute-done | bytes 663584 | tf_op jit(solution)/shard_map/ppermute | solution.py:29
  37.0 0.1 convert_add_fusion
  37.1 0.1 slice.32
  37.3 0.1 collective-permute-start.5
  37.4 2.5 %collective-permute-start.6 = (bf16[27,16,128]{2,1,0:T(8,128)(2,1)S(1)}, bf16[27,16,128]{2,1,0:T(8,128)(2,1)S(1)}, u32[]{:S(2)}, u32[]{:S(2)}) collective-permute-start(bf16[27,16,128]{2,1,0:T(8,128)(2,1)S(1)} %dynamic-slice_convert_fusion.2), channel_id=1, source_target_pairs={{0,1},{1,0},{2,3},{3,2},{4,5},{5,4},{6,7},{7,6},{8,9},{9,8},{10,11... | collective-permute-start | bytes 331784 | tf_op jit(solution)/shard_map/ppermute | solution.py:29
  39.9 3.5 %collective-permute-done.6 = bf16[27,16,128]{2,1,0:T(8,128)(2,1)S(1)} collective-permute-done((bf16[27,16,128]{2,1,0:T(8,128)(2,1)S(1)}, bf16[27,16,128]{2,1,0:T(8,128)(2,1)S(1)}, u32[]{:S(2)}, u32[]{:S(2)}) %collective-permute-start.6) | collective-permute-done | bytes 110624 | tf_op jit(solution)/shard_map/ppermute | solution.py:29
  43.5 1.6 %collective-permute-done.5 = bf16[27,32,128]{2,1,0:T(8,128)(2,1)S(1)} collective-permute-done((bf16[27,32,128]{2,1,0:T(8,128)(2,1)S(1)}, bf16[27,32,128]{2,1,0:T(8,128)(2,1)S(1)}, u32[]{:S(2)}, u32[]{:S(2)}) %collective-permute-start.5) | collective-permute-done | bytes 221216 | tf_op jit(solution)/shard_map/ppermute | solution.py:29
  45.1 0.1 convert_add_fusion.1
  45.2 2.5 %collective-permute-start.7 = (bf16[27,16,128]{2,1,0:T(8,128)(2,1)S(1)}, bf16[27,16,128]{2,1,0:T(8,128)(2,1)S(1)}, u32[]{:S(2)}, u32[]{:S(2)}) collective-permute-start(bf16[27,16,128]{2,1,0:T(8,128)(2,1)S(1)} %dynamic-slice_convert_fusion.1), channel_id=1, source_target_pairs={{0,1},{1,0},{2,3},{3,2},{4,5},{5,4},{6,7},{7,6},{8,9},{9,8},{10,11... | collective-permute-start | bytes 331784 | tf_op jit(solution)/shard_map/ppermute | solution.py:29
  47.7 0.4 collective-permute-start.8
  48.1 3.9 %collective-permute-done.8 = bf16[27,8,128]{2,1,0:T(8,128)(2,1)S(1)} collective-permute-done((bf16[27,8,128]{2,1,0:T(8,128)(2,1)S(1)}, bf16[27,8,128]{2,1,0:T(8,128)(2,1)S(1)}, u32[]{:S(2)}, u32[]{:S(2)}) %collective-permute-start.8) | collective-permute-done | bytes 55328 | tf_op jit(solution)/shard_map/ppermute | solution.py:29
  52.1 1.6 %collective-permute-start.9 = (bf16[27,12,128]{2,1,0:T(8,128)(2,1)S(1)}, bf16[27,12,128]{2,1,0:T(8,128)(2,1)S(1)}, u32[]{:S(2)}, u32[]{:S(2)}) collective-permute-start(bf16[27,12,128]{2,1,0:T(8,128)(2,1)S(1)} %pad_maximum_fusion), channel_id=1, source_target_pairs={{0,2},{1,3},{2,0},{3,1},{4,6},{5,7},{6,4},{7,5},{8,10},{9,11},{10,... | collective-permute-start | bytes 248840 | tf_op jit(solution)/shard_map/ppermute | solution.py:29
  53.7 3.2 %collective-permute-done.9 = bf16[27,12,128]{2,1,0:T(8,128)(2,1)S(1)} collective-permute-done((bf16[27,12,128]{2,1,0:T(8,128)(2,1)S(1)}, bf16[27,12,128]{2,1,0:T(8,128)(2,1)S(1)}, u32[]{:S(2)}, u32[]{:S(2)}) %collective-permute-start.9) | collective-permute-done | bytes 82976 | tf_op jit(solution)/shard_map/ppermute | solution.py:29
  57.0 2.8 %collective-permute-start.10 = (bf16[27,12,128]{2,1,0:T(8,128)(2,1)S(1)}, bf16[27,12,128]{2,1,0:T(8,128)(2,1)S(1)}, u32[]{:S(2)}, u32[]{:S(2)}) collective-permute-start(bf16[27,12,128]{2,1,0:T(8,128)(2,1)S(1)} %pad_maximum_fusion.1), channel_id=1, source_target_pairs={{0,4},{1,5},{2,6},{3,7},{4,0},{5,1},{6,2},{7,3},{8,12},{9,13},{10,... | collective-permute-start | bytes 248840 | tf_op jit(solution)/shard_map/ppermute | solution.py:29
  59.8 4.0 %collective-permute-done.10 = bf16[27,12,128]{2,1,0:T(8,128)(2,1)S(1)} collective-permute-done((bf16[27,12,128]{2,1,0:T(8,128)(2,1)S(1)}, bf16[27,12,128]{2,1,0:T(8,128)(2,1)S(1)}, u32[]{:S(2)}, u32[]{:S(2)}) %collective-permute-start.10) | collective-permute-done | bytes 82976 | tf_op jit(solution)/shard_map/ppermute | solution.py:29
  63.9 0.8 collective-permute-start.11
  64.7 4.0 %collective-permute-done.11 = bf16[27,12,128]{2,1,0:T(8,128)(2,1)S(1)} collective-permute-done((bf16[27,12,128]{2,1,0:T(8,128)(2,1)S(1)}, bf16[27,12,128]{2,1,0:T(8,128)(2,1)S(1)}, u32[]{:S(2)}, u32[]{:S(2)}) %collective-permute-start.11) | collective-permute-done | bytes 82976 | tf_op jit(solution)/shard_map/ppermute | solution.py:29
  68.7 0.6 collective-permute-start.12
  69.3 0.1 maximum_select_fusion.5
  69.4 0.5 collective-permute-start.13
  69.9 3.8 %collective-permute-done.13 = bf16[27,8,128]{2,1,0:T(8,128)(2,1)S(1)} collective-permute-done((bf16[27,8,128]{2,1,0:T(8,128)(2,1)S(1)}, bf16[27,8,128]{2,1,0:T(8,128)(2,1)S(1)}, u32[]{:S(2)}, u32[]{:S(2)}) %collective-permute-start.13) | collective-permute-done | bytes 55328 | tf_op jit(solution)/shard_map/ppermute | solution.py:29
  73.6 0.0 collective-permute-done.12
  73.6 0.1 maximum_select_fusion.1
  73.7 1.3 %collective-permute-start.14 = (bf16[27,32,128]{2,1,0:T(8,128)(2,1)S(1)}, bf16[27,32,128]{2,1,0:T(8,128)(2,1)S(1)}, u32[]{:S(2)}, u32[]{:S(2)}) collective-permute-start(bf16[27,32,128]{2,1,0:T(8,128)(2,1)S(1)} %maximum_select_fusion.1), channel_id=1, source_target_pairs={{0,16},{8,24},{16,0},{24,8},{1,17},{9,25},{17,1},{25,9},{2,18},{10... | collective-permute-start | bytes 663560 | tf_op jit(solution)/shard_map/ppermute | solution.py:29
  75.1 0.8 collective-permute-start.15
  75.8 4.0 %collective-permute-done.15 = bf16[27,16,128]{2,1,0:T(8,128)(2,1)S(1)} collective-permute-done((bf16[27,16,128]{2,1,0:T(8,128)(2,1)S(1)}, bf16[27,16,128]{2,1,0:T(8,128)(2,1)S(1)}, u32[]{:S(2)}, u32[]{:S(2)}) %collective-permute-start.15) | collective-permute-done | bytes 110624 | tf_op jit(solution)/shard_map/ppermute | solution.py:29
  79.9 0.0 collective-permute-done.14
  79.9 0.1 maximum_select_fusion.own2
  80.0 0.1 collective-permute-start.16
  80.1 0.1 maximum_select_fusion.2.own1
  80.2 0.6 collective-permute-start.17
  80.7 0.7 copy.10
  81.5 0.7 collective-permute-done.17.other1
  82.2 2.1 %normalize.1 = (f32[27,128,128]{2,1,0:T(8,128)}, f32[27,64,128]{2,1,0:T(8,128)}) custom-call(s32[1]{0:T(128)} %bitcast.side, bf16[27,64,128]{2,1,0:T(8,128)(2,1)S(1)} %maximum_select_fusion.own2, bf16[27,64,128]{2,1,0:T(8,128)(2,1)S(1)} %collective-permute-done.16.other2, bf16[27,32,128]{2,1,0:T(8,128)(2,1)S(1)} %maximum_select_fusion.2.own1, ...), custom_call_target="tpu_custom_call" | custom-call | tf_op jit(solution)/shard_map/normalize/pallas_call | solution.py:374
  (33 shorter events, 0.5 us)
Async XLA Ops:
  0.6 15.2 %copy-start = (bf16[27,128,128]{2,1,0:T(8,128)(2,1)S(1)}, bf16[27,128,128]{2,1,0:T(8,128)(2,1)}, u32[]{:S(2)}) copy-start(bf16[27,128,128]{2,1,0:T(8,128)(2,1)} %second.1) | copy-start | bytes 2654212
  0.6 17.7 %copy-start.2 = (f32[128]{0:T(128)S(1)}, f32[128]{0:T(128)}, u32[]{:S(2)}) copy-start(f32[128]{0:T(128)} %param.10) | copy-start | bytes 1540
  0.7 17.7 %copy-start.3 = (f32[128]{0:T(128)S(1)}, f32[128]{0:T(128)}, u32[]{:S(2)}) copy-start(f32[128]{0:T(128)} %param.12) | copy-start | bytes 1540
  1.8 7.0 %collective-permute-start = (bf16[336,128]{1,0:T(8,128)(2,1)S(1)}, bf16[336,128]{1,0:T(8,128)(2,1)S(1)}, u32[]{:S(2)}, u32[]{:S(2)}) collective-permute-start(bf16[336,128]{1,0:T(8,128)(2,1)S(1)} %get-tuple-element.29), channel_id=1, source_target_pairs={{0,1},{1,2},{2,3},{3,4},{4,5},{5,6},{6,7},{8,9},{9,10},{10,11},{11... | collective-permute-start | bytes 258056 | tf_op jit(solution)/shard_map/ppermute | solution.py:78
  6.7 6.4 %collective-permute-start.1 = (bf16[336,128]{1,0:T(8,128)(2,1)S(1)}, bf16[336,128]{1,0:T(8,128)(2,1)S(1)}, u32[]{:S(2)}, u32[]{:S(2)}) collective-permute-start(bf16[336,128]{1,0:T(8,128)(2,1)S(1)} %get-tuple-element.30), channel_id=1, source_target_pairs={{1,0},{2,1},{3,2},{4,3},{5,4},{6,5},{7,6},{9,8},{10,9},{11,10},{12... | collective-permute-start | bytes 258056 | tf_op jit(solution)/shard_map/ppermute | solution.py:78
  13.2 5.2 %collective-permute-start.2 = (bf16[1040,128]{1,0:T(8,128)(2,1)S(1)}, bf16[1040,128]{1,0:T(8,128)(2,1)S(1)}, u32[]{:S(2)}, u32[]{:S(2)}) collective-permute-start(bf16[1040,128]{1,0:T(8,128)(2,1)S(1)} %get-tuple-element.31), channel_id=1, source_target_pairs={{0,8},{8,16},{16,24},{1,9},{9,17},{17,25},{2,10},{10,18},{18,26},{... | collective-permute-start | bytes 798728 | tf_op jit(solution)/shard_map/ppermute | solution.py:78
  14.5 5.1 %collective-permute-start.3 = (bf16[1040,128]{1,0:T(8,128)(2,1)S(1)}, bf16[1040,128]{1,0:T(8,128)(2,1)S(1)}, u32[]{:S(2)}, u32[]{:S(2)}) collective-permute-start(bf16[1040,128]{1,0:T(8,128)(2,1)S(1)} %get-tuple-element.32), channel_id=1, source_target_pairs={{8,0},{16,8},{24,16},{9,1},{17,9},{25,17},{10,2},{18,10},{26,18},{... | collective-permute-start | bytes 798728 | tf_op jit(solution)/shard_map/ppermute | solution.py:78
  15.8 1.0 %copy-start.1 = (bf16[27,64,128]{2,1,0:T(8,128)(2,1)S(1)}, bf16[27,64,128]{2,1,0:T(8,128)(2,1)}, u32[]{:S(2)}) copy-start(bf16[27,64,128]{2,1,0:T(8,128)(2,1)} %first.1) | copy-start | bytes 1327108
  30.4 6.6 %collective-permute-start.4 = (bf16[27,96,128]{2,1,0:T(8,128)(2,1)S(1)}, bf16[27,96,128]{2,1,0:T(8,128)(2,1)S(1)}, u32[]{:S(2)}, u32[]{:S(2)}) collective-permute-start(bf16[27,96,128]{2,1,0:T(8,128)(2,1)S(1)} %get-tuple-element.38), channel_id=1, source_target_pairs={{0,8},{8,0},{16,24},{24,16},{1,9},{9,1},{17,25},{25,17},{2,10},{10... | collective-permute-start | bytes 1990664 | tf_op jit(solution)/shard_map/ppermute | solution.py:29
  37.3 7.8 %collective-permute-start.5 = (bf16[27,32,128]{2,1,0:T(8,128)(2,1)S(1)}, bf16[27,32,128]{2,1,0:T(8,128)(2,1)S(1)}, u32[]{:S(2)}, u32[]{:S(2)}) collective-permute-start(bf16[27,32,128]{2,1,0:T(8,128)(2,1)S(1)} %dynamic-slice_convert_fusion), channel_id=1, source_target_pairs={{0,16},{8,24},{16,0},{24,8},{1,17},{9,25},{17,1},{25,9},{2,18},{10... | collective-permute-start | bytes 663560 | tf_op jit(solution)/shard_map/ppermute | solution.py:29
  37.4 6.0 %collective-permute-start.6 = (bf16[27,16,128]{2,1,0:T(8,128)(2,1)S(1)}, bf16[27,16,128]{2,1,0:T(8,128)(2,1)S(1)}, u32[]{:S(2)}, u32[]{:S(2)}) collective-permute-start(bf16[27,16,128]{2,1,0:T(8,128)(2,1)S(1)} %dynamic-slice_convert_fusion.2), channel_id=1, source_target_pairs={{0,1},{1,0},{2,3},{3,2},{4,5},{5,4},{6,7},{7,6},{8,9},{9,8},{10,11... | collective-permute-start | bytes 331784 | tf_op jit(solution)/shard_map/ppermute | solution.py:29
  45.2 6.8 %collective-permute-start.7 = (bf16[27,16,128]{2,1,0:T(8,128)(2,1)S(1)}, bf16[27,16,128]{2,1,0:T(8,128)(2,1)S(1)}, u32[]{:S(2)}, u32[]{:S(2)}) collective-permute-start(bf16[27,16,128]{2,1,0:T(8,128)(2,1)S(1)} %dynamic-slice_convert_fusion.1), channel_id=1, source_target_pairs={{0,1},{1,0},{2,3},{3,2},{4,5},{5,4},{6,7},{7,6},{8,9},{9,8},{10,11... | collective-permute-start | bytes 331784 | tf_op jit(solution)/shard_map/ppermute | solution.py:29
  47.7 4.2 %collective-permute-start.8 = (bf16[27,8,128]{2,1,0:T(8,128)(2,1)S(1)}, bf16[27,8,128]{2,1,0:T(8,128)(2,1)S(1)}, u32[]{:S(2)}, u32[]{:S(2)}) collective-permute-start(bf16[27,8,128]{2,1,0:T(8,128)(2,1)S(1)} %dynamic-slice_convert_fusion.4), channel_id=1, source_target_pairs={{0,16},{8,24},{16,0},{24,8},{1,17},{9,25},{17,1},{25,9},{2,18},{10... | collective-permute-start | bytes 165896 | tf_op jit(solution)/shard_map/ppermute | solution.py:29
  52.1 4.8 %collective-permute-start.9 = (bf16[27,12,128]{2,1,0:T(8,128)(2,1)S(1)}, bf16[27,12,128]{2,1,0:T(8,128)(2,1)S(1)}, u32[]{:S(2)}, u32[]{:S(2)}) collective-permute-start(bf16[27,12,128]{2,1,0:T(8,128)(2,1)S(1)} %pad_maximum_fusion), channel_id=1, source_target_pairs={{0,2},{1,3},{2,0},{3,1},{4,6},{5,7},{6,4},{7,5},{8,10},{9,11},{10,... | collective-permute-start | bytes 248840 | tf_op jit(solution)/shard_map/ppermute | solution.py:29
  57.0 6.8 %collective-permute-start.10 = (bf16[27,12,128]{2,1,0:T(8,128)(2,1)S(1)}, bf16[27,12,128]{2,1,0:T(8,128)(2,1)S(1)}, u32[]{:S(2)}, u32[]{:S(2)}) collective-permute-start(bf16[27,12,128]{2,1,0:T(8,128)(2,1)S(1)} %pad_maximum_fusion.1), channel_id=1, source_target_pairs={{0,4},{1,5},{2,6},{3,7},{4,0},{5,1},{6,2},{7,3},{8,12},{9,13},{10,... | collective-permute-start | bytes 248840 | tf_op jit(solution)/shard_map/ppermute | solution.py:29
  63.9 4.8 %collective-permute-start.11 = (bf16[27,12,128]{2,1,0:T(8,128)(2,1)S(1)}, bf16[27,12,128]{2,1,0:T(8,128)(2,1)S(1)}, u32[]{:S(2)}, u32[]{:S(2)}) collective-permute-start(bf16[27,12,128]{2,1,0:T(8,128)(2,1)S(1)} %add_convert_fusion), channel_id=1, source_target_pairs={{0,2},{1,3},{2,0},{3,1},{4,6},{5,7},{6,4},{7,5},{8,10},{9,11},{10,... | collective-permute-start | bytes 248840 | tf_op jit(solution)/shard_map/ppermute | solution.py:29
  68.7 4.9 %collective-permute-start.12 = (bf16[27,16,128]{2,1,0:T(8,128)(2,1)S(1)}, bf16[27,16,128]{2,1,0:T(8,128)(2,1)S(1)}, u32[]{:S(2)}, u32[]{:S(2)}) collective-permute-start(bf16[27,16,128]{2,1,0:T(8,128)(2,1)S(1)} %maximum_select_fusion.3), channel_id=1, source_target_pairs={{0,1},{1,0},{2,3},{3,2},{4,5},{5,4},{6,7},{7,6},{8,9},{9,8},{10,11... | collective-permute-start | bytes 331784 | tf_op jit(solution)/shard_map/ppermute | solution.py:29
  69.4 4.2 %collective-permute-start.13 = (bf16[27,8,128]{2,1,0:T(8,128)(2,1)S(1)}, bf16[27,8,128]{2,1,0:T(8,128)(2,1)S(1)}, u32[]{:S(2)}, u32[]{:S(2)}) collective-permute-start(bf16[27,8,128]{2,1,0:T(8,128)(2,1)S(1)} %maximum_select_fusion.5), channel_id=1, source_target_pairs={{0,16},{8,24},{16,0},{24,8},{1,17},{9,25},{17,1},{25,9},{2,18},{10... | collective-permute-start | bytes 165896 | tf_op jit(solution)/shard_map/ppermute | solution.py:29
  73.7 6.2 %collective-permute-start.14 = (bf16[27,32,128]{2,1,0:T(8,128)(2,1)S(1)}, bf16[27,32,128]{2,1,0:T(8,128)(2,1)S(1)}, u32[]{:S(2)}, u32[]{:S(2)}) collective-permute-start(bf16[27,32,128]{2,1,0:T(8,128)(2,1)S(1)} %maximum_select_fusion.1), channel_id=1, source_target_pairs={{0,16},{8,24},{16,0},{24,8},{1,17},{9,25},{17,1},{25,9},{2,18},{10... | collective-permute-start | bytes 663560 | tf_op jit(solution)/shard_map/ppermute | solution.py:29
  75.1 4.8 %collective-permute-start.15 = (bf16[27,16,128]{2,1,0:T(8,128)(2,1)S(1)}, bf16[27,16,128]{2,1,0:T(8,128)(2,1)S(1)}, u32[]{:S(2)}, u32[]{:S(2)}) collective-permute-start(bf16[27,16,128]{2,1,0:T(8,128)(2,1)S(1)} %maximum_select_fusion.4), channel_id=1, source_target_pairs={{0,1},{1,0},{2,3},{3,2},{4,5},{5,4},{6,7},{7,6},{8,9},{9,8},{10,11... | collective-permute-start | bytes 331784 | tf_op jit(solution)/shard_map/ppermute | solution.py:29
  80.0 2.2 %collective-permute-start.16 = (bf16[27,64,128]{2,1,0:T(8,128)(2,1)S(1)}, bf16[27,64,128]{2,1,0:T(8,128)(2,1)S(1)}, u32[]{:S(2)}, u32[]{:S(2)}) collective-permute-start(bf16[27,64,128]{2,1,0:T(8,128)(2,1)S(1)} %maximum_select_fusion.own2), channel_id=1, source_target_pairs={{0,8},{8,0},{16,24},{24,16},{1,9},{9,1},{17,25},{25,17},{2,10},{10... | collective-permute-start | bytes 1327112 | tf_op jit(solution)/shard_map/ppermute | solution.py:29
  80.2 2.0 %collective-permute-start.17 = (bf16[27,32,128]{2,1,0:T(8,128)(2,1)S(1)}, bf16[27,32,128]{2,1,0:T(8,128)(2,1)S(1)}, u32[]{:S(2)}, u32[]{:S(2)}) collective-permute-start(bf16[27,32,128]{2,1,0:T(8,128)(2,1)S(1)} %maximum_select_fusion.2.own1), channel_id=1, source_target_pairs={{0,8},{8,0},{16,24},{24,16},{1,9},{9,1},{17,25},{25,17},{2,10},{10... | collective-permute-start | bytes 663560 | tf_op jit(solution)/shard_map/ppermute | solution.py:29

commit v5 on v4

--- a/solution.py
+++ b/solution.py
@@ -35,50 +35,63 @@
 
 
 def halves(part, level):
-    half = part.shape[1] // 2
+    half = part.shape[0] // 2
     side = side_of(level)
-    sent = lax.dynamic_slice_in_dim(part, (1 - side) * half, half, 1).astype(BF)
-    kept = lax.dynamic_slice_in_dim(part, side * half, half, 1)
+    sent = lax.dynamic_slice_in_dim(part, (1 - side) * half, half, 0).astype(BF)
+    kept = lax.dynamic_slice_in_dim(part, side * half, half, 0)
     return sent, kept
 
 
 def joined(own, other, level):
     return jnp.where(
         side_of(level) == 0,
-        jnp.concatenate([own, other], axis=1),
-        jnp.concatenate([other, own], axis=1),
+        jnp.concatenate([own, other], axis=0),
+        jnp.concatenate([other, own], axis=0),
     )
 
 
-def summed_inner(second, first, levels):
-    middle, final = levels[:-1], levels[-1]
+def summed_everywhere(total, levels):
+    one, two, middle, final = levels[0], levels[1], levels[2:-1], levels[-1]
+    cut = total.shape[0] // 2
+    parts = [total[:cut], total[cut:]]
+    for order in ((one, two), (two, one)):
+        split = [halves(part, level) for part, level in zip(parts, order)]
+        got = lax.optimization_barrier(
+            [swap(sent, level) for (sent, _), level in zip(split, order)]
+        )
+        parts = [kept + other.astype(F32) for (_, kept), other in zip(split, got)]
+    both = jnp.concatenate(parts, axis=0)
     for level in middle:
-        sent2, kept2 = halves(second, level)
-        sent1, kept1 = halves(first, level)
-        cut = sent2.shape[1]
-        got = swap(jnp.concatenate([sent2, sent1], axis=1), level).astype(F32)
-        second, first = kept2 + got[:, :cut], kept1 + got[:, cut:]
-    cut = second.shape[1]
-    both = jnp.concatenate([second, first], axis=1).astype(BF)
+        sent, kept = halves(both, level)
+        both = kept + swap(sent, level).astype(F32)
+    both = both.astype(BF)
     both = (both.astype(F32) + swap(both, final).astype(F32)).astype(BF)
     for level in reversed(middle):
-        got = swap(both, level)
-        both = jnp.concatenate(
-            [joined(both[:, :cut], got[:, :cut], level), joined(both[:, cut:], got[:, cut:], level)],
-            axis=1,
-        )
-        cut *= 2
-    return both[:, :cut], both[:, cut:]
-
-
-def exchange(forward, backward, axis):
+        both = joined(both, swap(both, level), level)
+    cut = both.shape[0] // 2
+    parts = [both[:cut], both[cut:]]
+    for order in ((two, one), (one, two)):
+        got = lax.optimization_barrier([swap(part, level) for part, level in zip(parts, order)])
+        parts = [joined(own, other, level) for own, other, level in zip(parts, got, order)]
+    return parts
+
+
+def exchange(inner, outer, axis):
     count = lax.axis_size(axis)
-    ups = [(i, i + 1) for i in range(count - 1)]
-    downs = [(target, source) for source, target in ups]
-    return lax.ppermute(forward, axis, ups), lax.ppermute(backward, axis, downs)
-
-
-def pack_y_body(cx, cy, kz, hfield, hup, hmask, last, first, tile, field, up, mask, square, deep, sems):
+    pairs = [(i, i + 1) for i in range(1, count - 1, 2)]
+    outer = lax.ppermute(outer, axis, pairs + [(b, a) for a, b in pairs])
+    inner = lax.ppermute(inner, axis, [(i, i ^ 1) for i in range(count)])
+    return inner, outer
+
+
+def ends_of(odd, inner, outer):
+    first, second = inner[...], outer[...]
+    return jnp.where(odd, first, second), jnp.where(odd, second, first)
+
+
+def pack_y_body(
+    cx, cy, kz, odd, hfield, hup, hmask, inner, outer, tile, field, up, mask, square, deep, sems
+):
     copies = [
         pltpu.make_async_copy(source, target, sems.at[i])
         for i, (source, target) in enumerate(((hmask, mask), (hfield, field), (hup, up)))
@@ -90,33 +103,37 @@
     copies[0].wait()
     square[0:cells, 0 : 2 * kz] = mask[...].reshape(cells, 2 * kz).astype(F32)
     deep[...] = square[...].T
-    even = deep[pl.ds(0, kz, stride=2), :]
-    odd = deep[pl.ds(1, kz, stride=2), :]
-    tile[...] = (even + pltpu.roll(odd, LANES // 2, 1)).astype(BF)
+    at_even = deep[pl.ds(0, kz, stride=2), :]
+    at_odd = deep[pl.ds(1, kz, stride=2), :]
+    tile[...] = (at_even + pltpu.roll(at_odd, LANES // 2, 1)).astype(BF)
     copies[1].wait()
     copies[2].wait()
-    for ref, at_field, at_up in ((last, cy - FIELD_HALO, cy - 1), (first, 0, 0)):
+    for ref, end in ((inner, 1 - odd[0]), (outer, odd[0])):
         row = 0
         for rows in (
-            field[:, at_field : at_field + FIELD_HALO].reshape(-1, LANES),
-            up[:, at_up : at_up + 1].reshape(-1, LANES),
+            field[:, pl.ds(end * (cy - FIELD_HALO), FIELD_HALO)].reshape(-1, LANES),
+            up[:, pl.ds(end * (cy - 1), 1)].reshape(-1, LANES),
             tile[...],
         ):
             ref[row : row + rows.shape[0]] = rows
             row += rows.shape[0]
 
 
-def pack_x_body(cx, cy, kz, field, up, tile, left, right, last, first):
+def pack_x_body(
+    cx, cy, kz, odd, odd_y, field, up, tile, inner_y, outer_y, inner, outer, left, right
+):
+    left[...], right[...] = ends_of(odd_y[0] == 1, inner_y, outer_y)
     fh = FIELD_HALO
     nf, nu = cx * fh * kz, cx * 2 * kz
-    ends_f = [m[0:nf].reshape(cx, fh, kz, LANES) for m in (left, right)]
-    ends_u = [m[nf : nf + nu].reshape(cx, 1, 2 * kz, LANES) for m in (left, right)]
-    for ref, at_field, at_up in ((last, cx - fh, cx - 1), (first, 0, 0)):
+    for ref, end in ((inner, 1 - odd[0]), (outer, odd[0])):
+        at_field, at_up = end * (cx - fh), end * (cx - 1)
         row = 0
         parts = []
-        for r in range(at_field, at_field + fh):
-            parts += [ends_f[0][r], field[r], ends_f[1][r]]
-        parts += [ends_u[0][at_up], up[at_up], ends_u[1][at_up]]
+        for r in range(fh):
+            at = pl.multiple_of((at_field + r) * fh * kz, kz)
+            parts += [left[pl.ds(at, fh * kz)], field[at_field + r], right[pl.ds(at, fh * kz)]]
+        at = pl.multiple_of(nf + at_up * 2 * kz, kz)
+        parts += [left[pl.ds(at, 2 * kz)], up[at_up], right[pl.ds(at, 2 * kz)]]
         parts += [left[nf + nu :], tile[...], right[nf + nu :]]
         for part in parts:
             rows = part.reshape(-1, LANES)
@@ -146,10 +163,11 @@
 
 def compute_body(
     cx, cy, kz,
-    side, field, up, tile, left, right, low, high, w1, b1, w2, b2, w3,
+    side, field, up, tile, left, right, inner, outer, w1, b1, w2, b2, w3,
     features, sent, kept,
-    xp, xs, hp, hs, act, upf, outf, g2p, g2s, gate, g1, d2, d1,
+    low, high, xp, xs, hp, hs, act, upf, outf, g2p, g2s, gate, g1, d2, d1,
 ):
+    low[...], high[...] = ends_of(side[0] == 1, inner, outer)
     fh, mh = FIELD_HALO, MASK_HALO
     ex, ey, uy = cx + 2 * fh, cy + 2 * fh, cy + 2
     nf, nu = cx * fh * kz, cx * 2 * kz
@@ -321,14 +339,51 @@
         at += half
 
 
-def norm_body(side, own2, other2, own1, other1, out2, out1):
-    for own, other, out in ((own2, other2, out2), (own1, other1, out1)):
-        half = own.shape[1]
-        mine, rest = own[...].astype(F32), other[...].astype(F32)
-        total = jnp.sum(mine * mine) + jnp.sum(rest * rest)
-        scale = lax.rsqrt(jnp.full((1, LANES), total) / float(out.size) + 1e-06)
-        out[:, pl.ds(pl.multiple_of(side[0] * half, half), half)] = mine * scale
-        out[:, pl.ds(pl.multiple_of((1 - side[0]) * half, half), half)] = rest * scale
+def norm_body(side, own_a, own_b, other_a, other_b, out2, out1, held2, held1, sems):
+    taps = out2.shape[0]
+    split = own_a.shape[0]
+    rows_of = held2.shape[1] // 2, held1.shape[1] // 2
+    stride = sum(rows_of)
+
+    def rows(pair, start, count):
+        low, high = pair
+        parts = []
+        if start < split:
+            parts.append(low[start : min(start + count, split)])
+        if start + count > split:
+            parts.append(high[max(start, split) - split : start + count - split])
+        return jnp.concatenate(parts, axis=0).astype(F32)
+
+    def spans():
+        for t in range(taps):
+            for i, at in ((0, t * stride), (1, t * stride + rows_of[0])):
+                yield t, i, at
+
+    squares = [jnp.zeros((8, LANES), F32), jnp.zeros((8, LANES), F32)]
+    for t, i, at in spans():
+        for pair in ((own_a, own_b), (other_a, other_b)):
+            value = rows(pair, at, rows_of[i])
+            squares[i] += jnp.sum((value * value).reshape(-1, 8, LANES), axis=0)
+    scales = [
+        lax.rsqrt(jnp.full((1, LANES), jnp.sum(total)) / float(out.size) + 1e-06)
+        for total, out in zip(squares, (out2, out1))
+    ]
+    group = taps // 3
+    copies = []
+    for t, i, at in spans():
+        held, count = (held2, held1)[i], rows_of[i]
+        mine = pl.multiple_of(side[0] * count, count)
+        rest = pl.multiple_of((1 - side[0]) * count, count)
+        held[t, pl.ds(mine, count)] = rows((own_a, own_b), at, count) * scales[i]
+        held[t, pl.ds(rest, count)] = rows((other_a, other_b), at, count) * scales[i]
+        if i == 1 and (t + 1) % group == 0:
+            span = pl.ds(t + 1 - group, group)
+            for held, out in ((held2, out2), (held1, out1)):
+                copy = pltpu.make_async_copy(held.at[span], out.at[span], sems.at[len(copies)])
+                copy.start()
+                copies.append(copy)
+    for copy in copies:
+        copy.wait()
 
 
 PAIR_TAPS = ((1, 0), (2, 1), (None, 2), (0, None))
@@ -358,7 +413,6 @@
 def local_call(body, name, out, scratch=(), scalars=0, in_hbm=(), out_hbm=(), limit=24):
     def call(*args):
         vmem = pl.BlockSpec(memory_space=pltpu.VMEM)
-        plain = pl.BlockSpec()
         hbm = pl.BlockSpec(memory_space=pltpu.HBM)
         ins = [
             pl.BlockSpec(memory_space=pltpu.SMEM) if i < scalars else hbm if i in in_hbm else vmem
@@ -370,12 +424,14 @@
             else pltpu.with_memory_space_constraint(a, pltpu.HBM if i in in_hbm else pltpu.VMEM)
             for i, a in enumerate(args)
         ]
-        outs = [o if i in out_hbm else pltpu.VMEM(o.shape, o.dtype) for i, o in enumerate(out)]
+        outs = [
+            (pltpu.HBM if i in out_hbm else pltpu.VMEM)(o.shape, o.dtype) for i, o in enumerate(out)
+        ]
         return pl.pallas_call(
             body,
             out_shape=outs,
             in_specs=ins,
-            out_specs=[plain if i in out_hbm else vmem for i in range(len(out))],
+            out_specs=[hbm if i in out_hbm else vmem for i in range(len(out))],
             scratch_shapes=list(scratch),
             compiler_params=pltpu.CompilerParams(vmem_limit_bytes=limit << 20),
             name=name,
@@ -390,11 +446,12 @@
     part = functools.partial
     shape = jax.ShapeDtypeStruct
     levels = bit_levels(("gx", "gy"))
-    core, one, two = levels[:3]
+    core = levels[0]
     side = side_of(core).astype(jnp.int32).reshape(1)
+    odd_y = side_of(("gy", 1)).astype(jnp.int32).reshape(1)
     ex, ey, uy = cx + 2 * FIELD_HALO, cy + 2 * FIELD_HALO, cy + 2
     rows_y = cx * FIELD_HALO * kz + cx * 2 * kz + kz
-    last, first, tile, field, up = local_call(
+    inner, outer, tile, field, up = local_call(
         part(pack_y_body, cx, cy, kz),
         "pack_y",
         [shape((rows_y, LANES), BF)] * 2
@@ -402,9 +459,10 @@
         [pltpu.VMEM(basin_mask.shape, jnp.int32)]
         + [pltpu.VMEM((LANES, LANES), F32)] * 2
         + [pltpu.SemaphoreType.DMA((3,))],
-        in_hbm=(0, 1, 2),
-    )(volume, upstream, basin_mask)
-    left, right = exchange(last, first, "gy")
+        scalars=1,
+        in_hbm=(1, 2, 3),
+    )(odd_y, volume, upstream, basin_mask)
+    inner, outer = exchange(inner, outer, "gy")
     w1, w2, w3 = local_call(
         weights_body,
         "weights",
@@ -415,14 +473,16 @@
         ],
     )(w_first, w_second)
     rows_x = FIELD_HALO * ey * kz + uy * 2 * kz + 3 * kz
-    last, first = local_call(
-        part(pack_x_body, cx, cy, kz), "pack_x", [shape((rows_x, LANES), BF)] * 2
-    )(field, up, tile, left, right)
-    low, high = exchange(last, first, "gx")
+    inner, outer, left, right = local_call(
+        part(pack_x_body, cx, cy, kz),
+        "pack_x",
+        [shape((rows_x, LANES), BF)] * 2 + [shape((rows_y, LANES), BF)] * 2,
+        scalars=2,
+    )(side, odd_y, field, up, tile, inner, outer)
+    inner, outer = exchange(inner, outer, "gx")
     b1 = jnp.concatenate([b_first, b_first]).reshape(1, -1)
     b2 = jnp.concatenate([b_second, b_second]).reshape(1, -1)
-    cut = chan // 2
-    rows = cut + w_first.shape[1] // 2
+    rows = chan // 2 + w_first.shape[1] // 2
     pairs = (kz, 2 * chan)
     features, sent, kept = local_call(
         part(compute_body, cx, cy, kz),
@@ -432,7 +492,8 @@
             shape((taps, rows, chan), BF),
             shape((taps, rows, chan), F32),
         ],
-        [
+        [pltpu.VMEM((rows_x, LANES), BF)] * 2
+        + [
             pltpu.VMEM((ex, ey, kz, LANES), BF),
             pltpu.VMEM((ex, ey, kz, LANES), BF),
             pltpu.VMEM((cx + 4, cy + 4, *pairs), BF),
@@ -449,26 +510,22 @@
         ],
         scalars=1,
         limit=32,
-    )(side, field, up, tile, left, right, low, high, w1, b1, w2, b2, w3)
-    total = kept + swap(sent, core).astype(F32)
-    sent2, kept2 = halves(total[:, :cut], one)
-    sent1, kept1 = halves(total[:, cut:], two)
-    got2, got1 = lax.optimization_barrier((swap(sent2, one), swap(sent1, two)))
-    sent2, kept2 = halves(kept2 + got2.astype(F32), two)
-    sent1, kept1 = halves(kept1 + got1.astype(F32), one)
-    got2, got1 = lax.optimization_barrier((swap(sent2, two), swap(sent1, one)))
-    own2, own1 = summed_inner(kept2 + got2.astype(F32), kept1 + got1.astype(F32), levels[3:])
-    other2, other1 = lax.optimization_barrier((swap(own2, two), swap(own1, one)))
-    own2, own1 = joined(own2, other2, two), joined(own1, other1, one)
-    other2, other1 = lax.optimization_barrier((swap(own2, one), swap(own1, two)))
-    own2, own1 = joined(own2, other2, one), joined(own1, other1, two)
+    )(side, field, up, tile, left, right, inner, outer, w1, b1, w2, b2, w3)
+    total = kept.reshape(-1, chan) + swap(sent.reshape(-1, chan), core).astype(F32)
+    own = summed_everywhere(total, levels[1:])
+    other = [swap(part_of, core) for part_of in own]
     step_second, step_first = local_call(
         norm_body,
         "normalize",
         [shape(w_second.shape, F32), shape(w_first.shape, F32)],
+        [
+            pltpu.VMEM(w_second.shape, F32),
+            pltpu.VMEM(w_first.shape, F32),
+            pltpu.SemaphoreType.DMA((6,)),
+        ],
         scalars=1,
         out_hbm=(0, 1),
-    )(side, own2, swap(own2, core), own1, swap(own1, core))
+    )(side, *own, *other)
     return (features, step_first, step_second)
 
 

time: 84.6 us -> 78.8 us (0.931)
  waiting for transfers between devices: 36.7 us -> 29.4 us
  starting transfers between devices: 28.1 us -> 29.8 us
    ppermute x14, starting transfers between devices: 19.4 us -> 25.4 us  [swap(): lax.ppermute(part, axis, [(i, i ^ bit) for i in range(lax.axis_size(axis))])]
    ppermute x4, waiting for transfers between devices: 6.29 us -> 1.87 us  [the longest x2 1.87 us: exchange(): inner = lax.ppermute(inner, axis, [(i, i ^ 1) for i in range(count)])]
    ppermute x4, starting transfers between devices: 8.79 us -> 4.46 us  [the longest x2 3.13 us: exchange(): inner = lax.ppermute(inner, axis, [(i, i ^ 1) for i in range(count)])]
    ppermute x14, waiting for transfers between devices: 30.5 us -> 27.5 us  [swap(): lax.ppermute(part, axis, [(i, i ^ bit) for i in range(lax.axis_size(axis))])]
  transfers between devices with their start and end apart: 18 -> 18, of which waited for: 13 -> 15; matrix products, arithmetic and copies ran while one was open for 1% -> 1% of each run, Pallas kernels for 2% -> 2%
where the time goes in v5:
time: 78.8 us; the launch traced here: 78.6 us
  starting transfers between devices  29.8 us (38%)
  waiting for transfers between devices  29.4 us (37%)
  Pallas kernels  15.6 us (20%)
  local copies, waits for them, and re-layouts  1.95 us (2%)
  other arithmetic  1 us (1%)
  between operations  0.89 us (1%)
    ppermute x14, waiting for transfers between devices, swap(): lax.ppermute(part, axis, [(i, i ^ bit) for i in range(lax.axis_size(axis))])  27.5 us
    ppermute x14, starting transfers between devices, swap(): lax.ppermute(part, axis, [(i, i ^ bit) for i in range(lax.axis_size(axis))])  25.4 us
    pallas_call x5, Pallas kernels, call(): pl.pallas_call(body, out_shape=outs, in_specs=ins, out_specs=[hbm if i in...  15.6 us
    ppermute x2, starting transfers between devices, exchange(): inner = lax.ppermute(inner, axis, [(i, i ^ 1) for i in range(count)])  3.13 us
    ppermute x2, waiting for transfers between devices, exchange(): inner = lax.ppermute(inner, axis, [(i, i ^ 1) for i in range(count)])  1.87 us
    unnamed x9, local copies, waits for them, and re-layouts  1.72 us
  transfers between devices with their start and end apart: 18, of which 15 were waited for; matrix products, arithmetic and copies ran while one was open for 1% of the time, Pallas kernels for 2%

profile of v5, /device:TPU:0, one launch (start us, length us, event | category | flops | bytes accessed | tf_op | source)
XLA Modules:
  0.0 78.6 jit_solution(15619269523151114659)
XLA Ops:
  0.7 1.1 %pack_y.1 = (bf16[336,128]{1,0:T(8,128)(2,1)S(1)}, bf16[336,128]{1,0:T(8,128)(2,1)S(1)}, bf16[16,128]{1,0:T(8,128)(2,1)S(1)}, bf16[4,8,16,128]{3,2,1,0:T(8,128)(2,1)S(1)}, bf16[4,8,32,128]{3,2,1,0:T(8,128)(2,1)S(1)}) custom-call(s32[1]{0:T(128)} %bitcast.1.odd.odd_y, bf16[4,8,16,128]{3,2,1,0:T(8,128)(2,1)} %hfield.1, bf16[4,8,32,128]{3,2,1,0:T(8,128)(2,1)} %hup.1, ...), custom_call_target="tpu_custom_call" | custom-call | tf_op jit(solution)/shard_map/pack_y/pallas_call | solution.py:430
  1.8 3.1 %collective-permute-start = (bf16[336,128]{1,0:T(8,128)(2,1)S(1)}, bf16[336,128]{1,0:T(8,128)(2,1)S(1)}, u32[]{:S(2)}, u32[]{:S(2)}) collective-permute-start(bf16[336,128]{1,0:T(8,128)(2,1)S(1)} %get-tuple-element.31), channel_id=1, source_target_pairs={{0,1},{1,0},{2,3},{3,2},{4,5},{5,4},{6,7},{7,6},{8,9},{9,8},{10,11... | collective-permute-start | bytes 258056 | tf_op jit(solution)/shard_map/ppermute | solution.py:83
  4.9 0.7 collective-permute-start.1
  5.5 1.9 %collective-permute-done.inner_y = bf16[336,128]{1,0:T(8,128)(2,1)S(1)} collective-permute-done((bf16[336,128]{1,0:T(8,128)(2,1)S(1)}, bf16[336,128]{1,0:T(8,128)(2,1)S(1)}, u32[]{:S(2)}, u32[]{:S(2)}) %collective-permute-start) | collective-permute-done | bytes 86048 | tf_op jit(solution)/shard_map/ppermute | solution.py:83
  7.4 0.1 pack_x.1
  7.5 0.1 collective-permute-start.2
  7.6 0.7 collective-permute-start.3
  8.3 1.0 %copy-done.1 = bf16[27,64,128]{2,1,0:T(8,128)(2,1)S(1)} copy-done((bf16[27,64,128]{2,1,0:T(8,128)(2,1)S(1)}, bf16[27,64,128]{2,1,0:T(8,128)(2,1)}, u32[]{:S(2)}) %copy-start.1) | copy-done | bytes 442392
  9.3 1.5 %weights.1 = (bf16[2304,256]{1,0:T(8,128)(2,1)S(1)}, bf16[4608,256]{1,0:T(8,128)(2,1)S(1)}, bf16[4608,256]{1,0:T(8,128)(2,1)S(1)}) custom-call(bf16[27,64,128]{2,1,0:T(8,128)(2,1)S(1)} %copy-done.1, bf16[27,128,128]{2,1,0:T(8,128)(2,1)S(1)} %copy-done), custom_call_target="tpu_custom_call" | custom-call | tf_op jit(solution)/shard_map/weights/pallas_call | solution.py:430
  10.9 10.9 %compute.1 = (bf16[4,8,32,128]{3,2,1,0:T(8,128)(2,1)S(1)}, bf16[27,96,128]{2,1,0:T(8,128)(2,1)S(1)}, f32[27,96,128]{2,1,0:T(8,128)S(1)}) custom-call(s32[1]{0:T(128)} %bitcast.odd.side, bf16[4,8,16,128]{3,2,1,0:T(8,128)(2,1)S(1)} %get-tuple-element.28.field, bf16[4,8,32,128]{3,2,1,0:T(8,128)(2,1)S(1)} %get-tuple-element.29.up, ...), custom_call_target="tpu_custom_call" | custom-call | tf_op jit(solution)/shard_map/compute/pallas_call | solution.py:430
  21.8 5.0 %collective-permute-start.4 = (bf16[2592,128]{1,0:T(8,128)(2,1)S(1)}, bf16[2592,128]{1,0:T(8,128)(2,1)S(1)}, u32[]{:S(2)}, u32[]{:S(2)}) collective-permute-start(bf16[2592,128]{1,0:T(8,128)(2,1)S(1)} %bitcast.9), channel_id=1, source_target_pairs={{0,8},{8,0},{16,24},{24,16},{1,9},{9,1},{17,25},{25,17},{2,10},{10... | collective-permute-start | bytes 1990664 | tf_op jit(solution)/shard_map/ppermute | solution.py:29
  26.8 1.7 %collective-permute-done.4 = bf16[2592,128]{1,0:T(8,128)(2,1)S(1)} collective-permute-done((bf16[2592,128]{1,0:T(8,128)(2,1)S(1)}, bf16[2592,128]{1,0:T(8,128)(2,1)S(1)}, u32[]{:S(2)}, u32[]{:S(2)}) %collective-permute-start.4) | collective-permute-done | bytes 663584 | tf_op jit(solution)/shard_map/ppermute | solution.py:29
  28.5 0.1 bitcast_add_fusion
  28.6 0.1 fusion.5
  28.8 4.9 %collective-permute-start.6 = (bf16[648,128]{1,0:T(8,128)(2,1)S(1)}, bf16[648,128]{1,0:T(8,128)(2,1)S(1)}, u32[]{:S(2)}, u32[]{:S(2)}) collective-permute-start(bf16[648,128]{1,0:T(8,128)(2,1)S(1)} %dynamic-slice_convert_fusion), channel_id=1, source_target_pairs={{0,1},{1,0},{2,3},{3,2},{4,5},{5,4},{6,7},{7,6},{8,9},{9,8},{10,11... | collective-permute-start | bytes 497672 | tf_op jit(solution)/shard_map/ppermute | solution.py:29
  33.7 1.8 %collective-permute-start.5 = (bf16[648,128]{1,0:T(8,128)(2,1)S(1)}, bf16[648,128]{1,0:T(8,128)(2,1)S(1)}, u32[]{:S(2)}, u32[]{:S(2)}) collective-permute-start(bf16[648,128]{1,0:T(8,128)(2,1)S(1)} %dynamic-slice_convert_fusion.1), channel_id=1, source_target_pairs={{0,16},{8,24},{16,0},{24,8},{1,17},{9,25},{17,1},{25,9},{2,18},{10... | collective-permute-start | bytes 497672 | tf_op jit(solution)/shard_map/ppermute | solution.py:29
  35.5 2.9 %collective-permute-done.6 = bf16[648,128]{1,0:T(8,128)(2,1)S(1)} collective-permute-done((bf16[648,128]{1,0:T(8,128)(2,1)S(1)}, bf16[648,128]{1,0:T(8,128)(2,1)S(1)}, u32[]{:S(2)}, u32[]{:S(2)}) %collective-permute-start.6) | collective-permute-done | bytes 165920 | tf_op jit(solution)/shard_map/ppermute | solution.py:29
  38.5 1.5 %collective-permute-done.5 = bf16[648,128]{1,0:T(8,128)(2,1)S(1)} collective-permute-done((bf16[648,128]{1,0:T(8,128)(2,1)S(1)}, bf16[648,128]{1,0:T(8,128)(2,1)S(1)}, u32[]{:S(2)}, u32[]{:S(2)}) %collective-permute-start.5) | collective-permute-done | bytes 165920 | tf_op jit(solution)/shard_map/ppermute | solution.py:29
  40.1 1.6 %collective-permute-start.8 = (bf16[324,128]{1,0:T(8,128)(2,1)S(1)}, bf16[324,128]{1,0:T(8,128)(2,1)S(1)}, u32[]{:S(2)}, u32[]{:S(2)}) collective-permute-start(bf16[324,128]{1,0:T(8,128)(2,1)S(1)} %dynamic-slice_convert_fusion.2), channel_id=1, source_target_pairs={{0,16},{8,24},{16,0},{24,8},{1,17},{9,25},{17,1},{25,9},{2,18},{10... | collective-permute-start | bytes 248840 | tf_op jit(solution)/shard_map/ppermute | solution.py:29
  41.8 0.4 collective-permute-start.7
  42.1 2.5 %collective-permute-done.8 = bf16[324,128]{1,0:T(8,128)(2,1)S(1)} collective-permute-done((bf16[324,128]{1,0:T(8,128)(2,1)S(1)}, bf16[324,128]{1,0:T(8,128)(2,1)S(1)}, u32[]{:S(2)}, u32[]{:S(2)}) %collective-permute-start.8) | collective-permute-done | bytes 82976 | tf_op jit(solution)/shard_map/ppermute | solution.py:29
  44.6 1.7 %collective-permute-done.7 = bf16[324,128]{1,0:T(8,128)(2,1)S(1)} collective-permute-done((bf16[324,128]{1,0:T(8,128)(2,1)S(1)}, bf16[324,128]{1,0:T(8,128)(2,1)S(1)}, u32[]{:S(2)}, u32[]{:S(2)}) %collective-permute-start.7) | collective-permute-done | bytes 82976 | tf_op jit(solution)/shard_map/ppermute | solution.py:29
  46.3 0.2 fusion.1
  46.5 1.7 %collective-permute-start.9 = (bf16[324,128]{1,0:T(8,128)(2,1)S(1)}, bf16[324,128]{1,0:T(8,128)(2,1)S(1)}, u32[]{:S(2)}, u32[]{:S(2)}) collective-permute-start(bf16[324,128]{1,0:T(8,128)(2,1)S(1)} %fusion.1), channel_id=1, source_target_pairs={{0,2},{1,3},{2,0},{3,1},{4,6},{5,7},{6,4},{7,5},{8,10},{9,11},{10,... | collective-permute-start | bytes 248840 | tf_op jit(solution)/shard_map/ppermute | solution.py:29
  48.2 2.9 %collective-permute-done.9 = bf16[324,128]{1,0:T(8,128)(2,1)S(1)} collective-permute-done((bf16[324,128]{1,0:T(8,128)(2,1)S(1)}, bf16[324,128]{1,0:T(8,128)(2,1)S(1)}, u32[]{:S(2)}, u32[]{:S(2)}) %collective-permute-start.9) | collective-permute-done | bytes 82976 | tf_op jit(solution)/shard_map/ppermute | solution.py:29
  51.0 0.2 fusion.4
  51.2 3.2 %collective-permute-start.10 = (bf16[324,128]{1,0:T(8,128)(2,1)S(1)}, bf16[324,128]{1,0:T(8,128)(2,1)S(1)}, u32[]{:S(2)}, u32[]{:S(2)}) collective-permute-start(bf16[324,128]{1,0:T(8,128)(2,1)S(1)} %fusion.4), channel_id=1, source_target_pairs={{0,4},{1,5},{2,6},{3,7},{4,0},{5,1},{6,2},{7,3},{8,12},{9,13},{10,... | collective-permute-start | bytes 248840 | tf_op jit(solution)/shard_map/ppermute | solution.py:29
  54.4 2.5 %collective-permute-done.10 = bf16[324,128]{1,0:T(8,128)(2,1)S(1)} collective-permute-done((bf16[324,128]{1,0:T(8,128)(2,1)S(1)}, bf16[324,128]{1,0:T(8,128)(2,1)S(1)}, u32[]{:S(2)}, u32[]{:S(2)}) %collective-permute-start.10) | collective-permute-done | bytes 82976 | tf_op jit(solution)/shard_map/ppermute | solution.py:29
  57.0 1.5 %collective-permute-start.11 = (bf16[324,128]{1,0:T(8,128)(2,1)S(1)}, bf16[324,128]{1,0:T(8,128)(2,1)S(1)}, u32[]{:S(2)}, u32[]{:S(2)}) collective-permute-start(bf16[324,128]{1,0:T(8,128)(2,1)S(1)} %add_convert_fusion), channel_id=1, source_target_pairs={{0,2},{1,3},{2,0},{3,1},{4,6},{5,7},{6,4},{7,5},{8,10},{9,11},{10,... | collective-permute-start | bytes 248840 | tf_op jit(solution)/shard_map/ppermute | solution.py:29
  58.5 3.0 %collective-permute-done.11 = bf16[324,128]{1,0:T(8,128)(2,1)S(1)} collective-permute-done((bf16[324,128]{1,0:T(8,128)(2,1)S(1)}, bf16[324,128]{1,0:T(8,128)(2,1)S(1)}, u32[]{:S(2)}, u32[]{:S(2)}) %collective-permute-start.11) | collective-permute-done | bytes 82976 | tf_op jit(solution)/shard_map/ppermute | solution.py:29
  61.6 2.7 %collective-permute-start.12 = (bf16[324,128]{1,0:T(8,128)(2,1)S(1)}, bf16[324,128]{1,0:T(8,128)(2,1)S(1)}, u32[]{:S(2)}, u32[]{:S(2)}) collective-permute-start(bf16[324,128]{1,0:T(8,128)(2,1)S(1)} %get-tuple-element.56), channel_id=1, source_target_pairs={{0,1},{1,0},{2,3},{3,2},{4,5},{5,4},{6,7},{7,6},{8,9},{9,8},{10,11... | collective-permute-start | bytes 248840 | tf_op jit(solution)/shard_map/ppermute | solution.py:29
  64.3 0.7 collective-permute-start.13
  65.0 1.8 %collective-permute-done.12 = bf16[324,128]{1,0:T(8,128)(2,1)S(1)} collective-permute-done((bf16[324,128]{1,0:T(8,128)(2,1)S(1)}, bf16[324,128]{1,0:T(8,128)(2,1)S(1)}, u32[]{:S(2)}, u32[]{:S(2)}) %collective-permute-start.12) | collective-permute-done | bytes 82976 | tf_op jit(solution)/shard_map/ppermute | solution.py:29
  66.8 2.0 %collective-permute-done.13 = bf16[324,128]{1,0:T(8,128)(2,1)S(1)} collective-permute-done((bf16[324,128]{1,0:T(8,128)(2,1)S(1)}, bf16[324,128]{1,0:T(8,128)(2,1)S(1)}, u32[]{:S(2)}, u32[]{:S(2)}) %collective-permute-start.13) | collective-permute-done | bytes 82976 | tf_op jit(solution)/shard_map/ppermute | solution.py:29
  68.8 0.1 maximum_select_fusion.4
  68.8 0.1 collective-permute-start.15
  69.0 0.1 maximum_select_fusion.3
  69.1 1.2 %collective-permute-start.14 = (bf16[648,128]{1,0:T(8,128)(2,1)S(1)}, bf16[648,128]{1,0:T(8,128)(2,1)S(1)}, u32[]{:S(2)}, u32[]{:S(2)}) collective-permute-start(bf16[648,128]{1,0:T(8,128)(2,1)S(1)} %maximum_select_fusion.3), channel_id=1, source_target_pairs={{0,16},{8,24},{16,0},{24,8},{1,17},{9,25},{17,1},{25,9},{2,18},{10... | collective-permute-start | bytes 497672 | tf_op jit(solution)/shard_map/ppermute | solution.py:29
  70.3 4.0 %collective-permute-done.15 = bf16[648,128]{1,0:T(8,128)(2,1)S(1)} collective-permute-done((bf16[648,128]{1,0:T(8,128)(2,1)S(1)}, bf16[648,128]{1,0:T(8,128)(2,1)S(1)}, u32[]{:S(2)}, u32[]{:S(2)}) %collective-permute-start.15) | collective-permute-done | bytes 165920 | tf_op jit(solution)/shard_map/ppermute | solution.py:29
  74.3 0.2 collective-permute-done.14
  74.5 0.1 maximum_select_fusion.1.own_b
  74.6 0.1 collective-permute-start.17
  74.6 0.1 maximum_select_fusion.own_a
  74.7 0.6 collective-permute-start.16
  75.3 0.7 copy.10
  76.0 0.3 collective-permute-done.17.other_b
  76.3 0.5 collective-permute-done.16.other_a
  76.7 1.9 %normalize.1 = (f32[27,128,128]{2,1,0:T(8,128)}, f32[27,64,128]{2,1,0:T(8,128)}) custom-call(s32[1]{0:T(128)} %bitcast.odd.side, bf16[1296,128]{1,0:T(8,128)(2,1)S(1)} %maximum_select_fusion.own_a, bf16[1296,128]{1,0:T(8,128)(2,1)S(1)} %maximum_select_fusion.1.own_b, bf16[1296,128]{1,0:T(8,128)(2,1)S(1)} %collective-permute-done.16.other_a, ...), custom_call_target="tpu_custom_call" | custom-call | tf_op jit(solution)/shard_map/normalize/pallas_call | solution.py:430
  (22 shorter events, 0.4 us)
Async XLA Ops:
  0.6 7.6 %copy-start = (bf16[27,128,128]{2,1,0:T(8,128)(2,1)S(1)}, bf16[27,128,128]{2,1,0:T(8,128)(2,1)}, u32[]{:S(2)}) copy-start(bf16[27,128,128]{2,1,0:T(8,128)(2,1)} %second.1) | copy-start | bytes 2654212
  0.6 10.2 %copy-start.2 = (f32[128]{0:T(128)S(1)}, f32[128]{0:T(128)}, u32[]{:S(2)}) copy-start(f32[128]{0:T(128)} %param.10) | copy-start | bytes 1540
  0.7 10.2 %copy-start.3 = (f32[128]{0:T(128)S(1)}, f32[128]{0:T(128)}, u32[]{:S(2)}) copy-start(f32[128]{0:T(128)} %param.12) | copy-start | bytes 1540
  1.8 5.6 %collective-permute-start = (bf16[336,128]{1,0:T(8,128)(2,1)S(1)}, bf16[336,128]{1,0:T(8,128)(2,1)S(1)}, u32[]{:S(2)}, u32[]{:S(2)}) collective-permute-start(bf16[336,128]{1,0:T(8,128)(2,1)S(1)} %get-tuple-element.31), channel_id=1, source_target_pairs={{0,1},{1,0},{2,3},{3,2},{4,5},{5,4},{6,7},{7,6},{8,9},{9,8},{10,11... | collective-permute-start | bytes 258056 | tf_op jit(solution)/shard_map/ppermute | solution.py:83
  4.9 2.5 %collective-permute-start.1 = (bf16[336,128]{1,0:T(8,128)(2,1)S(1)}, bf16[336,128]{1,0:T(8,128)(2,1)S(1)}, u32[]{:S(2)}, u32[]{:S(2)}) collective-permute-start(bf16[336,128]{1,0:T(8,128)(2,1)S(1)} %get-tuple-element.32), channel_id=1, source_target_pairs={{1,2},{3,4},{5,6},{2,1},{4,3},{6,5},{9,10},{11,12},{13,14},{10,9},... | collective-permute-start | bytes 258056 | tf_op jit(solution)/shard_map/ppermute | solution.py:82
  7.5 3.4 %collective-permute-start.2 = (bf16[1040,128]{1,0:T(8,128)(2,1)S(1)}, bf16[1040,128]{1,0:T(8,128)(2,1)S(1)}, u32[]{:S(2)}, u32[]{:S(2)}) collective-permute-start(bf16[1040,128]{1,0:T(8,128)(2,1)S(1)} %get-tuple-element.35), channel_id=1, source_target_pairs={{0,8},{8,0},{16,24},{24,16},{1,9},{9,1},{17,25},{25,17},{2,10},{10... | collective-permute-start | bytes 798728 | tf_op jit(solution)/shard_map/ppermute | solution.py:83
  7.6 3.3 %collective-permute-start.3 = (bf16[1040,128]{1,0:T(8,128)(2,1)S(1)}, bf16[1040,128]{1,0:T(8,128)(2,1)S(1)}, u32[]{:S(2)}, u32[]{:S(2)}) collective-permute-start(bf16[1040,128]{1,0:T(8,128)(2,1)S(1)} %get-tuple-element.36), channel_id=1, source_target_pairs={{8,16},{16,8},{9,17},{17,9},{10,18},{18,10},{11,19},{19,11},{12,20... | collective-permute-start | bytes 798728 | tf_op jit(solution)/shard_map/ppermute | solution.py:82
  8.3 1.0 %copy-start.1 = (bf16[27,64,128]{2,1,0:T(8,128)(2,1)S(1)}, bf16[27,64,128]{2,1,0:T(8,128)(2,1)}, u32[]{:S(2)}) copy-start(bf16[27,64,128]{2,1,0:T(8,128)(2,1)} %first.1) | copy-start | bytes 1327108
  21.8 6.7 %collective-permute-start.4 = (bf16[2592,128]{1,0:T(8,128)(2,1)S(1)}, bf16[2592,128]{1,0:T(8,128)(2,1)S(1)}, u32[]{:S(2)}, u32[]{:S(2)}) collective-permute-start(bf16[2592,128]{1,0:T(8,128)(2,1)S(1)} %bitcast.9), channel_id=1, source_target_pairs={{0,8},{8,0},{16,24},{24,16},{1,9},{9,1},{17,25},{25,17},{2,10},{10... | collective-permute-start | bytes 1990664 | tf_op jit(solution)/shard_map/ppermute | solution.py:29
  28.8 9.7 %collective-permute-start.6 = (bf16[648,128]{1,0:T(8,128)(2,1)S(1)}, bf16[648,128]{1,0:T(8,128)(2,1)S(1)}, u32[]{:S(2)}, u32[]{:S(2)}) collective-permute-start(bf16[648,128]{1,0:T(8,128)(2,1)S(1)} %dynamic-slice_convert_fusion), channel_id=1, source_target_pairs={{0,1},{1,0},{2,3},{3,2},{4,5},{5,4},{6,7},{7,6},{8,9},{9,8},{10,11... | collective-permute-start | bytes 497672 | tf_op jit(solution)/shard_map/ppermute | solution.py:29
  33.7 6.3 %collective-permute-start.5 = (bf16[648,128]{1,0:T(8,128)(2,1)S(1)}, bf16[648,128]{1,0:T(8,128)(2,1)S(1)}, u32[]{:S(2)}, u32[]{:S(2)}) collective-permute-start(bf16[648,128]{1,0:T(8,128)(2,1)S(1)} %dynamic-slice_convert_fusion.1), channel_id=1, source_target_pairs={{0,16},{8,24},{16,0},{24,8},{1,17},{9,25},{17,1},{25,9},{2,18},{10... | collective-permute-start | bytes 497672 | tf_op jit(solution)/shard_map/ppermute | solution.py:29
  40.1 4.5 %collective-permute-start.8 = (bf16[324,128]{1,0:T(8,128)(2,1)S(1)}, bf16[324,128]{1,0:T(8,128)(2,1)S(1)}, u32[]{:S(2)}, u32[]{:S(2)}) collective-permute-start(bf16[324,128]{1,0:T(8,128)(2,1)S(1)} %dynamic-slice_convert_fusion.2), channel_id=1, source_target_pairs={{0,16},{8,24},{16,0},{24,8},{1,17},{9,25},{17,1},{25,9},{2,18},{10... | collective-permute-start | bytes 248840 | tf_op jit(solution)/shard_map/ppermute | solution.py:29
  41.8 4.5 %collective-permute-start.7 = (bf16[324,128]{1,0:T(8,128)(2,1)S(1)}, bf16[324,128]{1,0:T(8,128)(2,1)S(1)}, u32[]{:S(2)}, u32[]{:S(2)}) collective-permute-start(bf16[324,128]{1,0:T(8,128)(2,1)S(1)} %dynamic-slice_convert_fusion.3), channel_id=1, source_target_pairs={{0,1},{1,0},{2,3},{3,2},{4,5},{5,4},{6,7},{7,6},{8,9},{9,8},{10,11... | collective-permute-start | bytes 248840 | tf_op jit(solution)/shard_map/ppermute | solution.py:29
  46.5 4.5 %collective-permute-start.9 = (bf16[324,128]{1,0:T(8,128)(2,1)S(1)}, bf16[324,128]{1,0:T(8,128)(2,1)S(1)}, u32[]{:S(2)}, u32[]{:S(2)}) collective-permute-start(bf16[324,128]{1,0:T(8,128)(2,1)S(1)} %fusion.1), channel_id=1, source_target_pairs={{0,2},{1,3},{2,0},{3,1},{4,6},{5,7},{6,4},{7,5},{8,10},{9,11},{10,... | collective-permute-start | bytes 248840 | tf_op jit(solution)/shard_map/ppermute | solution.py:29
  51.2 5.7 %collective-permute-start.10 = (bf16[324,128]{1,0:T(8,128)(2,1)S(1)}, bf16[324,128]{1,0:T(8,128)(2,1)S(1)}, u32[]{:S(2)}, u32[]{:S(2)}) collective-permute-start(bf16[324,128]{1,0:T(8,128)(2,1)S(1)} %fusion.4), channel_id=1, source_target_pairs={{0,4},{1,5},{2,6},{3,7},{4,0},{5,1},{6,2},{7,3},{8,12},{9,13},{10,... | collective-permute-start | bytes 248840 | tf_op jit(solution)/shard_map/ppermute | solution.py:29
  57.0 4.5 %collective-permute-start.11 = (bf16[324,128]{1,0:T(8,128)(2,1)S(1)}, bf16[324,128]{1,0:T(8,128)(2,1)S(1)}, u32[]{:S(2)}, u32[]{:S(2)}) collective-permute-start(bf16[324,128]{1,0:T(8,128)(2,1)S(1)} %add_convert_fusion), channel_id=1, source_target_pairs={{0,2},{1,3},{2,0},{3,1},{4,6},{5,7},{6,4},{7,5},{8,10},{9,11},{10,... | collective-permute-start | bytes 248840 | tf_op jit(solution)/shard_map/ppermute | solution.py:29
  61.6 5.2 %collective-permute-start.12 = (bf16[324,128]{1,0:T(8,128)(2,1)S(1)}, bf16[324,128]{1,0:T(8,128)(2,1)S(1)}, u32[]{:S(2)}, u32[]{:S(2)}) collective-permute-start(bf16[324,128]{1,0:T(8,128)(2,1)S(1)} %get-tuple-element.56), channel_id=1, source_target_pairs={{0,1},{1,0},{2,3},{3,2},{4,5},{5,4},{6,7},{7,6},{8,9},{9,8},{10,11... | collective-permute-start | bytes 248840 | tf_op jit(solution)/shard_map/ppermute | solution.py:29
  64.3 4.5 %collective-permute-start.13 = (bf16[324,128]{1,0:T(8,128)(2,1)S(1)}, bf16[324,128]{1,0:T(8,128)(2,1)S(1)}, u32[]{:S(2)}, u32[]{:S(2)}) collective-permute-start(bf16[324,128]{1,0:T(8,128)(2,1)S(1)} %get-tuple-element.55), channel_id=1, source_target_pairs={{0,16},{8,24},{16,0},{24,8},{1,17},{9,25},{17,1},{25,9},{2,18},{10... | collective-permute-start | bytes 248840 | tf_op jit(solution)/shard_map/ppermute | solution.py:29
  68.8 5.4 %collective-permute-start.15 = (bf16[648,128]{1,0:T(8,128)(2,1)S(1)}, bf16[648,128]{1,0:T(8,128)(2,1)S(1)}, u32[]{:S(2)}, u32[]{:S(2)}) collective-permute-start(bf16[648,128]{1,0:T(8,128)(2,1)S(1)} %maximum_select_fusion.4), channel_id=1, source_target_pairs={{0,1},{1,0},{2,3},{3,2},{4,5},{5,4},{6,7},{7,6},{8,9},{9,8},{10,11... | collective-permute-start | bytes 497672 | tf_op jit(solution)/shard_map/ppermute | solution.py:29
  69.1 5.4 %collective-permute-start.14 = (bf16[648,128]{1,0:T(8,128)(2,1)S(1)}, bf16[648,128]{1,0:T(8,128)(2,1)S(1)}, u32[]{:S(2)}, u32[]{:S(2)}) collective-permute-start(bf16[648,128]{1,0:T(8,128)(2,1)S(1)} %maximum_select_fusion.3), channel_id=1, source_target_pairs={{0,16},{8,24},{16,0},{24,8},{1,17},{9,25},{17,1},{25,9},{2,18},{10... | collective-permute-start | bytes 497672 | tf_op jit(solution)/shard_map/ppermute | solution.py:29
  74.6 1.7 %collective-permute-start.17 = (bf16[1296,128]{1,0:T(8,128)(2,1)S(1)}, bf16[1296,128]{1,0:T(8,128)(2,1)S(1)}, u32[]{:S(2)}, u32[]{:S(2)}) collective-permute-start(bf16[1296,128]{1,0:T(8,128)(2,1)S(1)} %maximum_select_fusion.1.own_b), channel_id=1, source_target_pairs={{0,8},{8,0},{16,24},{24,16},{1,9},{9,1},{17,25},{25,17},{2,10},{10... | collective-permute-start | bytes 995336 | tf_op jit(solution)/shard_map/ppermute | solution.py:29
  74.7 2.0 %collective-permute-start.16 = (bf16[1296,128]{1,0:T(8,128)(2,1)S(1)}, bf16[1296,128]{1,0:T(8,128)(2,1)S(1)}, u32[]{:S(2)}, u32[]{:S(2)}) collective-permute-start(bf16[1296,128]{1,0:T(8,128)(2,1)S(1)} %maximum_select_fusion.own_a), channel_id=1, source_target_pairs={{0,8},{8,0},{16,24},{24,16},{1,9},{9,1},{17,25},{25,17},{2,10},{10... | collective-permute-start | bytes 995336 | tf_op jit(solution)/shard_map/ppermute | solution.py:29

commit v6 on v5

--- a/solution.py
+++ b/solution.py
@@ -89,12 +89,30 @@
     return jnp.where(odd, first, second), jnp.where(odd, second, first)
 
 
-def pack_y_body(
-    cx, cy, kz, odd, hfield, hup, hmask, inner, outer, tile, field, up, mask, square, deep, sems
+def put_rows(ref, parts):
+    row = 0
+    for part in parts:
+        rows = part.reshape(-1, LANES)
+        ref[row : row + rows.shape[0]] = rows
+        row += rows.shape[0]
+
+
+def pack_own_body(
+    cx, cy, kz, odd, odd_y, hfield, hup, hmask, hfirst, hsecond,
+    inner_y, outer_y, inner_x, outer_x, tile, field, up, w_first, w_second,
+    mask, square, deep, sems,
 ):
+    fh = FIELD_HALO
+    pairs = (
+        (hmask, mask),
+        (hfield, field),
+        (hup, up),
+        (hfirst, w_first),
+        (hsecond, w_second),
+    )
     copies = [
         pltpu.make_async_copy(source, target, sems.at[i])
-        for i, (source, target) in enumerate(((hmask, mask), (hfield, field), (hup, up)))
+        for i, (source, target) in enumerate(pairs)
     ]
     for copy in copies:
         copy.start()
@@ -108,37 +126,32 @@
     tile[...] = (at_even + pltpu.roll(at_odd, LANES // 2, 1)).astype(BF)
     copies[1].wait()
     copies[2].wait()
-    for ref, end in ((inner, 1 - odd[0]), (outer, odd[0])):
-        row = 0
-        for rows in (
-            field[:, pl.ds(end * (cy - FIELD_HALO), FIELD_HALO)].reshape(-1, LANES),
-            up[:, pl.ds(end * (cy - 1), 1)].reshape(-1, LANES),
-            tile[...],
-        ):
-            ref[row : row + rows.shape[0]] = rows
-            row += rows.shape[0]
-
-
-def pack_x_body(
-    cx, cy, kz, odd, odd_y, field, up, tile, inner_y, outer_y, inner, outer, left, right
-):
+    for ref, end in ((inner_y, 1 - odd_y[0]), (outer_y, odd_y[0])):
+        put_rows(
+            ref,
+            (field[:, pl.ds(end * (cy - fh), fh)], up[:, pl.ds(end * (cy - 1), 1)], tile[...]),
+        )
+    for ref, end in ((inner_x, 1 - odd[0]), (outer_x, odd[0])):
+        put_rows(
+            ref, (field[pl.ds(end * (cx - fh), fh)], up[pl.ds(end * (cx - 1), 1)], tile[...])
+        )
+    copies[3].wait()
+    copies[4].wait()
+
+
+def pack_corner_body(cx, cy, kz, odd, odd_y, inner_y, outer_y, inner, outer, left, right):
     left[...], right[...] = ends_of(odd_y[0] == 1, inner_y, outer_y)
     fh = FIELD_HALO
     nf, nu = cx * fh * kz, cx * 2 * kz
     for ref, end in ((inner, 1 - odd[0]), (outer, odd[0])):
-        at_field, at_up = end * (cx - fh), end * (cx - 1)
-        row = 0
         parts = []
         for r in range(fh):
-            at = pl.multiple_of((at_field + r) * fh * kz, kz)
-            parts += [left[pl.ds(at, fh * kz)], field[at_field + r], right[pl.ds(at, fh * kz)]]
-        at = pl.multiple_of(nf + at_up * 2 * kz, kz)
-        parts += [left[pl.ds(at, 2 * kz)], up[at_up], right[pl.ds(at, 2 * kz)]]
-        parts += [left[nf + nu :], tile[...], right[nf + nu :]]
-        for part in parts:
-            rows = part.reshape(-1, LANES)
-            ref[row : row + rows.shape[0]] = rows
-            row += rows.shape[0]
+            at = pl.multiple_of((end * (cx - fh) + r) * fh * kz, kz)
+            parts += [left[pl.ds(at, fh * kz)], right[pl.ds(at, fh * kz)]]
+        at = pl.multiple_of(nf + end * (cx - 1) * 2 * kz, kz)
+        parts += [left[pl.ds(at, 2 * kz)], right[pl.ds(at, 2 * kz)]]
+        parts += [left[nf + nu :], right[nf + nu :]]
+        put_rows(ref, parts)
 
 
 def side_pair(pair, kz, width):
@@ -163,22 +176,28 @@
 
 def compute_body(
     cx, cy, kz,
-    side, field, up, tile, left, right, inner, outer, w1, b1, w2, b2, w3,
+    side, field, up, tile, left, right, inner_x, outer_x, inner, outer, w1, b1, w2, b2, w3,
     features, sent, kept,
-    low, high, xp, xs, hp, hs, act, upf, outf, g2p, g2s, gate, g1, d2, d1,
+    low, high, low_ends, high_ends,
+    xp, xs, hp, hs, act, upf, outf, g2p, g2s, gate, g1, d2, d1,
 ):
-    low[...], high[...] = ends_of(side[0] == 1, inner, outer)
+    low[...], high[...] = ends_of(side[0] == 1, inner_x, outer_x)
+    low_ends[...], high_ends[...] = ends_of(side[0] == 1, inner, outer)
     fh, mh = FIELD_HALO, MASK_HALO
     ex, ey, uy = cx + 2 * fh, cy + 2 * fh, cy + 2
     nf, nu = cx * fh * kz, cx * 2 * kz
-    ne, nw = fh * ey * kz, uy * 2 * kz
+    nx, nw = fh * cy * kz, cy * 2 * kz
+    ne, nv = fh * 2 * fh * kz, 2 * kz
     xp[fh : fh + cx, fh : fh + cy] = field[...]
     xp[fh : fh + cx, 0:fh] = left[0:nf].reshape(cx, fh, kz, LANES)
     xp[fh : fh + cx, fh + cy :] = right[0:nf].reshape(cx, fh, kz, LANES)
-    xp[0:fh] = low[0:ne].reshape(fh, ey, kz, LANES)
-    xp[fh + cx :] = high[0:ne].reshape(fh, ey, kz, LANES)
-
-    def fill_side(i, carry):
+    for at, own, ends in ((0, low, low_ends), (fh + cx, high, high_ends)):
+        xp[at : at + fh, fh : fh + cy] = own[0:nx].reshape(fh, cy, kz, LANES)
+        block = ends[0:ne].reshape(fh, 2 * fh, kz, LANES)
+        xp[at : at + fh, 0:fh] = block[:, :fh]
+        xp[at : at + fh, fh + cy :] = block[:, fh:]
+
+    def fill_side(i):
         rows = xp[i].reshape(ey * kz, LANES).astype(F32)
         depth = lax.rem(lax.broadcasted_iota(jnp.int32, rows.shape, 0), kz)
         lane = lax.broadcasted_iota(jnp.int32, rows.shape, 1)
@@ -186,17 +205,18 @@
         below = jnp.where(depth == 0, 0.0, pltpu.roll(rows, 1, 0))
         both = jnp.where(lane < LANES // 2, above, below).astype(BF)
         xs[i] = both.reshape(ey, kz, LANES)
-        return carry
-
-    lax.fori_loop(0, ex, fill_side, 0)
+    for i in range(ex):
+        fill_side(i)
     span = uy * 2 * kz
 
     def put_up(x, y, cols, value):
         base = x * span + y * 2 * kz
         upf[base : base + cols * 2 * kz] = value.reshape(-1, LANES).astype(F32)
 
-    put_up(0, 0, uy, low[ne : ne + nw])
-    put_up(cx + 1, 0, uy, high[ne : ne + nw])
+    for x, own, ends in ((0, low, low_ends), (cx + 1, high, high_ends)):
+        put_up(x, 1, cy, own[nx : nx + nw])
+        put_up(x, 0, 1, ends[ne : ne + nv])
+        put_up(x, cy + 1, 1, ends[ne + nv : ne + 2 * nv])
     for x in range(cx):
         at = nf + x * 2 * kz
         put_up(x + 1, 0, 1, left[at : at + 2 * kz])
@@ -209,11 +229,13 @@
             value = jnp.broadcast_to(source[:, lane : lane + 1], (kz, LANES))
             act[x, y, :, parity * LANES : (parity + 1) * LANES] = value.astype(BF)
 
-    def three(ref, start):
-        return [ref[start + i * kz : start + (i + 1) * kz].astype(F32) for i in range(3)]
+    def three(ends, own):
+        at = ne + 2 * nv
+        rows = ends[at : at + kz], own[nx + nw :], ends[at + kz :]
+        return [part.astype(F32) for part in rows]
 
     rows_mid = [left[nf + nu :].astype(F32), tile[...].astype(F32), right[nf + nu :].astype(F32)]
-    rows_low, rows_high = three(low, ne + nw), three(high, ne + nw)
+    rows_low, rows_high = three(low_ends, low), three(high_ends, high)
     for x in range(cx + 2 * mh):
         if x < mh:
             sources, sx = rows_low, cx - mh + x
@@ -227,13 +249,16 @@
             put_mask(sources[0], sx, cy - mh + j, x, j)
             put_mask(sources[2], sx, j, x, mh + cy + j)
 
+    bias1 = jnp.concatenate([b1[...], b1[...]], axis=1)
+    bias2 = jnp.concatenate([b2[...], b2[...]], axis=1)
+
     hx, hy = cx + 4, cy + 4
-    step = 2
-
-    def first(i, carry):
+    step = 1
+
+    def first(i):
         at = i * step
         window = taps_of(xp, xs, at, step, hy)
-        z = jnp.dot(window, w1[...], preferred_element_type=F32) + b1[...]
+        z = jnp.dot(window, w1[...], preferred_element_type=F32) + bias1
         s = jax.nn.sigmoid(z)
         m = act[pl.ds(at, step)].reshape(step * hy * kz, 2 * LANES).astype(F32)
         h = z * s * m
@@ -242,24 +267,22 @@
         both = jnp.concatenate([above, below], axis=1).astype(BF)
         hs[pl.ds(at, step)] = both.reshape(step, hy, kz, 2 * LANES)
 
-        @pl.when(jnp.logical_and(i >= 2 // step, i < (2 + cx) // step))
-        def _():
+        if 2 // step <= i < (2 + cx) // step:
             factor = m * s * (1.0 + z * (1.0 - s))
             factor = factor.reshape(step, hy, kz, 2 * LANES)[:, 2 : 2 + cy]
             gate[pl.ds(at - 2, step)] = factor
 
-        return carry
-
-    lax.fori_loop(0, hx // step, first, 0)
-
-    def second(i, carry):
+    for i in range(hx // step):
+        first(i)
+
+    def second(i):
         at = i * step
         window = taps_of(hp, hs, at, step, uy)
-        z = jnp.dot(window, w2[...], preferred_element_type=F32) + b2[...]
+        z = jnp.dot(window, w2[...], preferred_element_type=F32) + bias2
         s = jax.nn.sigmoid(z)
         m = act[pl.ds(at + 1, step), 1 : 1 + uy].reshape(-1, 2 * LANES).astype(F32)
         rows = step * uy * kz
-        base = pl.multiple_of(at * span, 8)
+        base = at * span
         u = jnp.concatenate(
             [upf[pl.ds(base, rows, stride=2), :], upf[pl.ds(base + 1, rows, stride=2), :]], axis=1
         )
@@ -272,9 +295,8 @@
         out = z * s * m
         outf[pl.ds(base, rows, stride=2), :] = out[:, :LANES]
         outf[pl.ds(base + 1, rows, stride=2), :] = out[:, LANES:]
-        return carry
-
-    lax.fori_loop(0, (cx + 2) // step, second, 0)
+    for i in range((cx + 2) // step):
+        second(i)
     for x in range(cx):
         base = (x + 1) * span + 2 * kz
         rows = outf[base : base + cy * 2 * kz].astype(BF)
@@ -302,15 +324,14 @@
 
     rows = step * cy * kz
 
-    def grad(i, carry):
+    def grad(i):
         at = i * step
         window = taps_of(g2p, g2s, at, step, cy)
         e = jnp.dot(window, w3[...], preferred_element_type=F32)
         g = e * gate[pl.ds(at, step)].reshape(rows, 2 * LANES)
-        g1[pl.ds(pl.multiple_of(i * rows, rows), rows)] = g.astype(BF)
-        return carry
-
-    lax.fori_loop(0, cx // step, grad, 0)
+        g1[i * rows : (i + 1) * rows] = g.astype(BF)
+    for i in range(cx // step):
+        grad(i)
     right_side = g1[...]
     cells = cx * cy * kz
     half = LANES // 2
@@ -389,7 +410,7 @@
 PAIR_TAPS = ((1, 0), (2, 1), (None, 2), (0, None))
 
 
-def weights_body(first, second, w1, w2, w3):
+def weights_body(first, second, _, w1, w2, w3):
     taps = second.shape[0]
 
     def group(g, carry):
@@ -451,18 +472,31 @@
     odd_y = side_of(("gy", 1)).astype(jnp.int32).reshape(1)
     ex, ey, uy = cx + 2 * FIELD_HALO, cy + 2 * FIELD_HALO, cy + 2
     rows_y = cx * FIELD_HALO * kz + cx * 2 * kz + kz
-    inner, outer, tile, field, up = local_call(
-        part(pack_y_body, cx, cy, kz),
-        "pack_y",
+    rows_x = FIELD_HALO * cy * kz + cy * 2 * kz + kz
+    rows_e = FIELD_HALO * 2 * FIELD_HALO * kz + 2 * 2 * kz + 2 * kz
+    inner_y, outer_y, inner_x, outer_x, tile, field, up, w_one, w_two = local_call(
+        part(pack_own_body, cx, cy, kz),
+        "pack_own",
         [shape((rows_y, LANES), BF)] * 2
-        + [shape((kz, LANES), BF), shape(volume.shape, BF), shape(upstream.shape, BF)],
+        + [shape((rows_x, LANES), BF)] * 2
+        + [shape((kz, LANES), BF)]
+        + [shape(a.shape, BF) for a in (volume, upstream, w_first, w_second)],
         [pltpu.VMEM(basin_mask.shape, jnp.int32)]
         + [pltpu.VMEM((LANES, LANES), F32)] * 2
-        + [pltpu.SemaphoreType.DMA((3,))],
-        scalars=1,
-        in_hbm=(1, 2, 3),
-    )(odd_y, volume, upstream, basin_mask)
-    inner, outer = exchange(inner, outer, "gy")
+        + [pltpu.SemaphoreType.DMA((5,))],
+        scalars=2,
+        in_hbm=(2, 3, 4, 5, 6),
+    )(side, odd_y, volume, upstream, basin_mask, w_first, w_second)
+    inner_y, outer_y = exchange(inner_y, outer_y, "gy")
+    inner_x, outer_x = exchange(inner_x, outer_x, "gx")
+    inner, outer, left, right = local_call(
+        part(pack_corner_body, cx, cy, kz),
+        "pack_corner",
+        [shape((rows_e, LANES), BF)] * 2 + [shape((rows_y, LANES), BF)] * 2,
+        scalars=2,
+    )(side, odd_y, inner_y, outer_y)
+    corner = inner
+    inner, outer = exchange(inner, outer, "gx")
     w1, w2, w3 = local_call(
         weights_body,
         "weights",
@@ -471,17 +505,7 @@
             shape((4 * taps // 3 * chan, 2 * chan), BF),
             shape((4 * taps // 3 * chan, 2 * chan), BF),
         ],
-    )(w_first, w_second)
-    rows_x = FIELD_HALO * ey * kz + uy * 2 * kz + 3 * kz
-    inner, outer, left, right = local_call(
-        part(pack_x_body, cx, cy, kz),
-        "pack_x",
-        [shape((rows_x, LANES), BF)] * 2 + [shape((rows_y, LANES), BF)] * 2,
-        scalars=2,
-    )(side, odd_y, field, up, tile, inner, outer)
-    inner, outer = exchange(inner, outer, "gx")
-    b1 = jnp.concatenate([b_first, b_first]).reshape(1, -1)
-    b2 = jnp.concatenate([b_second, b_second]).reshape(1, -1)
+    )(w_one, w_two, corner)
     rows = chan // 2 + w_first.shape[1] // 2
     pairs = (kz, 2 * chan)
     features, sent, kept = local_call(
@@ -493,6 +517,7 @@
             shape((taps, rows, chan), F32),
         ],
         [pltpu.VMEM((rows_x, LANES), BF)] * 2
+        + [pltpu.VMEM((rows_e, LANES), BF)] * 2
         + [
             pltpu.VMEM((ex, ey, kz, LANES), BF),
             pltpu.VMEM((ex, ey, kz, LANES), BF),
@@ -510,7 +535,7 @@
         ],
         scalars=1,
         limit=32,
-    )(side, field, up, tile, left, right, inner, outer, w1, b1, w2, b2, w3)
+    )(side, field, up, tile, left, right, inner_x, outer_x, inner, outer, w1, b_first.reshape(1, -1), w2, b_second.reshape(1, -1), w3)
     total = kept.reshape(-1, chan) + swap(sent.reshape(-1, chan), core).astype(F32)
     own = summed_everywhere(total, levels[1:])
     other = [swap(part_of, core) for part_of in own]

time: 78.8 us -> 74.9 us (0.951)
  Pallas kernels: 15.6 us -> 13.4 us
  local copies, waits for them, and re-layouts: 1.95 us -> 0.93 us
    ppermute x14, starting transfers between devices: 25.4 us -> 22.2 us  [swap(): lax.ppermute(part, axis, [(i, i ^ bit) for i in range(lax.axis_size(axis))])]
    pallas_call x5, Pallas kernels: 15.6 us -> 13.4 us  [call(): pl.pallas_call(body, out_shape=outs, in_specs=ins, out_specs=[hbm if i in...]
    ppermute x2 -> x3, starting transfers between devices: 3.13 us -> 4.95 us  [exchange(): inner = lax.ppermute(inner, axis, [(i, i ^ 1) for i in range(count)])]
    unnamed x9 -> x5, local copies, waits for them, and re-layouts: 1.72 us -> 0.71 us
    ppermute x2 -> x3, waiting for transfers between devices: 1.87 us -> 1.12 us  [exchange(): inner = lax.ppermute(inner, axis, [(i, i ^ 1) for i in range(count)])]
    ppermute x2 -> x3, starting transfers between devices: 1.33 us -> 1.98 us  [exchange(): outer = lax.ppermute(outer, axis, pairs + [(b, a) for a, b in pairs])]
  transfers between devices with their start and end apart: 18 -> 20, of which waited for: 15 -> 15; matrix products, arithmetic and copies ran while one was open for 1% -> 1% of each run, Pallas kernels for 2% -> 2%
where the time goes in v6:
time: 74.9 us; the launch traced here: 74.7 us
  waiting for transfers between devices  29.4 us (39%)
  starting transfers between devices  29.1 us (39%)
  Pallas kernels  13.4 us (18%)
  other arithmetic  0.97 us (1%)
  local copies, waits for them, and re-layouts  0.93 us (1%)
  between operations  0.87 us (1%)
    ppermute x14, waiting for transfers between devices, swap(): lax.ppermute(part, axis, [(i, i ^ bit) for i in range(lax.axis_size(axis))])  28.3 us
    ppermute x14, starting transfers between devices, swap(): lax.ppermute(part, axis, [(i, i ^ bit) for i in range(lax.axis_size(axis))])  22.2 us
    pallas_call x5, Pallas kernels, call(): pl.pallas_call(body, out_shape=outs, in_specs=ins, out_specs=[hbm if i in...  13.4 us
    ppermute x3, starting transfers between devices, exchange(): inner = lax.ppermute(inner, axis, [(i, i ^ 1) for i in range(count)])  4.95 us
    ppermute x3, starting transfers between devices, exchange(): outer = lax.ppermute(outer, axis, pairs + [(b, a) for a, b in pairs])  1.98 us
  transfers between devices with their start and end apart: 20, of which 15 were waited for; matrix products, arithmetic and copies ran while one was open for 1% of the time, Pallas kernels for 2%

profile of v6, /device:TPU:0, one launch (start us, length us, event | category | flops | bytes accessed | tf_op | source)
XLA Modules:
  0.0 74.7 jit_solution(18432353801681226519)
XLA Ops:
  0.7 1.5 %pack_own.1 = (bf16[336,128]{1,0:T(8,128)(2,1)S(1)}, bf16[336,128]{1,0:T(8,128)(2,1)S(1)}, bf16[656,128]{1,0:T(8,128)(2,1)S(1)}, bf16[656,128]{1,0:T(8,128)(2,1)...) custom-call(s32[1]{0:T(128)} %bitcast.odd.side, ...), custom_call_target="tpu_custom_call" | custom-call | tf_op jit(solution)/shard_map/pack_own/pallas_call | solution.py:451
  2.2 3.1 %collective-permute-start = (bf16[336,128]{1,0:T(8,128)(2,1)S(1)}, bf16[336,128]{1,0:T(8,128)(2,1)S(1)}, u32[]{:S(2)}, u32[]{:S(2)}) collective-permute-start(bf16[336,128]{1,0:T(8,128)(2,1)S(1)} %get-tuple-element.35), channel_id=1, source_target_pairs={{0,1},{1,0},{2,3},{3,2},{4,5},{5,4},{6,7},{7,6},{8,9},{9,8},{10,11... | collective-permute-start | bytes 258056 | tf_op jit(solution)/shard_map/ppermute | solution.py:83
  5.3 0.7 collective-permute-start.1
  5.9 0.1 collective-permute-start.2
  6.0 0.7 collective-permute-start.3
  6.7 1.1 %collective-permute-done.inner_y = bf16[336,128]{1,0:T(8,128)(2,1)S(1)} collective-permute-done((bf16[336,128]{1,0:T(8,128)(2,1)S(1)}, bf16[336,128]{1,0:T(8,128)(2,1)S(1)}, u32[]{:S(2)}, u32[]{:S(2)}) %collective-permute-start) | collective-permute-done | bytes 86048 | tf_op jit(solution)/shard_map/ppermute | solution.py:83
  7.8 1.8 %collective-permute-start.4 = (bf16[384,128]{1,0:T(8,128)(2,1)S(1)}, bf16[384,128]{1,0:T(8,128)(2,1)S(1)}, u32[]{:S(2)}, u32[]{:S(2)}) collective-permute-start(bf16[384,128]{1,0:T(8,128)(2,1)S(1)} %get-tuple-element.41._), channel_id=1, source_target_pairs={{0,8},{8,0},{16,24},{24,16},{1,9},{9,1},{17,25},{25,17},{2,10},{10... | collective-permute-start | bytes 294920 | tf_op jit(solution)/shard_map/ppermute | solution.py:83
  9.7 0.7 collective-permute-start.5
  10.3 1.5 %weights.1 = (bf16[2304,256]{1,0:T(8,128)(2,1)S(1)}, bf16[4608,256]{1,0:T(8,128)(2,1)S(1)}, bf16[4608,256]{1,0:T(8,128)(2,1)S(1)}) custom-call(bf16[27,64,128]{2,1,0:T(8,128)(2,1)S(1)} %get-tuple-element.43.first, bf16[27,128,128]{2,1,0:T(8,128)(2,1)S(1)} %get-tuple-element.44.second, bf16[384,128]{1,0:T(8,128)(2,1)S(1)} %get-tuple-element.41._), custom_call_target="tpu_custom_call" | custom-call | tf_op jit(solution)/shard_map/weights/pallas_call | solution.py:451
  11.9 8.4 %compute.1 = (bf16[4,8,32,128]{3,2,1,0:T(8,128)(2,1)S(1)}, bf16[27,96,128]{2,1,0:T(8,128)(2,1)S(1)}, f32[27,96,128]{2,1,0:T(8,128)S(1)}) custom-call(s32[1]{0:T(128)} %bitcast.odd.side, bf16[4,8,16,128]{3,2,1,0:T(8,128)(2,1)S(1)} %get-tuple-element.32.field, bf16[4,8,32,128]{3,2,1,0:T(8,128)(2,1)S(1)} %get-tuple-element.33.up, ...), custom_call_target="tpu_custom_call" | custom-call | tf_op jit(solution)/shard_map/compute/pallas_call | solution.py:451
  20.4 3.7 %collective-permute-start.6 = (bf16[2592,128]{1,0:T(8,128)(2,1)S(1)}, bf16[2592,128]{1,0:T(8,128)(2,1)S(1)}, u32[]{:S(2)}, u32[]{:S(2)}) collective-permute-start(bf16[2592,128]{1,0:T(8,128)(2,1)S(1)} %bitcast.9), channel_id=1, source_target_pairs={{0,8},{8,0},{16,24},{24,16},{1,9},{9,1},{17,25},{25,17},{2,10},{10... | collective-permute-start | bytes 1990664 | tf_op jit(solution)/shard_map/ppermute | solution.py:29
  24.1 1.7 %collective-permute-done.6 = bf16[2592,128]{1,0:T(8,128)(2,1)S(1)} collective-permute-done((bf16[2592,128]{1,0:T(8,128)(2,1)S(1)}, bf16[2592,128]{1,0:T(8,128)(2,1)S(1)}, u32[]{:S(2)}, u32[]{:S(2)}) %collective-permute-start.6) | collective-permute-done | bytes 663584 | tf_op jit(solution)/shard_map/ppermute | solution.py:29
  25.9 0.1 bitcast_add_fusion
  26.0 0.1 fusion.5
  26.1 4.3 %collective-permute-start.8 = (bf16[648,128]{1,0:T(8,128)(2,1)S(1)}, bf16[648,128]{1,0:T(8,128)(2,1)S(1)}, u32[]{:S(2)}, u32[]{:S(2)}) collective-permute-start(bf16[648,128]{1,0:T(8,128)(2,1)S(1)} %dynamic-slice_convert_fusion), channel_id=1, source_target_pairs={{0,1},{1,0},{2,3},{3,2},{4,5},{5,4},{6,7},{7,6},{8,9},{9,8},{10,11... | collective-permute-start | bytes 497672 | tf_op jit(solution)/shard_map/ppermute | solution.py:29
  30.5 1.1 %collective-permute-start.7 = (bf16[648,128]{1,0:T(8,128)(2,1)S(1)}, bf16[648,128]{1,0:T(8,128)(2,1)S(1)}, u32[]{:S(2)}, u32[]{:S(2)}) collective-permute-start(bf16[648,128]{1,0:T(8,128)(2,1)S(1)} %dynamic-slice_convert_fusion.1), channel_id=1, source_target_pairs={{0,16},{8,24},{16,0},{24,8},{1,17},{9,25},{17,1},{25,9},{2,18},{10... | collective-permute-start | bytes 497672 | tf_op jit(solution)/shard_map/ppermute | solution.py:29
  31.6 3.6 %collective-permute-done.8 = bf16[648,128]{1,0:T(8,128)(2,1)S(1)} collective-permute-done((bf16[648,128]{1,0:T(8,128)(2,1)S(1)}, bf16[648,128]{1,0:T(8,128)(2,1)S(1)}, u32[]{:S(2)}, u32[]{:S(2)}) %collective-permute-start.8) | collective-permute-done | bytes 165920 | tf_op jit(solution)/shard_map/ppermute | solution.py:29
  35.2 1.5 %collective-permute-done.7 = bf16[648,128]{1,0:T(8,128)(2,1)S(1)} collective-permute-done((bf16[648,128]{1,0:T(8,128)(2,1)S(1)}, bf16[648,128]{1,0:T(8,128)(2,1)S(1)}, u32[]{:S(2)}, u32[]{:S(2)}) %collective-permute-start.7) | collective-permute-done | bytes 165920 | tf_op jit(solution)/shard_map/ppermute | solution.py:29
  36.9 0.9 %collective-permute-start.10 = (bf16[324,128]{1,0:T(8,128)(2,1)S(1)}, bf16[324,128]{1,0:T(8,128)(2,1)S(1)}, u32[]{:S(2)}, u32[]{:S(2)}) collective-permute-start(bf16[324,128]{1,0:T(8,128)(2,1)S(1)} %dynamic-slice_convert_fusion.2), channel_id=1, source_target_pairs={{0,16},{8,24},{16,0},{24,8},{1,17},{9,25},{17,1},{25,9},{2,18},{10... | collective-permute-start | bytes 248840 | tf_op jit(solution)/shard_map/ppermute | solution.py:29
  37.8 0.4 collective-permute-start.9
  38.2 3.2 %collective-permute-done.10 = bf16[324,128]{1,0:T(8,128)(2,1)S(1)} collective-permute-done((bf16[324,128]{1,0:T(8,128)(2,1)S(1)}, bf16[324,128]{1,0:T(8,128)(2,1)S(1)}, u32[]{:S(2)}, u32[]{:S(2)}) %collective-permute-start.10) | collective-permute-done | bytes 82976 | tf_op jit(solution)/shard_map/ppermute | solution.py:29
  41.4 1.0 %collective-permute-done.9 = bf16[324,128]{1,0:T(8,128)(2,1)S(1)} collective-permute-done((bf16[324,128]{1,0:T(8,128)(2,1)S(1)}, bf16[324,128]{1,0:T(8,128)(2,1)S(1)}, u32[]{:S(2)}, u32[]{:S(2)}) %collective-permute-start.9) | collective-permute-done | bytes 82976 | tf_op jit(solution)/shard_map/ppermute | solution.py:29
  42.4 0.2 fusion.1
  42.6 1.6 %collective-permute-start.11 = (bf16[324,128]{1,0:T(8,128)(2,1)S(1)}, bf16[324,128]{1,0:T(8,128)(2,1)S(1)}, u32[]{:S(2)}, u32[]{:S(2)}) collective-permute-start(bf16[324,128]{1,0:T(8,128)(2,1)S(1)} %fusion.1), channel_id=1, source_target_pairs={{0,2},{1,3},{2,0},{3,1},{4,6},{5,7},{6,4},{7,5},{8,10},{9,11},{10,... | collective-permute-start | bytes 248840 | tf_op jit(solution)/shard_map/ppermute | solution.py:29
  44.2 2.9 %collective-permute-done.11 = bf16[324,128]{1,0:T(8,128)(2,1)S(1)} collective-permute-done((bf16[324,128]{1,0:T(8,128)(2,1)S(1)}, bf16[324,128]{1,0:T(8,128)(2,1)S(1)}, u32[]{:S(2)}, u32[]{:S(2)}) %collective-permute-start.11) | collective-permute-done | bytes 82976 | tf_op jit(solution)/shard_map/ppermute | solution.py:29
  47.1 0.2 fusion.4
  47.3 3.2 %collective-permute-start.12 = (bf16[324,128]{1,0:T(8,128)(2,1)S(1)}, bf16[324,128]{1,0:T(8,128)(2,1)S(1)}, u32[]{:S(2)}, u32[]{:S(2)}) collective-permute-start(bf16[324,128]{1,0:T(8,128)(2,1)S(1)} %fusion.4), channel_id=1, source_target_pairs={{0,4},{1,5},{2,6},{3,7},{4,0},{5,1},{6,2},{7,3},{8,12},{9,13},{10,... | collective-permute-start | bytes 248840 | tf_op jit(solution)/shard_map/ppermute | solution.py:29
  50.5 2.5 %collective-permute-done.12 = bf16[324,128]{1,0:T(8,128)(2,1)S(1)} collective-permute-done((bf16[324,128]{1,0:T(8,128)(2,1)S(1)}, bf16[324,128]{1,0:T(8,128)(2,1)S(1)}, u32[]{:S(2)}, u32[]{:S(2)}) %collective-permute-start.12) | collective-permute-done | bytes 82976 | tf_op jit(solution)/shard_map/ppermute | solution.py:29
  53.0 1.5 %collective-permute-start.13 = (bf16[324,128]{1,0:T(8,128)(2,1)S(1)}, bf16[324,128]{1,0:T(8,128)(2,1)S(1)}, u32[]{:S(2)}, u32[]{:S(2)}) collective-permute-start(bf16[324,128]{1,0:T(8,128)(2,1)S(1)} %add_convert_fusion), channel_id=1, source_target_pairs={{0,2},{1,3},{2,0},{3,1},{4,6},{5,7},{6,4},{7,5},{8,10},{9,11},{10,... | collective-permute-start | bytes 248840 | tf_op jit(solution)/shard_map/ppermute | solution.py:29
  54.6 3.0 %collective-permute-done.13 = bf16[324,128]{1,0:T(8,128)(2,1)S(1)} collective-permute-done((bf16[324,128]{1,0:T(8,128)(2,1)S(1)}, bf16[324,128]{1,0:T(8,128)(2,1)S(1)}, u32[]{:S(2)}, u32[]{:S(2)}) %collective-permute-start.13) | collective-permute-done | bytes 82976 | tf_op jit(solution)/shard_map/ppermute | solution.py:29
  57.7 2.7 %collective-permute-start.14 = (bf16[324,128]{1,0:T(8,128)(2,1)S(1)}, bf16[324,128]{1,0:T(8,128)(2,1)S(1)}, u32[]{:S(2)}, u32[]{:S(2)}) collective-permute-start(bf16[324,128]{1,0:T(8,128)(2,1)S(1)} %get-tuple-element.64), channel_id=1, source_target_pairs={{0,1},{1,0},{2,3},{3,2},{4,5},{5,4},{6,7},{7,6},{8,9},{9,8},{10,11... | collective-permute-start | bytes 248840 | tf_op jit(solution)/shard_map/ppermute | solution.py:29
  60.4 0.6 collective-permute-start.15
  61.0 1.8 %collective-permute-done.14 = bf16[324,128]{1,0:T(8,128)(2,1)S(1)} collective-permute-done((bf16[324,128]{1,0:T(8,128)(2,1)S(1)}, bf16[324,128]{1,0:T(8,128)(2,1)S(1)}, u32[]{:S(2)}, u32[]{:S(2)}) %collective-permute-start.14) | collective-permute-done | bytes 82976 | tf_op jit(solution)/shard_map/ppermute | solution.py:29
  62.8 2.0 %collective-permute-done.15 = bf16[324,128]{1,0:T(8,128)(2,1)S(1)} collective-permute-done((bf16[324,128]{1,0:T(8,128)(2,1)S(1)}, bf16[324,128]{1,0:T(8,128)(2,1)S(1)}, u32[]{:S(2)}, u32[]{:S(2)}) %collective-permute-start.15) | collective-permute-done | bytes 82976 | tf_op jit(solution)/shard_map/ppermute | solution.py:29
  64.9 0.1 maximum_select_fusion.4
  64.9 0.1 collective-permute-start.17
  65.1 0.1 maximum_select_fusion.3
  65.1 1.2 %collective-permute-start.16 = (bf16[648,128]{1,0:T(8,128)(2,1)S(1)}, bf16[648,128]{1,0:T(8,128)(2,1)S(1)}, u32[]{:S(2)}, u32[]{:S(2)}) collective-permute-start(bf16[648,128]{1,0:T(8,128)(2,1)S(1)} %maximum_select_fusion.3), channel_id=1, source_target_pairs={{0,16},{8,24},{16,0},{24,8},{1,17},{9,25},{17,1},{25,9},{2,18},{10... | collective-permute-start | bytes 497672 | tf_op jit(solution)/shard_map/ppermute | solution.py:29
  66.4 4.0 %collective-permute-done.17 = bf16[648,128]{1,0:T(8,128)(2,1)S(1)} collective-permute-done((bf16[648,128]{1,0:T(8,128)(2,1)S(1)}, bf16[648,128]{1,0:T(8,128)(2,1)S(1)}, u32[]{:S(2)}, u32[]{:S(2)}) %collective-permute-start.17) | collective-permute-done | bytes 165920 | tf_op jit(solution)/shard_map/ppermute | solution.py:29
  70.3 0.2 collective-permute-done.16
  70.5 0.1 maximum_select_fusion.1.own_b
  70.6 0.1 collective-permute-start.19
  70.7 0.1 maximum_select_fusion.own_a
  70.8 0.6 collective-permute-start.18
  71.4 0.7 copy.10
  72.1 0.3 collective-permute-done.19.other_b
  72.3 0.5 collective-permute-done.18.other_a
  72.8 1.9 %normalize.1 = (f32[27,128,128]{2,1,0:T(8,128)}, f32[27,64,128]{2,1,0:T(8,128)}) custom-call(s32[1]{0:T(128)} %bitcast.odd.side, bf16[1296,128]{1,0:T(8,128)(2,1)S(1)} %maximum_select_fusion.own_a, bf16[1296,128]{1,0:T(8,128)(2,1)S(1)} %maximum_select_fusion.1.own_b, bf16[1296,128]{1,0:T(8,128)(2,1)S(1)} %collective-permute-done.18.other_a, ...), custom_call_target="tpu_custom_call" | custom-call | tf_op jit(solution)/shard_map/normalize/pallas_call | solution.py:451
  (20 shorter events, 0.4 us)
Async XLA Ops:
  0.6 11.3 %copy-start = (f32[128]{0:T(128)S(1)}, f32[128]{0:T(128)}, u32[]{:S(2)}) copy-start(f32[128]{0:T(128)} %param.10) | copy-start | bytes 1540
  0.7 11.3 %copy-start.1 = (f32[128]{0:T(128)S(1)}, f32[128]{0:T(128)}, u32[]{:S(2)}) copy-start(f32[128]{0:T(128)} %param.12) | copy-start | bytes 1540
  2.2 5.6 %collective-permute-start = (bf16[336,128]{1,0:T(8,128)(2,1)S(1)}, bf16[336,128]{1,0:T(8,128)(2,1)S(1)}, u32[]{:S(2)}, u32[]{:S(2)}) collective-permute-start(bf16[336,128]{1,0:T(8,128)(2,1)S(1)} %get-tuple-element.35), channel_id=1, source_target_pairs={{0,1},{1,0},{2,3},{3,2},{4,5},{5,4},{6,7},{7,6},{8,9},{9,8},{10,11... | collective-permute-start | bytes 258056 | tf_op jit(solution)/shard_map/ppermute | solution.py:83
  5.3 2.5 %collective-permute-start.1 = (bf16[336,128]{1,0:T(8,128)(2,1)S(1)}, bf16[336,128]{1,0:T(8,128)(2,1)S(1)}, u32[]{:S(2)}, u32[]{:S(2)}) collective-permute-start(bf16[336,128]{1,0:T(8,128)(2,1)S(1)} %get-tuple-element.36), channel_id=1, source_target_pairs={{1,2},{3,4},{5,6},{2,1},{4,3},{6,5},{9,10},{11,12},{13,14},{10,9},... | collective-permute-start | bytes 258056 | tf_op jit(solution)/shard_map/ppermute | solution.py:82
  5.9 6.0 %collective-permute-start.2 = (bf16[656,128]{1,0:T(8,128)(2,1)S(1)}, bf16[656,128]{1,0:T(8,128)(2,1)S(1)}, u32[]{:S(2)}, u32[]{:S(2)}) collective-permute-start(bf16[656,128]{1,0:T(8,128)(2,1)S(1)} %get-tuple-element.39), channel_id=1, source_target_pairs={{0,8},{8,0},{16,24},{24,16},{1,9},{9,1},{17,25},{25,17},{2,10},{10... | collective-permute-start | bytes 503816 | tf_op jit(solution)/shard_map/ppermute | solution.py:83
  6.0 5.9 %collective-permute-start.3 = (bf16[656,128]{1,0:T(8,128)(2,1)S(1)}, bf16[656,128]{1,0:T(8,128)(2,1)S(1)}, u32[]{:S(2)}, u32[]{:S(2)}) collective-permute-start(bf16[656,128]{1,0:T(8,128)(2,1)S(1)} %get-tuple-element.40), channel_id=1, source_target_pairs={{8,16},{16,8},{9,17},{17,9},{10,18},{18,10},{11,19},{19,11},{12,20... | collective-permute-start | bytes 503816 | tf_op jit(solution)/shard_map/ppermute | solution.py:82
  7.8 4.1 %collective-permute-start.4 = (bf16[384,128]{1,0:T(8,128)(2,1)S(1)}, bf16[384,128]{1,0:T(8,128)(2,1)S(1)}, u32[]{:S(2)}, u32[]{:S(2)}) collective-permute-start(bf16[384,128]{1,0:T(8,128)(2,1)S(1)} %get-tuple-element.41._), channel_id=1, source_target_pairs={{0,8},{8,0},{16,24},{24,16},{1,9},{9,1},{17,25},{25,17},{2,10},{10... | collective-permute-start | bytes 294920 | tf_op jit(solution)/shard_map/ppermute | solution.py:83
  9.7 2.2 %collective-permute-start.5 = (bf16[384,128]{1,0:T(8,128)(2,1)S(1)}, bf16[384,128]{1,0:T(8,128)(2,1)S(1)}, u32[]{:S(2)}, u32[]{:S(2)}) collective-permute-start(bf16[384,128]{1,0:T(8,128)(2,1)S(1)} %get-tuple-element.42), channel_id=1, source_target_pairs={{8,16},{16,8},{9,17},{17,9},{10,18},{18,10},{11,19},{19,11},{12,20... | collective-permute-start | bytes 294920 | tf_op jit(solution)/shard_map/ppermute | solution.py:82
  20.4 5.5 %collective-permute-start.6 = (bf16[2592,128]{1,0:T(8,128)(2,1)S(1)}, bf16[2592,128]{1,0:T(8,128)(2,1)S(1)}, u32[]{:S(2)}, u32[]{:S(2)}) collective-permute-start(bf16[2592,128]{1,0:T(8,128)(2,1)S(1)} %bitcast.9), channel_id=1, source_target_pairs={{0,8},{8,0},{16,24},{24,16},{1,9},{9,1},{17,25},{25,17},{2,10},{10... | collective-permute-start | bytes 1990664 | tf_op jit(solution)/shard_map/ppermute | solution.py:29
  26.1 9.1 %collective-permute-start.8 = (bf16[648,128]{1,0:T(8,128)(2,1)S(1)}, bf16[648,128]{1,0:T(8,128)(2,1)S(1)}, u32[]{:S(2)}, u32[]{:S(2)}) collective-permute-start(bf16[648,128]{1,0:T(8,128)(2,1)S(1)} %dynamic-slice_convert_fusion), channel_id=1, source_target_pairs={{0,1},{1,0},{2,3},{3,2},{4,5},{5,4},{6,7},{7,6},{8,9},{9,8},{10,11... | collective-permute-start | bytes 497672 | tf_op jit(solution)/shard_map/ppermute | solution.py:29
  30.5 6.3 %collective-permute-start.7 = (bf16[648,128]{1,0:T(8,128)(2,1)S(1)}, bf16[648,128]{1,0:T(8,128)(2,1)S(1)}, u32[]{:S(2)}, u32[]{:S(2)}) collective-permute-start(bf16[648,128]{1,0:T(8,128)(2,1)S(1)} %dynamic-slice_convert_fusion.1), channel_id=1, source_target_pairs={{0,16},{8,24},{16,0},{24,8},{1,17},{9,25},{17,1},{25,9},{2,18},{10... | collective-permute-start | bytes 497672 | tf_op jit(solution)/shard_map/ppermute | solution.py:29
  36.9 4.5 %collective-permute-start.10 = (bf16[324,128]{1,0:T(8,128)(2,1)S(1)}, bf16[324,128]{1,0:T(8,128)(2,1)S(1)}, u32[]{:S(2)}, u32[]{:S(2)}) collective-permute-start(bf16[324,128]{1,0:T(8,128)(2,1)S(1)} %dynamic-slice_convert_fusion.2), channel_id=1, source_target_pairs={{0,16},{8,24},{16,0},{24,8},{1,17},{9,25},{17,1},{25,9},{2,18},{10... | collective-permute-start | bytes 248840 | tf_op jit(solution)/shard_map/ppermute | solution.py:29
  37.8 4.5 %collective-permute-start.9 = (bf16[324,128]{1,0:T(8,128)(2,1)S(1)}, bf16[324,128]{1,0:T(8,128)(2,1)S(1)}, u32[]{:S(2)}, u32[]{:S(2)}) collective-permute-start(bf16[324,128]{1,0:T(8,128)(2,1)S(1)} %dynamic-slice_convert_fusion.3), channel_id=1, source_target_pairs={{0,1},{1,0},{2,3},{3,2},{4,5},{5,4},{6,7},{7,6},{8,9},{9,8},{10,11... | collective-permute-start | bytes 248840 | tf_op jit(solution)/shard_map/ppermute | solution.py:29
  42.6 4.5 %collective-permute-start.11 = (bf16[324,128]{1,0:T(8,128)(2,1)S(1)}, bf16[324,128]{1,0:T(8,128)(2,1)S(1)}, u32[]{:S(2)}, u32[]{:S(2)}) collective-permute-start(bf16[324,128]{1,0:T(8,128)(2,1)S(1)} %fusion.1), channel_id=1, source_target_pairs={{0,2},{1,3},{2,0},{3,1},{4,6},{5,7},{6,4},{7,5},{8,10},{9,11},{10,... | collective-permute-start | bytes 248840 | tf_op jit(solution)/shard_map/ppermute | solution.py:29
  47.3 5.7 %collective-permute-start.12 = (bf16[324,128]{1,0:T(8,128)(2,1)S(1)}, bf16[324,128]{1,0:T(8,128)(2,1)S(1)}, u32[]{:S(2)}, u32[]{:S(2)}) collective-permute-start(bf16[324,128]{1,0:T(8,128)(2,1)S(1)} %fusion.4), channel_id=1, source_target_pairs={{0,4},{1,5},{2,6},{3,7},{4,0},{5,1},{6,2},{7,3},{8,12},{9,13},{10,... | collective-permute-start | bytes 248840 | tf_op jit(solution)/shard_map/ppermute | solution.py:29
  53.0 4.5 %collective-permute-start.13 = (bf16[324,128]{1,0:T(8,128)(2,1)S(1)}, bf16[324,128]{1,0:T(8,128)(2,1)S(1)}, u32[]{:S(2)}, u32[]{:S(2)}) collective-permute-start(bf16[324,128]{1,0:T(8,128)(2,1)S(1)} %add_convert_fusion), channel_id=1, source_target_pairs={{0,2},{1,3},{2,0},{3,1},{4,6},{5,7},{6,4},{7,5},{8,10},{9,11},{10,... | collective-permute-start | bytes 248840 | tf_op jit(solution)/shard_map/ppermute | solution.py:29
  57.7 5.2 %collective-permute-start.14 = (bf16[324,128]{1,0:T(8,128)(2,1)S(1)}, bf16[324,128]{1,0:T(8,128)(2,1)S(1)}, u32[]{:S(2)}, u32[]{:S(2)}) collective-permute-start(bf16[324,128]{1,0:T(8,128)(2,1)S(1)} %get-tuple-element.64), channel_id=1, source_target_pairs={{0,1},{1,0},{2,3},{3,2},{4,5},{5,4},{6,7},{7,6},{8,9},{9,8},{10,11... | collective-permute-start | bytes 248840 | tf_op jit(solution)/shard_map/ppermute | solution.py:29
  60.4 4.5 %collective-permute-start.15 = (bf16[324,128]{1,0:T(8,128)(2,1)S(1)}, bf16[324,128]{1,0:T(8,128)(2,1)S(1)}, u32[]{:S(2)}, u32[]{:S(2)}) collective-permute-start(bf16[324,128]{1,0:T(8,128)(2,1)S(1)} %get-tuple-element.63), channel_id=1, source_target_pairs={{0,16},{8,24},{16,0},{24,8},{1,17},{9,25},{17,1},{25,9},{2,18},{10... | collective-permute-start | bytes 248840 | tf_op jit(solution)/shard_map/ppermute | solution.py:29
  64.9 5.4 %collective-permute-start.17 = (bf16[648,128]{1,0:T(8,128)(2,1)S(1)}, bf16[648,128]{1,0:T(8,128)(2,1)S(1)}, u32[]{:S(2)}, u32[]{:S(2)}) collective-permute-start(bf16[648,128]{1,0:T(8,128)(2,1)S(1)} %maximum_select_fusion.4), channel_id=1, source_target_pairs={{0,1},{1,0},{2,3},{3,2},{4,5},{5,4},{6,7},{7,6},{8,9},{9,8},{10,11... | collective-permute-start | bytes 497672 | tf_op jit(solution)/shard_map/ppermute | solution.py:29
  65.1 5.4 %collective-permute-start.16 = (bf16[648,128]{1,0:T(8,128)(2,1)S(1)}, bf16[648,128]{1,0:T(8,128)(2,1)S(1)}, u32[]{:S(2)}, u32[]{:S(2)}) collective-permute-start(bf16[648,128]{1,0:T(8,128)(2,1)S(1)} %maximum_select_fusion.3), channel_id=1, source_target_pairs={{0,16},{8,24},{16,0},{24,8},{1,17},{9,25},{17,1},{25,9},{2,18},{10... | collective-permute-start | bytes 497672 | tf_op jit(solution)/shard_map/ppermute | solution.py:29
  70.6 1.7 %collective-permute-start.19 = (bf16[1296,128]{1,0:T(8,128)(2,1)S(1)}, bf16[1296,128]{1,0:T(8,128)(2,1)S(1)}, u32[]{:S(2)}, u32[]{:S(2)}) collective-permute-start(bf16[1296,128]{1,0:T(8,128)(2,1)S(1)} %maximum_select_fusion.1.own_b), channel_id=1, source_target_pairs={{0,8},{8,0},{16,24},{24,16},{1,9},{9,1},{17,25},{25,17},{2,10},{10... | collective-permute-start | bytes 995336 | tf_op jit(solution)/shard_map/ppermute | solution.py:29
  70.8 2.0 %collective-permute-start.18 = (bf16[1296,128]{1,0:T(8,128)(2,1)S(1)}, bf16[1296,128]{1,0:T(8,128)(2,1)S(1)}, u32[]{:S(2)}, u32[]{:S(2)}) collective-permute-start(bf16[1296,128]{1,0:T(8,128)(2,1)S(1)} %maximum_select_fusion.own_a), channel_id=1, source_target_pairs={{0,8},{8,0},{16,24},{24,16},{1,9},{9,1},{17,25},{25,17},{2,10},{10... | collective-permute-start | bytes 995336 | tf_op jit(solution)/shard_map/ppermute | solution.py:29

commit v7 on v6

--- a/solution.py
+++ b/solution.py
@@ -52,13 +52,10 @@
 
 def summed_everywhere(total, levels):
     one, two, middle, final = levels[0], levels[1], levels[2:-1], levels[-1]
-    cut = total.shape[0] // 2
-    parts = [total[:cut], total[cut:]]
+    parts = total
     for order in ((one, two), (two, one)):
         split = [halves(part, level) for part, level in zip(parts, order)]
-        got = lax.optimization_barrier(
-            [swap(sent, level) for (sent, _), level in zip(split, order)]
-        )
+        got = [swap(sent, level) for (sent, _), level in zip(split, order)]
         parts = [kept + other.astype(F32) for (_, kept), other in zip(split, got)]
     both = jnp.concatenate(parts, axis=0)
     for level in middle:
@@ -71,7 +68,7 @@
     cut = both.shape[0] // 2
     parts = [both[:cut], both[cut:]]
     for order in ((two, one), (one, two)):
-        got = lax.optimization_barrier([swap(part, level) for part, level in zip(parts, order)])
+        got = [swap(part, level) for part, level in zip(parts, order)]
         parts = [joined(own, other, level) for own, other, level in zip(parts, got, order)]
     return parts
 
@@ -98,8 +95,8 @@
 
 
 def pack_own_body(
-    cx, cy, kz, odd, odd_y, hfield, hup, hmask, hfirst, hsecond,
-    inner_y, outer_y, inner_x, outer_x, tile, field, up, w_first, w_second,
+    cx, cy, kz, odd, odd_y, hfield, hup, hmask,
+    inner_y, outer_y, inner_x, outer_x, tile, field, up,
     mask, square, deep, sems,
 ):
     fh = FIELD_HALO
@@ -107,8 +104,6 @@
         (hmask, mask),
         (hfield, field),
         (hup, up),
-        (hfirst, w_first),
-        (hsecond, w_second),
     )
     copies = [
         pltpu.make_async_copy(source, target, sems.at[i])
@@ -135,8 +130,6 @@
         put_rows(
             ref, (field[pl.ds(end * (cx - fh), fh)], up[pl.ds(end * (cx - 1), 1)], tile[...])
         )
-    copies[3].wait()
-    copies[4].wait()
 
 
 def pack_corner_body(cx, cy, kz, odd, odd_y, inner_y, outer_y, inner, outer, left, right):
@@ -179,7 +172,7 @@
     side, field, up, tile, left, right, inner_x, outer_x, inner, outer, w1, b1, w2, b2, w3,
     features, sent, kept,
     low, high, low_ends, high_ends,
-    xp, xs, hp, hs, act, upf, outf, g2p, g2s, gate, g1, d2, d1,
+    xp, xs, hp, hs, act, upf, outf, g2p, g2s, gate, g1, d2, d1, shown, sem,
 ):
     low[...], high[...] = ends_of(side[0] == 1, inner_x, outer_x)
     low_ends[...], high_ends[...] = ends_of(side[0] == 1, inner, outer)
@@ -300,7 +293,9 @@
     for x in range(cx):
         base = (x + 1) * span + 2 * kz
         rows = outf[base : base + cy * 2 * kz].astype(BF)
-        features[x] = rows.reshape(cy, 2 * kz, LANES)
+        shown[x] = rows.reshape(cy, 2 * kz, LANES)
+    show = pltpu.make_async_copy(shown, features, sem)
+    show.start()
 
     own = hp[2 : 2 + cx, 2 : 2 + cy].reshape(-1, 2 * LANES)
     turned = own.T
@@ -358,6 +353,7 @@
         sent[:, at : at + half] = total[:, pl.ds(other, half)].astype(BF)
         kept[:, at : at + half] = total[:, pl.ds(mine, half)]
         at += half
+    show.wait()
 
 
 def norm_body(side, own_a, own_b, other_a, other_b, out2, out1, held2, held1, sems):
@@ -389,7 +385,7 @@
         lax.rsqrt(jnp.full((1, LANES), jnp.sum(total)) / float(out.size) + 1e-06)
         for total, out in zip(squares, (out2, out1))
     ]
-    group = taps // 3
+    group = taps // 9
     copies = []
     for t, i, at in spans():
         held, count = (held2, held1)[i], rows_of[i]
@@ -410,11 +406,17 @@
 PAIR_TAPS = ((1, 0), (2, 1), (None, 2), (0, None))
 
 
-def weights_body(first, second, _, w1, w2, w3):
+def weights_body(hfirst, hsecond, _, w1, w2, w3, first, second, sems):
     taps = second.shape[0]
-
-    def group(g, carry):
-        for source, out, turn in ((first, w1, False), (second, w2, False), (second, w3, True)):
+    copies = [
+        pltpu.make_async_copy(hfirst, first, sems.at[0]),
+        pltpu.make_async_copy(hsecond, second, sems.at[1]),
+    ]
+    for copy in copies:
+        copy.start()
+
+    def group(g, kinds):
+        for source, out, turn in kinds:
             depth, width = source.shape[1:]
             if turn:
                 block = [source[taps - 1 - 3 * g - c].astype(F32).T.astype(BF) for c in range(3)]
@@ -426,9 +428,13 @@
                 for c, tap in enumerate(row):
                     value = none if tap is None else block[tap]
                     out[pl.ds(at, depth), c * width : (c + 1) * width] = value
-        return carry
-
-    lax.fori_loop(0, taps // 3, group, 0)
+
+    for copy, kinds in zip(copies, (((first, w1, False),), ((second, w2, False), (second, w3, True)))):
+        copy.wait()
+
+        @pl.loop(0, taps // 3)
+        def _(g):
+            group(g, kinds)
 
 
 def local_call(body, name, out, scratch=(), scalars=0, in_hbm=(), out_hbm=(), limit=24):
@@ -474,19 +480,19 @@
     rows_y = cx * FIELD_HALO * kz + cx * 2 * kz + kz
     rows_x = FIELD_HALO * cy * kz + cy * 2 * kz + kz
     rows_e = FIELD_HALO * 2 * FIELD_HALO * kz + 2 * 2 * kz + 2 * kz
-    inner_y, outer_y, inner_x, outer_x, tile, field, up, w_one, w_two = local_call(
+    inner_y, outer_y, inner_x, outer_x, tile, field, up = local_call(
         part(pack_own_body, cx, cy, kz),
         "pack_own",
         [shape((rows_y, LANES), BF)] * 2
         + [shape((rows_x, LANES), BF)] * 2
         + [shape((kz, LANES), BF)]
-        + [shape(a.shape, BF) for a in (volume, upstream, w_first, w_second)],
+        + [shape(a.shape, BF) for a in (volume, upstream)],
         [pltpu.VMEM(basin_mask.shape, jnp.int32)]
         + [pltpu.VMEM((LANES, LANES), F32)] * 2
-        + [pltpu.SemaphoreType.DMA((5,))],
+        + [pltpu.SemaphoreType.DMA((3,))],
         scalars=2,
-        in_hbm=(2, 3, 4, 5, 6),
-    )(side, odd_y, volume, upstream, basin_mask, w_first, w_second)
+        in_hbm=(2, 3, 4),
+    )(side, odd_y, volume, upstream, basin_mask)
     inner_y, outer_y = exchange(inner_y, outer_y, "gy")
     inner_x, outer_x = exchange(inner_x, outer_x, "gx")
     inner, outer, left, right = local_call(
@@ -505,7 +511,13 @@
             shape((4 * taps // 3 * chan, 2 * chan), BF),
             shape((4 * taps // 3 * chan, 2 * chan), BF),
         ],
-    )(w_one, w_two, corner)
+        [
+            pltpu.VMEM(w_first.shape, BF),
+            pltpu.VMEM(w_second.shape, BF),
+            pltpu.SemaphoreType.DMA((2,)),
+        ],
+        in_hbm=(0, 1),
+    )(w_first, w_second, corner)
     rows = chan // 2 + w_first.shape[1] // 2
     pairs = (kz, 2 * chan)
     features, sent, kept = local_call(
@@ -532,11 +544,19 @@
             pltpu.VMEM((cx * cy * kz, 2 * chan), BF),
             pltpu.VMEM(w_second.shape, F32),
             pltpu.VMEM(w_first.shape, F32),
+            pltpu.VMEM((cx, cy, 2 * kz, chan), BF),
+            pltpu.SemaphoreType.DMA(()),
         ],
         scalars=1,
+        out_hbm=(0,),
         limit=32,
     )(side, field, up, tile, left, right, inner_x, outer_x, inner, outer, w1, b_first.reshape(1, -1), w2, b_second.reshape(1, -1), w3)
-    total = kept.reshape(-1, chan) + swap(sent.reshape(-1, chan), core).astype(F32)
+    sent, kept = sent.reshape(-1, chan), kept.reshape(-1, chan)
+    cut = kept.shape[0] // 2
+    total = [
+        kept_half + swap(sent_half, core).astype(F32)
+        for sent_half, kept_half in ((sent[:cut], kept[:cut]), (sent[cut:], kept[cut:]))
+    ]
     own = summed_everywhere(total, levels[1:])
     other = [swap(part_of, core) for part_of in own]
     step_second, step_first = local_call(
@@ -546,7 +566,7 @@
         [
             pltpu.VMEM(w_second.shape, F32),
             pltpu.VMEM(w_first.shape, F32),
-            pltpu.SemaphoreType.DMA((6,)),
+            pltpu.SemaphoreType.DMA((18,)),
         ],
         scalars=1,
         out_hbm=(0, 1),

time: 74.9 us -> 72.2 us (0.964)
  waiting for transfers between devices: 29.4 us -> 27.2 us
  Pallas kernels: 13.4 us -> 14.3 us
    ppermute x14 -> x15, waiting for transfers between devices: 28.3 us -> 26.1 us  [swap(): lax.ppermute(part, axis, [(i, i ^ bit) for i in range(lax.axis_size(axis))])]
    pallas_call x5, Pallas kernels: 13.4 us -> 14.3 us  [call(): pl.pallas_call(body, out_shape=outs, in_specs=ins, out_specs=[hbm if i in...]
    ppermute x14 -> x15, starting transfers between devices: 22.2 us -> 21.5 us  [swap(): lax.ppermute(part, axis, [(i, i ^ bit) for i in range(lax.axis_size(axis))])]
  transfers between devices with their start and end apart: 20 -> 21, of which waited for: 15 -> 15; matrix products, arithmetic and copies ran while one was open for 1% -> 1% of each run, Pallas kernels for 2% -> 4%
where the time goes in v7:
time: 72.2 us; the launch traced here: 72 us
  starting transfers between devices  28.4 us (39%)
  waiting for transfers between devices  27.2 us (38%)
  Pallas kernels  14.3 us (20%)
  other arithmetic  1 us (1%)
  between operations  0.88 us (1%)
    ppermute x15, waiting for transfers between devices, swap(): lax.ppermute(part, axis, [(i, i ^ bit) for i in range(lax.axis_size(axis))])  26.1 us
    ppermute x15, starting transfers between devices, swap(): lax.ppermute(part, axis, [(i, i ^ bit) for i in range(lax.axis_size(axis))])  21.5 us
    pallas_call x5, Pallas kernels, call(): pl.pallas_call(body, out_shape=outs, in_specs=ins, out_specs=[hbm if i in...  14.3 us
    ppermute x3, starting transfers between devices, exchange(): inner = lax.ppermute(inner, axis, [(i, i ^ 1) for i in range(count)])  4.95 us
    ppermute x3, starting transfers between devices, exchange(): outer = lax.ppermute(outer, axis, pairs + [(b, a) for a, b in pairs])  1.98 us
  transfers between devices with their start and end apart: 21, of which 15 were waited for; matrix products, arithmetic and copies ran while one was open for 1% of the time, Pallas kernels for 4%

profile of v7, /device:TPU:0, one launch (start us, length us, event | category | flops | bytes accessed | tf_op | source)
XLA Modules:
  0.0 72.0 jit_solution(8632064321868767073)
XLA Ops:
  0.7 1.1 %pack_own.1 = (bf16[336,128]{1,0:T(8,128)(2,1)S(1)}, bf16[336,128]{1,0:T(8,128)(2,1)S(1)}, bf16[656,128]{1,0:T(8,128)(2,1)S(1)}, bf16[656,128]{1,0:T(8,128)(2,1)...) custom-call(s32[1]{0:T(128)} %bitcast.odd.side, ...), custom_call_target="tpu_custom_call" | custom-call | tf_op jit(solution)/shard_map/pack_own/pallas_call | solution.py:457
  1.8 3.1 %collective-permute-start = (bf16[336,128]{1,0:T(8,128)(2,1)S(1)}, bf16[336,128]{1,0:T(8,128)(2,1)S(1)}, u32[]{:S(2)}, u32[]{:S(2)}) collective-permute-start(bf16[336,128]{1,0:T(8,128)(2,1)S(1)} %get-tuple-element.25), channel_id=1, source_target_pairs={{0,1},{1,0},{2,3},{3,2},{4,5},{5,4},{6,7},{7,6},{8,9},{9,8},{10,11... | collective-permute-start | bytes 258056 | tf_op jit(solution)/shard_map/ppermute | solution.py:80
  4.8 0.7 collective-permute-start.1
  5.5 0.1 collective-permute-start.2
  5.6 0.7 collective-permute-start.3
  6.2 1.1 %collective-permute-done.inner_y = bf16[336,128]{1,0:T(8,128)(2,1)S(1)} collective-permute-done((bf16[336,128]{1,0:T(8,128)(2,1)S(1)}, bf16[336,128]{1,0:T(8,128)(2,1)S(1)}, u32[]{:S(2)}, u32[]{:S(2)}) %collective-permute-start) | collective-permute-done | bytes 86048 | tf_op jit(solution)/shard_map/ppermute | solution.py:80
  7.4 1.8 %collective-permute-start.4 = (bf16[384,128]{1,0:T(8,128)(2,1)S(1)}, bf16[384,128]{1,0:T(8,128)(2,1)S(1)}, u32[]{:S(2)}, u32[]{:S(2)}) collective-permute-start(bf16[384,128]{1,0:T(8,128)(2,1)S(1)} %get-tuple-element.31._), channel_id=1, source_target_pairs={{0,8},{8,0},{16,24},{24,16},{1,9},{9,1},{17,25},{25,17},{2,10},{10... | collective-permute-start | bytes 294920 | tf_op jit(solution)/shard_map/ppermute | solution.py:80
  9.2 0.7 collective-permute-start.5
  9.9 2.7 %weights.1 = (bf16[2304,256]{1,0:T(8,128)(2,1)S(1)}, bf16[4608,256]{1,0:T(8,128)(2,1)S(1)}, bf16[4608,256]{1,0:T(8,128)(2,1)S(1)}) custom-call(bf16[27,64,128]{2,1,0:T(8,128)(2,1)} %hfirst.1, bf16[27,128,128]{2,1,0:T(8,128)(2,1)} %hsecond.1, bf16[384,128]{1,0:T(8,128)(2,1)S(1)} %get-tuple-element.31._), custom_call_target="tpu_custom_call" | custom-call | tf_op jit(solution)/shard_map/weights/pallas_call | solution.py:457
  12.7 8.4 %compute.1 = (bf16[4,8,32,128]{3,2,1,0:T(8,128)(2,1)}, bf16[27,96,128]{2,1,0:T(8,128)(2,1)S(1)}, f32[27,96,128]{2,1,0:T(8,128)S(1)}) custom-call(s32[1]{0:T(128)} %bitcast.odd.side, bf16[4,8,16,128]{3,2,1,0:T(8,128)(2,1)S(1)} %get-tuple-element.22.field, bf16[4,8,32,128]{3,2,1,0:T(8,128)(2,1)S(1)} %get-tuple-element.23.up, ...), custom_call_target="tpu_custom_call" | custom-call | tf_op jit(solution)/shard_map/compute/pallas_call | solution.py:457
  21.2 2.5 %collective-permute-start.6 = (bf16[1296,128]{1,0:T(8,128)(2,1)S(1)}, bf16[1296,128]{1,0:T(8,128)(2,1)S(1)}, u32[]{:S(2)}, u32[]{:S(2)}) collective-permute-start(bf16[1296,128]{1,0:T(8,128)(2,1)S(1)} %get-tuple-element.44), channel_id=1, source_target_pairs={{0,8},{8,0},{16,24},{24,16},{1,9},{9,1},{17,25},{25,17},{2,10},{10... | collective-permute-start | bytes 995336 | tf_op jit(solution)/shard_map/ppermute | solution.py:29
  23.8 0.1 collective-permute-start.9
  23.8 1.2 %collective-permute-done.6 = bf16[1296,128]{1,0:T(8,128)(2,1)S(1)} collective-permute-done((bf16[1296,128]{1,0:T(8,128)(2,1)S(1)}, bf16[1296,128]{1,0:T(8,128)(2,1)S(1)}, u32[]{:S(2)}, u32[]{:S(2)}) %collective-permute-start.6) | collective-permute-done | bytes 331808 | tf_op jit(solution)/shard_map/ppermute | solution.py:29
  25.0 0.5 collective-permute-done.9
  25.5 0.1 slice_add_fusion
  25.7 4.3 %collective-permute-start.10 = (bf16[648,128]{1,0:T(8,128)(2,1)S(1)}, bf16[648,128]{1,0:T(8,128)(2,1)S(1)}, u32[]{:S(2)}, u32[]{:S(2)}) collective-permute-start(bf16[648,128]{1,0:T(8,128)(2,1)S(1)} %dynamic-slice_convert_fusion), channel_id=1, source_target_pairs={{0,1},{1,0},{2,3},{3,2},{4,5},{5,4},{6,7},{7,6},{8,9},{9,8},{10,11... | collective-permute-start | bytes 497672 | tf_op jit(solution)/shard_map/ppermute | solution.py:29
  30.0 1.1 %collective-permute-start.7 = (bf16[648,128]{1,0:T(8,128)(2,1)S(1)}, bf16[648,128]{1,0:T(8,128)(2,1)S(1)}, u32[]{:S(2)}, u32[]{:S(2)}) collective-permute-start(bf16[648,128]{1,0:T(8,128)(2,1)S(1)} %dynamic-slice_convert_fusion.1), channel_id=1, source_target_pairs={{0,16},{8,24},{16,0},{24,8},{1,17},{9,25},{17,1},{25,9},{2,18},{10... | collective-permute-start | bytes 497672 | tf_op jit(solution)/shard_map/ppermute | solution.py:29
  31.2 3.6 %collective-permute-done.10 = bf16[648,128]{1,0:T(8,128)(2,1)S(1)} collective-permute-done((bf16[648,128]{1,0:T(8,128)(2,1)S(1)}, bf16[648,128]{1,0:T(8,128)(2,1)S(1)}, u32[]{:S(2)}, u32[]{:S(2)}) %collective-permute-start.10) | collective-permute-done | bytes 165920 | tf_op jit(solution)/shard_map/ppermute | solution.py:29
  34.9 0.9 %collective-permute-start.11 = (bf16[324,128]{1,0:T(8,128)(2,1)S(1)}, bf16[324,128]{1,0:T(8,128)(2,1)S(1)}, u32[]{:S(2)}, u32[]{:S(2)}) collective-permute-start(bf16[324,128]{1,0:T(8,128)(2,1)S(1)} %dynamic-slice_convert_fusion.2), channel_id=1, source_target_pairs={{0,16},{8,24},{16,0},{24,8},{1,17},{9,25},{17,1},{25,9},{2,18},{10... | collective-permute-start | bytes 248840 | tf_op jit(solution)/shard_map/ppermute | solution.py:29
  35.8 0.6 collective-permute-done.7
  36.4 1.2 %collective-permute-start.8 = (bf16[324,128]{1,0:T(8,128)(2,1)S(1)}, bf16[324,128]{1,0:T(8,128)(2,1)S(1)}, u32[]{:S(2)}, u32[]{:S(2)}) collective-permute-start(bf16[324,128]{1,0:T(8,128)(2,1)S(1)} %dynamic-slice_convert_fusion.3), channel_id=1, source_target_pairs={{0,1},{1,0},{2,3},{3,2},{4,5},{5,4},{6,7},{7,6},{8,9},{9,8},{10,11... | collective-permute-start | bytes 248840 | tf_op jit(solution)/shard_map/ppermute | solution.py:29
  37.6 1.8 %collective-permute-done.11 = bf16[324,128]{1,0:T(8,128)(2,1)S(1)} collective-permute-done((bf16[324,128]{1,0:T(8,128)(2,1)S(1)}, bf16[324,128]{1,0:T(8,128)(2,1)S(1)}, u32[]{:S(2)}, u32[]{:S(2)}) %collective-permute-start.11) | collective-permute-done | bytes 82976 | tf_op jit(solution)/shard_map/ppermute | solution.py:29
  39.4 1.5 %collective-permute-done.8 = bf16[324,128]{1,0:T(8,128)(2,1)S(1)} collective-permute-done((bf16[324,128]{1,0:T(8,128)(2,1)S(1)}, bf16[324,128]{1,0:T(8,128)(2,1)S(1)}, u32[]{:S(2)}, u32[]{:S(2)}) %collective-permute-start.8) | collective-permute-done | bytes 82976 | tf_op jit(solution)/shard_map/ppermute | solution.py:29
  41.0 0.2 fusion.1
  41.2 2.3 %collective-permute-start.12 = (bf16[324,128]{1,0:T(8,128)(2,1)S(1)}, bf16[324,128]{1,0:T(8,128)(2,1)S(1)}, u32[]{:S(2)}, u32[]{:S(2)}) collective-permute-start(bf16[324,128]{1,0:T(8,128)(2,1)S(1)} %fusion.1), channel_id=1, source_target_pairs={{0,2},{1,3},{2,0},{3,1},{4,6},{5,7},{6,4},{7,5},{8,10},{9,11},{10,... | collective-permute-start | bytes 248840 | tf_op jit(solution)/shard_map/ppermute | solution.py:29
  43.5 2.4 %collective-permute-done.12 = bf16[324,128]{1,0:T(8,128)(2,1)S(1)} collective-permute-done((bf16[324,128]{1,0:T(8,128)(2,1)S(1)}, bf16[324,128]{1,0:T(8,128)(2,1)S(1)}, u32[]{:S(2)}, u32[]{:S(2)}) %collective-permute-start.12) | collective-permute-done | bytes 82976 | tf_op jit(solution)/shard_map/ppermute | solution.py:29
  45.9 0.2 fusion.4
  46.1 3.4 %collective-permute-start.13 = (bf16[324,128]{1,0:T(8,128)(2,1)S(1)}, bf16[324,128]{1,0:T(8,128)(2,1)S(1)}, u32[]{:S(2)}, u32[]{:S(2)}) collective-permute-start(bf16[324,128]{1,0:T(8,128)(2,1)S(1)} %fusion.4), channel_id=1, source_target_pairs={{0,4},{1,5},{2,6},{3,7},{4,0},{5,1},{6,2},{7,3},{8,12},{9,13},{10,... | collective-permute-start | bytes 248840 | tf_op jit(solution)/shard_map/ppermute | solution.py:29
  49.5 2.5 %collective-permute-done.13 = bf16[324,128]{1,0:T(8,128)(2,1)S(1)} collective-permute-done((bf16[324,128]{1,0:T(8,128)(2,1)S(1)}, bf16[324,128]{1,0:T(8,128)(2,1)S(1)}, u32[]{:S(2)}, u32[]{:S(2)}) %collective-permute-start.13) | collective-permute-done | bytes 82976 | tf_op jit(solution)/shard_map/ppermute | solution.py:29
  52.0 1.7 %collective-permute-start.14 = (bf16[324,128]{1,0:T(8,128)(2,1)S(1)}, bf16[324,128]{1,0:T(8,128)(2,1)S(1)}, u32[]{:S(2)}, u32[]{:S(2)}) collective-permute-start(bf16[324,128]{1,0:T(8,128)(2,1)S(1)} %add_convert_fusion), channel_id=1, source_target_pairs={{0,2},{1,3},{2,0},{3,1},{4,6},{5,7},{6,4},{7,5},{8,10},{9,11},{10,... | collective-permute-start | bytes 248840 | tf_op jit(solution)/shard_map/ppermute | solution.py:29
  53.8 2.8 %collective-permute-done.14 = bf16[324,128]{1,0:T(8,128)(2,1)S(1)} collective-permute-done((bf16[324,128]{1,0:T(8,128)(2,1)S(1)}, bf16[324,128]{1,0:T(8,128)(2,1)S(1)}, u32[]{:S(2)}, u32[]{:S(2)}) %collective-permute-start.14) | collective-permute-done | bytes 82976 | tf_op jit(solution)/shard_map/ppermute | solution.py:29
  56.6 0.1 maximum_select_fusion.2
  56.7 0.8 %collective-permute-start.17 = (bf16[324,128]{1,0:T(8,128)(2,1)S(1)}, bf16[324,128]{1,0:T(8,128)(2,1)S(1)}, u32[]{:S(2)}, u32[]{:S(2)}) collective-permute-start(bf16[324,128]{1,0:T(8,128)(2,1)S(1)} %get-tuple-element.45), channel_id=1, source_target_pairs={{0,16},{8,24},{16,0},{24,8},{1,17},{9,25},{17,1},{25,9},{2,18},{10... | collective-permute-start | bytes 248840 | tf_op jit(solution)/shard_map/ppermute | solution.py:29
  57.5 1.0 %collective-permute-start.15 = (bf16[324,128]{1,0:T(8,128)(2,1)S(1)}, bf16[324,128]{1,0:T(8,128)(2,1)S(1)}, u32[]{:S(2)}, u32[]{:S(2)}) collective-permute-start(bf16[324,128]{1,0:T(8,128)(2,1)S(1)} %get-tuple-element.46), channel_id=1, source_target_pairs={{0,1},{1,0},{2,3},{3,2},{4,5},{5,4},{6,7},{7,6},{8,9},{9,8},{10,11... | collective-permute-start | bytes 248840 | tf_op jit(solution)/shard_map/ppermute | solution.py:29
  58.5 3.6 %collective-permute-done.17 = bf16[324,128]{1,0:T(8,128)(2,1)S(1)} collective-permute-done((bf16[324,128]{1,0:T(8,128)(2,1)S(1)}, bf16[324,128]{1,0:T(8,128)(2,1)S(1)}, u32[]{:S(2)}, u32[]{:S(2)}) %collective-permute-start.17) | collective-permute-done | bytes 82976 | tf_op jit(solution)/shard_map/ppermute | solution.py:29
  62.1 0.1 maximum_select_fusion.4
  62.1 0.6 collective-permute-start.18
  62.8 0.1 maximum_select_fusion.3
  62.8 1.3 %collective-permute-start.16 = (bf16[648,128]{1,0:T(8,128)(2,1)S(1)}, bf16[648,128]{1,0:T(8,128)(2,1)S(1)}, u32[]{:S(2)}, u32[]{:S(2)}) collective-permute-start(bf16[648,128]{1,0:T(8,128)(2,1)S(1)} %maximum_select_fusion.3), channel_id=1, source_target_pairs={{0,16},{8,24},{16,0},{24,8},{1,17},{9,25},{17,1},{25,9},{2,18},{10... | collective-permute-start | bytes 497672 | tf_op jit(solution)/shard_map/ppermute | solution.py:29
  64.1 3.5 %collective-permute-done.18 = bf16[648,128]{1,0:T(8,128)(2,1)S(1)} collective-permute-done((bf16[648,128]{1,0:T(8,128)(2,1)S(1)}, bf16[648,128]{1,0:T(8,128)(2,1)S(1)}, u32[]{:S(2)}, u32[]{:S(2)}) %collective-permute-start.18) | collective-permute-done | bytes 165920 | tf_op jit(solution)/shard_map/ppermute | solution.py:29
  67.6 0.1 maximum_select_fusion.1.own_b
  67.6 0.1 collective-permute-start.20
  67.7 0.5 collective-permute-done.16
  68.2 0.1 maximum_select_fusion.own_a
  68.3 0.1 collective-permute-start.19
  68.4 0.9 %collective-permute-done.20.other_b = bf16[1296,128]{1,0:T(8,128)(2,1)S(1)} collective-permute-done((bf16[1296,128]{1,0:T(8,128)(2,1)S(1)}, bf16[1296,128]{1,0:T(8,128)(2,1)S(1)}, u32[]{:S(2)}, u32[]{:S(2)}) %collective-permute-start.20) | collective-permute-done | bytes 331808 | tf_op jit(solution)/shard_map/ppermute | solution.py:29
  69.3 0.7 collective-permute-done.19.other_a
  70.0 2.0 %normalize.1 = (f32[27,128,128]{2,1,0:T(8,128)}, f32[27,64,128]{2,1,0:T(8,128)}) custom-call(s32[1]{0:T(128)} %bitcast.odd.side, bf16[1296,128]{1,0:T(8,128)(2,1)S(1)} %maximum_select_fusion.own_a, bf16[1296,128]{1,0:T(8,128)(2,1)S(1)} %maximum_select_fusion.1.own_b, bf16[1296,128]{1,0:T(8,128)(2,1)S(1)} %collective-permute-done.19.other_a, ...), custom_call_target="tpu_custom_call" | custom-call | tf_op jit(solution)/shard_map/normalize/pallas_call | solution.py:457
  (22 shorter events, 0.4 us)
Async XLA Ops:
  0.6 12.1 %copy-start = (f32[128]{0:T(128)S(1)}, f32[128]{0:T(128)}, u32[]{:S(2)}) copy-start(f32[128]{0:T(128)} %param.10) | copy-start | bytes 1540
  0.6 12.1 %copy-start.1 = (f32[128]{0:T(128)S(1)}, f32[128]{0:T(128)}, u32[]{:S(2)}) copy-start(f32[128]{0:T(128)} %param.12) | copy-start | bytes 1540
  1.8 5.6 %collective-permute-start = (bf16[336,128]{1,0:T(8,128)(2,1)S(1)}, bf16[336,128]{1,0:T(8,128)(2,1)S(1)}, u32[]{:S(2)}, u32[]{:S(2)}) collective-permute-start(bf16[336,128]{1,0:T(8,128)(2,1)S(1)} %get-tuple-element.25), channel_id=1, source_target_pairs={{0,1},{1,0},{2,3},{3,2},{4,5},{5,4},{6,7},{7,6},{8,9},{9,8},{10,11... | collective-permute-start | bytes 258056 | tf_op jit(solution)/shard_map/ppermute | solution.py:80
  4.8 2.5 %collective-permute-start.1 = (bf16[336,128]{1,0:T(8,128)(2,1)S(1)}, bf16[336,128]{1,0:T(8,128)(2,1)S(1)}, u32[]{:S(2)}, u32[]{:S(2)}) collective-permute-start(bf16[336,128]{1,0:T(8,128)(2,1)S(1)} %get-tuple-element.26), channel_id=1, source_target_pairs={{1,2},{3,4},{5,6},{2,1},{4,3},{6,5},{9,10},{11,12},{13,14},{10,9},... | collective-permute-start | bytes 258056 | tf_op jit(solution)/shard_map/ppermute | solution.py:79
  5.5 7.2 %collective-permute-start.2 = (bf16[656,128]{1,0:T(8,128)(2,1)S(1)}, bf16[656,128]{1,0:T(8,128)(2,1)S(1)}, u32[]{:S(2)}, u32[]{:S(2)}) collective-permute-start(bf16[656,128]{1,0:T(8,128)(2,1)S(1)} %get-tuple-element.29), channel_id=1, source_target_pairs={{0,8},{8,0},{16,24},{24,16},{1,9},{9,1},{17,25},{25,17},{2,10},{10... | collective-permute-start | bytes 503816 | tf_op jit(solution)/shard_map/ppermute | solution.py:80
  5.6 7.1 %collective-permute-start.3 = (bf16[656,128]{1,0:T(8,128)(2,1)S(1)}, bf16[656,128]{1,0:T(8,128)(2,1)S(1)}, u32[]{:S(2)}, u32[]{:S(2)}) collective-permute-start(bf16[656,128]{1,0:T(8,128)(2,1)S(1)} %get-tuple-element.30), channel_id=1, source_target_pairs={{8,16},{16,8},{9,17},{17,9},{10,18},{18,10},{11,19},{19,11},{12,20... | collective-permute-start | bytes 503816 | tf_op jit(solution)/shard_map/ppermute | solution.py:79
  7.4 5.2 %collective-permute-start.4 = (bf16[384,128]{1,0:T(8,128)(2,1)S(1)}, bf16[384,128]{1,0:T(8,128)(2,1)S(1)}, u32[]{:S(2)}, u32[]{:S(2)}) collective-permute-start(bf16[384,128]{1,0:T(8,128)(2,1)S(1)} %get-tuple-element.31._), channel_id=1, source_target_pairs={{0,8},{8,0},{16,24},{24,16},{1,9},{9,1},{17,25},{25,17},{2,10},{10... | collective-permute-start | bytes 294920 | tf_op jit(solution)/shard_map/ppermute | solution.py:80
  9.2 3.4 %collective-permute-start.5 = (bf16[384,128]{1,0:T(8,128)(2,1)S(1)}, bf16[384,128]{1,0:T(8,128)(2,1)S(1)}, u32[]{:S(2)}, u32[]{:S(2)}) collective-permute-start(bf16[384,128]{1,0:T(8,128)(2,1)S(1)} %get-tuple-element.32), channel_id=1, source_target_pairs={{8,16},{16,8},{9,17},{17,9},{10,18},{18,10},{11,19},{19,11},{12,20... | collective-permute-start | bytes 294920 | tf_op jit(solution)/shard_map/ppermute | solution.py:79
  21.2 3.8 %collective-permute-start.6 = (bf16[1296,128]{1,0:T(8,128)(2,1)S(1)}, bf16[1296,128]{1,0:T(8,128)(2,1)S(1)}, u32[]{:S(2)}, u32[]{:S(2)}) collective-permute-start(bf16[1296,128]{1,0:T(8,128)(2,1)S(1)} %get-tuple-element.44), channel_id=1, source_target_pairs={{0,8},{8,0},{16,24},{24,16},{1,9},{9,1},{17,25},{25,17},{2,10},{10... | collective-permute-start | bytes 995336 | tf_op jit(solution)/shard_map/ppermute | solution.py:29
  23.8 1.7 %collective-permute-start.9 = (bf16[1296,128]{1,0:T(8,128)(2,1)S(1)}, bf16[1296,128]{1,0:T(8,128)(2,1)S(1)}, u32[]{:S(2)}, u32[]{:S(2)}) collective-permute-start(bf16[1296,128]{1,0:T(8,128)(2,1)S(1)} %get-tuple-element.43), channel_id=1, source_target_pairs={{0,8},{8,0},{16,24},{24,16},{1,9},{9,1},{17,25},{25,17},{2,10},{10... | collective-permute-start | bytes 995336 | tf_op jit(solution)/shard_map/ppermute | solution.py:29
  25.7 9.1 %collective-permute-start.10 = (bf16[648,128]{1,0:T(8,128)(2,1)S(1)}, bf16[648,128]{1,0:T(8,128)(2,1)S(1)}, u32[]{:S(2)}, u32[]{:S(2)}) collective-permute-start(bf16[648,128]{1,0:T(8,128)(2,1)S(1)} %dynamic-slice_convert_fusion), channel_id=1, source_target_pairs={{0,1},{1,0},{2,3},{3,2},{4,5},{5,4},{6,7},{7,6},{8,9},{9,8},{10,11... | collective-permute-start | bytes 497672 | tf_op jit(solution)/shard_map/ppermute | solution.py:29
  30.0 6.3 %collective-permute-start.7 = (bf16[648,128]{1,0:T(8,128)(2,1)S(1)}, bf16[648,128]{1,0:T(8,128)(2,1)S(1)}, u32[]{:S(2)}, u32[]{:S(2)}) collective-permute-start(bf16[648,128]{1,0:T(8,128)(2,1)S(1)} %dynamic-slice_convert_fusion.1), channel_id=1, source_target_pairs={{0,16},{8,24},{16,0},{24,8},{1,17},{9,25},{17,1},{25,9},{2,18},{10... | collective-permute-start | bytes 497672 | tf_op jit(solution)/shard_map/ppermute | solution.py:29
  34.9 4.5 %collective-permute-start.11 = (bf16[324,128]{1,0:T(8,128)(2,1)S(1)}, bf16[324,128]{1,0:T(8,128)(2,1)S(1)}, u32[]{:S(2)}, u32[]{:S(2)}) collective-permute-start(bf16[324,128]{1,0:T(8,128)(2,1)S(1)} %dynamic-slice_convert_fusion.2), channel_id=1, source_target_pairs={{0,16},{8,24},{16,0},{24,8},{1,17},{9,25},{17,1},{25,9},{2,18},{10... | collective-permute-start | bytes 248840 | tf_op jit(solution)/shard_map/ppermute | solution.py:29
  36.4 4.5 %collective-permute-start.8 = (bf16[324,128]{1,0:T(8,128)(2,1)S(1)}, bf16[324,128]{1,0:T(8,128)(2,1)S(1)}, u32[]{:S(2)}, u32[]{:S(2)}) collective-permute-start(bf16[324,128]{1,0:T(8,128)(2,1)S(1)} %dynamic-slice_convert_fusion.3), channel_id=1, source_target_pairs={{0,1},{1,0},{2,3},{3,2},{4,5},{5,4},{6,7},{7,6},{8,9},{9,8},{10,11... | collective-permute-start | bytes 248840 | tf_op jit(solution)/shard_map/ppermute | solution.py:29
  41.2 4.7 %collective-permute-start.12 = (bf16[324,128]{1,0:T(8,128)(2,1)S(1)}, bf16[324,128]{1,0:T(8,128)(2,1)S(1)}, u32[]{:S(2)}, u32[]{:S(2)}) collective-permute-start(bf16[324,128]{1,0:T(8,128)(2,1)S(1)} %fusion.1), channel_id=1, source_target_pairs={{0,2},{1,3},{2,0},{3,1},{4,6},{5,7},{6,4},{7,5},{8,10},{9,11},{10,... | collective-permute-start | bytes 248840 | tf_op jit(solution)/shard_map/ppermute | solution.py:29
  46.1 5.9 %collective-permute-start.13 = (bf16[324,128]{1,0:T(8,128)(2,1)S(1)}, bf16[324,128]{1,0:T(8,128)(2,1)S(1)}, u32[]{:S(2)}, u32[]{:S(2)}) collective-permute-start(bf16[324,128]{1,0:T(8,128)(2,1)S(1)} %fusion.4), channel_id=1, source_target_pairs={{0,4},{1,5},{2,6},{3,7},{4,0},{5,1},{6,2},{7,3},{8,12},{9,13},{10,... | collective-permute-start | bytes 248840 | tf_op jit(solution)/shard_map/ppermute | solution.py:29
  52.0 4.5 %collective-permute-start.14 = (bf16[324,128]{1,0:T(8,128)(2,1)S(1)}, bf16[324,128]{1,0:T(8,128)(2,1)S(1)}, u32[]{:S(2)}, u32[]{:S(2)}) collective-permute-start(bf16[324,128]{1,0:T(8,128)(2,1)S(1)} %add_convert_fusion), channel_id=1, source_target_pairs={{0,2},{1,3},{2,0},{3,1},{4,6},{5,7},{6,4},{7,5},{8,10},{9,11},{10,... | collective-permute-start | bytes 248840 | tf_op jit(solution)/shard_map/ppermute | solution.py:29
  56.7 5.4 %collective-permute-start.17 = (bf16[324,128]{1,0:T(8,128)(2,1)S(1)}, bf16[324,128]{1,0:T(8,128)(2,1)S(1)}, u32[]{:S(2)}, u32[]{:S(2)}) collective-permute-start(bf16[324,128]{1,0:T(8,128)(2,1)S(1)} %get-tuple-element.45), channel_id=1, source_target_pairs={{0,16},{8,24},{16,0},{24,8},{1,17},{9,25},{17,1},{25,9},{2,18},{10... | collective-permute-start | bytes 248840 | tf_op jit(solution)/shard_map/ppermute | solution.py:29
  57.5 5.3 %collective-permute-start.15 = (bf16[324,128]{1,0:T(8,128)(2,1)S(1)}, bf16[324,128]{1,0:T(8,128)(2,1)S(1)}, u32[]{:S(2)}, u32[]{:S(2)}) collective-permute-start(bf16[324,128]{1,0:T(8,128)(2,1)S(1)} %get-tuple-element.46), channel_id=1, source_target_pairs={{0,1},{1,0},{2,3},{3,2},{4,5},{5,4},{6,7},{7,6},{8,9},{9,8},{10,11... | collective-permute-start | bytes 248840 | tf_op jit(solution)/shard_map/ppermute | solution.py:29
  62.1 5.4 %collective-permute-start.18 = (bf16[648,128]{1,0:T(8,128)(2,1)S(1)}, bf16[648,128]{1,0:T(8,128)(2,1)S(1)}, u32[]{:S(2)}, u32[]{:S(2)}) collective-permute-start(bf16[648,128]{1,0:T(8,128)(2,1)S(1)} %maximum_select_fusion.4), channel_id=1, source_target_pairs={{0,1},{1,0},{2,3},{3,2},{4,5},{5,4},{6,7},{7,6},{8,9},{9,8},{10,11... | collective-permute-start | bytes 497672 | tf_op jit(solution)/shard_map/ppermute | solution.py:29
  62.8 5.4 %collective-permute-start.16 = (bf16[648,128]{1,0:T(8,128)(2,1)S(1)}, bf16[648,128]{1,0:T(8,128)(2,1)S(1)}, u32[]{:S(2)}, u32[]{:S(2)}) collective-permute-start(bf16[648,128]{1,0:T(8,128)(2,1)S(1)} %maximum_select_fusion.3), channel_id=1, source_target_pairs={{0,16},{8,24},{16,0},{24,8},{1,17},{9,25},{17,1},{25,9},{2,18},{10... | collective-permute-start | bytes 497672 | tf_op jit(solution)/shard_map/ppermute | solution.py:29
  67.6 1.7 %collective-permute-start.20 = (bf16[1296,128]{1,0:T(8,128)(2,1)S(1)}, bf16[1296,128]{1,0:T(8,128)(2,1)S(1)}, u32[]{:S(2)}, u32[]{:S(2)}) collective-permute-start(bf16[1296,128]{1,0:T(8,128)(2,1)S(1)} %maximum_select_fusion.1.own_b), channel_id=1, source_target_pairs={{0,8},{8,0},{16,24},{24,16},{1,9},{9,1},{17,25},{25,17},{2,10},{10... | collective-permute-start | bytes 995336 | tf_op jit(solution)/shard_map/ppermute | solution.py:29
  68.3 1.7 %collective-permute-start.19 = (bf16[1296,128]{1,0:T(8,128)(2,1)S(1)}, bf16[1296,128]{1,0:T(8,128)(2,1)S(1)}, u32[]{:S(2)}, u32[]{:S(2)}) collective-permute-start(bf16[1296,128]{1,0:T(8,128)(2,1)S(1)} %maximum_select_fusion.own_a), channel_id=1, source_target_pairs={{0,8},{8,0},{16,24},{24,16},{1,9},{9,1},{17,25},{25,17},{2,10},{10... | collective-permute-start | bytes 995336 | tf_op jit(solution)/shard_map/ppermute | solution.py:29

commit v8 on v7

--- a/solution.py
+++ b/solution.py
@@ -11,6 +11,7 @@
 F32 = jnp.float32
 LANES = 128
 FIELD_HALO = 3
+CHAINS = 3
 MASK_HALO = 2
 
 
@@ -51,26 +52,22 @@
 
 
 def summed_everywhere(total, levels):
-    one, two, middle, final = levels[0], levels[1], levels[2:-1], levels[-1]
-    parts = total
-    for order in ((one, two), (two, one)):
+    early, final = levels[:-1], levels[-1]
+    pieces = 2 ** len(early)
+    rows = [part.shape[0] for part in total]
+    parts = [jnp.pad(part, ((0, -part.shape[0] % pieces), (0, 0))) for part in total]
+    turns = [i % len(early) for i in range(len(parts))]
+    steps = list(zip(*(early[i:] + early[:i] for i in turns)))
+    for order in steps:
         split = [halves(part, level) for part, level in zip(parts, order)]
         got = [swap(sent, level) for (sent, _), level in zip(split, order)]
         parts = [kept + other.astype(F32) for (_, kept), other in zip(split, got)]
-    both = jnp.concatenate(parts, axis=0)
-    for level in middle:
-        sent, kept = halves(both, level)
-        both = kept + swap(sent, level).astype(F32)
-    both = both.astype(BF)
-    both = (both.astype(F32) + swap(both, final).astype(F32)).astype(BF)
-    for level in reversed(middle):
-        both = joined(both, swap(both, level), level)
-    cut = both.shape[0] // 2
-    parts = [both[:cut], both[cut:]]
-    for order in ((two, one), (one, two)):
+    parts = [part.astype(BF) for part in parts]
+    parts = [(part.astype(F32) + swap(part, final).astype(F32)).astype(BF) for part in parts]
+    for order in reversed(steps):
         got = [swap(part, level) for part, level in zip(parts, order)]
         parts = [joined(own, other, level) for own, other, level in zip(parts, got, order)]
-    return parts
+    return [part[:count] for part, count in zip(parts, rows)]
 
 
 def exchange(inner, outer, axis):
@@ -169,10 +166,10 @@
 
 def compute_body(
     cx, cy, kz,
-    side, field, up, tile, left, right, inner_x, outer_x, inner, outer, w1, b1, w2, b2, w3,
+    side, field, up, tile, left, right, inner_x, outer_x, inner, outer, w1, b1, w2, b2, second_taps,
     features, sent, kept,
     low, high, low_ends, high_ends,
-    xp, xs, hp, hs, act, upf, outf, g2p, g2s, gate, g1, d2, d1, shown, sem,
+    xp, xs, hp, hs, act, upf, outf, g2p, g2s, gate, g1, d2, d1, shown, w3, sem,
 ):
     low[...], high[...] = ends_of(side[0] == 1, inner_x, outer_x)
     low_ends[...], high_ends[...] = ends_of(side[0] == 1, inner, outer)
@@ -267,6 +264,11 @@
 
     for i in range(hx // step):
         first(i)
+
+    taps, chan = second_taps.shape[:2]
+    for g in range(taps // 3):
+        block = [second_taps[taps - 1 - 3 * g - c].astype(F32).T.astype(BF) for c in range(3)]
+        put_pair_weights(w3, g * 4 * chan, block)
 
     def second(i):
         at = i * step
@@ -356,19 +358,20 @@
     show.wait()
 
 
-def norm_body(side, own_a, own_b, other_a, other_b, out2, out1, held2, held1, sems):
+def norm_body(chains, side, *refs):
+    own, other = refs[:chains], refs[chains : 2 * chains]
+    out2, out1, held2, held1, sems = refs[2 * chains :]
     taps = out2.shape[0]
-    split = own_a.shape[0]
     rows_of = held2.shape[1] // 2, held1.shape[1] // 2
     stride = sum(rows_of)
 
-    def rows(pair, start, count):
-        low, high = pair
+    def rows(refs, start, count):
         parts = []
-        if start < split:
-            parts.append(low[start : min(start + count, split)])
-        if start + count > split:
-            parts.append(high[max(start, split) - split : start + count - split])
+        for ref in refs:
+            low, high = max(start, 0), min(start + count, ref.shape[0])
+            if low < high:
+                parts.append(ref[low:high])
+            start -= ref.shape[0]
         return jnp.concatenate(parts, axis=0).astype(F32)
 
     def spans():
@@ -378,21 +381,21 @@
 
     squares = [jnp.zeros((8, LANES), F32), jnp.zeros((8, LANES), F32)]
     for t, i, at in spans():
-        for pair in ((own_a, own_b), (other_a, other_b)):
+        for pair in (own, other):
             value = rows(pair, at, rows_of[i])
             squares[i] += jnp.sum((value * value).reshape(-1, 8, LANES), axis=0)
     scales = [
         lax.rsqrt(jnp.full((1, LANES), jnp.sum(total)) / float(out.size) + 1e-06)
         for total, out in zip(squares, (out2, out1))
     ]
-    group = taps // 9
+    group = taps // 3
     copies = []
     for t, i, at in spans():
         held, count = (held2, held1)[i], rows_of[i]
         mine = pl.multiple_of(side[0] * count, count)
         rest = pl.multiple_of((1 - side[0]) * count, count)
-        held[t, pl.ds(mine, count)] = rows((own_a, own_b), at, count) * scales[i]
-        held[t, pl.ds(rest, count)] = rows((other_a, other_b), at, count) * scales[i]
+        held[t, pl.ds(mine, count)] = rows(own, at, count) * scales[i]
+        held[t, pl.ds(rest, count)] = rows(other, at, count) * scales[i]
         if i == 1 and (t + 1) % group == 0:
             span = pl.ds(t + 1 - group, group)
             for held, out in ((held2, out2), (held1, out1)):
@@ -406,35 +409,30 @@
 PAIR_TAPS = ((1, 0), (2, 1), (None, 2), (0, None))
 
 
-def weights_body(hfirst, hsecond, _, w1, w2, w3, first, second, sems):
-    taps = second.shape[0]
+def put_pair_weights(out, at, block):
+    depth, width = block[0].shape
+    none = jnp.zeros((depth, width), BF)
+    for r, row in enumerate(PAIR_TAPS):
+        for c, tap in enumerate(row):
+            value = none if tap is None else block[tap]
+            out[pl.ds(at + r * depth, depth), c * width : (c + 1) * width] = value
+
+
+def weights_body(hfirst, hsecond, _, w1, w2, second, first, sems):
     copies = [
         pltpu.make_async_copy(hfirst, first, sems.at[0]),
         pltpu.make_async_copy(hsecond, second, sems.at[1]),
     ]
     for copy in copies:
         copy.start()
-
-    def group(g, kinds):
-        for source, out, turn in kinds:
-            depth, width = source.shape[1:]
-            if turn:
-                block = [source[taps - 1 - 3 * g - c].astype(F32).T.astype(BF) for c in range(3)]
-            else:
-                block = [source[3 * g + c] for c in range(3)]
-            none = jnp.zeros((depth, width), BF)
-            for r, row in enumerate(PAIR_TAPS):
-                at = pl.multiple_of(g * 4 * depth + r * depth, depth)
-                for c, tap in enumerate(row):
-                    value = none if tap is None else block[tap]
-                    out[pl.ds(at, depth), c * width : (c + 1) * width] = value
-
-    for copy, kinds in zip(copies, (((first, w1, False),), ((second, w2, False), (second, w3, True)))):
+    for copy, source, out in zip(copies, (first, second), (w1, w2)):
         copy.wait()
-
-        @pl.loop(0, taps // 3)
+        depth = source.shape[1]
+
+        @pl.loop(0, source.shape[0] // 3)
         def _(g):
-            group(g, kinds)
+            block = [source[3 * g + c] for c in range(3)]
+            put_pair_weights(out, pl.multiple_of(g * 4 * depth, depth), block)
 
 
 def local_call(body, name, out, scratch=(), scalars=0, in_hbm=(), out_hbm=(), limit=24):
@@ -503,19 +501,15 @@
     )(side, odd_y, inner_y, outer_y)
     corner = inner
     inner, outer = exchange(inner, outer, "gx")
-    w1, w2, w3 = local_call(
+    w1, w2, second_taps = local_call(
         weights_body,
         "weights",
         [
             shape((4 * taps // 3 * w_first.shape[1], 2 * chan), BF),
             shape((4 * taps // 3 * chan, 2 * chan), BF),
-            shape((4 * taps // 3 * chan, 2 * chan), BF),
+            shape(w_second.shape, BF),
         ],
-        [
-            pltpu.VMEM(w_first.shape, BF),
-            pltpu.VMEM(w_second.shape, BF),
-            pltpu.SemaphoreType.DMA((2,)),
-        ],
+        [pltpu.VMEM(w_first.shape, BF), pltpu.SemaphoreType.DMA((2,))],
         in_hbm=(0, 1),
     )(w_first, w_second, corner)
     rows = chan // 2 + w_first.shape[1] // 2
@@ -545,28 +539,29 @@
             pltpu.VMEM(w_second.shape, F32),
             pltpu.VMEM(w_first.shape, F32),
             pltpu.VMEM((cx, cy, 2 * kz, chan), BF),
+            pltpu.VMEM((4 * taps // 3 * chan, 2 * chan), BF),
             pltpu.SemaphoreType.DMA(()),
         ],
         scalars=1,
         out_hbm=(0,),
         limit=32,
-    )(side, field, up, tile, left, right, inner_x, outer_x, inner, outer, w1, b_first.reshape(1, -1), w2, b_second.reshape(1, -1), w3)
+    )(side, field, up, tile, left, right, inner_x, outer_x, inner, outer, w1, b_first.reshape(1, -1), w2, b_second.reshape(1, -1), second_taps)
     sent, kept = sent.reshape(-1, chan), kept.reshape(-1, chan)
-    cut = kept.shape[0] // 2
-    total = [
-        kept_half + swap(sent_half, core).astype(F32)
-        for sent_half, kept_half in ((sent[:cut], kept[:cut]), (sent[cut:], kept[cut:]))
-    ]
+    cut = kept.shape[0] // CHAINS
+    total = []
+    for i in range(CHAINS):
+        span = slice(i * cut, (i + 1) * cut)
+        total.append(kept[span] + swap(sent[span], core).astype(F32))
     own = summed_everywhere(total, levels[1:])
     other = [swap(part_of, core) for part_of in own]
     step_second, step_first = local_call(
-        norm_body,
+        part(norm_body, CHAINS),
         "normalize",
         [shape(w_second.shape, F32), shape(w_first.shape, F32)],
         [
             pltpu.VMEM(w_second.shape, F32),
             pltpu.VMEM(w_first.shape, F32),
-            pltpu.SemaphoreType.DMA((18,)),
+            pltpu.SemaphoreType.DMA((6,)),
         ],
         scalars=1,
         out_hbm=(0, 1),

time: 72.2 us -> 68.2 us (0.945)
  waiting for transfers between devices: 27.2 us -> 11.6 us
  starting transfers between devices: 28.4 us -> 41.1 us
  Pallas kernels: 14.3 us -> 13.3 us
    ppermute x15 -> x27, waiting for transfers between devices: 26.1 us -> 10.4 us  [swap(): lax.ppermute(part, axis, [(i, i ^ bit) for i in range(lax.axis_size(axis))])]
    ppermute x15 -> x27, starting transfers between devices: 21.5 us -> 34.2 us  [swap(): lax.ppermute(part, axis, [(i, i ^ bit) for i in range(lax.axis_size(axis))])]
    pallas_call x5, Pallas kernels: 14.3 us -> 13.3 us  [call(): pl.pallas_call(body, out_shape=outs, in_specs=ins, out_specs=[hbm if i in...]
  transfers between devices with their start and end apart: 21 -> 33, of which waited for: 15 -> 18; matrix products, arithmetic and copies ran while one was open for 1% -> 1% of each run, Pallas kernels for 4% -> 3%
where the time goes in v8:
time: 68.2 us; the launch traced here: 68 us
  starting transfers between devices  41.1 us (60%)
  Pallas kernels  13.3 us (20%)
  waiting for transfers between devices  11.6 us (17%)
  between operations  1.1 us (2%)
    ppermute x27, starting transfers between devices, swap(): lax.ppermute(part, axis, [(i, i ^ bit) for i in range(lax.axis_size(axis))])  34.2 us
    pallas_call x5, Pallas kernels, call(): pl.pallas_call(body, out_shape=outs, in_specs=ins, out_specs=[hbm if i in...  13.3 us
    ppermute x27, waiting for transfers between devices, swap(): lax.ppermute(part, axis, [(i, i ^ bit) for i in range(lax.axis_size(axis))])  10.4 us
    ppermute x3, starting transfers between devices, exchange(): inner = lax.ppermute(inner, axis, [(i, i ^ 1) for i in range(count)])  4.95 us
    ppermute x3, starting transfers between devices, exchange(): outer = lax.ppermute(outer, axis, pairs + [(b, a) for a, b in pairs])  1.98 us
  transfers between devices with their start and end apart: 33, of which 18 were waited for; matrix products, arithmetic and copies ran while one was open for 1% of the time, Pallas kernels for 3%

profile of v8, /device:TPU:0, one launch (start us, length us, event | category | flops | bytes accessed | tf_op | source)
XLA Modules:
  0.0 68.0 jit_solution(14093754053320775153)
XLA Ops:
  0.7 1.1 %pack_own.1 = (bf16[336,128]{1,0:T(8,128)(2,1)S(1)}, bf16[336,128]{1,0:T(8,128)(2,1)S(1)}, bf16[656,128]{1,0:T(8,128)(2,1)S(1)}, bf16[656,128]{1,0:T(8,128)(2,1)...) custom-call(s32[1]{0:T(128)} %bitcast.odd.side, ...), custom_call_target="tpu_custom_call" | custom-call | tf_op jit(solution)/shard_map/pack_own/pallas_call | solution.py:455
  1.8 3.1 %collective-permute-start = (bf16[336,128]{1,0:T(8,128)(2,1)S(1)}, bf16[336,128]{1,0:T(8,128)(2,1)S(1)}, u32[]{:S(2)}, u32[]{:S(2)}) collective-permute-start(bf16[336,128]{1,0:T(8,128)(2,1)S(1)} %get-tuple-element.25), channel_id=1, source_target_pairs={{0,1},{1,0},{2,3},{3,2},{4,5},{5,4},{6,7},{7,6},{8,9},{9,8},{10,11... | collective-permute-start | bytes 258056 | tf_op jit(solution)/shard_map/ppermute | solution.py:77
  4.8 0.7 collective-permute-start.1
  5.6 0.7 collective-permute-start.3
  6.2 1.1 %collective-permute-done.inner_y = bf16[336,128]{1,0:T(8,128)(2,1)S(1)} collective-permute-done((bf16[336,128]{1,0:T(8,128)(2,1)S(1)}, bf16[336,128]{1,0:T(8,128)(2,1)S(1)}, u32[]{:S(2)}, u32[]{:S(2)}) %collective-permute-start) | collective-permute-done | bytes 86048 | tf_op jit(solution)/shard_map/ppermute | solution.py:77
  7.4 1.8 %collective-permute-start.4 = (bf16[384,128]{1,0:T(8,128)(2,1)S(1)}, bf16[384,128]{1,0:T(8,128)(2,1)S(1)}, u32[]{:S(2)}, u32[]{:S(2)}) collective-permute-start(bf16[384,128]{1,0:T(8,128)(2,1)S(1)} %get-tuple-element.31._), channel_id=1, source_target_pairs={{0,8},{8,0},{16,24},{24,16},{1,9},{9,1},{17,25},{25,17},{2,10},{10... | collective-permute-start | bytes 294920 | tf_op jit(solution)/shard_map/ppermute | solution.py:77
  9.2 0.7 collective-permute-start.5
  10.0 1.7 %weights.1 = (bf16[2304,256]{1,0:T(8,128)(2,1)S(1)}, bf16[4608,256]{1,0:T(8,128)(2,1)S(1)}, bf16[27,128,128]{2,1,0:T(8,128)(2,1)S(1)}) custom-call(bf16[27,64,128]{2,1,0:T(8,128)(2,1)} %hfirst.1, bf16[27,128,128]{2,1,0:T(8,128)(2,1)} %hsecond.1, bf16[384,128]{1,0:T(8,128)(2,1)S(1)} %get-tuple-element.31._), custom_call_target="tpu_custom_call" | custom-call | tf_op jit(solution)/shard_map/weights/pallas_call | solution.py:455
  11.8 8.6 %compute.1 = (bf16[4,8,32,128]{3,2,1,0:T(8,128)(2,1)}, bf16[27,96,128]{2,1,0:T(8,128)(2,1)S(1)}, f32[27,96,128]{2,1,0:T(8,128)S(1)}) custom-call(s32[1]{0:T(128)} %bitcast.odd.side, bf16[4,8,16,128]{3,2,1,0:T(8,128)(2,1)S(1)} %get-tuple-element.22.field, bf16[4,8,32,128]{3,2,1,0:T(8,128)(2,1)S(1)} %get-tuple-element.23.up, ...), custom_call_target="tpu_custom_call" | custom-call | tf_op jit(solution)/shard_map/compute/pallas_call | solution.py:455
  20.4 3.5 %collective-permute-start.22 = (bf16[864,128]{1,0:T(8,128)(2,1)S(1)}, bf16[864,128]{1,0:T(8,128)(2,1)S(1)}, u32[]{:S(2)}, u32[]{:S(2)}) collective-permute-start(bf16[864,128]{1,0:T(8,128)(2,1)S(1)} %bitcast.17), channel_id=1, source_target_pairs={{0,8},{8,0},{16,24},{24,16},{1,9},{9,1},{17,25},{25,17},{2,10},{10... | collective-permute-start | bytes 663560 | tf_op jit(solution)/shard_map/ppermute | solution.py:30
  24.0 0.4 collective-permute-start.6
  24.5 0.5 collective-permute-done.22
  25.0 5.1 %collective-permute-start.23 = (bf16[432,128]{1,0:T(8,128)(2,1)S(1)}, bf16[432,128]{1,0:T(8,128)(2,1)S(1)}, u32[]{:S(2)}, u32[]{:S(2)}) collective-permute-start(bf16[432,128]{1,0:T(8,128)(2,1)S(1)} %dynamic-slice_convert_fusion), channel_id=1, source_target_pairs={{0,2},{1,3},{2,0},{3,1},{4,6},{5,7},{6,4},{7,5},{8,10},{9,11},{10,... | collective-permute-start | bytes 331784 | tf_op jit(solution)/shard_map/ppermute | solution.py:30
  30.2 0.9 %collective-permute-start.15 = (bf16[432,128]{1,0:T(8,128)(2,1)S(1)}, bf16[432,128]{1,0:T(8,128)(2,1)S(1)}, u32[]{:S(2)}, u32[]{:S(2)}) collective-permute-start(bf16[432,128]{1,0:T(8,128)(2,1)S(1)} %dynamic-slice_convert_fusion.1), channel_id=1, source_target_pairs={{0,1},{1,0},{2,3},{3,2},{4,5},{5,4},{6,7},{7,6},{8,9},{9,8},{10,11... | collective-permute-start | bytes 331784 | tf_op jit(solution)/shard_map/ppermute | solution.py:30
  31.2 1.1 %collective-permute-start.7 = (bf16[432,128]{1,0:T(8,128)(2,1)S(1)}, bf16[432,128]{1,0:T(8,128)(2,1)S(1)}, u32[]{:S(2)}, u32[]{:S(2)}) collective-permute-start(bf16[432,128]{1,0:T(8,128)(2,1)S(1)} %dynamic-slice_convert_fusion.2), channel_id=1, source_target_pairs={{0,16},{8,24},{16,0},{24,8},{1,17},{9,25},{17,1},{25,9},{2,18},{10... | collective-permute-start | bytes 331784 | tf_op jit(solution)/shard_map/ppermute | solution.py:30
  32.3 1.4 %collective-permute-done.23 = bf16[432,128]{1,0:T(8,128)(2,1)S(1)} collective-permute-done((bf16[432,128]{1,0:T(8,128)(2,1)S(1)}, bf16[432,128]{1,0:T(8,128)(2,1)S(1)}, u32[]{:S(2)}, u32[]{:S(2)}) %collective-permute-start.23) | collective-permute-done | bytes 110624 | tf_op jit(solution)/shard_map/ppermute | solution.py:30
  33.8 1.2 %collective-permute-start.24 = (bf16[216,128]{1,0:T(8,128)(2,1)S(1)}, bf16[216,128]{1,0:T(8,128)(2,1)S(1)}, u32[]{:S(2)}, u32[]{:S(2)}) collective-permute-start(bf16[216,128]{1,0:T(8,128)(2,1)S(1)} %dynamic-slice_convert_fusion.3), channel_id=1, source_target_pairs={{0,16},{8,24},{16,0},{24,8},{1,17},{9,25},{17,1},{25,9},{2,18},{10... | collective-permute-start | bytes 165896 | tf_op jit(solution)/shard_map/ppermute | solution.py:30
  35.0 0.3 collective-permute-done.15
  35.4 1.5 %collective-permute-start.16 = (bf16[216,128]{1,0:T(8,128)(2,1)S(1)}, bf16[216,128]{1,0:T(8,128)(2,1)S(1)}, u32[]{:S(2)}, u32[]{:S(2)}) collective-permute-start(bf16[216,128]{1,0:T(8,128)(2,1)S(1)} %dynamic-slice_convert_fusion.4), channel_id=1, source_target_pairs={{0,2},{1,3},{2,0},{3,1},{4,6},{5,7},{6,4},{7,5},{8,10},{9,11},{10,... | collective-permute-start | bytes 165896 | tf_op jit(solution)/shard_map/ppermute | solution.py:30
  36.9 0.7 %collective-permute-start.8 = (bf16[216,128]{1,0:T(8,128)(2,1)S(1)}, bf16[216,128]{1,0:T(8,128)(2,1)S(1)}, u32[]{:S(2)}, u32[]{:S(2)}) collective-permute-start(bf16[216,128]{1,0:T(8,128)(2,1)S(1)} %dynamic-slice_convert_fusion.5), channel_id=1, source_target_pairs={{0,1},{1,0},{2,3},{3,2},{4,5},{5,4},{6,7},{7,6},{8,9},{9,8},{10,11... | collective-permute-start | bytes 165896 | tf_op jit(solution)/shard_map/ppermute | solution.py:30
  37.6 0.4 collective-permute-done.24
  38.1 1.1 %collective-permute-start.25 = (bf16[108,128]{1,0:T(8,128)(2,1)S(1)}, bf16[108,128]{1,0:T(8,128)(2,1)S(1)}, u32[]{:S(2)}, u32[]{:S(2)}) collective-permute-start(bf16[108,128]{1,0:T(8,128)(2,1)S(1)} %dynamic-slice_convert_fusion.6), channel_id=1, source_target_pairs={{0,1},{1,0},{2,3},{3,2},{4,5},{5,4},{6,7},{7,6},{8,9},{9,8},{10,11... | collective-permute-start | bytes 82952 | tf_op jit(solution)/shard_map/ppermute | solution.py:30
  39.1 0.5 collective-permute-done.16
  39.7 1.2 %collective-permute-start.17 = (bf16[108,128]{1,0:T(8,128)(2,1)S(1)}, bf16[108,128]{1,0:T(8,128)(2,1)S(1)}, u32[]{:S(2)}, u32[]{:S(2)}) collective-permute-start(bf16[108,128]{1,0:T(8,128)(2,1)S(1)} %dynamic-slice_convert_fusion.7), channel_id=1, source_target_pairs={{0,16},{8,24},{16,0},{24,8},{1,17},{9,25},{17,1},{25,9},{2,18},{10... | collective-permute-start | bytes 82952 | tf_op jit(solution)/shard_map/ppermute | solution.py:30
  40.9 0.3 collective-permute-done.8
  41.2 0.9 %collective-permute-start.9 = (bf16[108,128]{1,0:T(8,128)(2,1)S(1)}, bf16[108,128]{1,0:T(8,128)(2,1)S(1)}, u32[]{:S(2)}, u32[]{:S(2)}) collective-permute-start(bf16[108,128]{1,0:T(8,128)(2,1)S(1)} %dynamic-slice_convert_fusion.8), channel_id=1, source_target_pairs={{0,2},{1,3},{2,0},{3,1},{4,6},{5,7},{6,4},{7,5},{8,10},{9,11},{10,... | collective-permute-start | bytes 82952 | tf_op jit(solution)/shard_map/ppermute | solution.py:30
  42.2 2.7 %collective-permute-start.26 = (bf16[108,128]{1,0:T(8,128)(2,1)S(1)}, bf16[108,128]{1,0:T(8,128)(2,1)S(1)}, u32[]{:S(2)}, u32[]{:S(2)}) collective-permute-start(bf16[108,128]{1,0:T(8,128)(2,1)S(1)} %add_convert_fusion.1), channel_id=1, source_target_pairs={{0,4},{1,5},{2,6},{3,7},{4,0},{5,1},{6,2},{7,3},{8,12},{9,13},{10,... | collective-permute-start | bytes 82952 | tf_op jit(solution)/shard_map/ppermute | solution.py:30
  44.9 1.4 %collective-permute-start.18 = (bf16[108,128]{1,0:T(8,128)(2,1)S(1)}, bf16[108,128]{1,0:T(8,128)(2,1)S(1)}, u32[]{:S(2)}, u32[]{:S(2)}) collective-permute-start(bf16[108,128]{1,0:T(8,128)(2,1)S(1)} %add_convert_fusion.3), channel_id=1, source_target_pairs={{0,4},{1,5},{2,6},{3,7},{4,0},{5,1},{6,2},{7,3},{8,12},{9,13},{10,... | collective-permute-start | bytes 82952 | tf_op jit(solution)/shard_map/ppermute | solution.py:30
  46.3 1.6 %collective-permute-start.10 = (bf16[108,128]{1,0:T(8,128)(2,1)S(1)}, bf16[108,128]{1,0:T(8,128)(2,1)S(1)}, u32[]{:S(2)}, u32[]{:S(2)}) collective-permute-start(bf16[108,128]{1,0:T(8,128)(2,1)S(1)} %add_convert_fusion.5), channel_id=1, source_target_pairs={{0,4},{1,5},{2,6},{3,7},{4,0},{5,1},{6,2},{7,3},{8,12},{9,13},{10,... | collective-permute-start | bytes 82952 | tf_op jit(solution)/shard_map/ppermute | solution.py:30
  48.0 1.2 %collective-permute-start.27 = (bf16[108,128]{1,0:T(8,128)(2,1)S(1)}, bf16[108,128]{1,0:T(8,128)(2,1)S(1)}, u32[]{:S(2)}, u32[]{:S(2)}) collective-permute-start(bf16[108,128]{1,0:T(8,128)(2,1)S(1)} %add_convert_fusion), channel_id=1, source_target_pairs={{0,1},{1,0},{2,3},{3,2},{4,5},{5,4},{6,7},{7,6},{8,9},{9,8},{10,11... | collective-permute-start | bytes 82952 | tf_op jit(solution)/shard_map/ppermute | solution.py:30
  49.1 0.6 collective-permute-done.18
  49.7 1.2 %collective-permute-start.19 = (bf16[108,128]{1,0:T(8,128)(2,1)S(1)}, bf16[108,128]{1,0:T(8,128)(2,1)S(1)}, u32[]{:S(2)}, u32[]{:S(2)}) collective-permute-start(bf16[108,128]{1,0:T(8,128)(2,1)S(1)} %add_convert_fusion.2), channel_id=1, source_target_pairs={{0,16},{8,24},{16,0},{24,8},{1,17},{9,25},{17,1},{25,9},{2,18},{10... | collective-permute-start | bytes 82952 | tf_op jit(solution)/shard_map/ppermute | solution.py:30
  50.9 0.3 collective-permute-done.10
  51.2 1.6 %collective-permute-start.11 = (bf16[108,128]{1,0:T(8,128)(2,1)S(1)}, bf16[108,128]{1,0:T(8,128)(2,1)S(1)}, u32[]{:S(2)}, u32[]{:S(2)}) collective-permute-start(bf16[108,128]{1,0:T(8,128)(2,1)S(1)} %add_convert_fusion.4), channel_id=1, source_target_pairs={{0,2},{1,3},{2,0},{3,1},{4,6},{5,7},{6,4},{7,5},{8,10},{9,11},{10,... | collective-permute-start | bytes 82952 | tf_op jit(solution)/shard_map/ppermute | solution.py:30
  52.8 0.8 %collective-permute-start.28 = (bf16[216,128]{1,0:T(8,128)(2,1)S(1)}, bf16[216,128]{1,0:T(8,128)(2,1)S(1)}, u32[]{:S(2)}, u32[]{:S(2)}) collective-permute-start(bf16[216,128]{1,0:T(8,128)(2,1)S(1)} %maximum_select_fusion.8), channel_id=1, source_target_pairs={{0,16},{8,24},{16,0},{24,8},{1,17},{9,25},{17,1},{25,9},{2,18},{10... | collective-permute-start | bytes 165896 | tf_op jit(solution)/shard_map/ppermute | solution.py:30
  53.7 1.6 %collective-permute-start.20 = (bf16[216,128]{1,0:T(8,128)(2,1)S(1)}, bf16[216,128]{1,0:T(8,128)(2,1)S(1)}, u32[]{:S(2)}, u32[]{:S(2)}) collective-permute-start(bf16[216,128]{1,0:T(8,128)(2,1)S(1)} %maximum_select_fusion.7), channel_id=1, source_target_pairs={{0,2},{1,3},{2,0},{3,1},{4,6},{5,7},{6,4},{7,5},{8,10},{9,11},{10,... | collective-permute-start | bytes 165896 | tf_op jit(solution)/shard_map/ppermute | solution.py:30
  55.3 0.1 collective-permute-done.11
  55.5 0.7 collective-permute-start.12
  56.1 1.1 %collective-permute-done.28 = bf16[216,128]{1,0:T(8,128)(2,1)S(1)} collective-permute-done((bf16[216,128]{1,0:T(8,128)(2,1)S(1)}, bf16[216,128]{1,0:T(8,128)(2,1)S(1)}, u32[]{:S(2)}, u32[]{:S(2)}) %collective-permute-start.28) | collective-permute-done | bytes 55328 | tf_op jit(solution)/shard_map/ppermute | solution.py:30
  57.3 1.0 %collective-permute-start.29 = (bf16[432,128]{1,0:T(8,128)(2,1)S(1)}, bf16[432,128]{1,0:T(8,128)(2,1)S(1)}, u32[]{:S(2)}, u32[]{:S(2)}) collective-permute-start(bf16[432,128]{1,0:T(8,128)(2,1)S(1)} %maximum_select_fusion.5), channel_id=1, source_target_pairs={{0,2},{1,3},{2,0},{3,1},{4,6},{5,7},{6,4},{7,5},{8,10},{9,11},{10,... | collective-permute-start | bytes 331784 | tf_op jit(solution)/shard_map/ppermute | solution.py:30
  58.3 1.2 %collective-permute-start.21 = (bf16[432,128]{1,0:T(8,128)(2,1)S(1)}, bf16[432,128]{1,0:T(8,128)(2,1)S(1)}, u32[]{:S(2)}, u32[]{:S(2)}) collective-permute-start(bf16[432,128]{1,0:T(8,128)(2,1)S(1)} %maximum_select_fusion.4), channel_id=1, source_target_pairs={{0,1},{1,0},{2,3},{3,2},{4,5},{5,4},{6,7},{7,6},{8,9},{9,8},{10,11... | collective-permute-start | bytes 331784 | tf_op jit(solution)/shard_map/ppermute | solution.py:30
  59.5 0.2 collective-permute-done.12
  59.7 1.3 %collective-permute-start.13 = (bf16[432,128]{1,0:T(8,128)(2,1)S(1)}, bf16[432,128]{1,0:T(8,128)(2,1)S(1)}, u32[]{:S(2)}, u32[]{:S(2)}) collective-permute-start(bf16[432,128]{1,0:T(8,128)(2,1)S(1)} %maximum_select_fusion.3), channel_id=1, source_target_pairs={{0,16},{8,24},{16,0},{24,8},{1,17},{9,25},{17,1},{25,9},{2,18},{10... | collective-permute-start | bytes 331784 | tf_op jit(solution)/shard_map/ppermute | solution.py:30
  61.0 1.1 %collective-permute-done.29 = bf16[432,128]{1,0:T(8,128)(2,1)S(1)} collective-permute-done((bf16[432,128]{1,0:T(8,128)(2,1)S(1)}, bf16[432,128]{1,0:T(8,128)(2,1)S(1)}, u32[]{:S(2)}, u32[]{:S(2)}) %collective-permute-start.29) | collective-permute-done | bytes 110624 | tf_op jit(solution)/shard_map/ppermute | solution.py:30
  62.3 0.9 %collective-permute-done.21 = bf16[432,128]{1,0:T(8,128)(2,1)S(1)} collective-permute-done((bf16[432,128]{1,0:T(8,128)(2,1)S(1)}, bf16[432,128]{1,0:T(8,128)(2,1)S(1)}, u32[]{:S(2)}, u32[]{:S(2)}) %collective-permute-start.21) | collective-permute-done | bytes 110624 | tf_op jit(solution)/shard_map/ppermute | solution.py:30
  63.3 1.2 %collective-permute-done.13 = bf16[432,128]{1,0:T(8,128)(2,1)S(1)} collective-permute-done((bf16[432,128]{1,0:T(8,128)(2,1)S(1)}, bf16[432,128]{1,0:T(8,128)(2,1)S(1)}, u32[]{:S(2)}, u32[]{:S(2)}) %collective-permute-start.13) | collective-permute-done | bytes 110624 | tf_op jit(solution)/shard_map/ppermute | solution.py:30
  64.8 1.4 %collective-permute-done.30.refs_3_ = bf16[864,128]{1,0:T(8,128)(2,1)S(1)} collective-permute-done((bf16[864,128]{1,0:T(8,128)(2,1)S(1)}, bf16[864,128]{1,0:T(8,128)(2,1)S(1)}, u32[]{:S(2)}, u32[]{:S(2)}) %collective-permute-start.30) | collective-permute-done | bytes 221216 | tf_op jit(solution)/shard_map/ppermute | solution.py:30
  66.1 1.9 %normalize.1 = (f32[27,128,128]{2,1,0:T(8,128)}, f32[27,64,128]{2,1,0:T(8,128)}) custom-call(s32[1]{0:T(128)} %bitcast.odd.side, bf16[864,128]{1,0:T(8,128)(2,1)S(1)} %maximum_select_fusion.refs_0_, bf16[864,128]{1,0:T(8,128)(2,1)S(1)} %maximum_select_fusion.1.refs_1_, bf16[864,128]{1,0:T(8,128)(2,1)S(1)} %maximum_select_fusion.2.refs_2_, ...), custom_call_target="tpu_custom_call" | custom-call | tf_op jit(solution)/shard_map/normalize/pallas_call | solution.py:455
  (62 shorter events, 1.6 us)
Async XLA Ops:
  0.6 11.1 %copy-start = (f32[128]{0:T(128)S(1)}, f32[128]{0:T(128)}, u32[]{:S(2)}) copy-start(f32[128]{0:T(128)} %param.10) | copy-start | bytes 1540
  0.6 11.1 %copy-start.1 = (f32[128]{0:T(128)S(1)}, f32[128]{0:T(128)}, u32[]{:S(2)}) copy-start(f32[128]{0:T(128)} %param.12) | copy-start | bytes 1540
  1.8 5.6 %collective-permute-start = (bf16[336,128]{1,0:T(8,128)(2,1)S(1)}, bf16[336,128]{1,0:T(8,128)(2,1)S(1)}, u32[]{:S(2)}, u32[]{:S(2)}) collective-permute-start(bf16[336,128]{1,0:T(8,128)(2,1)S(1)} %get-tuple-element.25), channel_id=1, source_target_pairs={{0,1},{1,0},{2,3},{3,2},{4,5},{5,4},{6,7},{7,6},{8,9},{9,8},{10,11... | collective-permute-start | bytes 258056 | tf_op jit(solution)/shard_map/ppermute | solution.py:77
  4.8 2.5 %collective-permute-start.1 = (bf16[336,128]{1,0:T(8,128)(2,1)S(1)}, bf16[336,128]{1,0:T(8,128)(2,1)S(1)}, u32[]{:S(2)}, u32[]{:S(2)}) collective-permute-start(bf16[336,128]{1,0:T(8,128)(2,1)S(1)} %get-tuple-element.26), channel_id=1, source_target_pairs={{1,2},{3,4},{5,6},{2,1},{4,3},{6,5},{9,10},{11,12},{13,14},{10,9},... | collective-permute-start | bytes 258056 | tf_op jit(solution)/shard_map/ppermute | solution.py:76
  5.5 6.2 %collective-permute-start.2 = (bf16[656,128]{1,0:T(8,128)(2,1)S(1)}, bf16[656,128]{1,0:T(8,128)(2,1)S(1)}, u32[]{:S(2)}, u32[]{:S(2)}) collective-permute-start(bf16[656,128]{1,0:T(8,128)(2,1)S(1)} %get-tuple-element.29), channel_id=1, source_target_pairs={{0,8},{8,0},{16,24},{24,16},{1,9},{9,1},{17,25},{25,17},{2,10},{10... | collective-permute-start | bytes 503816 | tf_op jit(solution)/shard_map/ppermute | solution.py:77
  5.6 6.1 %collective-permute-start.3 = (bf16[656,128]{1,0:T(8,128)(2,1)S(1)}, bf16[656,128]{1,0:T(8,128)(2,1)S(1)}, u32[]{:S(2)}, u32[]{:S(2)}) collective-permute-start(bf16[656,128]{1,0:T(8,128)(2,1)S(1)} %get-tuple-element.30), channel_id=1, source_target_pairs={{8,16},{16,8},{9,17},{17,9},{10,18},{18,10},{11,19},{19,11},{12,20... | collective-permute-start | bytes 503816 | tf_op jit(solution)/shard_map/ppermute | solution.py:76
  7.4 4.3 %collective-permute-start.4 = (bf16[384,128]{1,0:T(8,128)(2,1)S(1)}, bf16[384,128]{1,0:T(8,128)(2,1)S(1)}, u32[]{:S(2)}, u32[]{:S(2)}) collective-permute-start(bf16[384,128]{1,0:T(8,128)(2,1)S(1)} %get-tuple-element.31._), channel_id=1, source_target_pairs={{0,8},{8,0},{16,24},{24,16},{1,9},{9,1},{17,25},{25,17},{2,10},{10... | collective-permute-start | bytes 294920 | tf_op jit(solution)/shard_map/ppermute | solution.py:77
  9.2 2.5 %collective-permute-start.5 = (bf16[384,128]{1,0:T(8,128)(2,1)S(1)}, bf16[384,128]{1,0:T(8,128)(2,1)S(1)}, u32[]{:S(2)}, u32[]{:S(2)}) collective-permute-start(bf16[384,128]{1,0:T(8,128)(2,1)S(1)} %get-tuple-element.32), channel_id=1, source_target_pairs={{8,16},{16,8},{9,17},{17,9},{10,18},{18,10},{11,19},{19,11},{12,20... | collective-permute-start | bytes 294920 | tf_op jit(solution)/shard_map/ppermute | solution.py:76
  20.4 4.6 %collective-permute-start.22 = (bf16[864,128]{1,0:T(8,128)(2,1)S(1)}, bf16[864,128]{1,0:T(8,128)(2,1)S(1)}, u32[]{:S(2)}, u32[]{:S(2)}) collective-permute-start(bf16[864,128]{1,0:T(8,128)(2,1)S(1)} %bitcast.17), channel_id=1, source_target_pairs={{0,8},{8,0},{16,24},{24,16},{1,9},{9,1},{17,25},{25,17},{2,10},{10... | collective-permute-start | bytes 663560 | tf_op jit(solution)/shard_map/ppermute | solution.py:30
  23.9 6.3 %collective-permute-start.14 = (bf16[864,128]{1,0:T(8,128)(2,1)S(1)}, bf16[864,128]{1,0:T(8,128)(2,1)S(1)}, u32[]{:S(2)}, u32[]{:S(2)}) collective-permute-start(bf16[864,128]{1,0:T(8,128)(2,1)S(1)} %bitcast.16), channel_id=1, source_target_pairs={{0,8},{8,0},{16,24},{24,16},{1,9},{9,1},{17,25},{25,17},{2,10},{10... | collective-permute-start | bytes 663560 | tf_op jit(solution)/shard_map/ppermute | solution.py:30
  24.0 7.2 %collective-permute-start.6 = (bf16[864,128]{1,0:T(8,128)(2,1)S(1)}, bf16[864,128]{1,0:T(8,128)(2,1)S(1)}, u32[]{:S(2)}, u32[]{:S(2)}) collective-permute-start(bf16[864,128]{1,0:T(8,128)(2,1)S(1)} %bitcast.15), channel_id=1, source_target_pairs={{0,8},{8,0},{16,24},{24,16},{1,9},{9,1},{17,25},{25,17},{2,10},{10... | collective-permute-start | bytes 663560 | tf_op jit(solution)/shard_map/ppermute | solution.py:30
  25.0 8.7 %collective-permute-start.23 = (bf16[432,128]{1,0:T(8,128)(2,1)S(1)}, bf16[432,128]{1,0:T(8,128)(2,1)S(1)}, u32[]{:S(2)}, u32[]{:S(2)}) collective-permute-start(bf16[432,128]{1,0:T(8,128)(2,1)S(1)} %dynamic-slice_convert_fusion), channel_id=1, source_target_pairs={{0,2},{1,3},{2,0},{3,1},{4,6},{5,7},{6,4},{7,5},{8,10},{9,11},{10,... | collective-permute-start | bytes 331784 | tf_op jit(solution)/shard_map/ppermute | solution.py:30
  30.2 5.1 %collective-permute-start.15 = (bf16[432,128]{1,0:T(8,128)(2,1)S(1)}, bf16[432,128]{1,0:T(8,128)(2,1)S(1)}, u32[]{:S(2)}, u32[]{:S(2)}) collective-permute-start(bf16[432,128]{1,0:T(8,128)(2,1)S(1)} %dynamic-slice_convert_fusion.1), channel_id=1, source_target_pairs={{0,1},{1,0},{2,3},{3,2},{4,5},{5,4},{6,7},{7,6},{8,9},{9,8},{10,11... | collective-permute-start | bytes 331784 | tf_op jit(solution)/shard_map/ppermute | solution.py:30
  31.2 5.7 %collective-permute-start.7 = (bf16[432,128]{1,0:T(8,128)(2,1)S(1)}, bf16[432,128]{1,0:T(8,128)(2,1)S(1)}, u32[]{:S(2)}, u32[]{:S(2)}) collective-permute-start(bf16[432,128]{1,0:T(8,128)(2,1)S(1)} %dynamic-slice_convert_fusion.2), channel_id=1, source_target_pairs={{0,16},{8,24},{16,0},{24,8},{1,17},{9,25},{17,1},{25,9},{2,18},{10... | collective-permute-start | bytes 331784 | tf_op jit(solution)/shard_map/ppermute | solution.py:30
  33.8 4.2 %collective-permute-start.24 = (bf16[216,128]{1,0:T(8,128)(2,1)S(1)}, bf16[216,128]{1,0:T(8,128)(2,1)S(1)}, u32[]{:S(2)}, u32[]{:S(2)}) collective-permute-start(bf16[216,128]{1,0:T(8,128)(2,1)S(1)} %dynamic-slice_convert_fusion.3), channel_id=1, source_target_pairs={{0,16},{8,24},{16,0},{24,8},{1,17},{9,25},{17,1},{25,9},{2,18},{10... | collective-permute-start | bytes 165896 | tf_op jit(solution)/shard_map/ppermute | solution.py:30
  35.4 4.2 %collective-permute-start.16 = (bf16[216,128]{1,0:T(8,128)(2,1)S(1)}, bf16[216,128]{1,0:T(8,128)(2,1)S(1)}, u32[]{:S(2)}, u32[]{:S(2)}) collective-permute-start(bf16[216,128]{1,0:T(8,128)(2,1)S(1)} %dynamic-slice_convert_fusion.4), channel_id=1, source_target_pairs={{0,2},{1,3},{2,0},{3,1},{4,6},{5,7},{6,4},{7,5},{8,10},{9,11},{10,... | collective-permute-start | bytes 165896 | tf_op jit(solution)/shard_map/ppermute | solution.py:30
  36.9 4.2 %collective-permute-start.8 = (bf16[216,128]{1,0:T(8,128)(2,1)S(1)}, bf16[216,128]{1,0:T(8,128)(2,1)S(1)}, u32[]{:S(2)}, u32[]{:S(2)}) collective-permute-start(bf16[216,128]{1,0:T(8,128)(2,1)S(1)} %dynamic-slice_convert_fusion.5), channel_id=1, source_target_pairs={{0,1},{1,0},{2,3},{3,2},{4,5},{5,4},{6,7},{7,6},{8,9},{9,8},{10,11... | collective-permute-start | bytes 165896 | tf_op jit(solution)/shard_map/ppermute | solution.py:30
  38.1 4.1 %collective-permute-start.25 = (bf16[108,128]{1,0:T(8,128)(2,1)S(1)}, bf16[108,128]{1,0:T(8,128)(2,1)S(1)}, u32[]{:S(2)}, u32[]{:S(2)}) collective-permute-start(bf16[108,128]{1,0:T(8,128)(2,1)S(1)} %dynamic-slice_convert_fusion.6), channel_id=1, source_target_pairs={{0,1},{1,0},{2,3},{3,2},{4,5},{5,4},{6,7},{7,6},{8,9},{9,8},{10,11... | collective-permute-start | bytes 82952 | tf_op jit(solution)/shard_map/ppermute | solution.py:30
  39.7 5.2 %collective-permute-start.17 = (bf16[108,128]{1,0:T(8,128)(2,1)S(1)}, bf16[108,128]{1,0:T(8,128)(2,1)S(1)}, u32[]{:S(2)}, u32[]{:S(2)}) collective-permute-start(bf16[108,128]{1,0:T(8,128)(2,1)S(1)} %dynamic-slice_convert_fusion.7), channel_id=1, source_target_pairs={{0,16},{8,24},{16,0},{24,8},{1,17},{9,25},{17,1},{25,9},{2,18},{10... | collective-permute-start | bytes 82952 | tf_op jit(solution)/shard_map/ppermute | solution.py:30
  41.2 5.1 %collective-permute-start.9 = (bf16[108,128]{1,0:T(8,128)(2,1)S(1)}, bf16[108,128]{1,0:T(8,128)(2,1)S(1)}, u32[]{:S(2)}, u32[]{:S(2)}) collective-permute-start(bf16[108,128]{1,0:T(8,128)(2,1)S(1)} %dynamic-slice_convert_fusion.8), channel_id=1, source_target_pairs={{0,2},{1,3},{2,0},{3,1},{4,6},{5,7},{6,4},{7,5},{8,10},{9,11},{10,... | collective-permute-start | bytes 82952 | tf_op jit(solution)/shard_map/ppermute | solution.py:30
  42.2 5.8 %collective-permute-start.26 = (bf16[108,128]{1,0:T(8,128)(2,1)S(1)}, bf16[108,128]{1,0:T(8,128)(2,1)S(1)}, u32[]{:S(2)}, u32[]{:S(2)}) collective-permute-start(bf16[108,128]{1,0:T(8,128)(2,1)S(1)} %add_convert_fusion.1), channel_id=1, source_target_pairs={{0,4},{1,5},{2,6},{3,7},{4,0},{5,1},{6,2},{7,3},{8,12},{9,13},{10,... | collective-permute-start | bytes 82952 | tf_op jit(solution)/shard_map/ppermute | solution.py:30
  44.9 4.8 %collective-permute-start.18 = (bf16[108,128]{1,0:T(8,128)(2,1)S(1)}, bf16[108,128]{1,0:T(8,128)(2,1)S(1)}, u32[]{:S(2)}, u32[]{:S(2)}) collective-permute-start(bf16[108,128]{1,0:T(8,128)(2,1)S(1)} %add_convert_fusion.3), channel_id=1, source_target_pairs={{0,4},{1,5},{2,6},{3,7},{4,0},{5,1},{6,2},{7,3},{8,12},{9,13},{10,... | collective-permute-start | bytes 82952 | tf_op jit(solution)/shard_map/ppermute | solution.py:30
  46.3 4.9 %collective-permute-start.10 = (bf16[108,128]{1,0:T(8,128)(2,1)S(1)}, bf16[108,128]{1,0:T(8,128)(2,1)S(1)}, u32[]{:S(2)}, u32[]{:S(2)}) collective-permute-start(bf16[108,128]{1,0:T(8,128)(2,1)S(1)} %add_convert_fusion.5), channel_id=1, source_target_pairs={{0,4},{1,5},{2,6},{3,7},{4,0},{5,1},{6,2},{7,3},{8,12},{9,13},{10,... | collective-permute-start | bytes 82952 | tf_op jit(solution)/shard_map/ppermute | solution.py:30
  48.0 4.8 %collective-permute-start.27 = (bf16[108,128]{1,0:T(8,128)(2,1)S(1)}, bf16[108,128]{1,0:T(8,128)(2,1)S(1)}, u32[]{:S(2)}, u32[]{:S(2)}) collective-permute-start(bf16[108,128]{1,0:T(8,128)(2,1)S(1)} %add_convert_fusion), channel_id=1, source_target_pairs={{0,1},{1,0},{2,3},{3,2},{4,5},{5,4},{6,7},{7,6},{8,9},{9,8},{10,11... | collective-permute-start | bytes 82952 | tf_op jit(solution)/shard_map/ppermute | solution.py:30
  49.7 3.9 %collective-permute-start.19 = (bf16[108,128]{1,0:T(8,128)(2,1)S(1)}, bf16[108,128]{1,0:T(8,128)(2,1)S(1)}, u32[]{:S(2)}, u32[]{:S(2)}) collective-permute-start(bf16[108,128]{1,0:T(8,128)(2,1)S(1)} %add_convert_fusion.2), channel_id=1, source_target_pairs={{0,16},{8,24},{16,0},{24,8},{1,17},{9,25},{17,1},{25,9},{2,18},{10... | collective-permute-start | bytes 82952 | tf_op jit(solution)/shard_map/ppermute | solution.py:30
  51.2 4.2 %collective-permute-start.11 = (bf16[108,128]{1,0:T(8,128)(2,1)S(1)}, bf16[108,128]{1,0:T(8,128)(2,1)S(1)}, u32[]{:S(2)}, u32[]{:S(2)}) collective-permute-start(bf16[108,128]{1,0:T(8,128)(2,1)S(1)} %add_convert_fusion.4), channel_id=1, source_target_pairs={{0,2},{1,3},{2,0},{3,1},{4,6},{5,7},{6,4},{7,5},{8,10},{9,11},{10,... | collective-permute-start | bytes 82952 | tf_op jit(solution)/shard_map/ppermute | solution.py:30
  52.8 4.4 %collective-permute-start.28 = (bf16[216,128]{1,0:T(8,128)(2,1)S(1)}, bf16[216,128]{1,0:T(8,128)(2,1)S(1)}, u32[]{:S(2)}, u32[]{:S(2)}) collective-permute-start(bf16[216,128]{1,0:T(8,128)(2,1)S(1)} %maximum_select_fusion.8), channel_id=1, source_target_pairs={{0,16},{8,24},{16,0},{24,8},{1,17},{9,25},{17,1},{25,9},{2,18},{10... | collective-permute-start | bytes 165896 | tf_op jit(solution)/shard_map/ppermute | solution.py:30
  53.7 4.6 %collective-permute-start.20 = (bf16[216,128]{1,0:T(8,128)(2,1)S(1)}, bf16[216,128]{1,0:T(8,128)(2,1)S(1)}, u32[]{:S(2)}, u32[]{:S(2)}) collective-permute-start(bf16[216,128]{1,0:T(8,128)(2,1)S(1)} %maximum_select_fusion.7), channel_id=1, source_target_pairs={{0,2},{1,3},{2,0},{3,1},{4,6},{5,7},{6,4},{7,5},{8,10},{9,11},{10,... | collective-permute-start | bytes 165896 | tf_op jit(solution)/shard_map/ppermute | solution.py:30
  55.5 4.2 %collective-permute-start.12 = (bf16[216,128]{1,0:T(8,128)(2,1)S(1)}, bf16[216,128]{1,0:T(8,128)(2,1)S(1)}, u32[]{:S(2)}, u32[]{:S(2)}) collective-permute-start(bf16[216,128]{1,0:T(8,128)(2,1)S(1)} %maximum_select_fusion.6), channel_id=1, source_target_pairs={{0,1},{1,0},{2,3},{3,2},{4,5},{5,4},{6,7},{7,6},{8,9},{9,8},{10,11... | collective-permute-start | bytes 165896 | tf_op jit(solution)/shard_map/ppermute | solution.py:30
  57.3 4.8 %collective-permute-start.29 = (bf16[432,128]{1,0:T(8,128)(2,1)S(1)}, bf16[432,128]{1,0:T(8,128)(2,1)S(1)}, u32[]{:S(2)}, u32[]{:S(2)}) collective-permute-start(bf16[432,128]{1,0:T(8,128)(2,1)S(1)} %maximum_select_fusion.5), channel_id=1, source_target_pairs={{0,2},{1,3},{2,0},{3,1},{4,6},{5,7},{6,4},{7,5},{8,10},{9,11},{10,... | collective-permute-start | bytes 331784 | tf_op jit(solution)/shard_map/ppermute | solution.py:30
  58.3 4.8 %collective-permute-start.21 = (bf16[432,128]{1,0:T(8,128)(2,1)S(1)}, bf16[432,128]{1,0:T(8,128)(2,1)S(1)}, u32[]{:S(2)}, u32[]{:S(2)}) collective-permute-start(bf16[432,128]{1,0:T(8,128)(2,1)S(1)} %maximum_select_fusion.4), channel_id=1, source_target_pairs={{0,1},{1,0},{2,3},{3,2},{4,5},{5,4},{6,7},{7,6},{8,9},{9,8},{10,11... | collective-permute-start | bytes 331784 | tf_op jit(solution)/shard_map/ppermute | solution.py:30
  59.7 4.8 %collective-permute-start.13 = (bf16[432,128]{1,0:T(8,128)(2,1)S(1)}, bf16[432,128]{1,0:T(8,128)(2,1)S(1)}, u32[]{:S(2)}, u32[]{:S(2)}) collective-permute-start(bf16[432,128]{1,0:T(8,128)(2,1)S(1)} %maximum_select_fusion.3), channel_id=1, source_target_pairs={{0,16},{8,24},{16,0},{24,8},{1,17},{9,25},{17,1},{25,9},{2,18},{10... | collective-permute-start | bytes 331784 | tf_op jit(solution)/shard_map/ppermute | solution.py:30
  62.2 2.5 %collective-permute-start.32 = (bf16[864,128]{1,0:T(8,128)(2,1)S(1)}, bf16[864,128]{1,0:T(8,128)(2,1)S(1)}, u32[]{:S(2)}, u32[]{:S(2)}) collective-permute-start(bf16[864,128]{1,0:T(8,128)(2,1)S(1)} %maximum_select_fusion.2.refs_2_), channel_id=1, source_target_pairs={{0,8},{8,0},{16,24},{24,16},{1,9},{9,1},{17,25},{25,17},{2,10},{10... | collective-permute-start | bytes 663560 | tf_op jit(solution)/shard_map/ppermute | solution.py:30
  63.2 1.5 %collective-permute-start.31 = (bf16[864,128]{1,0:T(8,128)(2,1)S(1)}, bf16[864,128]{1,0:T(8,128)(2,1)S(1)}, u32[]{:S(2)}, u32[]{:S(2)}) collective-permute-start(bf16[864,128]{1,0:T(8,128)(2,1)S(1)} %maximum_select_fusion.1.refs_1_), channel_id=1, source_target_pairs={{0,8},{8,0},{16,24},{24,16},{1,9},{9,1},{17,25},{25,17},{2,10},{10... | collective-permute-start | bytes 663560 | tf_op jit(solution)/shard_map/ppermute | solution.py:30
  64.6 1.5 %collective-permute-start.30 = (bf16[864,128]{1,0:T(8,128)(2,1)S(1)}, bf16[864,128]{1,0:T(8,128)(2,1)S(1)}, u32[]{:S(2)}, u32[]{:S(2)}) collective-permute-start(bf16[864,128]{1,0:T(8,128)(2,1)S(1)} %maximum_select_fusion.refs_0_), channel_id=1, source_target_pairs={{0,8},{8,0},{16,24},{24,16},{1,9},{9,1},{17,25},{25,17},{2,10},{10... | collective-permute-start | bytes 663560 | tf_op jit(solution)/shard_map/ppermute | solution.py:30

commit v9 on v8

--- a/solution.py
+++ b/solution.py
@@ -358,32 +358,48 @@
     show.wait()
 
 
-def norm_body(chains, side, *refs):
+def rows_of_chains(refs, start, count):
+    parts = []
+    for ref in refs:
+        low, high = max(start, 0), min(start + count, ref.shape[0])
+        if low < high:
+            parts.append(ref[low:high])
+        start -= ref.shape[0]
+    return jnp.concatenate(parts, axis=0).astype(F32)
+
+
+def squares_of(refs, taps, rows_of):
+    totals = [jnp.zeros((8, LANES), F32) for _ in rows_of]
+    at = 0
+    for _ in range(taps):
+        for i, count in enumerate(rows_of):
+            value = rows_of_chains(refs, at, count)
+            totals[i] += jnp.sum((value * value).reshape(-1, 8, LANES), axis=0)
+            at += count
+    return totals
+
+
+def squares_body(taps, rows_of, *refs):
+    for i, total in enumerate(squares_of(refs[:-1], taps, rows_of)):
+        refs[-1][i] = total
+
+
+def norm_body(chains, side, own_squares, *refs):
     own, other = refs[:chains], refs[chains : 2 * chains]
     out2, out1, held2, held1, sems = refs[2 * chains :]
     taps = out2.shape[0]
     rows_of = held2.shape[1] // 2, held1.shape[1] // 2
     stride = sum(rows_of)
 
-    def rows(refs, start, count):
-        parts = []
-        for ref in refs:
-            low, high = max(start, 0), min(start + count, ref.shape[0])
-            if low < high:
-                parts.append(ref[low:high])
-            start -= ref.shape[0]
-        return jnp.concatenate(parts, axis=0).astype(F32)
+    rows = rows_of_chains
 
     def spans():
         for t in range(taps):
             for i, at in ((0, t * stride), (1, t * stride + rows_of[0])):
                 yield t, i, at
 
-    squares = [jnp.zeros((8, LANES), F32), jnp.zeros((8, LANES), F32)]
-    for t, i, at in spans():
-        for pair in (own, other):
-            value = rows(pair, at, rows_of[i])
-            squares[i] += jnp.sum((value * value).reshape(-1, 8, LANES), axis=0)
+    squares = squares_of(other, taps, rows_of)
+    squares = [total + own_squares[i] for i, total in enumerate(squares)]
     scales = [
         lax.rsqrt(jnp.full((1, LANES), jnp.sum(total)) / float(out.size) + 1e-06)
         for total, out in zip(squares, (out2, out1))
@@ -554,6 +570,10 @@
         total.append(kept[span] + swap(sent[span], core).astype(F32))
     own = summed_everywhere(total, levels[1:])
     other = [swap(part_of, core) for part_of in own]
+    halves_of = chan // 2, w_first.shape[1] // 2
+    (squares,) = local_call(
+        part(squares_body, taps, halves_of), "squares", [shape((2, 8, LANES), F32)]
+    )(*own)
     step_second, step_first = local_call(
         part(norm_body, CHAINS),
         "normalize",
@@ -565,7 +585,7 @@
         ],
         scalars=1,
         out_hbm=(0, 1),
-    )(side, *own, *other)
+    )(side, squares, *own, *other)
     return (features, step_first, step_second)
 
 

time: 68.2 us -> 68.1 us (level)
    pallas_call x5 -> x6, Pallas kernels: 13.3 us -> 13.3 us  [call(): pl.pallas_call(body, out_shape=outs, in_specs=ins, out_specs=[hbm if i in...]
  transfers between devices with their start and end apart: 33 -> 33, of which waited for: 18 -> 17; matrix products, arithmetic and copies ran while one was open for 1% -> 1% of each run, Pallas kernels for 3% -> 3%
where the time goes in v9:
time: 68.1 us; the launch traced here: 67.9 us
  starting transfers between devices  41.1 us (60%)
  Pallas kernels  13.3 us (20%)
  waiting for transfers between devices  11.4 us (17%)
  between operations  1.12 us (2%)
    ppermute x27, starting transfers between devices, swap(): lax.ppermute(part, axis, [(i, i ^ bit) for i in range(lax.axis_size(axis))])  34.2 us
    pallas_call x6, Pallas kernels, call(): pl.pallas_call(body, out_shape=outs, in_specs=ins, out_specs=[hbm if i in...  13.3 us
    ppermute x27, waiting for transfers between devices, swap(): lax.ppermute(part, axis, [(i, i ^ bit) for i in range(lax.axis_size(axis))])  10.3 us
    ppermute x3, starting transfers between devices, exchange(): inner = lax.ppermute(inner, axis, [(i, i ^ 1) for i in range(count)])  4.95 us
    ppermute x3, starting transfers between devices, exchange(): outer = lax.ppermute(outer, axis, pairs + [(b, a) for a, b in pairs])  1.98 us
  transfers between devices with their start and end apart: 33, of which 17 were waited for; matrix products, arithmetic and copies ran while one was open for 1% of the time, Pallas kernels for 3%

profile of v9, /device:TPU:0, one launch (start us, length us, event | category | flops | bytes accessed | tf_op | source)
XLA Modules:
  0.0 67.9 jit_solution(14498862388448955146)
XLA Ops:
  0.7 1.1 %pack_own.1 = (bf16[336,128]{1,0:T(8,128)(2,1)S(1)}, bf16[336,128]{1,0:T(8,128)(2,1)S(1)}, bf16[656,128]{1,0:T(8,128)(2,1)S(1)}, bf16[656,128]{1,0:T(8,128)(2,1)...) custom-call(s32[1]{0:T(128)} %bitcast.odd.side, ...), custom_call_target="tpu_custom_call" | custom-call | tf_op jit(solution)/shard_map/pack_own/pallas_call | solution.py:471
  1.8 3.1 %collective-permute-start = (bf16[336,128]{1,0:T(8,128)(2,1)S(1)}, bf16[336,128]{1,0:T(8,128)(2,1)S(1)}, u32[]{:S(2)}, u32[]{:S(2)}) collective-permute-start(bf16[336,128]{1,0:T(8,128)(2,1)S(1)} %get-tuple-element.25), channel_id=1, source_target_pairs={{0,1},{1,0},{2,3},{3,2},{4,5},{5,4},{6,7},{7,6},{8,9},{9,8},{10,11... | collective-permute-start | bytes 258056 | tf_op jit(solution)/shard_map/ppermute | solution.py:77
  4.8 0.7 collective-permute-start.1
  5.6 0.7 collective-permute-start.3
  6.2 1.1 %collective-permute-done.inner_y = bf16[336,128]{1,0:T(8,128)(2,1)S(1)} collective-permute-done((bf16[336,128]{1,0:T(8,128)(2,1)S(1)}, bf16[336,128]{1,0:T(8,128)(2,1)S(1)}, u32[]{:S(2)}, u32[]{:S(2)}) %collective-permute-start) | collective-permute-done | bytes 86048 | tf_op jit(solution)/shard_map/ppermute | solution.py:77
  7.4 1.8 %collective-permute-start.4 = (bf16[384,128]{1,0:T(8,128)(2,1)S(1)}, bf16[384,128]{1,0:T(8,128)(2,1)S(1)}, u32[]{:S(2)}, u32[]{:S(2)}) collective-permute-start(bf16[384,128]{1,0:T(8,128)(2,1)S(1)} %get-tuple-element.31._), channel_id=1, source_target_pairs={{0,8},{8,0},{16,24},{24,16},{1,9},{9,1},{17,25},{25,17},{2,10},{10... | collective-permute-start | bytes 294920 | tf_op jit(solution)/shard_map/ppermute | solution.py:77
  9.2 0.7 collective-permute-start.5
  10.0 1.7 %weights.1 = (bf16[2304,256]{1,0:T(8,128)(2,1)S(1)}, bf16[4608,256]{1,0:T(8,128)(2,1)S(1)}, bf16[27,128,128]{2,1,0:T(8,128)(2,1)S(1)}) custom-call(bf16[27,64,128]{2,1,0:T(8,128)(2,1)} %hfirst.1, bf16[27,128,128]{2,1,0:T(8,128)(2,1)} %hsecond.1, bf16[384,128]{1,0:T(8,128)(2,1)S(1)} %get-tuple-element.31._), custom_call_target="tpu_custom_call" | custom-call | tf_op jit(solution)/shard_map/weights/pallas_call | solution.py:471
  11.8 8.6 %compute.1 = (bf16[4,8,32,128]{3,2,1,0:T(8,128)(2,1)}, bf16[27,96,128]{2,1,0:T(8,128)(2,1)S(1)}, f32[27,96,128]{2,1,0:T(8,128)S(1)}) custom-call(s32[1]{0:T(128)} %bitcast.odd.side, bf16[4,8,16,128]{3,2,1,0:T(8,128)(2,1)S(1)} %get-tuple-element.22.field, bf16[4,8,32,128]{3,2,1,0:T(8,128)(2,1)S(1)} %get-tuple-element.23.up, ...), custom_call_target="tpu_custom_call" | custom-call | tf_op jit(solution)/shard_map/compute/pallas_call | solution.py:471
  20.4 3.5 %collective-permute-start.22 = (bf16[864,128]{1,0:T(8,128)(2,1)S(1)}, bf16[864,128]{1,0:T(8,128)(2,1)S(1)}, u32[]{:S(2)}, u32[]{:S(2)}) collective-permute-start(bf16[864,128]{1,0:T(8,128)(2,1)S(1)} %bitcast.17), channel_id=1, source_target_pairs={{0,8},{8,0},{16,24},{24,16},{1,9},{9,1},{17,25},{25,17},{2,10},{10... | collective-permute-start | bytes 663560 | tf_op jit(solution)/shard_map/ppermute | solution.py:30
  24.0 0.4 collective-permute-start.6
  24.5 0.5 collective-permute-done.22
  25.0 5.1 %collective-permute-start.23 = (bf16[432,128]{1,0:T(8,128)(2,1)S(1)}, bf16[432,128]{1,0:T(8,128)(2,1)S(1)}, u32[]{:S(2)}, u32[]{:S(2)}) collective-permute-start(bf16[432,128]{1,0:T(8,128)(2,1)S(1)} %dynamic-slice_convert_fusion), channel_id=1, source_target_pairs={{0,2},{1,3},{2,0},{3,1},{4,6},{5,7},{6,4},{7,5},{8,10},{9,11},{10,... | collective-permute-start | bytes 331784 | tf_op jit(solution)/shard_map/ppermute | solution.py:30
  30.2 0.9 %collective-permute-start.15 = (bf16[432,128]{1,0:T(8,128)(2,1)S(1)}, bf16[432,128]{1,0:T(8,128)(2,1)S(1)}, u32[]{:S(2)}, u32[]{:S(2)}) collective-permute-start(bf16[432,128]{1,0:T(8,128)(2,1)S(1)} %dynamic-slice_convert_fusion.1), channel_id=1, source_target_pairs={{0,1},{1,0},{2,3},{3,2},{4,5},{5,4},{6,7},{7,6},{8,9},{9,8},{10,11... | collective-permute-start | bytes 331784 | tf_op jit(solution)/shard_map/ppermute | solution.py:30
  31.2 1.1 %collective-permute-start.7 = (bf16[432,128]{1,0:T(8,128)(2,1)S(1)}, bf16[432,128]{1,0:T(8,128)(2,1)S(1)}, u32[]{:S(2)}, u32[]{:S(2)}) collective-permute-start(bf16[432,128]{1,0:T(8,128)(2,1)S(1)} %dynamic-slice_convert_fusion.2), channel_id=1, source_target_pairs={{0,16},{8,24},{16,0},{24,8},{1,17},{9,25},{17,1},{25,9},{2,18},{10... | collective-permute-start | bytes 331784 | tf_op jit(solution)/shard_map/ppermute | solution.py:30
  32.3 1.4 %collective-permute-done.23 = bf16[432,128]{1,0:T(8,128)(2,1)S(1)} collective-permute-done((bf16[432,128]{1,0:T(8,128)(2,1)S(1)}, bf16[432,128]{1,0:T(8,128)(2,1)S(1)}, u32[]{:S(2)}, u32[]{:S(2)}) %collective-permute-start.23) | collective-permute-done | bytes 110624 | tf_op jit(solution)/shard_map/ppermute | solution.py:30
  33.8 1.2 %collective-permute-start.24 = (bf16[216,128]{1,0:T(8,128)(2,1)S(1)}, bf16[216,128]{1,0:T(8,128)(2,1)S(1)}, u32[]{:S(2)}, u32[]{:S(2)}) collective-permute-start(bf16[216,128]{1,0:T(8,128)(2,1)S(1)} %dynamic-slice_convert_fusion.3), channel_id=1, source_target_pairs={{0,16},{8,24},{16,0},{24,8},{1,17},{9,25},{17,1},{25,9},{2,18},{10... | collective-permute-start | bytes 165896 | tf_op jit(solution)/shard_map/ppermute | solution.py:30
  35.0 0.3 collective-permute-done.15
  35.4 1.5 %collective-permute-start.16 = (bf16[216,128]{1,0:T(8,128)(2,1)S(1)}, bf16[216,128]{1,0:T(8,128)(2,1)S(1)}, u32[]{:S(2)}, u32[]{:S(2)}) collective-permute-start(bf16[216,128]{1,0:T(8,128)(2,1)S(1)} %dynamic-slice_convert_fusion.4), channel_id=1, source_target_pairs={{0,2},{1,3},{2,0},{3,1},{4,6},{5,7},{6,4},{7,5},{8,10},{9,11},{10,... | collective-permute-start | bytes 165896 | tf_op jit(solution)/shard_map/ppermute | solution.py:30
  36.9 0.7 %collective-permute-start.8 = (bf16[216,128]{1,0:T(8,128)(2,1)S(1)}, bf16[216,128]{1,0:T(8,128)(2,1)S(1)}, u32[]{:S(2)}, u32[]{:S(2)}) collective-permute-start(bf16[216,128]{1,0:T(8,128)(2,1)S(1)} %dynamic-slice_convert_fusion.5), channel_id=1, source_target_pairs={{0,1},{1,0},{2,3},{3,2},{4,5},{5,4},{6,7},{7,6},{8,9},{9,8},{10,11... | collective-permute-start | bytes 165896 | tf_op jit(solution)/shard_map/ppermute | solution.py:30
  37.6 0.4 collective-permute-done.24
  38.1 1.1 %collective-permute-start.25 = (bf16[108,128]{1,0:T(8,128)(2,1)S(1)}, bf16[108,128]{1,0:T(8,128)(2,1)S(1)}, u32[]{:S(2)}, u32[]{:S(2)}) collective-permute-start(bf16[108,128]{1,0:T(8,128)(2,1)S(1)} %dynamic-slice_convert_fusion.6), channel_id=1, source_target_pairs={{0,1},{1,0},{2,3},{3,2},{4,5},{5,4},{6,7},{7,6},{8,9},{9,8},{10,11... | collective-permute-start | bytes 82952 | tf_op jit(solution)/shard_map/ppermute | solution.py:30
  39.1 0.5 collective-permute-done.16
  39.7 1.2 %collective-permute-start.17 = (bf16[108,128]{1,0:T(8,128)(2,1)S(1)}, bf16[108,128]{1,0:T(8,128)(2,1)S(1)}, u32[]{:S(2)}, u32[]{:S(2)}) collective-permute-start(bf16[108,128]{1,0:T(8,128)(2,1)S(1)} %dynamic-slice_convert_fusion.7), channel_id=1, source_target_pairs={{0,16},{8,24},{16,0},{24,8},{1,17},{9,25},{17,1},{25,9},{2,18},{10... | collective-permute-start | bytes 82952 | tf_op jit(solution)/shard_map/ppermute | solution.py:30
  40.9 0.3 collective-permute-done.8
  41.2 0.9 %collective-permute-start.9 = (bf16[108,128]{1,0:T(8,128)(2,1)S(1)}, bf16[108,128]{1,0:T(8,128)(2,1)S(1)}, u32[]{:S(2)}, u32[]{:S(2)}) collective-permute-start(bf16[108,128]{1,0:T(8,128)(2,1)S(1)} %dynamic-slice_convert_fusion.8), channel_id=1, source_target_pairs={{0,2},{1,3},{2,0},{3,1},{4,6},{5,7},{6,4},{7,5},{8,10},{9,11},{10,... | collective-permute-start | bytes 82952 | tf_op jit(solution)/shard_map/ppermute | solution.py:30
  42.2 2.7 %collective-permute-start.26 = (bf16[108,128]{1,0:T(8,128)(2,1)S(1)}, bf16[108,128]{1,0:T(8,128)(2,1)S(1)}, u32[]{:S(2)}, u32[]{:S(2)}) collective-permute-start(bf16[108,128]{1,0:T(8,128)(2,1)S(1)} %add_convert_fusion.1), channel_id=1, source_target_pairs={{0,4},{1,5},{2,6},{3,7},{4,0},{5,1},{6,2},{7,3},{8,12},{9,13},{10,... | collective-permute-start | bytes 82952 | tf_op jit(solution)/shard_map/ppermute | solution.py:30
  44.9 1.4 %collective-permute-start.18 = (bf16[108,128]{1,0:T(8,128)(2,1)S(1)}, bf16[108,128]{1,0:T(8,128)(2,1)S(1)}, u32[]{:S(2)}, u32[]{:S(2)}) collective-permute-start(bf16[108,128]{1,0:T(8,128)(2,1)S(1)} %add_convert_fusion.3), channel_id=1, source_target_pairs={{0,4},{1,5},{2,6},{3,7},{4,0},{5,1},{6,2},{7,3},{8,12},{9,13},{10,... | collective-permute-start | bytes 82952 | tf_op jit(solution)/shard_map/ppermute | solution.py:30
  46.3 1.6 %collective-permute-start.10 = (bf16[108,128]{1,0:T(8,128)(2,1)S(1)}, bf16[108,128]{1,0:T(8,128)(2,1)S(1)}, u32[]{:S(2)}, u32[]{:S(2)}) collective-permute-start(bf16[108,128]{1,0:T(8,128)(2,1)S(1)} %add_convert_fusion.5), channel_id=1, source_target_pairs={{0,4},{1,5},{2,6},{3,7},{4,0},{5,1},{6,2},{7,3},{8,12},{9,13},{10,... | collective-permute-start | bytes 82952 | tf_op jit(solution)/shard_map/ppermute | solution.py:30
  48.0 1.2 %collective-permute-start.27 = (bf16[108,128]{1,0:T(8,128)(2,1)S(1)}, bf16[108,128]{1,0:T(8,128)(2,1)S(1)}, u32[]{:S(2)}, u32[]{:S(2)}) collective-permute-start(bf16[108,128]{1,0:T(8,128)(2,1)S(1)} %add_convert_fusion), channel_id=1, source_target_pairs={{0,1},{1,0},{2,3},{3,2},{4,5},{5,4},{6,7},{7,6},{8,9},{9,8},{10,11... | collective-permute-start | bytes 82952 | tf_op jit(solution)/shard_map/ppermute | solution.py:30
  49.1 0.6 collective-permute-done.18
  49.7 1.2 %collective-permute-start.19 = (bf16[108,128]{1,0:T(8,128)(2,1)S(1)}, bf16[108,128]{1,0:T(8,128)(2,1)S(1)}, u32[]{:S(2)}, u32[]{:S(2)}) collective-permute-start(bf16[108,128]{1,0:T(8,128)(2,1)S(1)} %add_convert_fusion.2), channel_id=1, source_target_pairs={{0,16},{8,24},{16,0},{24,8},{1,17},{9,25},{17,1},{25,9},{2,18},{10... | collective-permute-start | bytes 82952 | tf_op jit(solution)/shard_map/ppermute | solution.py:30
  50.9 0.3 collective-permute-done.10
  51.2 1.6 %collective-permute-start.11 = (bf16[108,128]{1,0:T(8,128)(2,1)S(1)}, bf16[108,128]{1,0:T(8,128)(2,1)S(1)}, u32[]{:S(2)}, u32[]{:S(2)}) collective-permute-start(bf16[108,128]{1,0:T(8,128)(2,1)S(1)} %add_convert_fusion.4), channel_id=1, source_target_pairs={{0,2},{1,3},{2,0},{3,1},{4,6},{5,7},{6,4},{7,5},{8,10},{9,11},{10,... | collective-permute-start | bytes 82952 | tf_op jit(solution)/shard_map/ppermute | solution.py:30
  52.8 0.8 %collective-permute-start.28 = (bf16[216,128]{1,0:T(8,128)(2,1)S(1)}, bf16[216,128]{1,0:T(8,128)(2,1)S(1)}, u32[]{:S(2)}, u32[]{:S(2)}) collective-permute-start(bf16[216,128]{1,0:T(8,128)(2,1)S(1)} %maximum_select_fusion.8), channel_id=1, source_target_pairs={{0,16},{8,24},{16,0},{24,8},{1,17},{9,25},{17,1},{25,9},{2,18},{10... | collective-permute-start | bytes 165896 | tf_op jit(solution)/shard_map/ppermute | solution.py:30
  53.7 1.6 %collective-permute-start.20 = (bf16[216,128]{1,0:T(8,128)(2,1)S(1)}, bf16[216,128]{1,0:T(8,128)(2,1)S(1)}, u32[]{:S(2)}, u32[]{:S(2)}) collective-permute-start(bf16[216,128]{1,0:T(8,128)(2,1)S(1)} %maximum_select_fusion.7), channel_id=1, source_target_pairs={{0,2},{1,3},{2,0},{3,1},{4,6},{5,7},{6,4},{7,5},{8,10},{9,11},{10,... | collective-permute-start | bytes 165896 | tf_op jit(solution)/shard_map/ppermute | solution.py:30
  55.5 0.7 collective-permute-start.12
  56.1 1.1 %collective-permute-done.28 = bf16[216,128]{1,0:T(8,128)(2,1)S(1)} collective-permute-done((bf16[216,128]{1,0:T(8,128)(2,1)S(1)}, bf16[216,128]{1,0:T(8,128)(2,1)S(1)}, u32[]{:S(2)}, u32[]{:S(2)}) %collective-permute-start.28) | collective-permute-done | bytes 55328 | tf_op jit(solution)/shard_map/ppermute | solution.py:30
  57.3 1.0 %collective-permute-start.29 = (bf16[432,128]{1,0:T(8,128)(2,1)S(1)}, bf16[432,128]{1,0:T(8,128)(2,1)S(1)}, u32[]{:S(2)}, u32[]{:S(2)}) collective-permute-start(bf16[432,128]{1,0:T(8,128)(2,1)S(1)} %maximum_select_fusion.5), channel_id=1, source_target_pairs={{0,2},{1,3},{2,0},{3,1},{4,6},{5,7},{6,4},{7,5},{8,10},{9,11},{10,... | collective-permute-start | bytes 331784 | tf_op jit(solution)/shard_map/ppermute | solution.py:30
  58.3 1.2 %collective-permute-start.21 = (bf16[432,128]{1,0:T(8,128)(2,1)S(1)}, bf16[432,128]{1,0:T(8,128)(2,1)S(1)}, u32[]{:S(2)}, u32[]{:S(2)}) collective-permute-start(bf16[432,128]{1,0:T(8,128)(2,1)S(1)} %maximum_select_fusion.4), channel_id=1, source_target_pairs={{0,1},{1,0},{2,3},{3,2},{4,5},{5,4},{6,7},{7,6},{8,9},{9,8},{10,11... | collective-permute-start | bytes 331784 | tf_op jit(solution)/shard_map/ppermute | solution.py:30
  59.5 0.2 collective-permute-done.12
  59.7 1.3 %collective-permute-start.13 = (bf16[432,128]{1,0:T(8,128)(2,1)S(1)}, bf16[432,128]{1,0:T(8,128)(2,1)S(1)}, u32[]{:S(2)}, u32[]{:S(2)}) collective-permute-start(bf16[432,128]{1,0:T(8,128)(2,1)S(1)} %maximum_select_fusion.3), channel_id=1, source_target_pairs={{0,16},{8,24},{16,0},{24,8},{1,17},{9,25},{17,1},{25,9},{2,18},{10... | collective-permute-start | bytes 331784 | tf_op jit(solution)/shard_map/ppermute | solution.py:30
  61.0 1.1 %collective-permute-done.29 = bf16[432,128]{1,0:T(8,128)(2,1)S(1)} collective-permute-done((bf16[432,128]{1,0:T(8,128)(2,1)S(1)}, bf16[432,128]{1,0:T(8,128)(2,1)S(1)}, u32[]{:S(2)}, u32[]{:S(2)}) %collective-permute-start.29) | collective-permute-done | bytes 110624 | tf_op jit(solution)/shard_map/ppermute | solution.py:30
  62.3 0.9 %collective-permute-done.21 = bf16[432,128]{1,0:T(8,128)(2,1)S(1)} collective-permute-done((bf16[432,128]{1,0:T(8,128)(2,1)S(1)}, bf16[432,128]{1,0:T(8,128)(2,1)S(1)}, u32[]{:S(2)}, u32[]{:S(2)}) %collective-permute-start.21) | collective-permute-done | bytes 110624 | tf_op jit(solution)/shard_map/ppermute | solution.py:30
  63.3 1.2 %collective-permute-done.13 = bf16[432,128]{1,0:T(8,128)(2,1)S(1)} collective-permute-done((bf16[432,128]{1,0:T(8,128)(2,1)S(1)}, bf16[432,128]{1,0:T(8,128)(2,1)S(1)}, u32[]{:S(2)}, u32[]{:S(2)}) %collective-permute-start.13) | collective-permute-done | bytes 110624 | tf_op jit(solution)/shard_map/ppermute | solution.py:30
  64.7 0.1 squares.1.own_squares
  64.8 1.3 %collective-permute-done.30.refs_3_ = bf16[864,128]{1,0:T(8,128)(2,1)S(1)} collective-permute-done((bf16[864,128]{1,0:T(8,128)(2,1)S(1)}, bf16[864,128]{1,0:T(8,128)(2,1)S(1)}, u32[]{:S(2)}, u32[]{:S(2)}) %collective-permute-start.30) | collective-permute-done | bytes 221216 | tf_op jit(solution)/shard_map/ppermute | solution.py:30
  66.1 1.8 %normalize.1 = (f32[27,128,128]{2,1,0:T(8,128)}, f32[27,64,128]{2,1,0:T(8,128)}) custom-call(s32[1]{0:T(128)} %bitcast.odd.side, f32[2,8,128]{2,1,0:T(8,128)S(1)} %squares.1.own_squares, bf16[864,128]{1,0:T(8,128)(2,1)S(1)} %maximum_select_fusion.refs_0_, bf16[864,128]{1,0:T(8,128)(2,1)S(1)} %maximum_select_fusion.1.refs_1_, ...), custom_call_target="tpu_custom_call" | custom-call | tf_op jit(solution)/shard_map/normalize/pallas_call | solution.py:471
  (63 shorter events, 1.6 us)
Async XLA Ops:
  0.6 11.1 %copy-start = (f32[128]{0:T(128)S(1)}, f32[128]{0:T(128)}, u32[]{:S(2)}) copy-start(f32[128]{0:T(128)} %param.10) | copy-start | bytes 1540
  0.6 11.1 %copy-start.1 = (f32[128]{0:T(128)S(1)}, f32[128]{0:T(128)}, u32[]{:S(2)}) copy-start(f32[128]{0:T(128)} %param.12) | copy-start | bytes 1540
  1.8 5.6 %collective-permute-start = (bf16[336,128]{1,0:T(8,128)(2,1)S(1)}, bf16[336,128]{1,0:T(8,128)(2,1)S(1)}, u32[]{:S(2)}, u32[]{:S(2)}) collective-permute-start(bf16[336,128]{1,0:T(8,128)(2,1)S(1)} %get-tuple-element.25), channel_id=1, source_target_pairs={{0,1},{1,0},{2,3},{3,2},{4,5},{5,4},{6,7},{7,6},{8,9},{9,8},{10,11... | collective-permute-start | bytes 258056 | tf_op jit(solution)/shard_map/ppermute | solution.py:77
  4.8 2.5 %collective-permute-start.1 = (bf16[336,128]{1,0:T(8,128)(2,1)S(1)}, bf16[336,128]{1,0:T(8,128)(2,1)S(1)}, u32[]{:S(2)}, u32[]{:S(2)}) collective-permute-start(bf16[336,128]{1,0:T(8,128)(2,1)S(1)} %get-tuple-element.26), channel_id=1, source_target_pairs={{1,2},{3,4},{5,6},{2,1},{4,3},{6,5},{9,10},{11,12},{13,14},{10,9},... | collective-permute-start | bytes 258056 | tf_op jit(solution)/shard_map/ppermute | solution.py:76
  5.5 6.2 %collective-permute-start.2 = (bf16[656,128]{1,0:T(8,128)(2,1)S(1)}, bf16[656,128]{1,0:T(8,128)(2,1)S(1)}, u32[]{:S(2)}, u32[]{:S(2)}) collective-permute-start(bf16[656,128]{1,0:T(8,128)(2,1)S(1)} %get-tuple-element.29), channel_id=1, source_target_pairs={{0,8},{8,0},{16,24},{24,16},{1,9},{9,1},{17,25},{25,17},{2,10},{10... | collective-permute-start | bytes 503816 | tf_op jit(solution)/shard_map/ppermute | solution.py:77
  5.6 6.1 %collective-permute-start.3 = (bf16[656,128]{1,0:T(8,128)(2,1)S(1)}, bf16[656,128]{1,0:T(8,128)(2,1)S(1)}, u32[]{:S(2)}, u32[]{:S(2)}) collective-permute-start(bf16[656,128]{1,0:T(8,128)(2,1)S(1)} %get-tuple-element.30), channel_id=1, source_target_pairs={{8,16},{16,8},{9,17},{17,9},{10,18},{18,10},{11,19},{19,11},{12,20... | collective-permute-start | bytes 503816 | tf_op jit(solution)/shard_map/ppermute | solution.py:76
  7.4 4.3 %collective-permute-start.4 = (bf16[384,128]{1,0:T(8,128)(2,1)S(1)}, bf16[384,128]{1,0:T(8,128)(2,1)S(1)}, u32[]{:S(2)}, u32[]{:S(2)}) collective-permute-start(bf16[384,128]{1,0:T(8,128)(2,1)S(1)} %get-tuple-element.31._), channel_id=1, source_target_pairs={{0,8},{8,0},{16,24},{24,16},{1,9},{9,1},{17,25},{25,17},{2,10},{10... | collective-permute-start | bytes 294920 | tf_op jit(solution)/shard_map/ppermute | solution.py:77
  9.2 2.5 %collective-permute-start.5 = (bf16[384,128]{1,0:T(8,128)(2,1)S(1)}, bf16[384,128]{1,0:T(8,128)(2,1)S(1)}, u32[]{:S(2)}, u32[]{:S(2)}) collective-permute-start(bf16[384,128]{1,0:T(8,128)(2,1)S(1)} %get-tuple-element.32), channel_id=1, source_target_pairs={{8,16},{16,8},{9,17},{17,9},{10,18},{18,10},{11,19},{19,11},{12,20... | collective-permute-start | bytes 294920 | tf_op jit(solution)/shard_map/ppermute | solution.py:76
  20.4 4.6 %collective-permute-start.22 = (bf16[864,128]{1,0:T(8,128)(2,1)S(1)}, bf16[864,128]{1,0:T(8,128)(2,1)S(1)}, u32[]{:S(2)}, u32[]{:S(2)}) collective-permute-start(bf16[864,128]{1,0:T(8,128)(2,1)S(1)} %bitcast.17), channel_id=1, source_target_pairs={{0,8},{8,0},{16,24},{24,16},{1,9},{9,1},{17,25},{25,17},{2,10},{10... | collective-permute-start | bytes 663560 | tf_op jit(solution)/shard_map/ppermute | solution.py:30
  23.9 6.3 %collective-permute-start.14 = (bf16[864,128]{1,0:T(8,128)(2,1)S(1)}, bf16[864,128]{1,0:T(8,128)(2,1)S(1)}, u32[]{:S(2)}, u32[]{:S(2)}) collective-permute-start(bf16[864,128]{1,0:T(8,128)(2,1)S(1)} %bitcast.16), channel_id=1, source_target_pairs={{0,8},{8,0},{16,24},{24,16},{1,9},{9,1},{17,25},{25,17},{2,10},{10... | collective-permute-start | bytes 663560 | tf_op jit(solution)/shard_map/ppermute | solution.py:30
  24.0 7.2 %collective-permute-start.6 = (bf16[864,128]{1,0:T(8,128)(2,1)S(1)}, bf16[864,128]{1,0:T(8,128)(2,1)S(1)}, u32[]{:S(2)}, u32[]{:S(2)}) collective-permute-start(bf16[864,128]{1,0:T(8,128)(2,1)S(1)} %bitcast.15), channel_id=1, source_target_pairs={{0,8},{8,0},{16,24},{24,16},{1,9},{9,1},{17,25},{25,17},{2,10},{10... | collective-permute-start | bytes 663560 | tf_op jit(solution)/shard_map/ppermute | solution.py:30
  25.0 8.7 %collective-permute-start.23 = (bf16[432,128]{1,0:T(8,128)(2,1)S(1)}, bf16[432,128]{1,0:T(8,128)(2,1)S(1)}, u32[]{:S(2)}, u32[]{:S(2)}) collective-permute-start(bf16[432,128]{1,0:T(8,128)(2,1)S(1)} %dynamic-slice_convert_fusion), channel_id=1, source_target_pairs={{0,2},{1,3},{2,0},{3,1},{4,6},{5,7},{6,4},{7,5},{8,10},{9,11},{10,... | collective-permute-start | bytes 331784 | tf_op jit(solution)/shard_map/ppermute | solution.py:30
  30.2 5.1 %collective-permute-start.15 = (bf16[432,128]{1,0:T(8,128)(2,1)S(1)}, bf16[432,128]{1,0:T(8,128)(2,1)S(1)}, u32[]{:S(2)}, u32[]{:S(2)}) collective-permute-start(bf16[432,128]{1,0:T(8,128)(2,1)S(1)} %dynamic-slice_convert_fusion.1), channel_id=1, source_target_pairs={{0,1},{1,0},{2,3},{3,2},{4,5},{5,4},{6,7},{7,6},{8,9},{9,8},{10,11... | collective-permute-start | bytes 331784 | tf_op jit(solution)/shard_map/ppermute | solution.py:30
  31.2 5.7 %collective-permute-start.7 = (bf16[432,128]{1,0:T(8,128)(2,1)S(1)}, bf16[432,128]{1,0:T(8,128)(2,1)S(1)}, u32[]{:S(2)}, u32[]{:S(2)}) collective-permute-start(bf16[432,128]{1,0:T(8,128)(2,1)S(1)} %dynamic-slice_convert_fusion.2), channel_id=1, source_target_pairs={{0,16},{8,24},{16,0},{24,8},{1,17},{9,25},{17,1},{25,9},{2,18},{10... | collective-permute-start | bytes 331784 | tf_op jit(solution)/shard_map/ppermute | solution.py:30
  33.8 4.2 %collective-permute-start.24 = (bf16[216,128]{1,0:T(8,128)(2,1)S(1)}, bf16[216,128]{1,0:T(8,128)(2,1)S(1)}, u32[]{:S(2)}, u32[]{:S(2)}) collective-permute-start(bf16[216,128]{1,0:T(8,128)(2,1)S(1)} %dynamic-slice_convert_fusion.3), channel_id=1, source_target_pairs={{0,16},{8,24},{16,0},{24,8},{1,17},{9,25},{17,1},{25,9},{2,18},{10... | collective-permute-start | bytes 165896 | tf_op jit(solution)/shard_map/ppermute | solution.py:30
  35.4 4.2 %collective-permute-start.16 = (bf16[216,128]{1,0:T(8,128)(2,1)S(1)}, bf16[216,128]{1,0:T(8,128)(2,1)S(1)}, u32[]{:S(2)}, u32[]{:S(2)}) collective-permute-start(bf16[216,128]{1,0:T(8,128)(2,1)S(1)} %dynamic-slice_convert_fusion.4), channel_id=1, source_target_pairs={{0,2},{1,3},{2,0},{3,1},{4,6},{5,7},{6,4},{7,5},{8,10},{9,11},{10,... | collective-permute-start | bytes 165896 | tf_op jit(solution)/shard_map/ppermute | solution.py:30
  36.9 4.2 %collective-permute-start.8 = (bf16[216,128]{1,0:T(8,128)(2,1)S(1)}, bf16[216,128]{1,0:T(8,128)(2,1)S(1)}, u32[]{:S(2)}, u32[]{:S(2)}) collective-permute-start(bf16[216,128]{1,0:T(8,128)(2,1)S(1)} %dynamic-slice_convert_fusion.5), channel_id=1, source_target_pairs={{0,1},{1,0},{2,3},{3,2},{4,5},{5,4},{6,7},{7,6},{8,9},{9,8},{10,11... | collective-permute-start | bytes 165896 | tf_op jit(solution)/shard_map/ppermute | solution.py:30
  38.1 4.1 %collective-permute-start.25 = (bf16[108,128]{1,0:T(8,128)(2,1)S(1)}, bf16[108,128]{1,0:T(8,128)(2,1)S(1)}, u32[]{:S(2)}, u32[]{:S(2)}) collective-permute-start(bf16[108,128]{1,0:T(8,128)(2,1)S(1)} %dynamic-slice_convert_fusion.6), channel_id=1, source_target_pairs={{0,1},{1,0},{2,3},{3,2},{4,5},{5,4},{6,7},{7,6},{8,9},{9,8},{10,11... | collective-permute-start | bytes 82952 | tf_op jit(solution)/shard_map/ppermute | solution.py:30
  39.7 5.2 %collective-permute-start.17 = (bf16[108,128]{1,0:T(8,128)(2,1)S(1)}, bf16[108,128]{1,0:T(8,128)(2,1)S(1)}, u32[]{:S(2)}, u32[]{:S(2)}) collective-permute-start(bf16[108,128]{1,0:T(8,128)(2,1)S(1)} %dynamic-slice_convert_fusion.7), channel_id=1, source_target_pairs={{0,16},{8,24},{16,0},{24,8},{1,17},{9,25},{17,1},{25,9},{2,18},{10... | collective-permute-start | bytes 82952 | tf_op jit(solution)/shard_map/ppermute | solution.py:30
  41.2 5.1 %collective-permute-start.9 = (bf16[108,128]{1,0:T(8,128)(2,1)S(1)}, bf16[108,128]{1,0:T(8,128)(2,1)S(1)}, u32[]{:S(2)}, u32[]{:S(2)}) collective-permute-start(bf16[108,128]{1,0:T(8,128)(2,1)S(1)} %dynamic-slice_convert_fusion.8), channel_id=1, source_target_pairs={{0,2},{1,3},{2,0},{3,1},{4,6},{5,7},{6,4},{7,5},{8,10},{9,11},{10,... | collective-permute-start | bytes 82952 | tf_op jit(solution)/shard_map/ppermute | solution.py:30
  42.2 5.8 %collective-permute-start.26 = (bf16[108,128]{1,0:T(8,128)(2,1)S(1)}, bf16[108,128]{1,0:T(8,128)(2,1)S(1)}, u32[]{:S(2)}, u32[]{:S(2)}) collective-permute-start(bf16[108,128]{1,0:T(8,128)(2,1)S(1)} %add_convert_fusion.1), channel_id=1, source_target_pairs={{0,4},{1,5},{2,6},{3,7},{4,0},{5,1},{6,2},{7,3},{8,12},{9,13},{10,... | collective-permute-start | bytes 82952 | tf_op jit(solution)/shard_map/ppermute | solution.py:30
  44.9 4.8 %collective-permute-start.18 = (bf16[108,128]{1,0:T(8,128)(2,1)S(1)}, bf16[108,128]{1,0:T(8,128)(2,1)S(1)}, u32[]{:S(2)}, u32[]{:S(2)}) collective-permute-start(bf16[108,128]{1,0:T(8,128)(2,1)S(1)} %add_convert_fusion.3), channel_id=1, source_target_pairs={{0,4},{1,5},{2,6},{3,7},{4,0},{5,1},{6,2},{7,3},{8,12},{9,13},{10,... | collective-permute-start | bytes 82952 | tf_op jit(solution)/shard_map/ppermute | solution.py:30
  46.3 4.9 %collective-permute-start.10 = (bf16[108,128]{1,0:T(8,128)(2,1)S(1)}, bf16[108,128]{1,0:T(8,128)(2,1)S(1)}, u32[]{:S(2)}, u32[]{:S(2)}) collective-permute-start(bf16[108,128]{1,0:T(8,128)(2,1)S(1)} %add_convert_fusion.5), channel_id=1, source_target_pairs={{0,4},{1,5},{2,6},{3,7},{4,0},{5,1},{6,2},{7,3},{8,12},{9,13},{10,... | collective-permute-start | bytes 82952 | tf_op jit(solution)/shard_map/ppermute | solution.py:30
  48.0 4.8 %collective-permute-start.27 = (bf16[108,128]{1,0:T(8,128)(2,1)S(1)}, bf16[108,128]{1,0:T(8,128)(2,1)S(1)}, u32[]{:S(2)}, u32[]{:S(2)}) collective-permute-start(bf16[108,128]{1,0:T(8,128)(2,1)S(1)} %add_convert_fusion), channel_id=1, source_target_pairs={{0,1},{1,0},{2,3},{3,2},{4,5},{5,4},{6,7},{7,6},{8,9},{9,8},{10,11... | collective-permute-start | bytes 82952 | tf_op jit(solution)/shard_map/ppermute | solution.py:30
  49.7 3.9 %collective-permute-start.19 = (bf16[108,128]{1,0:T(8,128)(2,1)S(1)}, bf16[108,128]{1,0:T(8,128)(2,1)S(1)}, u32[]{:S(2)}, u32[]{:S(2)}) collective-permute-start(bf16[108,128]{1,0:T(8,128)(2,1)S(1)} %add_convert_fusion.2), channel_id=1, source_target_pairs={{0,16},{8,24},{16,0},{24,8},{1,17},{9,25},{17,1},{25,9},{2,18},{10... | collective-permute-start | bytes 82952 | tf_op jit(solution)/shard_map/ppermute | solution.py:30
  51.2 4.2 %collective-permute-start.11 = (bf16[108,128]{1,0:T(8,128)(2,1)S(1)}, bf16[108,128]{1,0:T(8,128)(2,1)S(1)}, u32[]{:S(2)}, u32[]{:S(2)}) collective-permute-start(bf16[108,128]{1,0:T(8,128)(2,1)S(1)} %add_convert_fusion.4), channel_id=1, source_target_pairs={{0,2},{1,3},{2,0},{3,1},{4,6},{5,7},{6,4},{7,5},{8,10},{9,11},{10,... | collective-permute-start | bytes 82952 | tf_op jit(solution)/shard_map/ppermute | solution.py:30
  52.8 4.4 %collective-permute-start.28 = (bf16[216,128]{1,0:T(8,128)(2,1)S(1)}, bf16[216,128]{1,0:T(8,128)(2,1)S(1)}, u32[]{:S(2)}, u32[]{:S(2)}) collective-permute-start(bf16[216,128]{1,0:T(8,128)(2,1)S(1)} %maximum_select_fusion.8), channel_id=1, source_target_pairs={{0,16},{8,24},{16,0},{24,8},{1,17},{9,25},{17,1},{25,9},{2,18},{10... | collective-permute-start | bytes 165896 | tf_op jit(solution)/shard_map/ppermute | solution.py:30
  53.7 4.6 %collective-permute-start.20 = (bf16[216,128]{1,0:T(8,128)(2,1)S(1)}, bf16[216,128]{1,0:T(8,128)(2,1)S(1)}, u32[]{:S(2)}, u32[]{:S(2)}) collective-permute-start(bf16[216,128]{1,0:T(8,128)(2,1)S(1)} %maximum_select_fusion.7), channel_id=1, source_target_pairs={{0,2},{1,3},{2,0},{3,1},{4,6},{5,7},{6,4},{7,5},{8,10},{9,11},{10,... | collective-permute-start | bytes 165896 | tf_op jit(solution)/shard_map/ppermute | solution.py:30
  55.5 4.2 %collective-permute-start.12 = (bf16[216,128]{1,0:T(8,128)(2,1)S(1)}, bf16[216,128]{1,0:T(8,128)(2,1)S(1)}, u32[]{:S(2)}, u32[]{:S(2)}) collective-permute-start(bf16[216,128]{1,0:T(8,128)(2,1)S(1)} %maximum_select_fusion.6), channel_id=1, source_target_pairs={{0,1},{1,0},{2,3},{3,2},{4,5},{5,4},{6,7},{7,6},{8,9},{9,8},{10,11... | collective-permute-start | bytes 165896 | tf_op jit(solution)/shard_map/ppermute | solution.py:30
  57.3 4.8 %collective-permute-start.29 = (bf16[432,128]{1,0:T(8,128)(2,1)S(1)}, bf16[432,128]{1,0:T(8,128)(2,1)S(1)}, u32[]{:S(2)}, u32[]{:S(2)}) collective-permute-start(bf16[432,128]{1,0:T(8,128)(2,1)S(1)} %maximum_select_fusion.5), channel_id=1, source_target_pairs={{0,2},{1,3},{2,0},{3,1},{4,6},{5,7},{6,4},{7,5},{8,10},{9,11},{10,... | collective-permute-start | bytes 331784 | tf_op jit(solution)/shard_map/ppermute | solution.py:30
  58.3 4.8 %collective-permute-start.21 = (bf16[432,128]{1,0:T(8,128)(2,1)S(1)}, bf16[432,128]{1,0:T(8,128)(2,1)S(1)}, u32[]{:S(2)}, u32[]{:S(2)}) collective-permute-start(bf16[432,128]{1,0:T(8,128)(2,1)S(1)} %maximum_select_fusion.4), channel_id=1, source_target_pairs={{0,1},{1,0},{2,3},{3,2},{4,5},{5,4},{6,7},{7,6},{8,9},{9,8},{10,11... | collective-permute-start | bytes 331784 | tf_op jit(solution)/shard_map/ppermute | solution.py:30
  59.7 4.8 %collective-permute-start.13 = (bf16[432,128]{1,0:T(8,128)(2,1)S(1)}, bf16[432,128]{1,0:T(8,128)(2,1)S(1)}, u32[]{:S(2)}, u32[]{:S(2)}) collective-permute-start(bf16[432,128]{1,0:T(8,128)(2,1)S(1)} %maximum_select_fusion.3), channel_id=1, source_target_pairs={{0,16},{8,24},{16,0},{24,8},{1,17},{9,25},{17,1},{25,9},{2,18},{10... | collective-permute-start | bytes 331784 | tf_op jit(solution)/shard_map/ppermute | solution.py:30
  62.2 2.6 %collective-permute-start.32 = (bf16[864,128]{1,0:T(8,128)(2,1)S(1)}, bf16[864,128]{1,0:T(8,128)(2,1)S(1)}, u32[]{:S(2)}, u32[]{:S(2)}) collective-permute-start(bf16[864,128]{1,0:T(8,128)(2,1)S(1)} %maximum_select_fusion.2.refs_2_), channel_id=1, source_target_pairs={{0,8},{8,0},{16,24},{24,16},{1,9},{9,1},{17,25},{25,17},{2,10},{10... | collective-permute-start | bytes 663560 | tf_op jit(solution)/shard_map/ppermute | solution.py:30
  63.2 1.6 %collective-permute-start.31 = (bf16[864,128]{1,0:T(8,128)(2,1)S(1)}, bf16[864,128]{1,0:T(8,128)(2,1)S(1)}, u32[]{:S(2)}, u32[]{:S(2)}) collective-permute-start(bf16[864,128]{1,0:T(8,128)(2,1)S(1)} %maximum_select_fusion.1.refs_1_), channel_id=1, source_target_pairs={{0,8},{8,0},{16,24},{24,16},{1,9},{9,1},{17,25},{25,17},{2,10},{10... | collective-permute-start | bytes 663560 | tf_op jit(solution)/shard_map/ppermute | solution.py:30
  64.6 1.5 %collective-permute-start.30 = (bf16[864,128]{1,0:T(8,128)(2,1)S(1)}, bf16[864,128]{1,0:T(8,128)(2,1)S(1)}, u32[]{:S(2)}, u32[]{:S(2)}) collective-permute-start(bf16[864,128]{1,0:T(8,128)(2,1)S(1)} %maximum_select_fusion.refs_0_), channel_id=1, source_target_pairs={{0,8},{8,0},{16,24},{24,16},{1,9},{9,1},{17,25},{25,17},{2,10},{10... | collective-permute-start | bytes 663560 | tf_op jit(solution)/shard_map/ppermute | solution.py:30
